TPU v7x, 128 devices: a whole 4x4x4 slice. The times are simulated.
128 devices in a mesh: grp: 32 (over z, x_hi, y), head: 4 (over x_lo, core).
Axes of the slice: x: 4 (x_hi: 2, x_lo: 2; x = x_hi * 2 + x_lo), y: 4, z: 4, core: 2. Of those that a mesh axis runs over, the one named last changes fastest.
Arguments:
- hidden_in: bfloat16 [32, 128, 2048], P('grp'), may hold values from -6 to 6
- attn_gain: float32 [2048], replicated, may hold values from 0.1 to 1.9
- w_query: bfloat16 [2048, 2048], P(None, 'head'), may hold values from -0.125 to 0.125
- w_key: bfloat16 [2048, 2048], P(None, 'head'), may hold values from -0.125 to 0.125
- w_value: bfloat16 [2048, 2048], P(None, 'head'), may hold values from -0.125 to 0.125
- w_out: bfloat16 [2048, 2048], P('head'), may hold values from -0.125 to 0.125
- cache: bfloat16 [2, 32, 4096, 2048], P(None, None, 'grp', 'head'), may hold values from -900 to 900
- prefix_len: int32 [32], replicated, may hold values from 1 to 4096, 65536 in all
- mlp_gain: float32 [2048], replicated, may hold values from 0.1 to 1.9
- expert_ids: int32 [32, 128, 8], P('grp'), may hold values from 0 to 63, all different within a row; in each aligned block of 128 rows (0 to 127, 128 to 255, ..., all dimensions but the last counted through in order) at most 24 rows name the same one
- route_weight: float32 [32, 128, 8], P('grp'), may hold values from 0.05 to 1
- w_gate: bfloat16 [64, 2048, 1024], P('grp', None, 'head'), may hold values from -0.125 to 0.125
- w_up: bfloat16 [64, 2048, 1024], P('grp', None, 'head'), may hold values from -0.125 to 0.125
- w_down: bfloat16 [64, 1024, 2048], P('grp', 'head'), may hold values from -0.1875 to 0.1875
Outputs:
- layer_out: bfloat16 [32, 128, 2048], P('grp', None, 'head')
Inputs may be any that keep to these rules, and one draw needn't show every extreme that they name: `expert_ids`: among one prompt's 128 tokens no expert is chosen more than 24 times; a token's 8 experts are distinct.
All inputs are finite; a program needn't handle non-finite values.
Results may differ from a plain program's by a relative error of at most 0.017.
The roundings to bfloat16 on the way count: a program that leaves them out, or rounds other values in their place, can miss the bound.
Values may be sent and summed in bfloat16 or wider, within the bound.
A program may use at most 128 MiB of HBM per device.

v0:
```python
import jax
import jax.numpy as jnp
from jax import lax
from jax.sharding import PartitionSpec as P

HD = 128
TOPK = 8


def rms_norm(values, gain):
    scale = lax.rsqrt(jnp.mean(values * values, axis=-1, keepdims=True) + 1e-05)
    return values * scale * gain


def rotate(tensor, position):
    half = HD // 2
    inverse = 10000.0 ** (-(jnp.arange(half).astype(jnp.float32) * 2.0) / HD)
    angle = position[:, None] * inverse[None, :]
    cosine = jnp.cos(angle)[:, None, :]
    sine = jnp.sin(angle)[:, None, :]
    first = tensor[..., :half]
    second = tensor[..., half:]
    return jnp.concatenate(
        [first * cosine - second * sine, second * cosine + first * sine], axis=-1
    )


def on_device(
    hidden_in,
    attn_gain,
    w_query,
    w_key,
    w_value,
    w_out,
    cache,
    prefix_len,
    mlp_gain,
    expert_ids,
    route_weight,
    w_gate,
    w_up,
    w_down,
):
    group_count = lax.axis_size("grp")
    head_count = lax.axis_size("head")
    my_prompt = lax.axis_index("grp")
    tokens = hidden_in.shape[1]
    width = hidden_in.shape[2]
    heads_here = w_query.shape[1] // HD
    length = prefix_len[my_prompt]
    rows = hidden_in[0].astype(jnp.float32)
    normed = rms_norm(rows, attn_gain).astype(jnp.bfloat16)
    position = (length + jnp.arange(tokens)).astype(jnp.float32)
    query = jnp.dot(normed, w_query, preferred_element_type=jnp.float32).reshape(
        tokens, heads_here, HD
    )
    key_new = jnp.dot(normed, w_key, preferred_element_type=jnp.float32).reshape(
        tokens, heads_here, HD
    )
    value_new = jnp.dot(normed, w_value, preferred_element_type=jnp.float32).reshape(
        tokens, heads_here, HD
    )
    query = (rotate(query, position) * HD ** (-0.5)).astype(jnp.bfloat16)
    key_new = rotate(key_new, position).astype(jnp.bfloat16)
    value_new = value_new.astype(jnp.bfloat16)
    relaid = lax.all_to_all(cache, "grp", split_axis=1, concat_axis=2, tiled=True)
    context = relaid.shape[2]
    cache_key = relaid[0, 0].reshape(context, heads_here, HD)
    cache_value = relaid[1, 0].reshape(context, heads_here, HD)
    score_old = jnp.einsum("qhd,khd->hqk", query, cache_key, preferred_element_type=jnp.float32)
    score_new = jnp.einsum("qhd,khd->hqk", query, key_new, preferred_element_type=jnp.float32)
    allow_old = (jnp.arange(context) < length)[None, None, :]
    allow_new = (jnp.arange(tokens)[None, :] <= jnp.arange(tokens)[:, None])[None, :, :]
    score_old = jnp.where(allow_old, score_old, -1e30)
    score_new = jnp.where(allow_new, score_new, -1e30)
    top = jnp.maximum(
        jnp.max(score_old, axis=-1, keepdims=True), jnp.max(score_new, axis=-1, keepdims=True)
    )
    prob_old = jnp.where(allow_old, jnp.exp(score_old - top), 0.0)
    prob_new = jnp.where(allow_new, jnp.exp(score_new - top), 0.0)
    total = jnp.sum(prob_old, axis=-1) + jnp.sum(prob_new, axis=-1)
    numer = jnp.einsum(
        "hqk,khd->qhd",
        prob_old.astype(jnp.bfloat16),
        cache_value,
        preferred_element_type=jnp.float32,
    )
    numer = numer + jnp.einsum(
        "hqk,khd->qhd", prob_new.astype(jnp.bfloat16), value_new, preferred_element_type=jnp.float32
    )
    attended = (
        (numer / jnp.transpose(total)[:, :, None])
        .reshape(tokens, heads_here * HD)
        .astype(jnp.bfloat16)
    )
    projected = jnp.dot(attended, w_out, preferred_element_type=jnp.float32)
    resid = rows + lax.psum(projected.astype(jnp.bfloat16), "head").astype(jnp.float32)
    mixed_in = rms_norm(resid, mlp_gain).astype(jnp.bfloat16)
    experts_here = w_gate.shape[0]
    expert_total = experts_here * group_count
    capacity = max(2, 3 * tokens * TOPK // (2 * expert_total))
    chosen = expert_ids[0].reshape(tokens * TOPK)
    weights = route_weight[0]
    one_hot = (chosen[:, None] == jnp.arange(expert_total)[None, :]).astype(jnp.int32)
    before = jnp.cumsum(one_hot, axis=0) - one_hot
    slot = jnp.sum(before * one_hot, axis=1)
    target = chosen * capacity + slot
    repeated = jnp.repeat(mixed_in, TOPK, axis=0)
    outgoing = jnp.zeros((expert_total * capacity, width), jnp.bfloat16).at[target].set(repeated)
    outgoing = outgoing.reshape(group_count, experts_here, capacity, width)
    arrived = lax.all_to_all(outgoing, "grp", split_axis=0, concat_axis=0, tiled=True)
    results = []
    for expert in range(experts_here):
        inputs = arrived[:, expert].reshape(group_count * capacity, width)
        gate = jnp.dot(inputs, w_gate[expert], preferred_element_type=jnp.float32)
        upper = jnp.dot(inputs, w_up[expert], preferred_element_type=jnp.float32)
        act = (jax.nn.silu(gate) * upper).astype(jnp.bfloat16)
        output = jnp.dot(act, w_down[expert], preferred_element_type=jnp.float32).astype(
            jnp.bfloat16
        )
        results.append(output.reshape(group_count, capacity, width))
    expert_out = jnp.stack(results, axis=1)
    share_width = width // head_count
    returned = lax.all_to_all(expert_out, "grp", split_axis=0, concat_axis=0, tiled=True)
    returned = returned.reshape(expert_total * capacity, width)
    picked = returned[target].reshape(tokens, TOPK, width)
    combined = jnp.einsum("tk,tkd->td", weights, picked.astype(jnp.float32))
    moe_share = lax.psum_scatter(
        combined.astype(jnp.bfloat16), "head", scatter_dimension=1, tiled=True
    ).astype(jnp.float32)
    resid_share = lax.dynamic_slice_in_dim(
        resid, lax.axis_index("head") * share_width, share_width, 1
    )
    return (resid_share + moe_share).astype(jnp.bfloat16)[None]


def solution(mesh):
    placed = (
        P("grp", None, None),
        P(),
        P(None, "head"),
        P(None, "head"),
        P(None, "head"),
        P("head", None),
        P(None, None, "grp", "head"),
        P(),
        P(),
        P("grp", None, None),
        P("grp", None, None),
        P("grp", None, "head"),
        P("grp", None, "head"),
        P("grp", "head", None),
    )
    return jax.shard_map(
        on_device, mesh=mesh, in_specs=placed, out_specs=P("grp", None, "head"), check_vma=False
    )
```

profile of v0, /device:TPU:10, one launch (start us, length us, event | category | flops | bytes accessed | tf_op | source)
XLA Modules:
  0.0 485.2 jit_solution(10138498314555336373)
XLA Ops:
  6.5 7.7 %copy.39 = bf16[2,32,128,512]{3,2,0,1:T(8,128)(2,1)} copy(bf16[2,32,128,512]{3,2,1,0:T(8,128)(2,1)} %param.20) | data formatting | bytes 16777216 | tf_op args[6]
  14.3 10.3 %all-to-all-start = ((bf16[2,32,128,512]{3,2,0,1:T(8,128)(2,1)}), bf16[2,32,128,512]{3,2,0,1:T(8,128)(2,1)}, u32[]{:S(2)}, u32[]{:S(2)}) async-start(bf16[2,32,128,512]{3,2,0,1:T(8,128)(2,1)} %copy.39), calls=%async_computation | async-start | bytes 16777216 | tf_op jit(solution)/shard_map/all_to_all | solution.py:66
  25.2 18.0 %reduce-window.6 = s32[64,8,128]{2,1,0:T(8,128)S(1)} reduce-window(s32[64,8,128]{2,1,0:T(8,128)S(1)} %fusion.67, s32[]{:T(128)} %constant.22.clone.1), window={size=1x1x128 pad=0_0x0_0x127_0}, to_apply=%region_6.7 | reduce-window | flops 8323072 | bytes 524292 | tf_op jit(solution)/shard_map/reduce-window
  43.6 4.0 copy.69
  47.5 4.0 copy.65
  51.6 4.0 copy.71
  63.0 83.8 %all-to-all-done = bf16[2,32,128,512]{3,2,0,1:T(8,128)(2,1)} async-done(((bf16[2,32,128,512]{3,2,0,1:T(8,128)(2,1)}), bf16[2,32,128,512]{3,2,0,1:T(8,128)(2,1)}, u32[]{:S(2)}, u32[]{:S(2)}) %all-to-all-start) | async-done | bytes 8388640 | tf_op jit(solution)/shard_map/all_to_all | solution.py:66
  146.8 5.9 %fusion.96 = (bf16[1,32,128,512]{3,2,0,1:T(8,128)(2,1)}, bf16[1,32,128,512]{3,2,0,1:T(8,128)(2,1)}) fusion(bf16[2,32,128,512]{3,2,0,1:T(8,128)(2,1)} %all-to-all-done), kind=kLoop, calls=%fused_computation.121 | loop fusion | bytes 16777216 | tf_op jit(solution)/shard_map/slice | solution.py:68
  152.7 6.9 %reshape.243 = bf16[4096,4,128]{2,1,0:T(4,128)(2,1)} reshape(bf16[1,32,128,512]{3,2,0,1:T(8,128)(2,1)} %get-tuple-element.6) | data formatting | bytes 8388608 | tf_op jit(solution)/shard_map/reshape;squeeze | solution.py:69
  159.6 6.9 %reshape.242 = bf16[4096,4,128]{2,1,0:T(4,128)(2,1)} reshape(bf16[1,32,128,512]{3,2,0,1:T(8,128)(2,1)} %get-tuple-element.5) | data formatting | bytes 8388608 | tf_op jit(solution)/shard_map/reshape;squeeze | solution.py:68
  166.5 3.8 select_reduce_fusion
  172.6 3.4 fusion.23
  176.1 2.6 fusion.28
  180.3 40.8 %all-reduce.2.cloned.1.call-done = bf16[128,2048]{1,0:T(8,128)(2,1)} async-done(((bf16[128,2048]{1,0:T(8,128)(2,1)}), bf16[128,2048]{1,0:T(8,128)(2,1)}) %all-reduce.2.cloned.1.call-update) | async-done | bytes 524304 | tf_op jit(solution)/shard_map/psum | solution.py:97
  224.6 10.4 %scatter_custom_fusion = bf16[1536,2048]{1,0:T(8,128)(2,1)} fusion(s32[1024]{0:T(1024)S(1)} %bitcast.138, bf16[]{:T(256)} %constant.49.clone.1, bf16[128,2048]{1,0:T(8,128)(2,1)S(1)} %multiply_convert_fusion), kind=kCustom, calls=%fused_computation.10 | custom fusion | bytes 6815746 | tf_op jit(solution)/shard_map/scatter | solution.py:109
  235.0 83.6 %all_to_all.19 = bf16[32,2,24,2048]{3,2,1,0:T(8,128)(2,1)S(1)} all-to-all(bf16[32,2,24,2048]{3,2,1,0:T(8,128)(2,1)} %bitcast.120), channel_id=1, replica_groups=mesh['grp'=32,'head'=4] {'grp'}, dimensions={0} | all-to-all | bytes 12582912 | tf_op jit(solution)/shard_map/all_to_all | solution.py:111
  324.3 7.9 %convolution_convert_fusion = bf16[768,2048]{1,0:T(8,128)(2,1)} fusion(bf16[768,2048]{1,0:T(8,128)(2,1)} %bitcast.126, bf16[2,256,2048]{2,1,0:T(8,128)(2,1)} %param.27, bf16[2,2048,256]{2,1,0:T(8,128)(2,1)} %param.26, f32[768,256]{1,0:T(8,128)} %fusion.35), kind=kOutput, calls=%fused_computation.19 | convolution fusion | flops 1613365248 | bytes 9175040 | tf_op jit(solution)/shard_map/dot_general | solution.py:118
  332.2 7.1 %convolution_convert_fusion.1 = bf16[768,2048]{1,0:T(8,128)(2,1)} fusion(bf16[768,2048]{1,0:T(8,128)(2,1)} %bitcast.124, bf16[2,256,2048]{2,1,0:T(8,128)(2,1)S(1)} %copy-done.11, bf16[2,2048,256]{2,1,0:T(8,128)(2,1)} %param.26, f32[768,256]{1,0:T(8,128)S(1)} %fusion.40), kind=kOutput, calls=%fused_computation.20 | convolution fusion | flops 1613365248 | bytes 9175040 | tf_op jit(solution)/shard_map/dot_general | solution.py:118
  339.4 6.1 %pad_maximum_fusion = bf16[32,2,24,2048]{3,2,1,0:T(8,128)(2,1)} fusion(bf16[32,1,24,2048]{3,2,1,0:T(8,128)(2,1)} %bitcast.127, bf16[32,1,24,2048]{3,2,1,0:T(8,128)(2,1)} %bitcast.128), kind=kLoop, calls=%fused_computation.6 | loop fusion | flops 3145728 | bytes 12582912 | tf_op jit(solution)/shard_map/stack | solution.py:122
  345.5 6.4 %all-to-all-start.2 = ((bf16[32,2,24,2048]{3,2,1,0:T(8,128)(2,1)}), bf16[32,2,24,2048]{3,2,1,0:T(8,128)(2,1)}, u32[]{:S(2)}, u32[]{:S(2)}) async-start(bf16[32,2,24,2048]{3,2,1,0:T(8,128)(2,1)} %pad_maximum_fusion), calls=%async_computation.2 | async-start | bytes 12582912 | tf_op jit(solution)/shard_map/all_to_all | solution.py:124
  352.1 86.8 %all-to-all-done.2 = bf16[32,2,24,2048]{3,2,1,0:T(8,128)(2,1)} async-done(((bf16[32,2,24,2048]{3,2,1,0:T(8,128)(2,1)}), bf16[32,2,24,2048]{3,2,1,0:T(8,128)(2,1)}, u32[]{:S(2)}, u32[]{:S(2)}) %all-to-all-start.2) | async-done | bytes 6291488 | tf_op jit(solution)/shard_map/all_to_all | solution.py:124
  439.0 12.8 %gather_fusion = bf16[1024,2048]{1,0:T(8,128)(2,1)} fusion(bf16[1536,2048]{1,0:T(8,128)(2,1)} %bitcast.32, s32[1024]{0:T(1024)S(1)} %broadcast_clamp_fusion), kind=kCustom, calls=%fused_computation | custom fusion | bytes 8392704 | tf_op jit(solution)/shard_map/gather | solution.py:126
  451.8 3.4 fusion.4
  456.3 20.3 %reduce-scatter.2.cloned.1.call-done = bf16[128,512]{1,0:T(8,128)(2,1)} async-done(((bf16[128,2048]{1,0:T(8,128)(2,1)}), bf16[128,512]{1,0:T(8,128)(2,1)}) %reduce-scatter.2.cloned.1.call-update) | async-done | bytes 131088 | tf_op jit(solution)/shard_map/reduce_scatter | solution.py:128
  (72 shorter events, 24.3 us)
Async XLA Ops:
  6.5 172.2 %copy-start = (bf16[512,2048]{1,0:T(8,128)(2,1)S(1)}, bf16[512,2048]{1,0:T(8,128)(2,1)}, u32[]{:S(2)}) copy-start(bf16[512,2048]{1,0:T(8,128)(2,1)} %param.19) | copy-start | bytes 6291460
  14.3 10.4 %copy-start.7 = (s32[1,128,8]{1,2,0:T(8,128)S(1)}, s32[1,128,8]{1,2,0:T(8,128)}, u32[]{:S(2)}) copy-start(s32[1,128,8]{1,2,0:T(8,128)} %param.23) | copy-start | bytes 12292
  14.3 132.5 %all-to-all-start = ((bf16[2,32,128,512]{3,2,0,1:T(8,128)(2,1)}), bf16[2,32,128,512]{3,2,0,1:T(8,128)(2,1)}, u32[]{:S(2)}, u32[]{:S(2)}) async-start(bf16[2,32,128,512]{3,2,0,1:T(8,128)(2,1)} %copy.39), calls=%async_computation | async-start | bytes 16777216 | tf_op jit(solution)/shard_map/all_to_all | solution.py:66
  24.6 196.5 %all-reduce.2.cloned.1.call-start = ((), (), s32[]{:S(2)}) async-start(), calls=%async_computation.4 | async-start | bytes 1048576 | tf_op jit(solution)/shard_map/psum | solution.py:97
  47.5 8.0 %copy-start.12 = (s32[32]{0:T(128)S(1)}, s32[32]{0:T(128)}, u32[]{:S(2)}) copy-start(s32[32]{0:T(128)} %param.21) | copy-start | bytes 388
  47.5 9.9 %copy-start.2 = (bf16[1,128,2048]{2,1,0:T(8,128)(2,1)S(1)}, bf16[1,128,2048]{2,1,0:T(8,128)(2,1)}, u32[]{:S(2)}) copy-start(bf16[1,128,2048]{2,1,0:T(8,128)(2,1)} %param.14) | copy-start | bytes 1572868
  47.5 10.4 %copy-start.6 = (f32[2048]{0:T(1024)S(1)}, f32[2048]{0:T(1024)}, u32[]{:S(2)}) copy-start(f32[2048]{0:T(1024)} %param.15) | copy-start | bytes 24580
  170.3 2.2 copy-start.3
  176.1 47.3 %copy-start.8 = (f32[2048]{0:T(1024)S(1)}, f32[2048]{0:T(1024)}, u32[]{:S(2)}) copy-start(f32[2048]{0:T(1024)} %param.22) | copy-start | bytes 24580
  318.6 2.8 copy-start.10
  319.8 1.7 copy-start.5
  319.8 3.6 copy-start.4
  324.3 7.9 %copy-start.11 = (bf16[2,256,2048]{2,1,0:T(8,128)(2,1)S(1)}, bf16[2,256,2048]{2,1,0:T(8,128)(2,1)}, u32[]{:S(2)}) copy-start(bf16[2,256,2048]{2,1,0:T(8,128)(2,1)} %param.27) | copy-start | bytes 6291460
  345.5 6.5 %copy-start.9 = (f32[1,128,8]{1,2,0:T(8,128)S(1)}, f32[1,128,8]{1,2,0:T(8,128)}, u32[]{:S(2)}) copy-start(f32[1,128,8]{1,2,0:T(8,128)} %param.24) | copy-start | bytes 12292
  345.5 93.5 %all-to-all-start.2 = ((bf16[32,2,24,2048]{3,2,1,0:T(8,128)(2,1)}), bf16[32,2,24,2048]{3,2,1,0:T(8,128)(2,1)}, u32[]{:S(2)}, u32[]{:S(2)}) async-start(bf16[32,2,24,2048]{3,2,1,0:T(8,128)(2,1)} %pad_maximum_fusion), calls=%async_computation.2 | async-start | bytes 12582912 | tf_op jit(solution)/shard_map/all_to_all | solution.py:124
  351.9 124.7 %reduce-scatter.2.cloned.1.call-start = ((), (), s32[]{:S(2)}) async-start(), calls=%async_computation.5 | async-start | bytes 655360 | tf_op jit(solution)/shard_map/reduce_scatter | solution.py:128
  439.0 39.3 %copy-start.1 = (bf16[512,2048]{1,0:T(8,128)(2,1)S(1)}, bf16[512,2048]{1,0:T(8,128)(2,1)}, u32[]{:S(2)}) copy-start(bf16[512,2048]{1,0:T(8,128)(2,1)} %param.19) | copy-start | bytes 6291460
Sparse Core Ops, SparseCore 0:
  180.2 40.8 all-reduce.1
  456.4 20.1 reduce-scatter.1
where the time goes:
time: 489 us; the launch traced here: 485 us
  waiting for transfers between devices  232 us (47%)
  blocking collectives  83.6 us (17%)
  local copies, waits for them, and re-layouts  68.1 us (14%)
  matrix products  37.4 us (8%)
  other arithmetic  33.7 us (7%)
  starting transfers between devices  16.8 us (3%)
  between operations  13.7 us (3%)
    all_to_all x1, waiting for transfers between devices, on_device(): lax.all_to_all(expert_out, 'grp', split_axis=0, concat_axis=0, tiled=True)  86.8 us
    all_to_all x1, waiting for transfers between devices, on_device(): lax.all_to_all(cache, 'grp', split_axis=1, concat_axis=2, tiled=True)  83.8 us
    all_to_all x1, blocking collectives, on_device(): lax.all_to_all(outgoing, 'grp', split_axis=0, concat_axis=0, tiled=True)  83.6 us
    psum x1, waiting for transfers between devices, on_device(): lax.psum(projected.astype(jnp.bfloat16), 'head').astype(jnp.float32)  40.8 us
    reduce_scatter x1, waiting for transfers between devices, on_device(): lax.psum_scatter(combined.astype(jnp.bfloat16), 'head', scatter_dimension...  20.3 us
    another operation x4, other arithmetic  18.2 us
    dot_general x2, matrix products, on_device(): jnp.dot(act, w_down[expert], preferred_element_type=jnp.float32)  15 us
    gather x1, local copies, waits for them, and re-layouts, on_device(): picked = returned[target].reshape(tokens, TOPK, width)  12.8 us
  transfers between devices with their start and end apart: 4, of which 4 were waited for; matrix products, arithmetic and copies ran while one was open for 8% of the time, Pallas kernels for 0%

commit v1 on v0

--- a/solution.py
+++ b/solution.py
@@ -1,6 +1,8 @@
 import jax
 import jax.numpy as jnp
 from jax import lax
+from jax.experimental import pallas as pl
+from jax.experimental.pallas import tpu as pltpu
 from jax.sharding import PartitionSpec as P
 
 HD = 128
@@ -23,6 +25,46 @@
     return jnp.concatenate(
         [first * cosine - second * sine, second * cosine + first * sine], axis=-1
     )
+
+
+def head_exchange(x, count, same_source, ident):
+    rows, cols = x.shape[-2], x.shape[-1]
+    mesh_kind = pl.DeviceIdType.MESH
+
+    def kernel(x_ref, o_ref, send_sem, recv_sem):
+        me = lax.axis_index("head")
+        group = lax.axis_index("grp")
+        barrier = pltpu.get_barrier_semaphore()
+        for step in range(1, count):
+            peer = lax.rem(me + step, count)
+            pl.semaphore_signal(barrier, inc=1, device_id=(group, peer), device_id_type=mesh_kind)
+        pl.semaphore_wait(barrier, count - 1)
+        copies = []
+        for step in range(1, count):
+            peer = lax.rem(me + step, count)
+            source = x_ref if same_source else x_ref.at[peer]
+            copy = pltpu.make_async_remote_copy(
+                src_ref=source,
+                dst_ref=o_ref.at[me],
+                send_sem=send_sem.at[step - 1],
+                recv_sem=recv_sem.at[step - 1],
+                device_id=(group, peer),
+                device_id_type=mesh_kind,
+            )
+            copy.start()
+            copies.append(copy)
+        o_ref[me] = x_ref[...] if same_source else x_ref[me]
+        for copy in copies:
+            copy.wait()
+
+    return pl.pallas_call(
+        kernel,
+        out_shape=jax.ShapeDtypeStruct((count, rows, cols), x.dtype),
+        in_specs=[pl.BlockSpec(memory_space=pltpu.VMEM)],
+        out_specs=pl.BlockSpec(memory_space=pltpu.VMEM),
+        scratch_shapes=[pltpu.SemaphoreType.DMA((count - 1,)), pltpu.SemaphoreType.DMA((count - 1,))],
+        compiler_params=pltpu.CompilerParams(collective_id=ident, has_side_effects=True),
+    )(x)
 
 
 def on_device(
@@ -94,19 +136,26 @@
         .astype(jnp.bfloat16)
     )
     projected = jnp.dot(attended, w_out, preferred_element_type=jnp.float32)
-    resid = rows + lax.psum(projected.astype(jnp.bfloat16), "head").astype(jnp.float32)
+    gathered = head_exchange(projected.astype(jnp.bfloat16), head_count, True, 0)
+    resid = rows + jnp.sum(gathered.astype(jnp.float32), axis=0)
     mixed_in = rms_norm(resid, mlp_gain).astype(jnp.bfloat16)
     experts_here = w_gate.shape[0]
     expert_total = experts_here * group_count
     capacity = max(2, 3 * tokens * TOPK // (2 * expert_total))
     chosen = expert_ids[0].reshape(tokens * TOPK)
     weights = route_weight[0]
-    one_hot = (chosen[:, None] == jnp.arange(expert_total)[None, :]).astype(jnp.int32)
-    before = jnp.cumsum(one_hot, axis=0) - one_hot
-    slot = jnp.sum(before * one_hot, axis=1)
+    pairs = tokens * TOPK
+    slots = expert_total * capacity
+    one_hot = (chosen[:, None] == jnp.arange(expert_total)[None, :]).astype(jnp.bfloat16)
+    earlier = (jnp.arange(pairs)[None, :] < jnp.arange(pairs)[:, None]).astype(jnp.bfloat16)
+    before = jnp.dot(earlier, one_hot, preferred_element_type=jnp.float32)
+    slot = jnp.sum(before * one_hot.astype(jnp.float32), axis=1).astype(jnp.int32)
     target = chosen * capacity + slot
-    repeated = jnp.repeat(mixed_in, TOPK, axis=0)
-    outgoing = jnp.zeros((expert_total * capacity, width), jnp.bfloat16).at[target].set(repeated)
+    place = (target[:, None] == jnp.arange(slots)[None, :]).reshape(tokens, TOPK, slots)
+    dispatch = jnp.sum(place.astype(jnp.float32), axis=1).astype(jnp.bfloat16)
+    outgoing = lax.dot_general(
+        dispatch, mixed_in, (((0,), (0,)), ((), ())), preferred_element_type=jnp.float32
+    ).astype(jnp.bfloat16)
     outgoing = outgoing.reshape(group_count, experts_here, capacity, width)
     arrived = lax.all_to_all(outgoing, "grp", split_axis=0, concat_axis=0, tiled=True)
     results = []
@@ -122,12 +171,16 @@
     expert_out = jnp.stack(results, axis=1)
     share_width = width // head_count
     returned = lax.all_to_all(expert_out, "grp", split_axis=0, concat_axis=0, tiled=True)
-    returned = returned.reshape(expert_total * capacity, width)
-    picked = returned[target].reshape(tokens, TOPK, width)
-    combined = jnp.einsum("tk,tkd->td", weights, picked.astype(jnp.float32))
-    moe_share = lax.psum_scatter(
-        combined.astype(jnp.bfloat16), "head", scatter_dimension=1, tiled=True
-    ).astype(jnp.float32)
+    returned = returned.reshape(slots, width)
+    weighting = jnp.sum(jnp.where(place, weights[:, :, None], 0.0), axis=1)
+    combined = jnp.zeros((tokens, width), jnp.float32)
+    for _ in range(3):
+        piece = weighting.astype(jnp.bfloat16)
+        weighting = weighting - piece.astype(jnp.float32)
+        combined = combined + jnp.dot(piece, returned, preferred_element_type=jnp.float32)
+    blocks = combined.reshape(tokens, head_count, share_width).transpose(1, 0, 2)
+    exchanged = head_exchange(blocks.astype(jnp.bfloat16), head_count, False, 1)
+    moe_share = jnp.sum(exchanged.astype(jnp.float32), axis=0)
     resid_share = lax.dynamic_slice_in_dim(
         resid, lax.axis_index("head") * share_width, share_width, 1
     )

time: 489 us -> 445 us (0.910)
  waiting for transfers between devices: 232 us -> 180 us
  Pallas kernels: 0 us -> 34.3 us
  local copies, waits for them, and re-layouts: 68.1 us -> 45.8 us
  between operations: 13.7 us -> 0.39 us
  matrix products: 37.4 us -> 50.6 us
  other arithmetic: 33.7 us -> 23 us
    psum x1 -> x0, waiting for transfers between devices: 40.8 us -> none  [on_device(): lax.psum(projected.astype(jnp.bfloat16), 'head').astype(jnp.float32)]
    pallas_call x0 -> x2, Pallas kernels: none -> 34.3 us  [head_exchange(): pl.pallas_call(kernel, out_shape=jax.ShapeDtypeStruct((count, rows, cols)...]
    reduce_scatter x1 -> x0, waiting for transfers between devices: 20.3 us -> none  [on_device(): lax.psum_scatter(combined.astype(jnp.bfloat16), 'head', scatter_dimension...]
    another operation x4 -> x1, other arithmetic: 18.2 us -> 0.07 us
    gather x1 -> x0, local copies, waits for them, and re-layouts: 12.8 us -> none  [on_device(): picked = returned[target].reshape(tokens, TOPK, width)]
    reduce_sum x1 -> x3, other arithmetic: 0.07 us -> 11 us  [the longest x1 7.73 us: on_device(): weighting = jnp.sum(jnp.where(place, weights[:, :, None], 0.0), axis=1)]
    dot_general x1 -> x5, matrix products: 3.42 us -> 14 us  [the longest x3 11.5 us: on_device(): jnp.dot(piece, returned, preferred_element_type=jnp.float32)]
    scatter x1 -> x0, local copies, waits for them, and re-layouts: 10.4 us -> none  [on_device(): jnp.zeros((expert_total * capacity, width), jnp.bfloat16).at[target]]
  transfers between devices with their start and end apart: 4 -> 2, of which waited for: 4 -> 2; matrix products, arithmetic and copies ran while one was open for 8% -> 7% of each run, Pallas kernels for 0% -> 0%
where the time goes in v1:
time: 445 us; the launch traced here: 439 us
  waiting for transfers between devices  180 us (40%)
  blocking collectives  86.9 us (20%)
  matrix products  50.6 us (11%)
  local copies, waits for them, and re-layouts  45.8 us (10%)
  Pallas kernels  34.3 us (8%)
  other arithmetic  23 us (5%)
  starting transfers between devices  17.4 us (4%)
    all_to_all x1, waiting for transfers between devices, on_device(): lax.all_to_all(cache, 'grp', split_axis=1, concat_axis=2, tiled=True)  91.4 us
    all_to_all x1, waiting for transfers between devices, on_device(): lax.all_to_all(expert_out, 'grp', split_axis=0, concat_axis=0, tiled=True)  88.7 us
    all_to_all x1, blocking collectives, on_device(): lax.all_to_all(outgoing, 'grp', split_axis=0, concat_axis=0, tiled=True)  86.9 us
    pallas_call x2, Pallas kernels, head_exchange(): pl.pallas_call(kernel, out_shape=jax.ShapeDtypeStruct((count, rows, cols)...  34.3 us
    dot_general x2, matrix products, on_device(): jnp.dot(act, w_down[expert], preferred_element_type=jnp.float32)  15.3 us
    dot_general x3, matrix products, on_device(): jnp.dot(piece, returned, preferred_element_type=jnp.float32)  11.5 us
    unnamed x44, local copies, waits for them, and re-layouts  10.2 us
    all_to_all x1, starting transfers between devices, on_device(): lax.all_to_all(cache, 'grp', split_axis=1, concat_axis=2, tiled=True)  10.2 us
  transfers between devices with their start and end apart: 2, of which 2 were waited for; matrix products, arithmetic and copies ran while one was open for 7% of the time, Pallas kernels for 0%

profile of v1, /device:TPU:10, one launch (start us, length us, event | category | flops | bytes accessed | tf_op | source)
XLA Modules:
  0.0 438.5 jit_solution(15676476371036716923)
XLA Ops:
  0.0 7.7 %copy.60 = bf16[2,32,128,512]{3,2,0,1:T(8,128)(2,1)} copy(bf16[2,32,128,512]{3,2,1,0:T(8,128)(2,1)} %param.20) | data formatting | bytes 16777216 | tf_op args[6]
  7.7 10.2 %all-to-all-start = ((bf16[2,32,128,512]{3,2,0,1:T(8,128)(2,1)}), bf16[2,32,128,512]{3,2,0,1:T(8,128)(2,1)}, u32[]{:S(2)}, u32[]{:S(2)}) async-start(bf16[2,32,128,512]{3,2,0,1:T(8,128)(2,1)} %copy.60), calls=%async_computation | async-start | bytes 16777216 | tf_op jit(solution)/shard_map/all_to_all | solution.py:108
  17.9 4.0 copy.88
  21.9 4.0 copy.84
  25.9 4.0 copy.90
  41.0 7.7 %select_reduce_fusion.1 = (f32[128,1536]{1,0:T(8,128)S(1)}, bf16[128,1536]{1,0:T(8,128)(2,1)}) fusion(f32[128,8]{1,0:T(8,128)} %copy.73, s32[128,8]{1,0:T(8,128)S(1)} %bitcast_add_fusion), kind=kLoop, calls=%fused_computation.7 | loop fusion | flops 7471104 | bytes 1187840 | tf_op jit(solution)/shard_map/reduce_sum | solution.py:175
  48.7 91.4 %all-to-all-done = bf16[2,32,128,512]{3,2,0,1:T(8,128)(2,1)} async-done(((bf16[2,32,128,512]{3,2,0,1:T(8,128)(2,1)}), bf16[2,32,128,512]{3,2,0,1:T(8,128)(2,1)}, u32[]{:S(2)}, u32[]{:S(2)}) %all-to-all-start) | async-done | bytes 8388640 | tf_op jit(solution)/shard_map/all_to_all | solution.py:108
  140.1 5.9 %fusion.100 = (bf16[1,32,128,512]{3,2,0,1:T(8,128)(2,1)}, bf16[1,32,128,512]{3,2,0,1:T(8,128)(2,1)}) fusion(bf16[2,32,128,512]{3,2,0,1:T(8,128)(2,1)} %all-to-all-done), kind=kLoop, calls=%fused_computation.126 | loop fusion | bytes 16777216 | tf_op jit(solution)/shard_map/slice | solution.py:110
  146.0 6.9 %reshape.197 = bf16[4096,4,128]{2,1,0:T(4,128)(2,1)} reshape(bf16[1,32,128,512]{3,2,0,1:T(8,128)(2,1)} %get-tuple-element.10) | data formatting | bytes 8388608 | tf_op jit(solution)/shard_map/reshape;squeeze | solution.py:111
  152.9 6.9 %reshape.196 = bf16[4096,4,128]{2,1,0:T(4,128)(2,1)} reshape(bf16[1,32,128,512]{3,2,0,1:T(8,128)(2,1)} %get-tuple-element.9) | data formatting | bytes 8388608 | tf_op jit(solution)/shard_map/reshape;squeeze | solution.py:110
  159.9 3.9 select_reduce_fusion
  166.0 3.4 fusion.20
  169.5 2.7 fusion.25
  173.5 25.8 %shard_map.136 = bf16[4,128,2048]{2,1,0:T(8,128)(2,1)} custom-call(bf16[128,2048]{1,0:T(8,128)(2,1)} %convolution_convert_fusion.3.x_ref), custom_call_target="tpu_custom_call" | custom-call | tf_op jit(solution)/shard_map/pallas_call | solution.py:60
  203.6 86.9 %all_to_all.19 = bf16[32,2,24,2048]{3,2,1,0:T(8,128)(2,1)S(1)} all-to-all(bf16[32,2,24,2048]{3,2,1,0:T(8,128)(2,1)S(1)} %bitcast.94), channel_id=1, replica_groups=mesh['grp'=32,'head'=4] {'grp'}, dimensions={0} | all-to-all | bytes 12582912 | tf_op jit(solution)/shard_map/all_to_all | solution.py:160
  297.1 7.9 %convolution_convert_fusion.1 = bf16[768,2048]{1,0:T(8,128)(2,1)} fusion(bf16[768,2048]{1,0:T(8,128)(2,1)} %bitcast.100, bf16[2,256,2048]{2,1,0:T(8,128)(2,1)} %param.27, bf16[2,2048,256]{2,1,0:T(8,128)(2,1)} %param.26, f32[768,256]{1,0:T(8,128)} %fusion.33), kind=kOutput, calls=%fused_computation.20 | convolution fusion | flops 1613365248 | bytes 9175040 | tf_op jit(solution)/shard_map/dot_general | solution.py:167
  305.0 7.4 %convolution_convert_fusion.2 = bf16[768,2048]{1,0:T(8,128)(2,1)} fusion(bf16[768,2048]{1,0:T(8,128)(2,1)} %bitcast.98, bf16[2,256,2048]{2,1,0:T(8,128)(2,1)S(1)} %copy-done.19, bf16[2,2048,256]{2,1,0:T(8,128)(2,1)} %param.26, f32[768,256]{1,0:T(8,128)} %fusion.38), kind=kOutput, calls=%fused_computation.21 | convolution fusion | flops 1613365248 | bytes 9175040 | tf_op jit(solution)/shard_map/dot_general | solution.py:167
  312.4 6.1 %pad_maximum_fusion = bf16[32,2,24,2048]{3,2,1,0:T(8,128)(2,1)} fusion(bf16[32,1,24,2048]{3,2,1,0:T(8,128)(2,1)} %bitcast.101, bf16[32,1,24,2048]{3,2,1,0:T(8,128)(2,1)} %bitcast.102), kind=kLoop, calls=%fused_computation.5 | loop fusion | flops 3145728 | bytes 12582912 | tf_op jit(solution)/shard_map/stack | solution.py:171
  318.4 7.2 %all-to-all-start.2 = ((bf16[32,2,24,2048]{3,2,1,0:T(8,128)(2,1)}), bf16[32,2,24,2048]{3,2,1,0:T(8,128)(2,1)}, u32[]{:S(2)}, u32[]{:S(2)}) async-start(bf16[32,2,24,2048]{3,2,1,0:T(8,128)(2,1)} %pad_maximum_fusion), calls=%async_computation.2 | async-start | bytes 12582912 | tf_op jit(solution)/shard_map/all_to_all | solution.py:173
  325.7 88.7 %all-to-all-done.2 = bf16[32,2,24,2048]{3,2,1,0:T(8,128)(2,1)} async-done(((bf16[32,2,24,2048]{3,2,1,0:T(8,128)(2,1)}), bf16[32,2,24,2048]{3,2,1,0:T(8,128)(2,1)}, u32[]{:S(2)}, u32[]{:S(2)}) %all-to-all-start.2) | async-done | bytes 6291488 | tf_op jit(solution)/shard_map/all_to_all | solution.py:173
  414.4 3.8 fusion.59
  418.2 3.8 convolution_add_fusion.1
  422.0 4.0 fusion.12
  427.3 8.4 %shard_map.137 = bf16[4,128,512]{2,1,0:T(8,128)(2,1)} custom-call(bf16[4,128,512]{2,1,0:T(8,128)(2,1)} %bitcast.108), custom_call_target="tpu_custom_call" | custom-call | tf_op jit(solution)/shard_map/pallas_call | solution.py:60
  (77 shorter events, 29.4 us)
Async XLA Ops:
  0.0 172.2 %copy-start = (bf16[512,2048]{1,0:T(8,128)(2,1)S(1)}, bf16[512,2048]{1,0:T(8,128)(2,1)}, u32[]{:S(2)}) copy-start(bf16[512,2048]{1,0:T(8,128)(2,1)} %param.19) | copy-start | bytes 6291460
  7.7 132.4 %all-to-all-start = ((bf16[2,32,128,512]{3,2,0,1:T(8,128)(2,1)}), bf16[2,32,128,512]{3,2,0,1:T(8,128)(2,1)}, u32[]{:S(2)}, u32[]{:S(2)}) async-start(bf16[2,32,128,512]{3,2,0,1:T(8,128)(2,1)} %copy.60), calls=%async_computation | async-start | bytes 16777216 | tf_op jit(solution)/shard_map/all_to_all | solution.py:108
  21.9 8.0 %copy-start.14 = (f32[1,128,8]{1,2,0:T(8,128)S(1)}, f32[1,128,8]{1,2,0:T(8,128)}, u32[]{:S(2)}) copy-start(f32[1,128,8]{1,2,0:T(8,128)} %param.24) | copy-start | bytes 12292
  21.9 8.7 %copy-start.15 = (s32[1,128,8]{1,2,0:T(8,128)S(1)}, s32[1,128,8]{1,2,0:T(8,128)}, u32[]{:S(2)}) copy-start(s32[1,128,8]{1,2,0:T(8,128)} %param.23) | copy-start | bytes 12292
  21.9 9.6 %copy-start.20 = (s32[32]{0:T(128)S(1)}, s32[32]{0:T(128)}, u32[]{:S(2)}) copy-start(s32[32]{0:T(128)} %param.21) | copy-start | bytes 388
  21.9 11.6 %copy-start.2 = (bf16[1,128,2048]{2,1,0:T(8,128)(2,1)S(1)}, bf16[1,128,2048]{2,1,0:T(8,128)(2,1)}, u32[]{:S(2)}) copy-start(bf16[1,128,2048]{2,1,0:T(8,128)(2,1)} %param.14) | copy-start | bytes 1572868
  25.9 8.0 %copy-start.12 = (f32[2048]{0:T(1024)S(1)}, f32[2048]{0:T(1024)}, u32[]{:S(2)}) copy-start(f32[2048]{0:T(1024)} %param.15) | copy-start | bytes 24580
  33.5 5.3 %copy-start.10 = (pred[128,128]{0,1:T(8,128)(4,1)}, pred[128,128]{0,1:T(8,128)(4,1)S(1)}, u32[]{:S(2)}) copy-start(pred[128,128]{0,1:T(8,128)(4,1)S(1)} %iota_compare_fusion.9) | copy-start | bytes 49156
  33.7 5.0 %copy-start.16 = (f32[128]{0:T(128)}, f32[128]{0:T(128)S(1)}, u32[]{:S(2)}) copy-start(f32[128]{0:T(128)S(1)} %add_rsqrt_fusion.1) | copy-start | bytes 1540
  38.8 0.7 copy-start.8
  159.9 3.9 copy-start.17
  163.8 2.2 copy-start.4
  166.0 3.4 copy-start.9
  166.0 3.4 copy-start.11
  173.5 28.2 %copy-start.13 = (f32[2048]{0:T(1024)S(1)}, f32[2048]{0:T(1024)}, u32[]{:S(2)}) copy-start(f32[2048]{0:T(1024)} %param.22) | copy-start | bytes 24580
  199.4 2.4 copy-start.7
  201.7 1.9 copy-start.3
  290.5 2.8 copy-start.18
  291.6 1.7 copy-start.6
  291.6 3.6 copy-start.5
  297.1 7.9 %copy-start.19 = (bf16[2,256,2048]{2,1,0:T(8,128)(2,1)S(1)}, bf16[2,256,2048]{2,1,0:T(8,128)(2,1)}, u32[]{:S(2)}) copy-start(bf16[2,256,2048]{2,1,0:T(8,128)(2,1)} %param.27) | copy-start | bytes 6291460
  318.4 96.0 %all-to-all-start.2 = ((bf16[32,2,24,2048]{3,2,1,0:T(8,128)(2,1)}), bf16[32,2,24,2048]{3,2,1,0:T(8,128)(2,1)}, u32[]{:S(2)}, u32[]{:S(2)}) async-start(bf16[32,2,24,2048]{3,2,1,0:T(8,128)(2,1)} %pad_maximum_fusion), calls=%async_computation.2 | async-start | bytes 12582912 | tf_op jit(solution)/shard_map/all_to_all | solution.py:173
  422.0 16.5 %copy-start.1 = (bf16[512,2048]{1,0:T(8,128)(2,1)S(1)}, bf16[512,2048]{1,0:T(8,128)(2,1)}, u32[]{:S(2)}) copy-start(bf16[512,2048]{1,0:T(8,128)(2,1)} %param.19) | copy-start | bytes 6291460

commit v2 on v1

--- a/solution.py
+++ b/solution.py
@@ -63,6 +63,55 @@
         in_specs=[pl.BlockSpec(memory_space=pltpu.VMEM)],
         out_specs=pl.BlockSpec(memory_space=pltpu.VMEM),
         scratch_shapes=[pltpu.SemaphoreType.DMA((count - 1,)), pltpu.SemaphoreType.DMA((count - 1,))],
+        compiler_params=pltpu.CompilerParams(collective_id=ident, has_side_effects=True),
+    )(x)
+
+
+def head_gather(x, ident):
+    mesh_kind = pl.DeviceIdType.MESH
+
+    def kernel(x_ref, o_ref, own_sem, send_sem, recv_sem):
+        me = lax.axis_index("head")
+        group = lax.axis_index("grp")
+        partner = me + 1 - 2 * lax.rem(me, 2)
+        across = lax.rem(me + 2, 4)
+        barrier = pltpu.get_barrier_semaphore()
+        for peer in (partner, across):
+            pl.semaphore_signal(barrier, inc=1, device_id=(group, peer), device_id_type=mesh_kind)
+        pl.semaphore_wait(barrier, 2)
+        own = pltpu.make_async_copy(x_ref, o_ref.at[me], own_sem)
+        own.start()
+        near = pltpu.make_async_remote_copy(
+            src_ref=x_ref, dst_ref=o_ref.at[me], send_sem=send_sem.at[0], recv_sem=recv_sem.at[0],
+            device_id=(group, partner), device_id_type=mesh_kind,
+        )
+        far = pltpu.make_async_remote_copy(
+            src_ref=x_ref, dst_ref=o_ref.at[me], send_sem=send_sem.at[1], recv_sem=recv_sem.at[1],
+            device_id=(group, across), device_id_type=mesh_kind,
+        )
+        near.start()
+        far.start()
+        far.wait_recv()
+        relay = pltpu.make_async_remote_copy(
+            src_ref=o_ref.at[across], dst_ref=o_ref.at[across], send_sem=send_sem.at[2],
+            recv_sem=recv_sem.at[2], device_id=(group, partner), device_id_type=mesh_kind,
+        )
+        relay.start()
+        own.wait()
+        near.wait()
+        far.wait_send()
+        relay.wait()
+
+    return pl.pallas_call(
+        kernel,
+        out_shape=jax.ShapeDtypeStruct((4,) + x.shape, x.dtype),
+        in_specs=[pl.BlockSpec(memory_space=pl.ANY)],
+        out_specs=pl.BlockSpec(memory_space=pl.ANY),
+        scratch_shapes=[
+            pltpu.SemaphoreType.DMA(()),
+            pltpu.SemaphoreType.DMA((3,)),
+            pltpu.SemaphoreType.DMA((3,)),
+        ],
         compiler_params=pltpu.CompilerParams(collective_id=ident, has_side_effects=True),
     )(x)
 
@@ -136,7 +185,7 @@
         .astype(jnp.bfloat16)
     )
     projected = jnp.dot(attended, w_out, preferred_element_type=jnp.float32)
-    gathered = head_exchange(projected.astype(jnp.bfloat16), head_count, True, 0)
+    gathered = head_gather(projected.astype(jnp.bfloat16), 0)
     resid = rows + jnp.sum(gathered.astype(jnp.float32), axis=0)
     mixed_in = rms_norm(resid, mlp_gain).astype(jnp.bfloat16)
     experts_here = w_gate.shape[0]
@@ -153,23 +202,29 @@
     target = chosen * capacity + slot
     place = (target[:, None] == jnp.arange(slots)[None, :]).reshape(tokens, TOPK, slots)
     dispatch = jnp.sum(place.astype(jnp.float32), axis=1).astype(jnp.bfloat16)
+    share_width = width // head_count
+    my_columns = lax.dynamic_slice_in_dim(
+        mixed_in, lax.axis_index("head") * share_width, share_width, 1
+    )
     outgoing = lax.dot_general(
-        dispatch, mixed_in, (((0,), (0,)), ((), ())), preferred_element_type=jnp.float32
+        dispatch, my_columns, (((0,), (0,)), ((), ())), preferred_element_type=jnp.float32
     ).astype(jnp.bfloat16)
-    outgoing = outgoing.reshape(group_count, experts_here, capacity, width)
+    outgoing = outgoing.reshape(group_count, experts_here, capacity, share_width)
     arrived = lax.all_to_all(outgoing, "grp", split_axis=0, concat_axis=0, tiled=True)
+    arrived = head_gather(arrived, 2)
     results = []
     for expert in range(experts_here):
-        inputs = arrived[:, expert].reshape(group_count * capacity, width)
-        gate = jnp.dot(inputs, w_gate[expert], preferred_element_type=jnp.float32)
-        upper = jnp.dot(inputs, w_up[expert], preferred_element_type=jnp.float32)
+        inputs = arrived[:, :, expert].reshape(head_count, group_count * capacity, share_width)
+        gate_w = w_gate[expert].reshape(head_count, share_width, -1)
+        up_w = w_up[expert].reshape(head_count, share_width, -1)
+        gate = jnp.einsum("qrc,qcf->rf", inputs, gate_w, preferred_element_type=jnp.float32)
+        upper = jnp.einsum("qrc,qcf->rf", inputs, up_w, preferred_element_type=jnp.float32)
         act = (jax.nn.silu(gate) * upper).astype(jnp.bfloat16)
         output = jnp.dot(act, w_down[expert], preferred_element_type=jnp.float32).astype(
             jnp.bfloat16
         )
         results.append(output.reshape(group_count, capacity, width))
     expert_out = jnp.stack(results, axis=1)
-    share_width = width // head_count
     returned = lax.all_to_all(expert_out, "grp", split_axis=0, concat_axis=0, tiled=True)
     returned = returned.reshape(slots, width)
     weighting = jnp.sum(jnp.where(place, weights[:, :, None], 0.0), axis=1)

time: 445 us -> 414 us (0.930)
  waiting for transfers between devices: 180 us -> 111 us
  Pallas kernels: 34.3 us -> 77.3 us
  local copies, waits for them, and re-layouts: 45.8 us -> 54.9 us
  blocking collectives: 86.9 us -> 79.2 us
  starting transfers between devices: 17.4 us -> 22.3 us
  matrix products: 50.6 us -> 46.1 us
    all_to_all x1, waiting for transfers between devices: 88.7 us -> 19.7 us  [on_device(): lax.all_to_all(outgoing, 'grp', split_axis=0, concat_axis=0, tiled=True)]
    pallas_call x0 -> x2, Pallas kernels: none -> 67.5 us  [head_gather(): pl.pallas_call(kernel, out_shape=jax.ShapeDtypeStruct((4,) + x.shape, x.d...]
    pallas_call x2 -> x1, Pallas kernels: 34.3 us -> 9.73 us  [head_exchange(): pl.pallas_call(kernel, out_shape=jax.ShapeDtypeStruct((count, rows, cols)...]
    dot_general x3, matrix products: 11.5 us -> 3.15 us  [on_device(): jnp.dot(piece, returned, preferred_element_type=jnp.float32)]
    all_to_all x1, blocking collectives: 86.9 us -> 79.2 us  [on_device(): lax.all_to_all(expert_out, 'grp', split_axis=0, concat_axis=0, tiled=True)]
    slice x1 -> x3, local copies, waits for them, and re-layouts: 1.11 us -> 8.36 us  [the longest x1 3.64 us: on_device(): arrived[:, :, expert]]
    all_to_all x1, starting transfers between devices: 7.24 us -> 12.1 us  [on_device(): lax.all_to_all(outgoing, 'grp', split_axis=0, concat_axis=0, tiled=True)]
    unnamed x44 -> x54, local copies, waits for them, and re-layouts: 10.2 us -> 10.8 us
  transfers between devices with their start and end apart: 2 -> 2, of which waited for: 2 -> 2; matrix products, arithmetic and copies ran while one was open for 7% -> 9% of each run, Pallas kernels for 0% -> 0%
where the time goes in v2:
time: 414 us; the launch traced here: 410 us
  waiting for transfers between devices  111 us (27%)
  blocking collectives  79.2 us (19%)
  Pallas kernels  77.3 us (19%)
  local copies, waits for them, and re-layouts  54.9 us (13%)
  matrix products  46.1 us (11%)
  starting transfers between devices  22.3 us (5%)
  other arithmetic  19.6 us (5%)
    all_to_all x1, waiting for transfers between devices, on_device(): lax.all_to_all(cache, 'grp', split_axis=1, concat_axis=2, tiled=True)  90.9 us
    all_to_all x1, blocking collectives, on_device(): lax.all_to_all(expert_out, 'grp', split_axis=0, concat_axis=0, tiled=True)  79.2 us
    pallas_call x2, Pallas kernels, head_gather(): pl.pallas_call(kernel, out_shape=jax.ShapeDtypeStruct((4,) + x.shape, x.d...  67.5 us
    all_to_all x1, waiting for transfers between devices, on_device(): lax.all_to_all(outgoing, 'grp', split_axis=0, concat_axis=0, tiled=True)  19.7 us
    dot_general x2, matrix products, on_device(): jnp.dot(act, w_down[expert], preferred_element_type=jnp.float32)  14.9 us
    all_to_all x1, starting transfers between devices, on_device(): lax.all_to_all(outgoing, 'grp', split_axis=0, concat_axis=0, tiled=True)  12.1 us
    unnamed x54, local copies, waits for them, and re-layouts  10.8 us
    all_to_all x1, starting transfers between devices, on_device(): lax.all_to_all(cache, 'grp', split_axis=1, concat_axis=2, tiled=True)  10.2 us
  transfers between devices with their start and end apart: 2, of which 2 were waited for; matrix products, arithmetic and copies ran while one was open for 9% of the time, Pallas kernels for 0%

profile of v2, /device:TPU:10, one launch (start us, length us, event | category | flops | bytes accessed | tf_op | source)
XLA Modules:
  0.0 410.3 jit_solution(1748943724011408909)
XLA Ops:
  0.0 7.7 %copy.60 = bf16[2,32,128,512]{3,2,0,1:T(8,128)(2,1)} copy(bf16[2,32,128,512]{3,2,1,0:T(8,128)(2,1)} %param.20) | data formatting | bytes 16777216 | tf_op args[6]
  7.8 10.2 %all-to-all-start = ((bf16[2,32,128,512]{3,2,0,1:T(8,128)(2,1)}), bf16[2,32,128,512]{3,2,0,1:T(8,128)(2,1)}, u32[]{:S(2)}, u32[]{:S(2)}) async-start(bf16[2,32,128,512]{3,2,0,1:T(8,128)(2,1)} %copy.60), calls=%async_computation | async-start | bytes 16777216 | tf_op jit(solution)/shard_map/all_to_all | solution.py:157
  17.9 3.9 copy.88
  21.9 4.0 copy.84
  25.9 4.0 copy.90
  42.3 7.0 %select_reduce_fusion.1 = (f32[128,1536]{1,0:T(8,128)S(1)}, bf16[128,1536]{1,0:T(8,128)(2,1)}) fusion(f32[128,8]{1,0:T(8,128)S(1)} %copy-done.15, s32[128,8]{1,0:T(8,128)S(1)} %bitcast_add_fusion), kind=kLoop, calls=%fused_computation.6 | loop fusion | flops 7471104 | bytes 1187840 | tf_op jit(solution)/shard_map/reduce_sum | solution.py:230
  49.3 90.9 %all-to-all-done = bf16[2,32,128,512]{3,2,0,1:T(8,128)(2,1)} async-done(((bf16[2,32,128,512]{3,2,0,1:T(8,128)(2,1)}), bf16[2,32,128,512]{3,2,0,1:T(8,128)(2,1)}, u32[]{:S(2)}, u32[]{:S(2)}) %all-to-all-start) | async-done | bytes 8388640 | tf_op jit(solution)/shard_map/all_to_all | solution.py:157
  140.2 5.9 %fusion.89 = (bf16[1,32,128,512]{3,2,0,1:T(8,128)(2,1)}, bf16[1,32,128,512]{3,2,0,1:T(8,128)(2,1)}) fusion(bf16[2,32,128,512]{3,2,0,1:T(8,128)(2,1)} %all-to-all-done), kind=kLoop, calls=%fused_computation.121 | loop fusion | bytes 16777216 | tf_op jit(solution)/shard_map/slice | solution.py:159
  146.0 6.9 %reshape.200 = bf16[4096,4,128]{2,1,0:T(4,128)(2,1)} reshape(bf16[1,32,128,512]{3,2,0,1:T(8,128)(2,1)} %get-tuple-element.9) | data formatting | bytes 8388608 | tf_op jit(solution)/shard_map/reshape;squeeze | solution.py:159
  152.9 3.9 select_reduce_fusion
  160.1 6.9 %reshape.201 = bf16[4096,4,128]{2,1,0:T(4,128)(2,1)} reshape(bf16[1,32,128,512]{3,2,0,1:T(8,128)(2,1)} %get-tuple-element.10) | data formatting | bytes 8388608 | tf_op jit(solution)/shard_map/reshape;squeeze | solution.py:160
  167.0 7.6 %fusion.22 = f32[128,4,128]{0,2,1:T(8,128)} fusion(bf16[4096,4,128]{2,1,0:T(4,128)(2,1)} %reshape.201, f32[4,128,4096]{2,1,0:T(8,128)} %copy-done.2, f32[4,128]{1,0:T(4,128)S(1)} %max.8, pred[4096]{0:T(1024)(128)(4,1)S(1)} %iota_compare_fusion.10), kind=kOutput, calls=%fused_computation.43 | convolution fusion | flops 545259520 | bytes 12851200 | tf_op jit(solution)/shard_map/hqk,khd->qhd/dot_general | solution.py:173
  174.6 2.7 fusion.27
  178.6 17.1 %shard_map.136 = bf16[4,128,2048]{2,1,0:T(8,128)(2,1)} custom-call(bf16[128,2048]{1,0:T(8,128)(2,1)} %convolution_convert_fusion.3.x_ref), custom_call_target="tpu_custom_call" | custom-call | tf_op jit(solution)/shard_map/pallas_call | solution.py:105
  199.9 12.1 %all-to-all-start.1 = ((bf16[32,2,24,512]{3,2,1,0:T(8,128)(2,1)}), bf16[32,2,24,512]{3,2,1,0:T(8,128)(2,1)S(1)}, u32[]{:S(2)}, u32[]{:S(2)}) async-start(bf16[32,2,24,512]{3,2,1,0:T(8,128)(2,1)} %bitcast.16), calls=%async_computation.1 | async-start | bytes 3145728 | tf_op jit(solution)/shard_map/all_to_all | solution.py:213
  212.0 3.2 fusion.91
  216.7 19.7 %all-to-all-done.1.x_ref = bf16[32,2,24,512]{3,2,1,0:T(8,128)(2,1)S(1)} async-done(((bf16[32,2,24,512]{3,2,1,0:T(8,128)(2,1)}), bf16[32,2,24,512]{3,2,1,0:T(8,128)(2,1)S(1)}, u32[]{:S(2)}, u32[]{:S(2)}) %all-to-all-start.1) | async-done | bytes 1572896 | tf_op jit(solution)/shard_map/all_to_all | solution.py:213
  237.6 50.5 %shard_map.137 = bf16[4,32,2,24,512]{4,3,2,1,0:T(8,128)(2,1)} custom-call(bf16[32,2,24,512]{3,2,1,0:T(8,128)(2,1)} %copy-done.4), custom_call_target="tpu_custom_call" | custom-call | tf_op jit(solution)/shard_map/pallas_call | solution.py:105
  288.1 3.6 fusion.90
  295.7 7.5 %convolution_convert_fusion.1 = bf16[768,2048]{1,0:T(8,128)(2,1)} fusion(bf16[4,768,512]{2,1,0:T(8,128)(2,1)} %bitcast.116, bf16[4,512,256]{2,1,0:T(8,128)(2,1)S(1)} %bitcast.126, bf16[2,256,2048]{2,1,0:T(8,128)(2,1)} %param.27, f32[768,256]{1,0:T(8,128)} %convolution_bitcast_fusion.3), kind=kOutput, calls=%fused_computation.20 | convolution fusion | flops 1613365248 | bytes 9175040 | tf_op jit(solution)/shard_map/dot_general | solution.py:223
  303.2 7.4 %convolution_convert_fusion = bf16[768,2048]{1,0:T(8,128)(2,1)} fusion(bf16[4,768,512]{2,1,0:T(8,128)(2,1)} %bitcast.114, bf16[4,512,256]{2,1,0:T(8,128)(2,1)S(1)} %bitcast.125, bf16[2,256,2048]{2,1,0:T(8,128)(2,1)} %param.27, f32[768,256]{1,0:T(8,128)} %convolution_bitcast_fusion.1), kind=kOutput, calls=%fused_computation.19 | convolution fusion | flops 1613365248 | bytes 9175040 | tf_op jit(solution)/shard_map/dot_general | solution.py:223
  310.6 3.4 pad_maximum_fusion
  314.1 79.2 %all_to_all.19 = bf16[32,2,24,2048]{3,2,1,0:T(8,128)(2,1)S(1)} all-to-all(bf16[32,2,24,2048]{3,2,1,0:T(8,128)(2,1)S(1)} %pad_maximum_fusion), channel_id=1, replica_groups=mesh['grp'=32,'head'=4] {'grp'}, dimensions={0} | all-to-all | bytes 12582912 | tf_op jit(solution)/shard_map/all_to_all | solution.py:228
  397.8 9.7 %shard_map.138 = bf16[4,128,512]{2,1,0:T(8,128)(2,1)} custom-call(bf16[4,128,512]{2,1,0:T(8,128)(2,1)} %bitcast.124), custom_call_target="tpu_custom_call" | custom-call | tf_op jit(solution)/shard_map/pallas_call | solution.py:60
  (91 shorter events, 34.8 us)
Async XLA Ops:
  0.0 177.3 %copy-start = (bf16[512,2048]{1,0:T(8,128)(2,1)S(1)}, bf16[512,2048]{1,0:T(8,128)(2,1)}, u32[]{:S(2)}) copy-start(bf16[512,2048]{1,0:T(8,128)(2,1)} %param.19) | copy-start | bytes 6291460
  7.8 132.4 %all-to-all-start = ((bf16[2,32,128,512]{3,2,0,1:T(8,128)(2,1)}), bf16[2,32,128,512]{3,2,0,1:T(8,128)(2,1)}, u32[]{:S(2)}, u32[]{:S(2)}) async-start(bf16[2,32,128,512]{3,2,0,1:T(8,128)(2,1)} %copy.60), calls=%async_computation | async-start | bytes 16777216 | tf_op jit(solution)/shard_map/all_to_all | solution.py:157
  21.9 8.0 %copy-start.21 = (s32[1,128,8]{1,2,0:T(8,128)S(1)}, s32[1,128,8]{1,2,0:T(8,128)}, u32[]{:S(2)}) copy-start(s32[1,128,8]{1,2,0:T(8,128)} %param.23) | copy-start | bytes 12292
  21.9 8.9 %copy-start.22 = (f32[1,128,8]{1,2,0:T(8,128)S(1)}, f32[1,128,8]{1,2,0:T(8,128)}, u32[]{:S(2)}) copy-start(f32[1,128,8]{1,2,0:T(8,128)} %param.24) | copy-start | bytes 12292
  21.9 9.6 %copy-start.25 = (s32[32]{0:T(128)S(1)}, s32[32]{0:T(128)}, u32[]{:S(2)}) copy-start(s32[32]{0:T(128)} %param.21) | copy-start | bytes 388
  21.9 12.9 %copy-start.3 = (bf16[1,128,2048]{2,1,0:T(8,128)(2,1)S(1)}, bf16[1,128,2048]{2,1,0:T(8,128)(2,1)}, u32[]{:S(2)}) copy-start(bf16[1,128,2048]{2,1,0:T(8,128)(2,1)} %param.14) | copy-start | bytes 1572868
  25.9 9.3 %copy-start.19 = (f32[2048]{0:T(1024)S(1)}, f32[2048]{0:T(1024)}, u32[]{:S(2)}) copy-start(f32[2048]{0:T(1024)} %param.15) | copy-start | bytes 24580
  32.1 10.2 %copy-start.15 = (f32[128,8]{1,0:T(8,128)S(1)}, f32[128,8]{1,0:T(8,128)}, u32[]{:S(2)}) copy-start(f32[128,8]{1,0:T(8,128)} %copy.73) | copy-start | bytes 12292
  34.8 5.3 %copy-start.17 = (pred[128,128]{0,1:T(8,128)(4,1)}, pred[128,128]{0,1:T(8,128)(4,1)S(1)}, u32[]{:S(2)}) copy-start(pred[128,128]{0,1:T(8,128)(4,1)S(1)} %iota_compare_fusion.9) | copy-start | bytes 49156
  35.0 5.0 %copy-start.23 = (f32[128]{0:T(128)}, f32[128]{0:T(128)S(1)}, u32[]{:S(2)}) copy-start(f32[128]{0:T(128)S(1)} %add_rsqrt_fusion.1) | copy-start | bytes 1540
  152.9 4.0 copy-start.24
  152.9 4.0 copy-start.16
  152.9 4.0 copy-start.18
  156.9 3.2 copy-start.2
  178.6 19.4 %copy-start.20 = (f32[512]{0:T(512)S(1)}, f32[512]{0:T(512)}, u32[]{:S(2)}) copy-start(f32[512]{0:T(512)} %dynamic-slice) | copy-start | bytes 6148
  195.7 2.4 copy-start.9
  199.9 36.6 %all-to-all-start.1 = ((bf16[32,2,24,512]{3,2,1,0:T(8,128)(2,1)}), bf16[32,2,24,512]{3,2,1,0:T(8,128)(2,1)S(1)}, u32[]{:S(2)}, u32[]{:S(2)}) async-start(bf16[32,2,24,512]{3,2,1,0:T(8,128)(2,1)} %bitcast.16), calls=%async_computation.1 | async-start | bytes 3145728 | tf_op jit(solution)/shard_map/all_to_all | solution.py:213
  212.0 3.3 copy-start.8
  288.1 3.7 copy-start.13
  291.7 3.9 copy-start.5
  291.7 3.9 copy-start.6
  293.7 2.0 copy-start.11
  295.7 7.5 %copy-start.10 = (bf16[1,2048,256]{2,1,0:T(8,128)(2,1)S(1)}, bf16[1,2048,256]{2,1,0:T(8,128)(2,1)}, u32[]{:S(2)}) copy-start(bf16[1,2048,256]{2,1,0:T(8,128)(2,1)} %get-tuple-element.16) | copy-start | bytes 3145732
  395.4 14.9 %copy-start.1 = (bf16[512,2048]{1,0:T(8,128)(2,1)S(1)}, bf16[512,2048]{1,0:T(8,128)(2,1)}, u32[]{:S(2)}) copy-start(bf16[512,2048]{1,0:T(8,128)(2,1)} %param.19) | copy-start | bytes 6291460
  (4 other events, 5.6 us)

commit v3 on v2

--- a/solution.py
+++ b/solution.py
@@ -27,42 +27,29 @@
     )
 
 
-def head_exchange(x, count, same_source, ident):
-    rows, cols = x.shape[-2], x.shape[-1]
+def peer_swap(x, across, ident):
     mesh_kind = pl.DeviceIdType.MESH
 
     def kernel(x_ref, o_ref, send_sem, recv_sem):
         me = lax.axis_index("head")
         group = lax.axis_index("grp")
+        peer = lax.rem(me + 2, 4) if across else me + 1 - 2 * lax.rem(me, 2)
         barrier = pltpu.get_barrier_semaphore()
-        for step in range(1, count):
-            peer = lax.rem(me + step, count)
-            pl.semaphore_signal(barrier, inc=1, device_id=(group, peer), device_id_type=mesh_kind)
-        pl.semaphore_wait(barrier, count - 1)
-        copies = []
-        for step in range(1, count):
-            peer = lax.rem(me + step, count)
-            source = x_ref if same_source else x_ref.at[peer]
-            copy = pltpu.make_async_remote_copy(
-                src_ref=source,
-                dst_ref=o_ref.at[me],
-                send_sem=send_sem.at[step - 1],
-                recv_sem=recv_sem.at[step - 1],
-                device_id=(group, peer),
-                device_id_type=mesh_kind,
-            )
-            copy.start()
-            copies.append(copy)
-        o_ref[me] = x_ref[...] if same_source else x_ref[me]
-        for copy in copies:
-            copy.wait()
+        pl.semaphore_signal(barrier, inc=1, device_id=(group, peer), device_id_type=mesh_kind)
+        pl.semaphore_wait(barrier, 1)
+        copy = pltpu.make_async_remote_copy(
+            src_ref=x_ref, dst_ref=o_ref, send_sem=send_sem, recv_sem=recv_sem,
+            device_id=(group, peer), device_id_type=mesh_kind,
+        )
+        copy.start()
+        copy.wait()
 
     return pl.pallas_call(
         kernel,
-        out_shape=jax.ShapeDtypeStruct((count, rows, cols), x.dtype),
-        in_specs=[pl.BlockSpec(memory_space=pltpu.VMEM)],
-        out_specs=pl.BlockSpec(memory_space=pltpu.VMEM),
-        scratch_shapes=[pltpu.SemaphoreType.DMA((count - 1,)), pltpu.SemaphoreType.DMA((count - 1,))],
+        out_shape=jax.ShapeDtypeStruct(x.shape, x.dtype),
+        in_specs=[pl.BlockSpec(memory_space=pl.ANY)],
+        out_specs=pl.BlockSpec(memory_space=pl.ANY),
+        scratch_shapes=[pltpu.SemaphoreType.DMA(()), pltpu.SemaphoreType.DMA(())],
         compiler_params=pltpu.CompilerParams(collective_id=ident, has_side_effects=True),
     )(x)
 
@@ -203,42 +190,63 @@
     place = (target[:, None] == jnp.arange(slots)[None, :]).reshape(tokens, TOPK, slots)
     dispatch = jnp.sum(place.astype(jnp.float32), axis=1).astype(jnp.bfloat16)
     share_width = width // head_count
-    my_columns = lax.dynamic_slice_in_dim(
-        mixed_in, lax.axis_index("head") * share_width, share_width, 1
-    )
+    head_at = lax.axis_index("head")
+    core = lax.rem(head_at, 2)
+    chip = head_at // 2
+    other_core = 1 - core
+    def halves(array, which):
+        split = array.reshape(array.shape[:-1] + (2, 2, share_width))
+        taken = lax.dynamic_index_in_dim(split, which, axis=split.ndim - 2, keepdims=False)
+        return taken.reshape(array.shape[:-1] + (2 * share_width,))
+
+    def row_halves(array, which):
+        split = array.reshape((2, 2, share_width) + array.shape[1:])
+        taken = lax.dynamic_index_in_dim(split, which, axis=1, keepdims=False)
+        return taken.reshape((2 * share_width,) + array.shape[1:])
+
+    half = 2 * share_width
     outgoing = lax.dot_general(
-        dispatch, my_columns, (((0,), (0,)), ((), ())), preferred_element_type=jnp.float32
+        dispatch, halves(mixed_in, core), (((0,), (0,)), ((), ())), preferred_element_type=jnp.float32
     ).astype(jnp.bfloat16)
-    outgoing = outgoing.reshape(group_count, experts_here, capacity, share_width)
+    outgoing = outgoing.reshape(group_count, experts_here, capacity, half)
     arrived = lax.all_to_all(outgoing, "grp", split_axis=0, concat_axis=0, tiled=True)
-    arrived = head_gather(arrived, 2)
-    results = []
+    arrived_other = peer_swap(arrived, False, 1)
+    mine_parts = []
+    other_parts = []
     for expert in range(experts_here):
-        inputs = arrived[:, :, expert].reshape(head_count, group_count * capacity, share_width)
-        gate_w = w_gate[expert].reshape(head_count, share_width, -1)
-        up_w = w_up[expert].reshape(head_count, share_width, -1)
-        gate = jnp.einsum("qrc,qcf->rf", inputs, gate_w, preferred_element_type=jnp.float32)
-        upper = jnp.einsum("qrc,qcf->rf", inputs, up_w, preferred_element_type=jnp.float32)
+        mine = arrived[:, expert].reshape(group_count * capacity, half)
+        other = arrived_other[:, expert].reshape(group_count * capacity, half)
+        gate = jnp.dot(mine, row_halves(w_gate[expert], core), preferred_element_type=jnp.float32)
+        gate = gate + jnp.dot(other, row_halves(w_gate[expert], other_core), preferred_element_type=jnp.float32)
+        upper = jnp.dot(mine, row_halves(w_up[expert], core), preferred_element_type=jnp.float32)
+        upper = upper + jnp.dot(other, row_halves(w_up[expert], other_core), preferred_element_type=jnp.float32)
         act = (jax.nn.silu(gate) * upper).astype(jnp.bfloat16)
-        output = jnp.dot(act, w_down[expert], preferred_element_type=jnp.float32).astype(
-            jnp.bfloat16
-        )
-        results.append(output.reshape(group_count, capacity, width))
-    expert_out = jnp.stack(results, axis=1)
-    returned = lax.all_to_all(expert_out, "grp", split_axis=0, concat_axis=0, tiled=True)
-    returned = returned.reshape(slots, width)
+        mine_parts.append(
+            jnp.dot(act, halves(w_down[expert], core), preferred_element_type=jnp.float32)
+            .astype(jnp.bfloat16)
+            .reshape(group_count, capacity, half)
+        )
+        other_parts.append(
+            jnp.dot(act, halves(w_down[expert], other_core), preferred_element_type=jnp.float32)
+            .astype(jnp.bfloat16)
+            .reshape(group_count, capacity, half)
+        )
+    mine_out = jnp.stack(mine_parts, axis=1)
+    partner_out = peer_swap(jnp.stack(other_parts, axis=1), False, 2)
+    pair_sum = (mine_out.astype(jnp.float32) + partner_out.astype(jnp.float32)).astype(jnp.bfloat16)
+    returned = lax.all_to_all(pair_sum, "grp", split_axis=0, concat_axis=0, tiled=True)
+    returned = returned.reshape(slots, half)
     weighting = jnp.sum(jnp.where(place, weights[:, :, None], 0.0), axis=1)
-    combined = jnp.zeros((tokens, width), jnp.float32)
+    combined = jnp.zeros((tokens, half), jnp.float32)
     for _ in range(3):
         piece = weighting.astype(jnp.bfloat16)
         weighting = weighting - piece.astype(jnp.float32)
         combined = combined + jnp.dot(piece, returned, preferred_element_type=jnp.float32)
-    blocks = combined.reshape(tokens, head_count, share_width).transpose(1, 0, 2)
-    exchanged = head_exchange(blocks.astype(jnp.bfloat16), head_count, False, 1)
-    moe_share = jnp.sum(exchanged.astype(jnp.float32), axis=0)
-    resid_share = lax.dynamic_slice_in_dim(
-        resid, lax.axis_index("head") * share_width, share_width, 1
-    )
+    combined = combined.reshape(tokens, 2, share_width)
+    keep = lax.dynamic_index_in_dim(combined, chip, axis=1, keepdims=False)
+    give = lax.dynamic_index_in_dim(combined, 1 - chip, axis=1, keepdims=False)
+    moe_share = keep + peer_swap(give, True, 3)
+    resid_share = lax.dynamic_slice_in_dim(resid, head_at * share_width, share_width, 1)
     return (resid_share + moe_share).astype(jnp.bfloat16)[None]
 
 

time: 414 us -> 361 us (0.87)
  blocking collectives: 79.2 us -> 0 us
  waiting for transfers between devices: 111 us -> 167 us
  Pallas kernels: 77.3 us -> 36.3 us
  local copies, waits for them, and re-layouts: 54.9 us -> 67.4 us
  matrix products: 46.1 us -> 36.4 us
  starting transfers between devices: 22.3 us -> 29 us
    all_to_all x1 -> x0, blocking collectives: 79.2 us -> none  [on_device(): lax.all_to_all(expert_out, 'grp', split_axis=0, concat_axis=0, tiled=True)]
    pallas_call x2 -> x1, Pallas kernels: 67.5 us -> 17.1 us  [head_gather(): pl.pallas_call(kernel, out_shape=jax.ShapeDtypeStruct((4,) + x.shape, x.d...]
    all_to_all x0 -> x1, waiting for transfers between devices: none -> 43.3 us  [on_device(): lax.all_to_all(pair_sum, 'grp', split_axis=0, concat_axis=0, tiled=True)]
    all_to_all x1, waiting for transfers between devices: 19.7 us -> 33.1 us  [on_device(): lax.all_to_all(outgoing, 'grp', split_axis=0, concat_axis=0, tiled=True)]
    pallas_call x1 -> x3, Pallas kernels: 9.73 us -> 19.3 us  [peer_swap(): pl.pallas_call(kernel, out_shape=jax.ShapeDtypeStruct(x.shape, x.dtype),...]
    dot_general x5 -> x13, matrix products: 20.5 us -> 12 us  [the longest x2 3.35 us: on_device(): jnp.dot(act, halves(w_down[expert], core), preferred_element_type=jnp.flo...]
    all_to_all x0 -> x1, starting transfers between devices: none -> 6.65 us  [on_device(): lax.all_to_all(pair_sum, 'grp', split_axis=0, concat_axis=0, tiled=True)]
    dynamic_slice x1 -> x6, local copies, waits for them, and re-layouts: 1.36 us -> 7.46 us  [the longest x3 4.18 us: halves(): lax.dynamic_index_in_dim(split, which, axis=split.ndim - 2, keepdims=False)]
  transfers between devices with their start and end apart: 2 -> 3, of which waited for: 2 -> 3; matrix products, arithmetic and copies ran while one was open for 9% -> 11% of each run, Pallas kernels for 0% -> 0%
where the time goes in v3:
time: 361 us; the launch traced here: 359 us
  waiting for transfers between devices  167 us (46%)
  local copies, waits for them, and re-layouts  67.4 us (19%)
  matrix products  36.4 us (10%)
  Pallas kernels  36.3 us (10%)
  starting transfers between devices  29 us (8%)
  other arithmetic  21.5 us (6%)
    all_to_all x1, waiting for transfers between devices, on_device(): lax.all_to_all(cache, 'grp', split_axis=1, concat_axis=2, tiled=True)  91.1 us
    all_to_all x1, waiting for transfers between devices, on_device(): lax.all_to_all(pair_sum, 'grp', split_axis=0, concat_axis=0, tiled=True)  43.3 us
    all_to_all x1, waiting for transfers between devices, on_device(): lax.all_to_all(outgoing, 'grp', split_axis=0, concat_axis=0, tiled=True)  33.1 us
    pallas_call x3, Pallas kernels, peer_swap(): pl.pallas_call(kernel, out_shape=jax.ShapeDtypeStruct(x.shape, x.dtype),...  19.3 us
    pallas_call x1, Pallas kernels, head_gather(): pl.pallas_call(kernel, out_shape=jax.ShapeDtypeStruct((4,) + x.shape, x.d...  17.1 us
    unnamed x77, local copies, waits for them, and re-layouts  13.2 us
    all_to_all x1, starting transfers between devices, on_device(): lax.all_to_all(outgoing, 'grp', split_axis=0, concat_axis=0, tiled=True)  12.1 us
    all_to_all x1, starting transfers between devices, on_device(): lax.all_to_all(cache, 'grp', split_axis=1, concat_axis=2, tiled=True)  10.2 us
  transfers between devices with their start and end apart: 3, of which 3 were waited for; matrix products, arithmetic and copies ran while one was open for 11% of the time, Pallas kernels for 0%

profile of v3, /device:TPU:10, one launch (start us, length us, event | category | flops | bytes accessed | tf_op | source)
XLA Modules:
  0.0 358.9 jit_solution(4238743406911683105)
XLA Ops:
  0.0 7.7 %copy.86 = bf16[2,32,128,512]{3,2,0,1:T(8,128)(2,1)} copy(bf16[2,32,128,512]{3,2,1,0:T(8,128)(2,1)} %param.20) | data formatting | bytes 16777216 | tf_op args[6]
  7.7 10.2 %all-to-all-start = ((bf16[2,32,128,512]{3,2,0,1:T(8,128)(2,1)}), bf16[2,32,128,512]{3,2,0,1:T(8,128)(2,1)}, u32[]{:S(2)}, u32[]{:S(2)}) async-start(bf16[2,32,128,512]{3,2,0,1:T(8,128)(2,1)} %copy.86), calls=%async_computation | async-start | bytes 16777216 | tf_op jit(solution)/shard_map/all_to_all | solution.py:144
  17.9 3.9 %copy.117 = bf16[512,2048]{1,0:T(8,128)(2,1)} copy(bf16[512,2048]{0,1:T(8,128)(2,1)} %bitcast.149) | data formatting | bytes 4194304 | tf_op jit(solution)/shard_map/dot_general | solution.py:135
  21.9 3.9 %copy.113 = bf16[512,2048]{1,0:T(8,128)(2,1)} copy(bf16[512,2048]{0,1:T(8,128)(2,1)} %bitcast.150) | data formatting | bytes 4194304 | tf_op jit(solution)/shard_map/dot_general | solution.py:132
  25.8 4.0 %copy.119 = bf16[512,2048]{1,0:T(8,128)(2,1)} copy(bf16[512,2048]{0,1:T(8,128)(2,1)} %bitcast.151) | data formatting | bytes 4194304 | tf_op jit(solution)/shard_map/dot_general | solution.py:138
  42.1 7.0 %select_reduce_fusion.1 = (f32[128,1536]{1,0:T(8,128)S(1)}, bf16[128,1536]{1,0:T(8,128)(2,1)}) fusion(f32[128,8]{1,0:T(8,128)S(1)} %copy-done.23, s32[128,8]{1,0:T(8,128)S(1)} %bitcast_add_fusion.1), kind=kLoop, calls=%fused_computation.6 | loop fusion | flops 7471104 | bytes 1187840 | tf_op jit(solution)/shard_map/reduce_sum | solution.py:239
  49.1 91.1 %all-to-all-done = bf16[2,32,128,512]{3,2,0,1:T(8,128)(2,1)} async-done(((bf16[2,32,128,512]{3,2,0,1:T(8,128)(2,1)}), bf16[2,32,128,512]{3,2,0,1:T(8,128)(2,1)}, u32[]{:S(2)}, u32[]{:S(2)}) %all-to-all-start) | async-done | bytes 8388640 | tf_op jit(solution)/shard_map/all_to_all | solution.py:144
  140.1 5.9 %fusion.65 = (bf16[1,32,128,512]{3,2,0,1:T(8,128)(2,1)}, bf16[1,32,128,512]{3,2,0,1:T(8,128)(2,1)}) fusion(bf16[2,32,128,512]{3,2,0,1:T(8,128)(2,1)} %all-to-all-done), kind=kLoop, calls=%fused_computation.119 | loop fusion | bytes 16777216 | tf_op jit(solution)/shard_map/slice | solution.py:146
  146.0 6.9 %reshape.280 = bf16[4096,4,128]{2,1,0:T(4,128)(2,1)} reshape(bf16[1,32,128,512]{3,2,0,1:T(8,128)(2,1)} %get-tuple-element.10) | data formatting | bytes 8388608 | tf_op jit(solution)/shard_map/reshape;squeeze | solution.py:147
  152.9 7.0 %reshape.279 = bf16[4096,4,128]{2,1,0:T(4,128)(2,1)} reshape(bf16[1,32,128,512]{3,2,0,1:T(8,128)(2,1)} %get-tuple-element.9) | data formatting | bytes 8388608 | tf_op jit(solution)/shard_map/reshape;squeeze | solution.py:146
  159.9 3.9 %select_reduce_fusion = (f32[4,128]{1,0:T(4,128)S(1)}, f32[4,128,4096]{2,1,0:T(8,128)S(1)}) fusion(pred[4096]{0:T(1024)(128)(4,1)S(1)} %iota_compare_fusion.10, bf16[4096,4,128]{2,1,0:T(4,128)(2,1)} %reshape.279, f32[128,4,64]{0,2,1:T(8,128)S(1)} %get-tuple-element.39, f32[128,4,64]{0,2,1:T(8,128)} %copy-done.20), kind=kOutput, calls=%fused_computation.1 | convolution fusion | flops 541261312 | bytes 12851200 | tf_op jit(solution)/shard_map/qhd,khd->hqk/dot_general | solution.py:148
  166.0 3.6 %fusion.19 = f32[128,4,128]{0,2,1:T(8,128)} fusion(bf16[4096,4,128]{2,1,0:T(4,128)(2,1)S(1)} %copy-done.5, f32[4,128,4096]{2,1,0:T(8,128)S(1)} %get-tuple-element.44, f32[4,128]{1,0:T(4,128)S(1)} %max.8, pred[4096]{0:T(1024)(128)(4,1)S(1)} %iota_compare_fusion.10), kind=kOutput, calls=%fused_computation.41 | convolution fusion | flops 545259520 | bytes 12851200 | tf_op jit(solution)/shard_map/hqk,khd->qhd/dot_general | solution.py:160
  169.7 2.7 fusion.24
  173.7 17.1 %shard_map.136 = bf16[4,128,2048]{2,1,0:T(8,128)(2,1)} custom-call(bf16[128,2048]{1,0:T(8,128)(2,1)} %convolution_convert_fusion.1.x_ref), custom_call_target="tpu_custom_call" | custom-call | tf_op jit(solution)/shard_map/pallas_call | solution.py:92
  199.3 2.7 convolution_convert_fusion
  201.9 12.1 %all-to-all-start.1 = ((bf16[32,2,24,1024]{3,2,1,0:T(8,128)(2,1)}), bf16[32,2,24,1024]{3,2,1,0:T(8,128)(2,1)}, u32[]{:S(2)}, u32[]{:S(2)}) async-start(bf16[32,2,24,1024]{3,2,1,0:T(8,128)(2,1)} %bitcast.126), calls=%async_computation.1 | async-start | bytes 6291456 | tf_op jit(solution)/shard_map/all_to_all | solution.py:212
  214.1 2.9 fusion.68
  225.5 33.1 %all-to-all-done.1.x_ref = bf16[32,2,24,1024]{3,2,1,0:T(8,128)(2,1)} async-done(((bf16[32,2,24,1024]{3,2,1,0:T(8,128)(2,1)}), bf16[32,2,24,1024]{3,2,1,0:T(8,128)(2,1)}, u32[]{:S(2)}, u32[]{:S(2)}) %all-to-all-start.1) | async-done | bytes 3145760 | tf_op jit(solution)/shard_map/all_to_all | solution.py:212
  258.5 6.0 %shard_map.137 = bf16[32,2,24,1024]{3,2,1,0:T(8,128)(2,1)} custom-call(bf16[32,2,24,1024]{3,2,1,0:T(8,128)(2,1)} %all-to-all-done.1.x_ref), custom_call_target="tpu_custom_call" | custom-call | tf_op jit(solution)/shard_map/pallas_call | solution.py:47
  278.0 6.0 %shard_map.138 = bf16[32,2,24,1024]{3,2,1,0:T(8,128)(2,1)} custom-call(bf16[32,2,24,1024]{3,2,1,0:T(8,128)(2,1)} %pad_maximum_fusion.x_ref), custom_call_target="tpu_custom_call" | custom-call | tf_op jit(solution)/shard_map/pallas_call | solution.py:47
  287.5 3.3 add_convert_fusion
  290.7 6.6 %all-to-all-start.2 = ((bf16[32,2,24,1024]{3,2,1,0:T(8,128)(2,1)}), bf16[32,2,24,1024]{3,2,1,0:T(8,128)(2,1)}, u32[]{:S(2)}, u32[]{:S(2)}) async-start(bf16[32,2,24,1024]{3,2,1,0:T(8,128)(2,1)} %add_convert_fusion), calls=%async_computation.2 | async-start | bytes 6291456 | tf_op jit(solution)/shard_map/all_to_all | solution.py:237
  297.4 43.3 %all-to-all-done.2 = bf16[32,2,24,1024]{3,2,1,0:T(8,128)(2,1)} async-done(((bf16[32,2,24,1024]{3,2,1,0:T(8,128)(2,1)}), bf16[32,2,24,1024]{3,2,1,0:T(8,128)(2,1)}, u32[]{:S(2)}, u32[]{:S(2)}) %all-to-all-start.2) | async-done | bytes 3145760 | tf_op jit(solution)/shard_map/all_to_all | solution.py:237
  349.9 7.2 %shard_map.139 = f32[128,512]{1,0:T(8,128)} custom-call(f32[128,512]{1,0:T(8,128)} %bitcast.157), custom_call_target="tpu_custom_call" | custom-call | tf_op jit(solution)/shard_map/pallas_call | solution.py:47
  (135 shorter events, 59.9 us)
Async XLA Ops:
  0.0 172.5 %copy-start = (bf16[512,2048]{1,0:T(8,128)(2,1)S(1)}, bf16[512,2048]{1,0:T(8,128)(2,1)}, u32[]{:S(2)}) copy-start(bf16[512,2048]{1,0:T(8,128)(2,1)} %param.19) | copy-start | bytes 6291460
  7.7 132.4 %all-to-all-start = ((bf16[2,32,128,512]{3,2,0,1:T(8,128)(2,1)}), bf16[2,32,128,512]{3,2,0,1:T(8,128)(2,1)}, u32[]{:S(2)}, u32[]{:S(2)}) async-start(bf16[2,32,128,512]{3,2,0,1:T(8,128)(2,1)} %copy.86), calls=%async_computation | async-start | bytes 16777216 | tf_op jit(solution)/shard_map/all_to_all | solution.py:144
  25.8 4.1 %copy-start.2 = (bf16[1,128,2048]{2,1,0:T(8,128)(2,1)S(1)}, bf16[1,128,2048]{2,1,0:T(8,128)(2,1)}, u32[]{:S(2)}) copy-start(bf16[1,128,2048]{2,1,0:T(8,128)(2,1)} %param.14) | copy-start | bytes 1572868
  25.8 6.0 %copy-start.29 = (f32[2048]{0:T(1024)S(1)}, f32[2048]{0:T(1024)}, u32[]{:S(2)}) copy-start(f32[2048]{0:T(1024)} %param.22) | copy-start | bytes 24580
  25.8 6.0 %copy-start.30 = (f32[1,128,8]{1,2,0:T(8,128)S(1)}, f32[1,128,8]{1,2,0:T(8,128)}, u32[]{:S(2)}) copy-start(f32[1,128,8]{1,2,0:T(8,128)} %param.24) | copy-start | bytes 12292
  25.8 6.7 %copy-start.31 = (s32[1,128,8]{1,2,0:T(8,128)S(1)}, s32[1,128,8]{1,2,0:T(8,128)}, u32[]{:S(2)}) copy-start(s32[1,128,8]{1,2,0:T(8,128)} %param.23) | copy-start | bytes 12292
  25.8 7.6 %copy-start.34 = (s32[32]{0:T(128)S(1)}, s32[32]{0:T(128)}, u32[]{:S(2)}) copy-start(s32[32]{0:T(128)} %param.21) | copy-start | bytes 388
  29.9 6.7 %copy-start.27 = (f32[2048]{0:T(1024)S(1)}, f32[2048]{0:T(1024)}, u32[]{:S(2)}) copy-start(f32[2048]{0:T(1024)} %param.15) | copy-start | bytes 24580
  34.0 5.0 %copy-start.4 = (bf16[512,2048]{1,0:T(8,128)(2,1)S(1)}, bf16[512,2048]{1,0:T(8,128)(2,1)}, u32[]{:S(2)}) copy-start(bf16[512,2048]{1,0:T(8,128)(2,1)} %copy.113) | copy-start | bytes 6291460
  36.1 3.8 %copy-start.25 = (pred[128,128]{0,1:T(8,128)(4,1)}, pred[128,128]{0,1:T(8,128)(4,1)S(1)}, u32[]{:S(2)}) copy-start(pred[128,128]{0,1:T(8,128)(4,1)S(1)} %iota_compare_fusion.9) | copy-start | bytes 49156
  36.3 3.5 copy-start.32
  36.6 5.5 %copy-start.23 = (f32[128,8]{1,0:T(8,128)S(1)}, f32[128,8]{1,0:T(8,128)}, u32[]{:S(2)}) copy-start(f32[128,8]{1,0:T(8,128)} %copy.99) | copy-start | bytes 12292
  159.9 3.9 %copy-start.33 = (f32[4,128]{1,0:T(4,128)S(1)}, f32[4,128]{1,0:T(4,128)}, u32[]{:S(2)}) copy-start(f32[4,128]{1,0:T(4,128)} %get-tuple-element.45) | copy-start | bytes 6148
  166.0 3.6 %copy-start.24 = (f32[4,128,128]{1,2,0:T(8,128)S(1)}, f32[4,128,128]{1,2,0:T(8,128)}, u32[]{:S(2)}) copy-start(f32[4,128,128]{1,2,0:T(8,128)} %get-tuple-element.46) | copy-start | bytes 786436
  166.0 3.6 %copy-start.26 = (pred[128,128]{0,1:T(8,128)(4,1)S(1)}, pred[128,128]{0,1:T(8,128)(4,1)}, u32[]{:S(2)}) copy-start(pred[128,128]{0,1:T(8,128)(4,1)} %copy-done.25) | copy-start | bytes 49156
  192.9 3.0 copy-start.6
  194.8 4.2 %copy-start.28 = (f32[2,1,512]{2,0,1:T(2,128)S(1)}, f32[2,1,512]{2,0,1:T(2,128)}, u32[]{:S(2)}) copy-start(f32[2,1,512]{2,0,1:T(2,128)} %constant_dynamic-slice_fusion.16) | copy-start | bytes 12292
  201.9 56.6 %all-to-all-start.1 = ((bf16[32,2,24,1024]{3,2,1,0:T(8,128)(2,1)}), bf16[32,2,24,1024]{3,2,1,0:T(8,128)(2,1)}, u32[]{:S(2)}, u32[]{:S(2)}) async-start(bf16[32,2,24,1024]{3,2,1,0:T(8,128)(2,1)} %bitcast.126), calls=%async_computation.1 | async-start | bytes 6291456 | tf_op jit(solution)/shard_map/all_to_all | solution.py:212
  266.8 2.3 copy-start.14
  266.8 2.9 copy-start.13
  278.0 6.0 %copy-start.7 = (bf16[256,2,1,512]{0,3,2,1:T(8,128)(2,1)S(1)}, bf16[256,2,1,512]{0,3,2,1:T(8,128)(2,1)}, u32[]{:S(2)}) copy-start(bf16[256,2,1,512]{0,3,2,1:T(8,128)(2,1)} %get-tuple-element.23) | copy-start | bytes 1572868
  284.1 3.4 copy-start.3
  290.7 49.9 %all-to-all-start.2 = ((bf16[32,2,24,1024]{3,2,1,0:T(8,128)(2,1)}), bf16[32,2,24,1024]{3,2,1,0:T(8,128)(2,1)}, u32[]{:S(2)}, u32[]{:S(2)}) async-start(bf16[32,2,24,1024]{3,2,1,0:T(8,128)(2,1)} %add_convert_fusion), calls=%async_computation.2 | async-start | bytes 6291456 | tf_op jit(solution)/shard_map/all_to_all | solution.py:237
  345.6 13.3 %copy-start.1 = (bf16[512,2048]{1,0:T(8,128)(2,1)S(1)}, bf16[512,2048]{1,0:T(8,128)(2,1)}, u32[]{:S(2)}) copy-start(bf16[512,2048]{1,0:T(8,128)(2,1)} %param.19) | copy-start | bytes 6291460
  (14 other events, 19.6 us)

commit v4 on v3

--- a/solution.py
+++ b/solution.py
@@ -101,6 +101,55 @@
         ],
         compiler_params=pltpu.CompilerParams(collective_id=ident, has_side_effects=True),
     )(x)
+
+
+def attend(length, query, key_new, value_new, relaid):
+    tokens = query.shape[0]
+    context = relaid.shape[2]
+    heads = query.shape[1] // HD
+
+    def kernel(length_ref, q_ref, kn_ref, vn_ref, k_ref, v_ref, o_ref):
+        limit = length_ref[0]
+        q = q_ref[...]
+        contract = (((1,), (1,)), ((), ()))
+        score_old = lax.dot_general(q, k_ref[0, 0], contract, preferred_element_type=jnp.float32)
+        score_new = lax.dot_general(q, kn_ref[...], contract, preferred_element_type=jnp.float32)
+        allow_old = lax.broadcasted_iota(jnp.int32, score_old.shape, 1) < limit
+        allow_new = lax.broadcasted_iota(jnp.int32, score_new.shape, 1) <= lax.broadcasted_iota(
+            jnp.int32, score_new.shape, 0
+        )
+        score_old = jnp.where(allow_old, score_old, -1e30)
+        score_new = jnp.where(allow_new, score_new, -1e30)
+        top = jnp.maximum(
+            jnp.max(score_old, axis=1, keepdims=True), jnp.max(score_new, axis=1, keepdims=True)
+        )
+        prob_old = jnp.where(allow_old, jnp.exp(score_old - top), 0.0)
+        prob_new = jnp.where(allow_new, jnp.exp(score_new - top), 0.0)
+        total = jnp.sum(prob_old, axis=1, keepdims=True) + jnp.sum(prob_new, axis=1, keepdims=True)
+        numer = jnp.dot(prob_old.astype(jnp.bfloat16), v_ref[0, 0], preferred_element_type=jnp.float32)
+        numer = numer + jnp.dot(
+            prob_new.astype(jnp.bfloat16), vn_ref[...], preferred_element_type=jnp.float32
+        )
+        o_ref[...] = (numer / total).astype(o_ref.dtype)
+
+    per_head = pl.BlockSpec((tokens, HD), lambda h, n: (0, h))
+    grid_spec = pltpu.PrefetchScalarGridSpec(
+        num_scalar_prefetch=1,
+        grid=(heads,),
+        in_specs=[
+            per_head,
+            per_head,
+            per_head,
+            pl.BlockSpec((1, 1, context, HD), lambda h, n: (0, 0, 0, h)),
+            pl.BlockSpec((1, 1, context, HD), lambda h, n: (1, 0, 0, h)),
+        ],
+        out_specs=per_head,
+    )
+    return pl.pallas_call(
+        kernel,
+        grid_spec=grid_spec,
+        out_shape=jax.ShapeDtypeStruct((tokens, heads * HD), jnp.bfloat16),
+    )(length.reshape(1), query, key_new, value_new, relaid, relaid)
 
 
 def on_device(
@@ -142,34 +191,12 @@
     key_new = rotate(key_new, position).astype(jnp.bfloat16)
     value_new = value_new.astype(jnp.bfloat16)
     relaid = lax.all_to_all(cache, "grp", split_axis=1, concat_axis=2, tiled=True)
-    context = relaid.shape[2]
-    cache_key = relaid[0, 0].reshape(context, heads_here, HD)
-    cache_value = relaid[1, 0].reshape(context, heads_here, HD)
-    score_old = jnp.einsum("qhd,khd->hqk", query, cache_key, preferred_element_type=jnp.float32)
-    score_new = jnp.einsum("qhd,khd->hqk", query, key_new, preferred_element_type=jnp.float32)
-    allow_old = (jnp.arange(context) < length)[None, None, :]
-    allow_new = (jnp.arange(tokens)[None, :] <= jnp.arange(tokens)[:, None])[None, :, :]
-    score_old = jnp.where(allow_old, score_old, -1e30)
-    score_new = jnp.where(allow_new, score_new, -1e30)
-    top = jnp.maximum(
-        jnp.max(score_old, axis=-1, keepdims=True), jnp.max(score_new, axis=-1, keepdims=True)
-    )
-    prob_old = jnp.where(allow_old, jnp.exp(score_old - top), 0.0)
-    prob_new = jnp.where(allow_new, jnp.exp(score_new - top), 0.0)
-    total = jnp.sum(prob_old, axis=-1) + jnp.sum(prob_new, axis=-1)
-    numer = jnp.einsum(
-        "hqk,khd->qhd",
-        prob_old.astype(jnp.bfloat16),
-        cache_value,
-        preferred_element_type=jnp.float32,
-    )
-    numer = numer + jnp.einsum(
-        "hqk,khd->qhd", prob_new.astype(jnp.bfloat16), value_new, preferred_element_type=jnp.float32
-    )
-    attended = (
-        (numer / jnp.transpose(total)[:, :, None])
-        .reshape(tokens, heads_here * HD)
-        .astype(jnp.bfloat16)
+    attended = attend(
+        length,
+        query.reshape(tokens, heads_here * HD),
+        key_new.reshape(tokens, heads_here * HD),
+        value_new.reshape(tokens, heads_here * HD),
+        relaid,
     )
     projected = jnp.dot(attended, w_out, preferred_element_type=jnp.float32)
     gathered = head_gather(projected.astype(jnp.bfloat16), 0)

time: 361 us -> 346 us (0.958)
  local copies, waits for them, and re-layouts: 67.4 us -> 56.8 us
  matrix products: 36.4 us -> 26.9 us
  Pallas kernels: 36.3 us -> 45 us
    another operation x2 -> x0, local copies, waits for them, and re-layouts: 13.9 us -> none  [the longest x1 6.98 us: on_device(): cache_key = relaid[0, 0].reshape(context, heads_here, HD)]
    dot_general x4 -> x1, matrix products: 11.8 us -> 2.42 us  [on_device(): jnp.dot(normed, w_value, preferred_element_type=jnp.float32)]
    pallas_call x0 -> x1, Pallas kernels: none -> 8.65 us  [attend(): pl.pallas_call(kernel, grid_spec=grid_spec, out_shape=jax.ShapeDtypeStruc...]
    all_to_all x0 -> x1, local copies, waits for them, and re-layouts: none -> 7.59 us  [on_device(): lax.all_to_all(cache, 'grp', split_axis=1, concat_axis=2, tiled=True)]
    slice x1 -> x0, local copies, waits for them, and re-layouts: 5.87 us -> none  [on_device(): cache_key = relaid[0, 0].reshape(context, heads_here, HD)]
    unnamed x77 -> x63, local copies, waits for them, and re-layouts: 13.2 us -> 14.9 us
  transfers between devices with their start and end apart: 3 -> 3, of which waited for: 3 -> 3; matrix products, arithmetic and copies ran while one was open for 11% -> 12% of each run, Pallas kernels for 0% -> 0%
where the time goes in v4:
time: 346 us; the launch traced here: 344 us
  waiting for transfers between devices  167 us (48%)
  local copies, waits for them, and re-layouts  56.8 us (16%)
  Pallas kernels  45 us (13%)
  starting transfers between devices  29 us (8%)
  matrix products  26.9 us (8%)
  other arithmetic  18.5 us (5%)
    all_to_all x1, waiting for transfers between devices, on_device(): lax.all_to_all(cache, 'grp', split_axis=1, concat_axis=2, tiled=True)  90.5 us
    all_to_all x1, waiting for transfers between devices, on_device(): lax.all_to_all(pair_sum, 'grp', split_axis=0, concat_axis=0, tiled=True)  43.3 us
    all_to_all x1, waiting for transfers between devices, on_device(): lax.all_to_all(outgoing, 'grp', split_axis=0, concat_axis=0, tiled=True)  33.1 us
    pallas_call x3, Pallas kernels, peer_swap(): pl.pallas_call(kernel, out_shape=jax.ShapeDtypeStruct(x.shape, x.dtype),...  19.3 us
    pallas_call x1, Pallas kernels, head_gather(): pl.pallas_call(kernel, out_shape=jax.ShapeDtypeStruct((4,) + x.shape, x.d...  17.1 us
    unnamed x63, local copies, waits for them, and re-layouts  14.9 us
    all_to_all x1, starting transfers between devices, on_device(): lax.all_to_all(outgoing, 'grp', split_axis=0, concat_axis=0, tiled=True)  12.1 us
    all_to_all x1, starting transfers between devices, on_device(): lax.all_to_all(cache, 'grp', split_axis=1, concat_axis=2, tiled=True)  10.2 us
  transfers between devices with their start and end apart: 3, of which 3 were waited for; matrix products, arithmetic and copies ran while one was open for 12% of the time, Pallas kernels for 0%

profile of v4, /device:TPU:10, one launch (start us, length us, event | category | flops | bytes accessed | tf_op | source)
XLA Modules:
  0.0 343.7 jit_solution(11110727107881364836)
XLA Ops:
  0.0 7.7 %copy.78 = bf16[2,32,128,512]{3,2,0,1:T(8,128)(2,1)} copy(bf16[2,32,128,512]{3,2,1,0:T(8,128)(2,1)} %param.20) | data formatting | bytes 16777216 | tf_op args[6]
  7.7 10.2 %all-to-all-start = ((bf16[2,32,128,512]{3,2,0,1:T(8,128)(2,1)}), bf16[2,32,128,512]{3,2,0,1:T(8,128)(2,1)}, u32[]{:S(2)}, u32[]{:S(2)}) async-start(bf16[2,32,128,512]{3,2,0,1:T(8,128)(2,1)} %copy.78), calls=%async_computation | async-start | bytes 16777216 | tf_op jit(solution)/shard_map/all_to_all | solution.py:193
  17.9 4.0 %copy.92 = bf16[512,2048]{1,0:T(8,128)(2,1)} copy(bf16[512,2048]{0,1:T(8,128)(2,1)} %bitcast.133) | data formatting | bytes 4194304 | tf_op jit(solution)/shard_map/dot_general | solution.py:184
  21.9 4.0 %copy.90 = bf16[512,2048]{1,0:T(8,128)(2,1)} copy(bf16[512,2048]{0,1:T(8,128)(2,1)} %bitcast.134) | data formatting | bytes 4194304 | tf_op jit(solution)/shard_map/dot_general | solution.py:181
  34.4 4.0 %copy.94 = bf16[512,2048]{1,0:T(8,128)(2,1)} copy(bf16[512,2048]{0,1:T(8,128)(2,1)} %bitcast.135) | data formatting | bytes 4194304 | tf_op jit(solution)/shard_map/dot_general | solution.py:187
  38.4 2.4 convolution_convert_fusion.6
  42.6 7.0 %select_reduce_fusion = (f32[128,1536]{1,0:T(8,128)S(1)}, bf16[128,1536]{1,0:T(8,128)(2,1)}) fusion(f32[128,8]{1,0:T(8,128)S(1)} %copy.82, s32[128,8]{1,0:T(8,128)S(1)} %bitcast_add_fusion.1), kind=kLoop, calls=%fused_computation.2 | loop fusion | flops 7471104 | bytes 1187840 | tf_op jit(solution)/shard_map/reduce_sum | solution.py:266
  49.6 90.5 %all-to-all-done = bf16[2,32,128,512]{3,2,0,1:T(8,128)(2,1)} async-done(((bf16[2,32,128,512]{3,2,0,1:T(8,128)(2,1)}), bf16[2,32,128,512]{3,2,0,1:T(8,128)(2,1)}, u32[]{:S(2)}, u32[]{:S(2)}) %all-to-all-start) | async-done | bytes 8388640 | tf_op jit(solution)/shard_map/all_to_all | solution.py:193
  140.1 7.6 %copy.79 = bf16[2,32,128,512]{3,2,1,0:T(8,128)(2,1)} copy(bf16[2,32,128,512]{3,2,0,1:T(8,128)(2,1)} %all-to-all-done) | data formatting | bytes 16777216 | tf_op jit(solution)/shard_map/all_to_all | solution.py:193
  147.7 8.6 %shard_map.136 = bf16[128,512]{1,0:T(8,128)(2,1)} custom-call(s32[1]{0:T(128)} %dynamic_slice.55.length_ref, bf16[128,512]{1,0:T(8,128)(2,1)} %copy.91.q_ref, bf16[128,512]{1,0:T(8,128)(2,1)} %copy.93.kn_ref, bf16[128,512]{1,0:T(8,128)(2,1)} %copy.95.vn_ref, bf16[2,1,4096,512]{3,2,1,0:T(8,128)(2,1)} %bitcast.104, bf16[2,1,4096,512]{3,2,1,0:T(8,128)(2,1)} %bitcast.105), custom_call_target="tpu_custom_call" | custom-call | tf_op jit(solution)/shard_map/pallas_call | solution.py:148
  158.6 17.1 %shard_map.137 = bf16[4,128,2048]{2,1,0:T(8,128)(2,1)} custom-call(bf16[128,2048]{1,0:T(8,128)(2,1)} %convolution_convert_fusion.1.x_ref), custom_call_target="tpu_custom_call" | custom-call | tf_op jit(solution)/shard_map/pallas_call | solution.py:92
  183.3 2.7 convolution_convert_fusion
  186.0 12.1 %all-to-all-start.1 = ((bf16[32,2,24,1024]{3,2,1,0:T(8,128)(2,1)}), bf16[32,2,24,1024]{3,2,1,0:T(8,128)(2,1)}, u32[]{:S(2)}, u32[]{:S(2)}) async-start(bf16[32,2,24,1024]{3,2,1,0:T(8,128)(2,1)} %bitcast.110), calls=%async_computation.1 | async-start | bytes 6291456 | tf_op jit(solution)/shard_map/all_to_all | solution.py:239
  198.2 2.9 fusion.28
  209.5 33.1 %all-to-all-done.1.x_ref = bf16[32,2,24,1024]{3,2,1,0:T(8,128)(2,1)} async-done(((bf16[32,2,24,1024]{3,2,1,0:T(8,128)(2,1)}), bf16[32,2,24,1024]{3,2,1,0:T(8,128)(2,1)}, u32[]{:S(2)}, u32[]{:S(2)}) %all-to-all-start.1) | async-done | bytes 3145760 | tf_op jit(solution)/shard_map/all_to_all | solution.py:239
  242.6 6.0 %shard_map.138 = bf16[32,2,24,1024]{3,2,1,0:T(8,128)(2,1)} custom-call(bf16[32,2,24,1024]{3,2,1,0:T(8,128)(2,1)} %all-to-all-done.1.x_ref), custom_call_target="tpu_custom_call" | custom-call | tf_op jit(solution)/shard_map/pallas_call | solution.py:47
  263.8 6.0 %shard_map.139 = bf16[32,2,24,1024]{3,2,1,0:T(8,128)(2,1)} custom-call(bf16[32,2,24,1024]{3,2,1,0:T(8,128)(2,1)} %pad_maximum_fusion.x_ref), custom_call_target="tpu_custom_call" | custom-call | tf_op jit(solution)/shard_map/pallas_call | solution.py:47
  272.3 3.3 add_convert_fusion
  275.6 6.7 %all-to-all-start.2 = ((bf16[32,2,24,1024]{3,2,1,0:T(8,128)(2,1)}), bf16[32,2,24,1024]{3,2,1,0:T(8,128)(2,1)}, u32[]{:S(2)}, u32[]{:S(2)}) async-start(bf16[32,2,24,1024]{3,2,1,0:T(8,128)(2,1)} %add_convert_fusion), calls=%async_computation.2 | async-start | bytes 6291456 | tf_op jit(solution)/shard_map/all_to_all | solution.py:264
  282.2 43.3 %all-to-all-done.2 = bf16[32,2,24,1024]{3,2,1,0:T(8,128)(2,1)} async-done(((bf16[32,2,24,1024]{3,2,1,0:T(8,128)(2,1)}), bf16[32,2,24,1024]{3,2,1,0:T(8,128)(2,1)}, u32[]{:S(2)}, u32[]{:S(2)}) %all-to-all-start.2) | async-done | bytes 3145760 | tf_op jit(solution)/shard_map/all_to_all | solution.py:264
  325.5 2.5 fusion.9
  328.0 2.5 convolution_add_fusion.5
  330.5 2.6 convolution_add_fusion.4
  334.7 7.2 %shard_map.140 = f32[128,512]{1,0:T(8,128)} custom-call(f32[128,512]{1,0:T(8,128)} %bitcast.141), custom_call_target="tpu_custom_call" | custom-call | tf_op jit(solution)/shard_map/pallas_call | solution.py:47
  (116 shorter events, 49.2 us)
Async XLA Ops:
  0.0 156.4 %copy-start = (bf16[512,2048]{1,0:T(8,128)(2,1)S(1)}, bf16[512,2048]{1,0:T(8,128)(2,1)}, u32[]{:S(2)}) copy-start(bf16[512,2048]{1,0:T(8,128)(2,1)} %param.19) | copy-start | bytes 6291460
  7.7 132.4 %all-to-all-start = ((bf16[2,32,128,512]{3,2,0,1:T(8,128)(2,1)}), bf16[2,32,128,512]{3,2,0,1:T(8,128)(2,1)}, u32[]{:S(2)}, u32[]{:S(2)}) async-start(bf16[2,32,128,512]{3,2,0,1:T(8,128)(2,1)} %copy.78), calls=%async_computation | async-start | bytes 16777216 | tf_op jit(solution)/shard_map/all_to_all | solution.py:193
  21.9 4.0 %copy-start.2 = (bf16[1,128,2048]{2,1,0:T(8,128)(2,1)S(1)}, bf16[1,128,2048]{2,1,0:T(8,128)(2,1)}, u32[]{:S(2)}) copy-start(bf16[1,128,2048]{2,1,0:T(8,128)(2,1)} %param.14) | copy-start | bytes 1572868
  21.9 5.9 %copy-start.27 = (s32[32]{0:T(128)S(1)}, s32[32]{0:T(128)}, u32[]{:S(2)}) copy-start(s32[32]{0:T(128)} %param.21) | copy-start | bytes 388
  25.9 3.6 %copy-start.23 = (f32[2048]{0:T(1024)S(1)}, f32[2048]{0:T(1024)}, u32[]{:S(2)}) copy-start(f32[2048]{0:T(1024)} %param.15) | copy-start | bytes 24580
  27.9 4.1 %copy-start.4 = (bf16[512,2048]{1,0:T(8,128)(2,1)S(1)}, bf16[512,2048]{1,0:T(8,128)(2,1)}, u32[]{:S(2)}) copy-start(bf16[512,2048]{1,0:T(8,128)(2,1)} %copy.90) | copy-start | bytes 6291460
  38.4 3.2 copy-start.24
  38.4 3.2 copy-start.25
  38.4 3.3 copy-start.26
  177.7 3.0 copy-start.5
  179.6 1.6 copy-start.6
  186.0 56.6 %all-to-all-start.1 = ((bf16[32,2,24,1024]{3,2,1,0:T(8,128)(2,1)}), bf16[32,2,24,1024]{3,2,1,0:T(8,128)(2,1)}, u32[]{:S(2)}, u32[]{:S(2)}) async-start(bf16[32,2,24,1024]{3,2,1,0:T(8,128)(2,1)} %bitcast.110), calls=%async_computation.1 | async-start | bytes 6291456 | tf_op jit(solution)/shard_map/all_to_all | solution.py:239
  203.0 2.2 copy-start.12
  250.9 2.3 copy-start.14
  253.7 1.1 copy-start.16
  255.4 1.1 copy-start.10
  258.1 1.8 copy-start.17
  258.1 1.2 copy-start.11
  259.1 1.1 copy-start.22
  263.8 6.0 %copy-start.7 = (bf16[256,2,1,512]{0,3,2,1:T(8,128)(2,1)S(1)}, bf16[256,2,1,512]{0,3,2,1:T(8,128)(2,1)}, u32[]{:S(2)}) copy-start(bf16[256,2,1,512]{0,3,2,1:T(8,128)(2,1)} %get-tuple-element.21) | copy-start | bytes 1572868
  269.9 1.8 copy-start.19
  269.9 2.4 copy-start.3
  275.6 49.9 %all-to-all-start.2 = ((bf16[32,2,24,1024]{3,2,1,0:T(8,128)(2,1)}), bf16[32,2,24,1024]{3,2,1,0:T(8,128)(2,1)}, u32[]{:S(2)}, u32[]{:S(2)}) async-start(bf16[32,2,24,1024]{3,2,1,0:T(8,128)(2,1)} %add_convert_fusion), calls=%async_computation.2 | async-start | bytes 6291456 | tf_op jit(solution)/shard_map/all_to_all | solution.py:264
  330.5 13.3 %copy-start.1 = (bf16[512,2048]{1,0:T(8,128)(2,1)S(1)}, bf16[512,2048]{1,0:T(8,128)(2,1)}, u32[]{:S(2)}) copy-start(bf16[512,2048]{1,0:T(8,128)(2,1)} %param.19) | copy-start | bytes 6291460
  (7 other events, 7.3 us)

commit v5 on v4

--- a/solution.py
+++ b/solution.py
@@ -103,16 +103,16 @@
     )(x)
 
 
-def attend(length, query, key_new, value_new, relaid):
+def attend(length, query, key_new, value_new, keys, values):
     tokens = query.shape[0]
-    context = relaid.shape[2]
+    context = keys.shape[0]
     heads = query.shape[1] // HD
 
     def kernel(length_ref, q_ref, kn_ref, vn_ref, k_ref, v_ref, o_ref):
         limit = length_ref[0]
         q = q_ref[...]
         contract = (((1,), (1,)), ((), ()))
-        score_old = lax.dot_general(q, k_ref[0, 0], contract, preferred_element_type=jnp.float32)
+        score_old = lax.dot_general(q, k_ref[...], contract, preferred_element_type=jnp.float32)
         score_new = lax.dot_general(q, kn_ref[...], contract, preferred_element_type=jnp.float32)
         allow_old = lax.broadcasted_iota(jnp.int32, score_old.shape, 1) < limit
         allow_new = lax.broadcasted_iota(jnp.int32, score_new.shape, 1) <= lax.broadcasted_iota(
@@ -126,7 +126,7 @@
         prob_old = jnp.where(allow_old, jnp.exp(score_old - top), 0.0)
         prob_new = jnp.where(allow_new, jnp.exp(score_new - top), 0.0)
         total = jnp.sum(prob_old, axis=1, keepdims=True) + jnp.sum(prob_new, axis=1, keepdims=True)
-        numer = jnp.dot(prob_old.astype(jnp.bfloat16), v_ref[0, 0], preferred_element_type=jnp.float32)
+        numer = jnp.dot(prob_old.astype(jnp.bfloat16), v_ref[...], preferred_element_type=jnp.float32)
         numer = numer + jnp.dot(
             prob_new.astype(jnp.bfloat16), vn_ref[...], preferred_element_type=jnp.float32
         )
@@ -140,8 +140,8 @@
             per_head,
             per_head,
             per_head,
-            pl.BlockSpec((1, 1, context, HD), lambda h, n: (0, 0, 0, h)),
-            pl.BlockSpec((1, 1, context, HD), lambda h, n: (1, 0, 0, h)),
+            pl.BlockSpec((context, HD), lambda h, n: (0, h)),
+            pl.BlockSpec((context, HD), lambda h, n: (0, h)),
         ],
         out_specs=per_head,
     )
@@ -149,7 +149,7 @@
         kernel,
         grid_spec=grid_spec,
         out_shape=jax.ShapeDtypeStruct((tokens, heads * HD), jnp.bfloat16),
-    )(length.reshape(1), query, key_new, value_new, relaid, relaid)
+    )(length.reshape(1), query, key_new, value_new, keys, values)
 
 
 def on_device(
@@ -190,13 +190,19 @@
     query = (rotate(query, position) * HD ** (-0.5)).astype(jnp.bfloat16)
     key_new = rotate(key_new, position).astype(jnp.bfloat16)
     value_new = value_new.astype(jnp.bfloat16)
-    relaid = lax.all_to_all(cache, "grp", split_axis=1, concat_axis=2, tiled=True)
+    keys, values = [
+        lax.all_to_all(cache[part], "grp", split_axis=0, concat_axis=0, tiled=True).reshape(
+            group_count * cache.shape[2], heads_here * HD
+        )
+        for part in range(2)
+    ]
     attended = attend(
         length,
         query.reshape(tokens, heads_here * HD),
         key_new.reshape(tokens, heads_here * HD),
         value_new.reshape(tokens, heads_here * HD),
-        relaid,
+        keys,
+        values,
     )
     projected = jnp.dot(attended, w_out, preferred_element_type=jnp.float32)
     gathered = head_gather(projected.astype(jnp.bfloat16), 0)

time: 346 us -> 328 us (0.948)
  waiting for transfers between devices: 167 us -> 101 us
  blocking collectives: 0 us -> 61.6 us
  local copies, waits for them, and re-layouts: 56.8 us -> 46.8 us
  starting transfers between devices: 29 us -> 24.2 us
    all_to_all x1, waiting for transfers between devices: 90.5 us -> 24.2 us  [on_device(): lax.all_to_all(cache[part], 'grp', split_axis=0, concat_axis=0, tiled=True)]
    all_to_all x0 -> x1, blocking collectives: none -> 61.6 us  [on_device(): lax.all_to_all(cache[part], 'grp', split_axis=0, concat_axis=0, tiled=True)]
    all_to_all x1 -> x0, local copies, waits for them, and re-layouts: 7.59 us -> none  [on_device(): lax.all_to_all(cache, 'grp', split_axis=1, concat_axis=2, tiled=True)]
    unnamed x63 -> x60, local copies, waits for them, and re-layouts: 14.9 us -> 7.4 us
    squeeze x0 -> x1, local copies, waits for them, and re-layouts: none -> 5.3 us  [on_device(): cache[part]]
    all_to_all x1, starting transfers between devices: 10.2 us -> 5.61 us  [on_device(): lax.all_to_all(cache[part], 'grp', split_axis=0, concat_axis=0, tiled=True)]
  transfers between devices with their start and end apart: 3 -> 3, of which waited for: 3 -> 3; matrix products, arithmetic and copies ran while one was open for 12% -> 13% of each run, Pallas kernels for 0% -> 0%
where the time goes in v5:
time: 328 us; the launch traced here: 326 us
  waiting for transfers between devices  101 us (31%)
  blocking collectives  61.6 us (19%)
  local copies, waits for them, and re-layouts  46.8 us (14%)
  Pallas kernels  44.9 us (14%)
  matrix products  26.9 us (8%)
  starting transfers between devices  24.2 us (7%)
  other arithmetic  20.5 us (6%)
    all_to_all x1, blocking collectives, on_device(): lax.all_to_all(cache[part], 'grp', split_axis=0, concat_axis=0, tiled=True)  61.6 us
    all_to_all x1, waiting for transfers between devices, on_device(): lax.all_to_all(pair_sum, 'grp', split_axis=0, concat_axis=0, tiled=True)  43.3 us
    all_to_all x1, waiting for transfers between devices, on_device(): lax.all_to_all(outgoing, 'grp', split_axis=0, concat_axis=0, tiled=True)  33.3 us
    all_to_all x1, waiting for transfers between devices, on_device(): lax.all_to_all(cache[part], 'grp', split_axis=0, concat_axis=0, tiled=True)  24.2 us
    pallas_call x3, Pallas kernels, peer_swap(): pl.pallas_call(kernel, out_shape=jax.ShapeDtypeStruct(x.shape, x.dtype),...  19.3 us
    pallas_call x1, Pallas kernels, head_gather(): pl.pallas_call(kernel, out_shape=jax.ShapeDtypeStruct((4,) + x.shape, x.d...  17.1 us
    all_to_all x1, starting transfers between devices, on_device(): lax.all_to_all(outgoing, 'grp', split_axis=0, concat_axis=0, tiled=True)  11.9 us
    pallas_call x1, Pallas kernels, attend(): pl.pallas_call(kernel, grid_spec=grid_spec, out_shape=jax.ShapeDtypeStruc...  8.58 us
  transfers between devices with their start and end apart: 3, of which 3 were waited for; matrix products, arithmetic and copies ran while one was open for 13% of the time, Pallas kernels for 0%

profile of v5, /device:TPU:10, one launch (start us, length us, event | category | flops | bytes accessed | tf_op | source)
XLA Modules:
  0.0 326.2 jit_solution(9434398788021350772)
XLA Ops:
  0.0 5.3 %slice_bitcast_fusion = (bf16[32,128,512]{2,1,0:T(8,128)(2,1)}, bf16[32,128,512]{2,1,0:T(8,128)(2,1)S(1)}) fusion(bf16[2,32,128,512]{3,2,1,0:T(8,128)(2,1)} %param.20), kind=kLoop, calls=%fused_computation.6 | loop fusion | bytes 16777216 | tf_op jit(solution)/shard_map/squeeze | solution.py:194
  5.3 61.6 %all_to_all.20 = bf16[32,128,512]{2,1,0:T(8,128)(2,1)} all-to-all(bf16[32,128,512]{2,1,0:T(8,128)(2,1)S(1)} %get-tuple-element.10), channel_id=1, replica_groups=mesh['grp'=32,'head'=4] {'grp'}, dimensions={0} | all-to-all | bytes 8388608 | tf_op jit(solution)/shard_map/all_to_all | solution.py:194
  66.9 5.6 %all-to-all-start.1 = ((bf16[32,128,512]{2,1,0:T(8,128)(2,1)}), bf16[32,128,512]{2,1,0:T(8,128)(2,1)}, u32[]{:S(2)}, u32[]{:S(2)}) async-start(bf16[32,128,512]{2,1,0:T(8,128)(2,1)} %get-tuple-element.9), calls=%async_computation.1 | async-start | bytes 8388608 | tf_op jit(solution)/shard_map/all_to_all | solution.py:194
  72.5 4.0 %copy.72 = bf16[512,2048]{1,0:T(8,128)(2,1)} copy(bf16[512,2048]{0,1:T(8,128)(2,1)} %bitcast.137) | data formatting | bytes 4194304 | tf_op jit(solution)/shard_map/dot_general | solution.py:184
  76.5 4.0 %copy.70 = bf16[512,2048]{1,0:T(8,128)(2,1)} copy(bf16[512,2048]{0,1:T(8,128)(2,1)} %bitcast.138) | data formatting | bytes 4194304 | tf_op jit(solution)/shard_map/dot_general | solution.py:181
  88.9 3.9 %copy.74 = bf16[512,2048]{1,0:T(8,128)(2,1)} copy(bf16[512,2048]{0,1:T(8,128)(2,1)} %bitcast.139) | data formatting | bytes 4194304 | tf_op jit(solution)/shard_map/dot_general | solution.py:187
  92.8 2.4 convolution_convert_fusion.6
  97.1 7.0 %select_reduce_fusion = (f32[128,1536]{1,0:T(8,128)S(1)}, bf16[128,1536]{1,0:T(8,128)(2,1)}) fusion(f32[128,8]{1,0:T(8,128)S(1)} %copy.62, s32[128,8]{1,0:T(8,128)S(1)} %bitcast_add_fusion.1), kind=kLoop, calls=%fused_computation.2 | loop fusion | flops 7471104 | bytes 1187840 | tf_op jit(solution)/shard_map/reduce_sum | solution.py:272
  104.1 24.2 %all-to-all-done.1 = bf16[32,128,512]{2,1,0:T(8,128)(2,1)} async-done(((bf16[32,128,512]{2,1,0:T(8,128)(2,1)}), bf16[32,128,512]{2,1,0:T(8,128)(2,1)}, u32[]{:S(2)}, u32[]{:S(2)}) %all-to-all-start.1) | async-done | bytes 4194336 | tf_op jit(solution)/shard_map/all_to_all | solution.py:194
  128.3 8.6 %shard_map.136 = bf16[128,512]{1,0:T(8,128)(2,1)} custom-call(s32[1]{0:T(128)} %dynamic_slice.55.length_ref, bf16[128,512]{1,0:T(8,128)(2,1)} %copy.71.q_ref, bf16[128,512]{1,0:T(8,128)(2,1)} %copy.73.kn_ref, bf16[128,512]{1,0:T(8,128)(2,1)} %copy.75.vn_ref, bf16[4096,512]{1,0:T(8,128)(2,1)} %bitcast.109, bf16[4096,512]{1,0:T(8,128)(2,1)} %bitcast.16.v_ref), custom_call_target="tpu_custom_call" | custom-call | tf_op jit(solution)/shard_map/pallas_call | solution.py:148
  139.1 17.1 %shard_map.137 = bf16[4,128,2048]{2,1,0:T(8,128)(2,1)} custom-call(bf16[128,2048]{1,0:T(8,128)(2,1)} %convolution_convert_fusion.1.x_ref), custom_call_target="tpu_custom_call" | custom-call | tf_op jit(solution)/shard_map/pallas_call | solution.py:92
  163.8 2.7 convolution_convert_fusion
  166.5 11.9 %all-to-all-start.2 = ((bf16[32,2,24,1024]{3,2,1,0:T(8,128)(2,1)}), bf16[32,2,24,1024]{3,2,1,0:T(8,128)(2,1)}, u32[]{:S(2)}, u32[]{:S(2)}) async-start(bf16[32,2,24,1024]{3,2,1,0:T(8,128)(2,1)} %bitcast.114), calls=%async_computation.2 | async-start | bytes 6291456 | tf_op jit(solution)/shard_map/all_to_all | solution.py:245
  178.4 2.7 fusion.28
  189.6 33.3 %all-to-all-done.2.x_ref = bf16[32,2,24,1024]{3,2,1,0:T(8,128)(2,1)} async-done(((bf16[32,2,24,1024]{3,2,1,0:T(8,128)(2,1)}), bf16[32,2,24,1024]{3,2,1,0:T(8,128)(2,1)}, u32[]{:S(2)}, u32[]{:S(2)}) %all-to-all-start.2) | async-done | bytes 3145760 | tf_op jit(solution)/shard_map/all_to_all | solution.py:245
  222.8 6.0 %shard_map.138 = bf16[32,2,24,1024]{3,2,1,0:T(8,128)(2,1)} custom-call(bf16[32,2,24,1024]{3,2,1,0:T(8,128)(2,1)} %all-to-all-done.2.x_ref), custom_call_target="tpu_custom_call" | custom-call | tf_op jit(solution)/shard_map/pallas_call | solution.py:47
  245.4 6.0 %shard_map.139 = bf16[32,2,24,1024]{3,2,1,0:T(8,128)(2,1)} custom-call(bf16[32,2,24,1024]{3,2,1,0:T(8,128)(2,1)} %pad_maximum_fusion.x_ref), custom_call_target="tpu_custom_call" | custom-call | tf_op jit(solution)/shard_map/pallas_call | solution.py:47
  252.8 5.1 %add_convert_fusion = bf16[32,2,24,1024]{3,2,1,0:T(8,128)(2,1)} fusion(bf16[32,2,24,1024]{3,2,1,0:T(8,128)(2,1)} %shard_map.139, bf16[32,1,24,1024]{3,2,1,0:T(8,128)(2,1)S(1)} %bitcast.122, bf16[32,1,24,1024]{3,2,1,0:T(8,128)(2,1)S(1)} %bitcast.119), kind=kLoop, calls=%fused_computation | loop fusion | flops 7864320 | bytes 9437184 | tf_op jit(solution)/shard_map/convert_element_type | solution.py:269
  257.9 6.7 %all-to-all-start.3 = ((bf16[32,2,24,1024]{3,2,1,0:T(8,128)(2,1)}), bf16[32,2,24,1024]{3,2,1,0:T(8,128)(2,1)}, u32[]{:S(2)}, u32[]{:S(2)}) async-start(bf16[32,2,24,1024]{3,2,1,0:T(8,128)(2,1)} %add_convert_fusion), calls=%async_computation.3 | async-start | bytes 6291456 | tf_op jit(solution)/shard_map/all_to_all | solution.py:270
  264.7 43.3 %all-to-all-done.3 = bf16[32,2,24,1024]{3,2,1,0:T(8,128)(2,1)} async-done(((bf16[32,2,24,1024]{3,2,1,0:T(8,128)(2,1)}), bf16[32,2,24,1024]{3,2,1,0:T(8,128)(2,1)}, u32[]{:S(2)}, u32[]{:S(2)}) %all-to-all-start.3) | async-done | bytes 3145760 | tf_op jit(solution)/shard_map/all_to_all | solution.py:270
  307.9 2.5 fusion.9
  310.4 2.5 convolution_add_fusion.5
  312.9 2.6 convolution_add_fusion.4
  317.2 7.2 %shard_map.140 = f32[128,512]{1,0:T(8,128)} custom-call(f32[128,512]{1,0:T(8,128)} %bitcast.145), custom_call_target="tpu_custom_call" | custom-call | tf_op jit(solution)/shard_map/pallas_call | solution.py:47
  (114 shorter events, 49.4 us)
Async XLA Ops:
  0.0 136.9 %copy-start = (bf16[512,2048]{1,0:T(8,128)(2,1)S(1)}, bf16[512,2048]{1,0:T(8,128)(2,1)}, u32[]{:S(2)}) copy-start(bf16[512,2048]{1,0:T(8,128)(2,1)} %param.19) | copy-start | bytes 6291460
  66.9 61.4 %all-to-all-start.1 = ((bf16[32,128,512]{2,1,0:T(8,128)(2,1)}), bf16[32,128,512]{2,1,0:T(8,128)(2,1)}, u32[]{:S(2)}, u32[]{:S(2)}) async-start(bf16[32,128,512]{2,1,0:T(8,128)(2,1)} %get-tuple-element.9), calls=%async_computation.1 | async-start | bytes 8388608 | tf_op jit(solution)/shard_map/all_to_all | solution.py:194
  76.5 4.0 %copy-start.2 = (bf16[1,128,2048]{2,1,0:T(8,128)(2,1)S(1)}, bf16[1,128,2048]{2,1,0:T(8,128)(2,1)}, u32[]{:S(2)}) copy-start(bf16[1,128,2048]{2,1,0:T(8,128)(2,1)} %param.14) | copy-start | bytes 1572868
  76.5 5.9 %copy-start.26 = (s32[32]{0:T(128)S(1)}, s32[32]{0:T(128)}, u32[]{:S(2)}) copy-start(s32[32]{0:T(128)} %param.21) | copy-start | bytes 388
  80.5 3.5 %copy-start.22 = (f32[2048]{0:T(1024)S(1)}, f32[2048]{0:T(1024)}, u32[]{:S(2)}) copy-start(f32[2048]{0:T(1024)} %param.15) | copy-start | bytes 24580
  82.4 4.0 %copy-start.3 = (bf16[512,2048]{1,0:T(8,128)(2,1)S(1)}, bf16[512,2048]{1,0:T(8,128)(2,1)}, u32[]{:S(2)}) copy-start(bf16[512,2048]{1,0:T(8,128)(2,1)} %copy.70) | copy-start | bytes 6291460
  92.8 3.2 copy-start.23
  92.8 3.2 copy-start.24
  92.8 4.1 %copy-start.25 = (f32[1,128,8]{1,2,0:T(8,128)S(1)}, f32[1,128,8]{1,2,0:T(8,128)}, u32[]{:S(2)}) copy-start(f32[1,128,8]{1,2,0:T(8,128)} %param.24) | copy-start | bytes 12292
  158.2 3.1 copy-start.5
  160.1 1.6 copy-start.6
  166.5 56.3 %all-to-all-start.2 = ((bf16[32,2,24,1024]{3,2,1,0:T(8,128)(2,1)}), bf16[32,2,24,1024]{3,2,1,0:T(8,128)(2,1)}, u32[]{:S(2)}, u32[]{:S(2)}) async-start(bf16[32,2,24,1024]{3,2,1,0:T(8,128)(2,1)} %bitcast.114), calls=%async_computation.2 | async-start | bytes 6291456 | tf_op jit(solution)/shard_map/all_to_all | solution.py:245
  183.2 2.2 copy-start.12
  231.1 2.3 copy-start.16
  233.9 1.1 copy-start.11
  235.0 1.1 copy-start.21
  236.7 2.2 copy-start.8
  237.1 2.4 copy-start.14
  238.8 1.2 copy-start.13
  240.6 1.1 copy-start.20
  245.4 6.0 %copy-start.18 = (bf16[768,256]{1,0:T(8,128)(2,1)S(1)}, bf16[768,256]{1,0:T(8,128)(2,1)}, u32[]{:S(2)}) copy-start(bf16[768,256]{1,0:T(8,128)(2,1)} %copy-done.17) | copy-start | bytes 1179652
  251.4 1.4 copy-start.4
  257.9 50.0 %all-to-all-start.3 = ((bf16[32,2,24,1024]{3,2,1,0:T(8,128)(2,1)}), bf16[32,2,24,1024]{3,2,1,0:T(8,128)(2,1)}, u32[]{:S(2)}, u32[]{:S(2)}) async-start(bf16[32,2,24,1024]{3,2,1,0:T(8,128)(2,1)} %add_convert_fusion), calls=%async_computation.3 | async-start | bytes 6291456 | tf_op jit(solution)/shard_map/all_to_all | solution.py:270
  312.9 13.3 %copy-start.1 = (bf16[512,2048]{1,0:T(8,128)(2,1)S(1)}, bf16[512,2048]{1,0:T(8,128)(2,1)}, u32[]{:S(2)}) copy-start(bf16[512,2048]{1,0:T(8,128)(2,1)} %param.19) | copy-start | bytes 6291460
  (6 other events, 6.2 us)

commit v6 on v5

--- a/solution.py
+++ b/solution.py
@@ -50,55 +50,6 @@
         in_specs=[pl.BlockSpec(memory_space=pl.ANY)],
         out_specs=pl.BlockSpec(memory_space=pl.ANY),
         scratch_shapes=[pltpu.SemaphoreType.DMA(()), pltpu.SemaphoreType.DMA(())],
-        compiler_params=pltpu.CompilerParams(collective_id=ident, has_side_effects=True),
-    )(x)
-
-
-def head_gather(x, ident):
-    mesh_kind = pl.DeviceIdType.MESH
-
-    def kernel(x_ref, o_ref, own_sem, send_sem, recv_sem):
-        me = lax.axis_index("head")
-        group = lax.axis_index("grp")
-        partner = me + 1 - 2 * lax.rem(me, 2)
-        across = lax.rem(me + 2, 4)
-        barrier = pltpu.get_barrier_semaphore()
-        for peer in (partner, across):
-            pl.semaphore_signal(barrier, inc=1, device_id=(group, peer), device_id_type=mesh_kind)
-        pl.semaphore_wait(barrier, 2)
-        own = pltpu.make_async_copy(x_ref, o_ref.at[me], own_sem)
-        own.start()
-        near = pltpu.make_async_remote_copy(
-            src_ref=x_ref, dst_ref=o_ref.at[me], send_sem=send_sem.at[0], recv_sem=recv_sem.at[0],
-            device_id=(group, partner), device_id_type=mesh_kind,
-        )
-        far = pltpu.make_async_remote_copy(
-            src_ref=x_ref, dst_ref=o_ref.at[me], send_sem=send_sem.at[1], recv_sem=recv_sem.at[1],
-            device_id=(group, across), device_id_type=mesh_kind,
-        )
-        near.start()
-        far.start()
-        far.wait_recv()
-        relay = pltpu.make_async_remote_copy(
-            src_ref=o_ref.at[across], dst_ref=o_ref.at[across], send_sem=send_sem.at[2],
-            recv_sem=recv_sem.at[2], device_id=(group, partner), device_id_type=mesh_kind,
-        )
-        relay.start()
-        own.wait()
-        near.wait()
-        far.wait_send()
-        relay.wait()
-
-    return pl.pallas_call(
-        kernel,
-        out_shape=jax.ShapeDtypeStruct((4,) + x.shape, x.dtype),
-        in_specs=[pl.BlockSpec(memory_space=pl.ANY)],
-        out_specs=pl.BlockSpec(memory_space=pl.ANY),
-        scratch_shapes=[
-            pltpu.SemaphoreType.DMA(()),
-            pltpu.SemaphoreType.DMA((3,)),
-            pltpu.SemaphoreType.DMA((3,)),
-        ],
         compiler_params=pltpu.CompilerParams(collective_id=ident, has_side_effects=True),
     )(x)
 
@@ -150,6 +101,56 @@
         grid_spec=grid_spec,
         out_shape=jax.ShapeDtypeStruct((tokens, heads * HD), jnp.bfloat16),
     )(length.reshape(1), query, key_new, value_new, keys, values)
+
+
+def head_reduce(x, base, ident):
+    mesh_kind = pl.DeviceIdType.MESH
+
+    def kernel(x_ref, base_ref, o_ref, slots, send_sem, recv_sem):
+        me = lax.axis_index("head")
+        group = lax.axis_index("grp")
+        partner = me + 1 - 2 * lax.rem(me, 2)
+        across = lax.rem(me + 2, 4)
+        barrier = pltpu.get_barrier_semaphore()
+        for peer in (partner, across):
+            pl.semaphore_signal(barrier, inc=1, device_id=(group, peer), device_id_type=mesh_kind)
+        pl.semaphore_wait(barrier, 2)
+        near = pltpu.make_async_remote_copy(
+            src_ref=x_ref, dst_ref=slots.at[0], send_sem=send_sem.at[0], recv_sem=recv_sem.at[0],
+            device_id=(group, partner), device_id_type=mesh_kind,
+        )
+        far = pltpu.make_async_remote_copy(
+            src_ref=x_ref, dst_ref=slots.at[1], send_sem=send_sem.at[1], recv_sem=recv_sem.at[1],
+            device_id=(group, across), device_id_type=mesh_kind,
+        )
+        near.start()
+        far.start()
+        far.wait_recv()
+        relay = pltpu.make_async_remote_copy(
+            src_ref=slots.at[1], dst_ref=slots.at[2], send_sem=send_sem.at[2],
+            recv_sem=recv_sem.at[2], device_id=(group, partner), device_id_type=mesh_kind,
+        )
+        relay.start()
+        near.wait()
+        far.wait_send()
+        relay.wait()
+        total = base_ref[...] + x_ref[...].astype(jnp.float32)
+        for slot in range(3):
+            total = total + slots[slot].astype(jnp.float32)
+        o_ref[...] = total
+
+    return pl.pallas_call(
+        kernel,
+        out_shape=jax.ShapeDtypeStruct(x.shape, jnp.float32),
+        in_specs=[pl.BlockSpec(memory_space=pltpu.VMEM), pl.BlockSpec(memory_space=pltpu.VMEM)],
+        out_specs=pl.BlockSpec(memory_space=pltpu.VMEM),
+        scratch_shapes=[
+            pltpu.VMEM((3,) + x.shape, x.dtype),
+            pltpu.SemaphoreType.DMA((3,)),
+            pltpu.SemaphoreType.DMA((3,)),
+        ],
+        compiler_params=pltpu.CompilerParams(collective_id=ident, has_side_effects=True),
+    )(x, base)
 
 
 def on_device(
@@ -205,8 +206,7 @@
         values,
     )
     projected = jnp.dot(attended, w_out, preferred_element_type=jnp.float32)
-    gathered = head_gather(projected.astype(jnp.bfloat16), 0)
-    resid = rows + jnp.sum(gathered.astype(jnp.float32), axis=0)
+    resid = head_reduce(projected.astype(jnp.bfloat16), rows, 0)
     mixed_in = rms_norm(resid, mlp_gain).astype(jnp.bfloat16)
     experts_here = w_gate.shape[0]
     expert_total = experts_here * group_count
@@ -270,11 +270,13 @@
     returned = lax.all_to_all(pair_sum, "grp", split_axis=0, concat_axis=0, tiled=True)
     returned = returned.reshape(slots, half)
     weighting = jnp.sum(jnp.where(place, weights[:, :, None], 0.0), axis=1)
-    combined = jnp.zeros((tokens, half), jnp.float32)
+    pieces = []
     for _ in range(3):
         piece = weighting.astype(jnp.bfloat16)
         weighting = weighting - piece.astype(jnp.float32)
-        combined = combined + jnp.dot(piece, returned, preferred_element_type=jnp.float32)
+        pieces.append(piece)
+    combined = jnp.dot(jnp.concatenate(pieces, axis=0), returned, preferred_element_type=jnp.float32)
+    combined = combined.reshape(3, tokens, half).sum(axis=0)
     combined = combined.reshape(tokens, 2, share_width)
     keep = lax.dynamic_index_in_dim(combined, chip, axis=1, keepdims=False)
     give = lax.dynamic_index_in_dim(combined, 1 - chip, axis=1, keepdims=False)

time: 328 us -> 321 us (0.979)
  matrix products: 26.9 us -> 22.4 us
  waiting for transfers between devices: 101 us -> 96.5 us
    all_to_all x1, waiting for transfers between devices: 33.3 us -> 28.4 us  [on_device(): lax.all_to_all(outgoing, 'grp', split_axis=0, concat_axis=0, tiled=True)]
    unnamed x60 -> x58, local copies, waits for them, and re-layouts: 7.4 us -> 11 us
    dot_general x3 -> x1, matrix products: 7.55 us -> 4.25 us  [on_device(): jnp.dot(jnp.concatenate(pieces, axis=0), returned, preferred_element_type...]
    reduce_sum x2 -> x1, other arithmetic: 9.1 us -> 6.96 us  [on_device(): dispatch = jnp.sum(place.astype(jnp.float32), axis=1).astype(jnp.bfloat16)]
  transfers between devices with their start and end apart: 3 -> 3, of which waited for: 3 -> 3; matrix products, arithmetic and copies ran while one was open for 13% -> 14% of each run, Pallas kernels for 0% -> 0%
where the time goes in v6:
time: 321 us; the launch traced here: 320 us
  waiting for transfers between devices  96.5 us (30%)
  blocking collectives  61.6 us (19%)
  local copies, waits for them, and re-layouts  46.6 us (15%)
  Pallas kernels  44.2 us (14%)
  starting transfers between devices  26.9 us (8%)
  matrix products  22.4 us (7%)
  other arithmetic  21.1 us (7%)
    all_to_all x1, blocking collectives, on_device(): lax.all_to_all(cache[part], 'grp', split_axis=0, concat_axis=0, tiled=True)  61.6 us
    all_to_all x1, waiting for transfers between devices, on_device(): lax.all_to_all(pair_sum, 'grp', split_axis=0, concat_axis=0, tiled=True)  43.1 us
    all_to_all x1, waiting for transfers between devices, on_device(): lax.all_to_all(outgoing, 'grp', split_axis=0, concat_axis=0, tiled=True)  28.4 us
    all_to_all x1, waiting for transfers between devices, on_device(): lax.all_to_all(cache[part], 'grp', split_axis=0, concat_axis=0, tiled=True)  25 us
    pallas_call x3, Pallas kernels, peer_swap(): pl.pallas_call(kernel, out_shape=jax.ShapeDtypeStruct(x.shape, x.dtype),...  19.3 us
    pallas_call x1, Pallas kernels, head_reduce(): pl.pallas_call(kernel, out_shape=jax.ShapeDtypeStruct(x.shape, jnp.float3...  16.3 us
    all_to_all x1, starting transfers between devices, on_device(): lax.all_to_all(outgoing, 'grp', split_axis=0, concat_axis=0, tiled=True)  13.6 us
    unnamed x58, local copies, waits for them, and re-layouts  11 us
  transfers between devices with their start and end apart: 3, of which 3 were waited for; matrix products, arithmetic and copies ran while one was open for 14% of the time, Pallas kernels for 0%

profile of v6, /device:TPU:10, one launch (start us, length us, event | category | flops | bytes accessed | tf_op | source)
XLA Modules:
  0.0 319.9 jit_solution(531802627005491190)
XLA Ops:
  0.0 5.3 %slice_bitcast_fusion = (bf16[32,128,512]{2,1,0:T(8,128)(2,1)}, bf16[32,128,512]{2,1,0:T(8,128)(2,1)S(1)}) fusion(bf16[2,32,128,512]{3,2,1,0:T(8,128)(2,1)} %param.20), kind=kLoop, calls=%fused_computation.5 | loop fusion | bytes 16777216 | tf_op jit(solution)/shard_map/squeeze | solution.py:195
  5.3 61.6 %all_to_all.20 = bf16[32,128,512]{2,1,0:T(8,128)(2,1)} all-to-all(bf16[32,128,512]{2,1,0:T(8,128)(2,1)S(1)} %get-tuple-element.8), channel_id=1, replica_groups=mesh['grp'=32,'head'=4] {'grp'}, dimensions={0} | all-to-all | bytes 8388608 | tf_op jit(solution)/shard_map/all_to_all | solution.py:195
  66.9 5.6 %all-to-all-start.1 = ((bf16[32,128,512]{2,1,0:T(8,128)(2,1)}), bf16[32,128,512]{2,1,0:T(8,128)(2,1)}, u32[]{:S(2)}, u32[]{:S(2)}) async-start(bf16[32,128,512]{2,1,0:T(8,128)(2,1)} %get-tuple-element.7), calls=%async_computation.1 | async-start | bytes 8388608 | tf_op jit(solution)/shard_map/all_to_all | solution.py:195
  72.5 4.0 %copy.81 = bf16[512,2048]{1,0:T(8,128)(2,1)} copy(bf16[512,2048]{0,1:T(8,128)(2,1)} %bitcast.135) | data formatting | bytes 4194304 | tf_op jit(solution)/shard_map/dot_general | solution.py:185
  76.5 4.0 %copy.79 = bf16[512,2048]{1,0:T(8,128)(2,1)} copy(bf16[512,2048]{0,1:T(8,128)(2,1)} %bitcast.136) | data formatting | bytes 4194304 | tf_op jit(solution)/shard_map/dot_general | solution.py:182
  82.2 2.4 fusion.19
  87.0 4.0 %copy.83 = bf16[512,2048]{1,0:T(8,128)(2,1)} copy(bf16[512,2048]{0,1:T(8,128)(2,1)} %bitcast.137) | data formatting | bytes 4194304 | tf_op jit(solution)/shard_map/dot_general | solution.py:188
  91.0 2.4 convolution_convert_fusion.6
  95.2 7.0 %convert_reduce_fusion = (bf16[128,1536]{1,0:T(8,128)(2,1)S(1)}, f32[128,1536]{1,0:T(8,128)}) fusion(s32[128,8]{1,0:T(8,128)S(1)} %bitcast_add_fusion.1, f32[128,8]{1,0:T(8,128)S(1)} %copy.72), kind=kLoop, calls=%fused_computation.1 | loop fusion | flops 7471104 | bytes 1187840 | tf_op jit(solution)/shard_map/reduce_sum | solution.py:224
  103.3 25.0 %all-to-all-done.1 = bf16[32,128,512]{2,1,0:T(8,128)(2,1)} async-done(((bf16[32,128,512]{2,1,0:T(8,128)(2,1)}), bf16[32,128,512]{2,1,0:T(8,128)(2,1)}, u32[]{:S(2)}, u32[]{:S(2)}) %all-to-all-start.1) | async-done | bytes 4194336 | tf_op jit(solution)/shard_map/all_to_all | solution.py:195
  128.3 8.6 %shard_map.136 = bf16[128,512]{1,0:T(8,128)(2,1)} custom-call(s32[1]{0:T(128)} %dynamic_slice.55.length_ref, bf16[128,512]{1,0:T(8,128)(2,1)} %copy.80.q_ref, bf16[128,512]{1,0:T(8,128)(2,1)} %copy.82.kn_ref, bf16[128,512]{1,0:T(8,128)(2,1)} %copy.84.vn_ref, bf16[4096,512]{1,0:T(8,128)(2,1)} %bitcast.106, bf16[4096,512]{1,0:T(8,128)(2,1)} %bitcast.16.v_ref), custom_call_target="tpu_custom_call" | custom-call | tf_op jit(solution)/shard_map/pallas_call | solution.py:99
  139.1 16.3 %shard_map.137 = f32[128,2048]{1,0:T(8,128)} custom-call(bf16[128,2048]{1,0:T(8,128)(2,1)} %convolution_convert_fusion.1.x_ref, f32[128,2048]{1,0:T(8,128)} %convert_bitcast_fusion.base_ref), custom_call_target="tpu_custom_call" | custom-call | tf_op jit(solution)/shard_map/pallas_call | solution.py:142
  159.6 2.6 convolution_convert_fusion
  162.2 13.6 %all-to-all-start.2 = ((bf16[32,2,24,1024]{3,2,1,0:T(8,128)(2,1)}), bf16[32,2,24,1024]{3,2,1,0:T(8,128)(2,1)S(1)}, u32[]{:S(2)}, u32[]{:S(2)}) async-start(bf16[32,2,24,1024]{3,2,1,0:T(8,128)(2,1)} %bitcast.111), calls=%async_computation.2 | async-start | bytes 6291456 | tf_op jit(solution)/shard_map/all_to_all | solution.py:245
  175.8 3.2 fusion.25
  191.0 28.4 %all-to-all-done.2.x_ref = bf16[32,2,24,1024]{3,2,1,0:T(8,128)(2,1)S(1)} async-done(((bf16[32,2,24,1024]{3,2,1,0:T(8,128)(2,1)}), bf16[32,2,24,1024]{3,2,1,0:T(8,128)(2,1)S(1)}, u32[]{:S(2)}, u32[]{:S(2)}) %all-to-all-start.2) | async-done | bytes 3145760 | tf_op jit(solution)/shard_map/all_to_all | solution.py:245
  221.0 6.0 %shard_map.138 = bf16[32,2,24,1024]{3,2,1,0:T(8,128)(2,1)} custom-call(bf16[32,2,24,1024]{3,2,1,0:T(8,128)(2,1)} %copy-done.2), custom_call_target="tpu_custom_call" | custom-call | tf_op jit(solution)/shard_map/pallas_call | solution.py:47
  227.1 2.4 fusion.23
  241.4 6.0 %shard_map.139 = bf16[32,2,24,1024]{3,2,1,0:T(8,128)(2,1)} custom-call(bf16[32,2,24,1024]{3,2,1,0:T(8,128)(2,1)} %pad_maximum_fusion.x_ref), custom_call_target="tpu_custom_call" | custom-call | tf_op jit(solution)/shard_map/pallas_call | solution.py:47
  248.1 5.2 %add_convert_fusion = bf16[32,2,24,1024]{3,2,1,0:T(8,128)(2,1)} fusion(bf16[32,2,24,1024]{3,2,1,0:T(8,128)(2,1)} %shard_map.139, bf16[32,1,24,1024]{3,2,1,0:T(8,128)(2,1)S(1)} %bitcast.119, bf16[32,1,24,1024]{3,2,1,0:T(8,128)(2,1)S(1)} %bitcast.116), kind=kLoop, calls=%fused_computation | loop fusion | flops 7864320 | bytes 9437184 | tf_op jit(solution)/shard_map/convert_element_type | solution.py:269
  253.3 7.8 %all-to-all-start.3 = ((bf16[32,2,24,1024]{3,2,1,0:T(8,128)(2,1)}), bf16[32,2,24,1024]{3,2,1,0:T(8,128)(2,1)}, u32[]{:S(2)}, u32[]{:S(2)}) async-start(bf16[32,2,24,1024]{3,2,1,0:T(8,128)(2,1)} %add_convert_fusion), calls=%async_computation.3 | async-start | bytes 6291456 | tf_op jit(solution)/shard_map/all_to_all | solution.py:270
  261.3 43.1 %all-to-all-done.3 = bf16[32,2,24,1024]{3,2,1,0:T(8,128)(2,1)} async-done(((bf16[32,2,24,1024]{3,2,1,0:T(8,128)(2,1)}), bf16[32,2,24,1024]{3,2,1,0:T(8,128)(2,1)}, u32[]{:S(2)}, u32[]{:S(2)}) %all-to-all-start.3) | async-done | bytes 3145760 | tf_op jit(solution)/shard_map/all_to_all | solution.py:270
  304.3 4.3 %convolution_reduce_fusion = f32[128,1024]{1,0:T(8,128)} fusion(bf16[3,128,1536]{2,1,0:T(8,128)(2,1)S(1)} %bitcast.143, bf16[1536,1024,1]{1,0,2:T(8,128)(2,1)} %bitcast.49), kind=kOutput, calls=%fused_computation.15 | convolution fusion | flops 1208221696 | bytes 4849664 | tf_op jit(solution)/shard_map/dot_general | solution.py:278
  310.7 7.2 %shard_map.140 = f32[128,512]{1,0:T(8,128)} custom-call(f32[128,512]{1,0:T(8,128)} %bitcast.144), custom_call_target="tpu_custom_call" | custom-call | tf_op jit(solution)/shard_map/pallas_call | solution.py:47
  (110 shorter events, 43.5 us)
Async XLA Ops:
  0.0 136.9 %copy-start = (bf16[512,2048]{1,0:T(8,128)(2,1)S(1)}, bf16[512,2048]{1,0:T(8,128)(2,1)}, u32[]{:S(2)}) copy-start(bf16[512,2048]{1,0:T(8,128)(2,1)} %param.19) | copy-start | bytes 6291460
  66.9 61.4 %all-to-all-start.1 = ((bf16[32,128,512]{2,1,0:T(8,128)(2,1)}), bf16[32,128,512]{2,1,0:T(8,128)(2,1)}, u32[]{:S(2)}, u32[]{:S(2)}) async-start(bf16[32,128,512]{2,1,0:T(8,128)(2,1)} %get-tuple-element.7), calls=%async_computation.1 | async-start | bytes 8388608 | tf_op jit(solution)/shard_map/all_to_all | solution.py:195
  76.5 4.0 %copy-start.26 = (s32[32]{0:T(128)S(1)}, s32[32]{0:T(128)}, u32[]{:S(2)}) copy-start(s32[32]{0:T(128)} %param.21) | copy-start | bytes 388
  76.5 5.3 %copy-start.4 = (bf16[1,128,2048]{2,1,0:T(8,128)(2,1)S(1)}, bf16[1,128,2048]{2,1,0:T(8,128)(2,1)}, u32[]{:S(2)}) copy-start(bf16[1,128,2048]{2,1,0:T(8,128)(2,1)} %param.14) | copy-start | bytes 1572868
  76.5 5.7 %copy-start.22 = (f32[2048]{0:T(1024)S(1)}, f32[2048]{0:T(1024)}, u32[]{:S(2)}) copy-start(f32[2048]{0:T(1024)} %param.15) | copy-start | bytes 24580
  80.5 4.1 %copy-start.5 = (bf16[512,2048]{1,0:T(8,128)(2,1)S(1)}, bf16[512,2048]{1,0:T(8,128)(2,1)}, u32[]{:S(2)}) copy-start(bf16[512,2048]{1,0:T(8,128)(2,1)} %copy.79) | copy-start | bytes 6291460
  91.0 3.2 copy-start.24
  91.0 4.1 %copy-start.25 = (f32[1,128,8]{1,2,0:T(8,128)S(1)}, f32[1,128,8]{1,2,0:T(8,128)}, u32[]{:S(2)}) copy-start(f32[1,128,8]{1,2,0:T(8,128)} %param.24) | copy-start | bytes 12292
  139.1 17.7 %copy-start.23 = (f32[2048]{0:T(1024)S(1)}, f32[2048]{0:T(1024)}, u32[]{:S(2)}) copy-start(f32[2048]{0:T(1024)} %param.22) | copy-start | bytes 24580
  162.2 57.1 %all-to-all-start.2 = ((bf16[32,2,24,1024]{3,2,1,0:T(8,128)(2,1)}), bf16[32,2,24,1024]{3,2,1,0:T(8,128)(2,1)S(1)}, u32[]{:S(2)}, u32[]{:S(2)}) async-start(bf16[32,2,24,1024]{3,2,1,0:T(8,128)(2,1)} %bitcast.111), calls=%async_computation.2 | async-start | bytes 6291456 | tf_op jit(solution)/shard_map/all_to_all | solution.py:245
  183.5 2.2 copy-start.15
  185.9 1.8 copy-start.6
  185.9 2.3 copy-start.7
  219.4 1.6 copy-start.2
  227.1 2.8 copy-start.3
  230.3 1.3 copy-start.18
  232.1 1.1 copy-start.21
  233.8 1.1 copy-start.11
  234.2 1.3 copy-start.17
  234.9 1.2 copy-start.16
  241.4 6.0 %copy-start.9 = (bf16[256,2,1,512]{0,3,2,1:T(8,128)(2,1)S(1)}, bf16[256,2,1,512]{0,3,2,1:T(8,128)(2,1)}, u32[]{:S(2)}) copy-start(bf16[256,2,1,512]{0,3,2,1:T(8,128)(2,1)} %get-tuple-element.21) | copy-start | bytes 1572868
  253.3 7.8 %copy-start.8 = (f32[128,1536]{1,0:T(8,128)S(1)}, f32[128,1536]{1,0:T(8,128)}, u32[]{:S(2)}) copy-start(f32[128,1536]{1,0:T(8,128)} %get-tuple-element.6) | copy-start | bytes 2359300
  253.3 51.1 %all-to-all-start.3 = ((bf16[32,2,24,1024]{3,2,1,0:T(8,128)(2,1)}), bf16[32,2,24,1024]{3,2,1,0:T(8,128)(2,1)}, u32[]{:S(2)}, u32[]{:S(2)}) async-start(bf16[32,2,24,1024]{3,2,1,0:T(8,128)(2,1)} %add_convert_fusion), calls=%async_computation.3 | async-start | bytes 6291456 | tf_op jit(solution)/shard_map/all_to_all | solution.py:270
  304.3 15.5 %copy-start.1 = (bf16[512,2048]{1,0:T(8,128)(2,1)S(1)}, bf16[512,2048]{1,0:T(8,128)(2,1)}, u32[]{:S(2)}) copy-start(bf16[512,2048]{1,0:T(8,128)(2,1)} %param.19) | copy-start | bytes 6291460
  (6 other events, 6.3 us)

commit v7 on v6

--- a/solution.py
+++ b/solution.py
@@ -243,30 +243,28 @@
     ).astype(jnp.bfloat16)
     outgoing = outgoing.reshape(group_count, experts_here, capacity, half)
     arrived = lax.all_to_all(outgoing, "grp", split_axis=0, concat_axis=0, tiled=True)
-    arrived_other = peer_swap(arrived, False, 1)
-    mine_parts = []
-    other_parts = []
+    partners = [(index, index ^ 1) for index in range(head_count)]
+    arrived_other = [
+        lax.ppermute(arrived[:, expert], "head", partners) for expert in range(experts_here)
+    ]
+    pair_sums = []
     for expert in range(experts_here):
         mine = arrived[:, expert].reshape(group_count * capacity, half)
-        other = arrived_other[:, expert].reshape(group_count * capacity, half)
+        other = arrived_other[expert].reshape(group_count * capacity, half)
         gate = jnp.dot(mine, row_halves(w_gate[expert], core), preferred_element_type=jnp.float32)
         gate = gate + jnp.dot(other, row_halves(w_gate[expert], other_core), preferred_element_type=jnp.float32)
         upper = jnp.dot(mine, row_halves(w_up[expert], core), preferred_element_type=jnp.float32)
         upper = upper + jnp.dot(other, row_halves(w_up[expert], other_core), preferred_element_type=jnp.float32)
         act = (jax.nn.silu(gate) * upper).astype(jnp.bfloat16)
-        mine_parts.append(
-            jnp.dot(act, halves(w_down[expert], core), preferred_element_type=jnp.float32)
+        mine_part = jnp.dot(act, halves(w_down[expert], core), preferred_element_type=jnp.float32)
+        other_part = jnp.dot(act, halves(w_down[expert], other_core), preferred_element_type=jnp.float32)
+        partner_part = lax.ppermute(other_part.astype(jnp.bfloat16), "head", partners)
+        pair_sums.append(
+            (mine_part.astype(jnp.bfloat16).astype(jnp.float32) + partner_part.astype(jnp.float32))
             .astype(jnp.bfloat16)
             .reshape(group_count, capacity, half)
         )
-        other_parts.append(
-            jnp.dot(act, halves(w_down[expert], other_core), preferred_element_type=jnp.float32)
-            .astype(jnp.bfloat16)
-            .reshape(group_count, capacity, half)
-        )
-    mine_out = jnp.stack(mine_parts, axis=1)
-    partner_out = peer_swap(jnp.stack(other_parts, axis=1), False, 2)
-    pair_sum = (mine_out.astype(jnp.float32) + partner_out.astype(jnp.float32)).astype(jnp.bfloat16)
+    pair_sum = jnp.stack(pair_sums, axis=1)
     returned = lax.all_to_all(pair_sum, "grp", split_axis=0, concat_axis=0, tiled=True)
     returned = returned.reshape(slots, half)
     weighting = jnp.sum(jnp.where(place, weights[:, :, None], 0.0), axis=1)

time: 321 us -> 318 us (level)
  waiting for transfers between devices: 96.5 us -> 109 us
  Pallas kernels: 44.2 us -> 32.8 us
  other arithmetic: 21.1 us -> 16 us
    pallas_call x3 -> x1, Pallas kernels: 19.3 us -> 7.68 us  [peer_swap(): pl.pallas_call(kernel, out_shape=jax.ShapeDtypeStruct(x.shape, x.dtype),...]
    all_to_all x1, waiting for transfers between devices: 28.4 us -> 37.6 us  [on_device(): lax.all_to_all(outgoing, 'grp', split_axis=0, concat_axis=0, tiled=True)]
    convert_element_type x1 -> x0, other arithmetic: 5.2 us -> none  [on_device(): (mine_out.astype(jnp.float32) + partner_out.astype(jnp.float32)).astype(j...]
    squeeze x0 -> x1, local copies, waits for them, and re-layouts: none -> 4.58 us  [on_device(): arrived[:, expert]]
    unnamed x58 -> x48, local copies, waits for them, and re-layouts: 11 us -> 8.24 us
  transfers between devices with their start and end apart: 3 -> 7, of which waited for: 3 -> 5; matrix products, arithmetic and copies ran while one was open for 14% -> 16% of each run, Pallas kernels for 0% -> 0%
where the time goes in v7:
time: 318 us; the launch traced here: 316 us
  waiting for transfers between devices  109 us (34%)
  blocking collectives  61.6 us (19%)
  local copies, waits for them, and re-layouts  43.6 us (14%)
  Pallas kernels  32.8 us (10%)
  starting transfers between devices  28.4 us (9%)
  matrix products  25.2 us (8%)
  other arithmetic  16 us (5%)
    all_to_all x1, blocking collectives, on_device(): lax.all_to_all(cache[part], 'grp', split_axis=0, concat_axis=0, tiled=True)  61.6 us
    all_to_all x1, waiting for transfers between devices, on_device(): lax.all_to_all(pair_sum, 'grp', split_axis=0, concat_axis=0, tiled=True)  43.2 us
    all_to_all x1, waiting for transfers between devices, on_device(): lax.all_to_all(outgoing, 'grp', split_axis=0, concat_axis=0, tiled=True)  37.6 us
    all_to_all x1, waiting for transfers between devices, on_device(): lax.all_to_all(cache[part], 'grp', split_axis=0, concat_axis=0, tiled=True)  24.9 us
    pallas_call x1, Pallas kernels, head_reduce(): pl.pallas_call(kernel, out_shape=jax.ShapeDtypeStruct(x.shape, jnp.float3...  16.4 us
    all_to_all x1, starting transfers between devices, on_device(): lax.all_to_all(outgoing, 'grp', split_axis=0, concat_axis=0, tiled=True)  13.8 us
    pallas_call x1, Pallas kernels, attend(): pl.pallas_call(kernel, grid_spec=grid_spec, out_shape=jax.ShapeDtypeStruc...  8.71 us
    unnamed x48, local copies, waits for them, and re-layouts  8.24 us
  transfers between devices with their start and end apart: 7, of which 5 were waited for; matrix products, arithmetic and copies ran while one was open for 16% of the time, Pallas kernels for 0%

profile of v7, /device:TPU:10, one launch (start us, length us, event | category | flops | bytes accessed | tf_op | source)
XLA Modules:
  0.0 316.5 jit_solution(3179398371326293363)
XLA Ops:
  0.0 5.3 %slice_bitcast_fusion = (bf16[32,128,512]{2,1,0:T(8,128)(2,1)}, bf16[32,128,512]{2,1,0:T(8,128)(2,1)S(1)}) fusion(bf16[2,32,128,512]{3,2,1,0:T(8,128)(2,1)} %param.20), kind=kLoop, calls=%fused_computation.4 | loop fusion | bytes 16777216 | tf_op jit(solution)/shard_map/squeeze | solution.py:195
  5.3 61.6 %all_to_all.20 = bf16[32,128,512]{2,1,0:T(8,128)(2,1)} all-to-all(bf16[32,128,512]{2,1,0:T(8,128)(2,1)S(1)} %get-tuple-element.8), channel_id=1, replica_groups=mesh['grp'=32,'head'=4] {'grp'}, dimensions={0} | all-to-all | bytes 8388608 | tf_op jit(solution)/shard_map/all_to_all | solution.py:195
  66.8 5.6 %all-to-all-start.1 = ((bf16[32,128,512]{2,1,0:T(8,128)(2,1)}), bf16[32,128,512]{2,1,0:T(8,128)(2,1)}, u32[]{:S(2)}, u32[]{:S(2)}) async-start(bf16[32,128,512]{2,1,0:T(8,128)(2,1)} %get-tuple-element.7), calls=%async_computation.1 | async-start | bytes 8388608 | tf_op jit(solution)/shard_map/all_to_all | solution.py:195
  72.5 4.0 %copy.88 = bf16[512,2048]{1,0:T(8,128)(2,1)} copy(bf16[512,2048]{0,1:T(8,128)(2,1)} %bitcast.133) | data formatting | bytes 4194304 | tf_op jit(solution)/shard_map/dot_general | solution.py:185
  76.4 4.0 %copy.86 = bf16[512,2048]{1,0:T(8,128)(2,1)} copy(bf16[512,2048]{0,1:T(8,128)(2,1)} %bitcast.134) | data formatting | bytes 4194304 | tf_op jit(solution)/shard_map/dot_general | solution.py:182
  82.3 2.4 fusion.19
  87.1 3.9 %copy.90 = bf16[512,2048]{1,0:T(8,128)(2,1)} copy(bf16[512,2048]{0,1:T(8,128)(2,1)} %bitcast.135) | data formatting | bytes 4194304 | tf_op jit(solution)/shard_map/dot_general | solution.py:188
  91.1 2.4 convolution_convert_fusion.6
  95.3 7.0 %convert_reduce_fusion = (bf16[128,1536]{1,0:T(8,128)(2,1)S(1)}, f32[128,1536]{1,0:T(8,128)}) fusion(s32[128,8]{1,0:T(8,128)S(1)} %bitcast_add_fusion.1, f32[128,8]{1,0:T(8,128)S(1)} %copy.77), kind=kLoop, calls=%fused_computation | loop fusion | flops 7471104 | bytes 1187840 | tf_op jit(solution)/shard_map/reduce_sum | solution.py:224
  103.4 24.9 %all-to-all-done.1 = bf16[32,128,512]{2,1,0:T(8,128)(2,1)} async-done(((bf16[32,128,512]{2,1,0:T(8,128)(2,1)}), bf16[32,128,512]{2,1,0:T(8,128)(2,1)}, u32[]{:S(2)}, u32[]{:S(2)}) %all-to-all-start.1) | async-done | bytes 4194336 | tf_op jit(solution)/shard_map/all_to_all | solution.py:195
  128.3 8.7 %shard_map.136 = bf16[128,512]{1,0:T(8,128)(2,1)} custom-call(s32[1]{0:T(128)} %dynamic_slice.55.length_ref, bf16[128,512]{1,0:T(8,128)(2,1)} %copy.87.q_ref, bf16[128,512]{1,0:T(8,128)(2,1)} %copy.89.kn_ref, bf16[128,512]{1,0:T(8,128)(2,1)} %copy.91.vn_ref, bf16[4096,512]{1,0:T(8,128)(2,1)} %bitcast.112, bf16[4096,512]{1,0:T(8,128)(2,1)} %bitcast.16.v_ref), custom_call_target="tpu_custom_call" | custom-call | tf_op jit(solution)/shard_map/pallas_call | solution.py:99
  137.0 2.2 convolution_convert_fusion.1.x_ref
  139.2 16.4 %shard_map.137 = f32[128,2048]{1,0:T(8,128)} custom-call(bf16[128,2048]{1,0:T(8,128)(2,1)} %convolution_convert_fusion.1.x_ref, f32[128,2048]{1,0:T(8,128)} %convert_bitcast_fusion.base_ref), custom_call_target="tpu_custom_call" | custom-call | tf_op jit(solution)/shard_map/pallas_call | solution.py:142
  159.8 2.7 convolution_convert_fusion
  162.4 13.8 %all-to-all-start.2 = ((bf16[32,2,24,1024]{3,2,1,0:T(8,128)(2,1)}), bf16[32,2,24,1024]{3,2,1,0:T(8,128)(2,1)}, u32[]{:S(2)}, u32[]{:S(2)}) async-start(bf16[32,2,24,1024]{3,2,1,0:T(8,128)(2,1)} %bitcast.117), calls=%async_computation.2 | async-start | bytes 6291456 | tf_op jit(solution)/shard_map/all_to_all | solution.py:245
  182.2 37.6 %all-to-all-done.2 = bf16[32,2,24,1024]{3,2,1,0:T(8,128)(2,1)} async-done(((bf16[32,2,24,1024]{3,2,1,0:T(8,128)(2,1)}), bf16[32,2,24,1024]{3,2,1,0:T(8,128)(2,1)}, u32[]{:S(2)}, u32[]{:S(2)}) %all-to-all-start.2) | async-done | bytes 3145760 | tf_op jit(solution)/shard_map/all_to_all | solution.py:245
  219.8 4.6 %slice_bitcast_fusion.3 = (bf16[32,24,1024]{2,1,0:T(8,128)(2,1)}, bf16[32,24,1024]{2,1,0:T(8,128)(2,1)}, bf16[32,1,24,1024]{3,2,1,0:T(8,128)(2,1)S(1)}, bf16[32,1,24,1024]{3,2,1,0:T(8,128)(2,1)}) fusion(bf16[32,2,24,1024]{3,2,1,0:T(8,128)(2,1)} %all-to-all-done.2), kind=kLoop, calls=%fused_computation.78 | loop fusion | bytes 9437184 | tf_op jit(solution)/shard_map/squeeze | solution.py:248
  227.2 2.3 copy.94
  236.2 2.0 convolution_add_fusion.3
  238.2 2.0 fusion.3
  249.3 7.8 %all-to-all-start.3 = ((bf16[32,2,24,1024]{3,2,1,0:T(8,128)(2,1)}), bf16[32,2,24,1024]{3,2,1,0:T(8,128)(2,1)}, u32[]{:S(2)}, u32[]{:S(2)}) async-start(bf16[32,2,24,1024]{3,2,1,0:T(8,128)(2,1)} %pad_maximum_fusion), calls=%async_computation.3 | async-start | bytes 6291456 | tf_op jit(solution)/shard_map/all_to_all | solution.py:268
  257.3 43.2 %all-to-all-done.3 = bf16[32,2,24,1024]{3,2,1,0:T(8,128)(2,1)} async-done(((bf16[32,2,24,1024]{3,2,1,0:T(8,128)(2,1)}), bf16[32,2,24,1024]{3,2,1,0:T(8,128)(2,1)}, u32[]{:S(2)}, u32[]{:S(2)}) %all-to-all-start.3) | async-done | bytes 3145760 | tf_op jit(solution)/shard_map/all_to_all | solution.py:268
  300.5 4.2 %convolution_reduce_fusion = f32[128,1024]{1,0:T(8,128)} fusion(bf16[3,128,1536]{2,1,0:T(8,128)(2,1)S(1)} %bitcast.145, bf16[1536,1024,1]{1,0,2:T(8,128)(2,1)} %bitcast.51), kind=kOutput, calls=%fused_computation.16 | convolution fusion | flops 1208221696 | bytes 4849664 | tf_op jit(solution)/shard_map/dot_general | solution.py:276
  306.9 7.7 %shard_map.138 = f32[128,512]{1,0:T(8,128)} custom-call(f32[128,512]{1,0:T(8,128)} %bitcast.146), custom_call_target="tpu_custom_call" | custom-call | tf_op jit(solution)/shard_map/pallas_call | solution.py:47
  (104 shorter events, 39.8 us)
Async XLA Ops:
  0.0 137.0 %copy-start = (bf16[512,2048]{1,0:T(8,128)(2,1)S(1)}, bf16[512,2048]{1,0:T(8,128)(2,1)}, u32[]{:S(2)}) copy-start(bf16[512,2048]{1,0:T(8,128)(2,1)} %param.19) | copy-start | bytes 6291460
  66.8 61.4 %all-to-all-start.1 = ((bf16[32,128,512]{2,1,0:T(8,128)(2,1)}), bf16[32,128,512]{2,1,0:T(8,128)(2,1)}, u32[]{:S(2)}, u32[]{:S(2)}) async-start(bf16[32,128,512]{2,1,0:T(8,128)(2,1)} %get-tuple-element.7), calls=%async_computation.1 | async-start | bytes 8388608 | tf_op jit(solution)/shard_map/all_to_all | solution.py:195
  76.4 4.0 %copy-start.21 = (s32[32]{0:T(128)S(1)}, s32[32]{0:T(128)}, u32[]{:S(2)}) copy-start(s32[32]{0:T(128)} %param.21) | copy-start | bytes 388
  76.4 5.4 %copy-start.3 = (bf16[1,128,2048]{2,1,0:T(8,128)(2,1)S(1)}, bf16[1,128,2048]{2,1,0:T(8,128)(2,1)}, u32[]{:S(2)}) copy-start(bf16[1,128,2048]{2,1,0:T(8,128)(2,1)} %param.14) | copy-start | bytes 1572868
  76.4 5.8 %copy-start.17 = (f32[2048]{0:T(1024)S(1)}, f32[2048]{0:T(1024)}, u32[]{:S(2)}) copy-start(f32[2048]{0:T(1024)} %param.15) | copy-start | bytes 24580
  80.5 4.2 %copy-start.4 = (bf16[512,2048]{1,0:T(8,128)(2,1)S(1)}, bf16[512,2048]{1,0:T(8,128)(2,1)}, u32[]{:S(2)}) copy-start(bf16[512,2048]{1,0:T(8,128)(2,1)} %copy.86) | copy-start | bytes 6291460
  91.1 3.2 %copy-start.19 = (s32[1,128,8]{1,2,0:T(8,128)S(1)}, s32[1,128,8]{1,2,0:T(8,128)}, u32[]{:S(2)}) copy-start(s32[1,128,8]{1,2,0:T(8,128)} %param.23) | copy-start | bytes 12292
  91.1 4.1 %copy-start.20 = (f32[1,128,8]{1,2,0:T(8,128)S(1)}, f32[1,128,8]{1,2,0:T(8,128)}, u32[]{:S(2)}) copy-start(f32[1,128,8]{1,2,0:T(8,128)} %param.24) | copy-start | bytes 12292
  139.2 17.8 %copy-start.18 = (f32[2048]{0:T(1024)S(1)}, f32[2048]{0:T(1024)}, u32[]{:S(2)}) copy-start(f32[2048]{0:T(1024)} %param.22) | copy-start | bytes 24580
  162.4 13.8 %copy-start.10 = (bf16[2,2048,256]{2,1,0:T(8,128)(2,1)S(1)}, bf16[2,2048,256]{2,1,0:T(8,128)(2,1)}, u32[]{:S(2)}) copy-start(bf16[2,2048,256]{2,1,0:T(8,128)(2,1)} %param.25) | copy-start | bytes 6291460
  162.4 57.4 %all-to-all-start.2 = ((bf16[32,2,24,1024]{3,2,1,0:T(8,128)(2,1)}), bf16[32,2,24,1024]{3,2,1,0:T(8,128)(2,1)}, u32[]{:S(2)}, u32[]{:S(2)}) async-start(bf16[32,2,24,1024]{3,2,1,0:T(8,128)(2,1)} %bitcast.117), calls=%async_computation.2 | async-start | bytes 6291456 | tf_op jit(solution)/shard_map/all_to_all | solution.py:245
  176.2 2.0 copy-start.11
  178.2 2.3 copy-start.12
  219.8 4.6 %copy-start.7 = (bf16[1,2048,256]{2,1,0:T(8,128)(2,1)S(1)}, bf16[1,2048,256]{2,1,0:T(8,128)(2,1)}, u32[]{:S(2)}) copy-start(bf16[1,2048,256]{2,1,0:T(8,128)(2,1)} %get-tuple-element.17) | copy-start | bytes 3145732
  224.4 11.3 %collective-permute-start = (bf16[32,24,1024]{2,1,0:T(8,128)(2,1)}, bf16[32,24,1024]{2,1,0:T(8,128)(2,1)}, u32[]{:S(2)}, u32[]{:S(2)}) collective-permute-start(bf16[32,24,1024]{2,1,0:T(8,128)(2,1)} %get-tuple-element.9), channel_id=1, source_target_pairs={{0,1},{1,0},{2,3},{3,2},{4,5},{5,4},{6,7},{7,6},{8,9},{9,8},{10,11... | collective-permute-start | bytes 4718600 | tf_op jit(solution)/shard_map/ppermute | solution.py:248
  231.4 2.0 copy-start.14
  231.5 2.4 copy-start.13
  232.8 8.6 %collective-permute-start.2 = (bf16[32,24,1024]{2,1,0:T(8,128)(2,1)S(1)}, bf16[32,24,1024]{2,1,0:T(8,128)(2,1)S(1)}, u32[]{:S(2)}, u32[]{:S(2)}) collective-permute-start(bf16[32,24,1024]{2,1,0:T(8,128)(2,1)S(1)} %copy-done.15), channel_id=1, source_target_pairs={{0,1},{1,0},{2,3},{3,2},{4,5},{5,4},{6,7},{7,6},{8,9},{9,8},{10,11... | collective-permute-start | bytes 4718600 | tf_op jit(solution)/shard_map/ppermute | solution.py:248
  235.7 2.5 copy-start.16
  240.8 3.6 %collective-permute-start.1 = (bf16[768,1024]{1,0:T(8,128)(2,1)S(1)}, bf16[768,1024]{1,0:T(8,128)(2,1)S(1)}, u32[]{:S(2)}, u32[]{:S(2)}) collective-permute-start(bf16[768,1024]{1,0:T(8,128)(2,1)S(1)} %convolution_convert_fusion.4), channel_id=1, source_target_pairs={{0,1},{1,0},{2,3},{3,2},{4,5},{5,4},{6,7},{7,6},{8,9},{9,8},{10,11... | collective-permute-start | bytes 4718600 | tf_op jit(solution)/shard_map/ppermute | solution.py:261
  243.2 3.5 %collective-permute-start.3 = (bf16[768,1024]{1,0:T(8,128)(2,1)S(1)}, bf16[768,1024]{1,0:T(8,128)(2,1)S(1)}, u32[]{:S(2)}, u32[]{:S(2)}) collective-permute-start(bf16[768,1024]{1,0:T(8,128)(2,1)S(1)} %convolution_convert_fusion.2), channel_id=1, source_target_pairs={{0,1},{1,0},{2,3},{3,2},{4,5},{5,4},{6,7},{7,6},{8,9},{9,8},{10,11... | collective-permute-start | bytes 4718600 | tf_op jit(solution)/shard_map/ppermute | solution.py:261
  249.3 7.8 %copy-start.8 = (f32[128,1536]{1,0:T(8,128)S(1)}, f32[128,1536]{1,0:T(8,128)}, u32[]{:S(2)}) copy-start(f32[128,1536]{1,0:T(8,128)} %get-tuple-element.6) | copy-start | bytes 2359300
  249.3 51.2 %all-to-all-start.3 = ((bf16[32,2,24,1024]{3,2,1,0:T(8,128)(2,1)}), bf16[32,2,24,1024]{3,2,1,0:T(8,128)(2,1)}, u32[]{:S(2)}, u32[]{:S(2)}) async-start(bf16[32,2,24,1024]{3,2,1,0:T(8,128)(2,1)} %pad_maximum_fusion), calls=%async_computation.3 | async-start | bytes 6291456 | tf_op jit(solution)/shard_map/all_to_all | solution.py:268
  300.5 16.0 %copy-start.1 = (bf16[512,2048]{1,0:T(8,128)(2,1)S(1)}, bf16[512,2048]{1,0:T(8,128)(2,1)}, u32[]{:S(2)}) copy-start(bf16[512,2048]{1,0:T(8,128)(2,1)} %param.19) | copy-start | bytes 6291460
  (5 other events, 7.8 us)

commit v8 on v7

--- a/solution.py
+++ b/solution.py
@@ -244,13 +244,11 @@
     outgoing = outgoing.reshape(group_count, experts_here, capacity, half)
     arrived = lax.all_to_all(outgoing, "grp", split_axis=0, concat_axis=0, tiled=True)
     partners = [(index, index ^ 1) for index in range(head_count)]
-    arrived_other = [
-        lax.ppermute(arrived[:, expert], "head", partners) for expert in range(experts_here)
-    ]
+    arrived_other = lax.ppermute(arrived, "head", partners)
     pair_sums = []
     for expert in range(experts_here):
         mine = arrived[:, expert].reshape(group_count * capacity, half)
-        other = arrived_other[expert].reshape(group_count * capacity, half)
+        other = arrived_other[:, expert].reshape(group_count * capacity, half)
         gate = jnp.dot(mine, row_halves(w_gate[expert], core), preferred_element_type=jnp.float32)
         gate = gate + jnp.dot(other, row_halves(w_gate[expert], other_core), preferred_element_type=jnp.float32)
         upper = jnp.dot(mine, row_halves(w_up[expert], core), preferred_element_type=jnp.float32)

time: 318 us -> 302 us (0.950)
  blocking collectives: 61.6 us -> 116 us
  waiting for transfers between devices: 109 us -> 71 us
  starting transfers between devices: 28.4 us -> 12.2 us
  local copies, waits for them, and re-layouts: 43.6 us -> 32.5 us
  matrix products: 25.2 us -> 20.8 us
    all_to_all x0 -> x1, blocking collectives: none -> 54.4 us  [on_device(): lax.all_to_all(outgoing, 'grp', split_axis=0, concat_axis=0, tiled=True)]
    all_to_all x1 -> x0, waiting for transfers between devices: 37.6 us -> none  [on_device(): lax.all_to_all(outgoing, 'grp', split_axis=0, concat_axis=0, tiled=True)]
    all_to_all x1 -> x0, starting transfers between devices: 13.8 us -> none  [on_device(): lax.all_to_all(outgoing, 'grp', split_axis=0, concat_axis=0, tiled=True)]
    unnamed x48 -> x28, local copies, waits for them, and re-layouts: 8.24 us -> 2.03 us
    squeeze x1 -> x0, local copies, waits for them, and re-layouts: 4.58 us -> none  [on_device(): arrived[:, expert]]
    slice x0 -> x2, local copies, waits for them, and re-layouts: none -> 4.4 us  [the longest x1 2.2 us: on_device(): mine = arrived[:, expert].reshape(group_count * capacity, half)]
  transfers between devices with their start and end apart: 7 -> 5, of which waited for: 5 -> 4; matrix products, arithmetic and copies ran while one was open for 16% -> 14% of each run, Pallas kernels for 0% -> 0%
where the time goes in v8:
time: 302 us
  blocking collectives  116 us (38%)
  waiting for transfers between devices  71 us (24%)
  Pallas kernels  32.7 us (11%)
  local copies, waits for them, and re-layouts  32.5 us (11%)
  matrix products  20.8 us (7%)
  other arithmetic  16 us (5%)
  starting transfers between devices  12.2 us (4%)
    all_to_all x1, blocking collectives, on_device(): lax.all_to_all(cache[part], 'grp', split_axis=0, concat_axis=0, tiled=True)  61.6 us
    all_to_all x1, blocking collectives, on_device(): lax.all_to_all(outgoing, 'grp', split_axis=0, concat_axis=0, tiled=True)  54.4 us
    all_to_all x1, waiting for transfers between devices, on_device(): lax.all_to_all(pair_sum, 'grp', split_axis=0, concat_axis=0, tiled=True)  43.2 us
    all_to_all x1, waiting for transfers between devices, on_device(): lax.all_to_all(cache[part], 'grp', split_axis=0, concat_axis=0, tiled=True)  25 us
    pallas_call x1, Pallas kernels, head_reduce(): pl.pallas_call(kernel, out_shape=jax.ShapeDtypeStruct(x.shape, jnp.float3...  16.4 us
    pallas_call x1, Pallas kernels, attend(): pl.pallas_call(kernel, grid_spec=grid_spec, out_shape=jax.ShapeDtypeStruc...  8.67 us
    pallas_call x1, Pallas kernels, peer_swap(): pl.pallas_call(kernel, out_shape=jax.ShapeDtypeStruct(x.shape, x.dtype),...  7.69 us
    reduce_sum x1, other arithmetic, on_device(): dispatch = jnp.sum(place.astype(jnp.float32), axis=1).astype(jnp.bfloat16)  6.97 us
  transfers between devices with their start and end apart: 5, of which 4 were waited for; matrix products, arithmetic and copies ran while one was open for 14% of the time, Pallas kernels for 0%

profile of v8, /device:TPU:10, one launch (start us, length us, event | category | flops | bytes accessed | tf_op | source)
XLA Modules:
  0.0 301.6 jit_solution(9950114194466987252)
XLA Ops:
  0.0 5.3 %slice_bitcast_fusion = (bf16[32,128,512]{2,1,0:T(8,128)(2,1)}, bf16[32,128,512]{2,1,0:T(8,128)(2,1)S(1)}) fusion(bf16[2,32,128,512]{3,2,1,0:T(8,128)(2,1)} %param.20), kind=kLoop, calls=%fused_computation.4 | loop fusion | bytes 16777216 | tf_op jit(solution)/shard_map/squeeze | solution.py:195
  5.3 61.6 %all_to_all.20 = bf16[32,128,512]{2,1,0:T(8,128)(2,1)} all-to-all(bf16[32,128,512]{2,1,0:T(8,128)(2,1)S(1)} %get-tuple-element.8), channel_id=1, replica_groups=mesh['grp'=32,'head'=4] {'grp'}, dimensions={0} | all-to-all | bytes 8388608 | tf_op jit(solution)/shard_map/all_to_all | solution.py:195
  66.8 5.6 %all-to-all-start.1 = ((bf16[32,128,512]{2,1,0:T(8,128)(2,1)}), bf16[32,128,512]{2,1,0:T(8,128)(2,1)}, u32[]{:S(2)}, u32[]{:S(2)}) async-start(bf16[32,128,512]{2,1,0:T(8,128)(2,1)} %get-tuple-element.7), calls=%async_computation.1 | async-start | bytes 8388608 | tf_op jit(solution)/shard_map/all_to_all | solution.py:195
  72.5 3.9 %copy.88 = bf16[512,2048]{1,0:T(8,128)(2,1)} copy(bf16[512,2048]{0,1:T(8,128)(2,1)} %bitcast.133) | data formatting | bytes 4194304 | tf_op jit(solution)/shard_map/dot_general | solution.py:185
  76.4 4.0 %copy.86 = bf16[512,2048]{1,0:T(8,128)(2,1)} copy(bf16[512,2048]{0,1:T(8,128)(2,1)} %bitcast.134) | data formatting | bytes 4194304 | tf_op jit(solution)/shard_map/dot_general | solution.py:182
  82.1 2.4 fusion.19
  87.0 3.9 %copy.90 = bf16[512,2048]{1,0:T(8,128)(2,1)} copy(bf16[512,2048]{0,1:T(8,128)(2,1)} %bitcast.135) | data formatting | bytes 4194304 | tf_op jit(solution)/shard_map/dot_general | solution.py:188
  90.9 2.4 convolution_convert_fusion.6
  95.1 7.0 %convert_reduce_fusion = (bf16[128,1536]{1,0:T(8,128)(2,1)S(1)}, f32[128,1536]{1,0:T(8,128)}) fusion(s32[128,8]{1,0:T(8,128)S(1)} %bitcast_add_fusion.1, f32[128,8]{1,0:T(8,128)S(1)} %copy.77), kind=kLoop, calls=%fused_computation | loop fusion | flops 7471104 | bytes 1187840 | tf_op jit(solution)/shard_map/reduce_sum | solution.py:224
  103.2 25.0 %all-to-all-done.1 = bf16[32,128,512]{2,1,0:T(8,128)(2,1)} async-done(((bf16[32,128,512]{2,1,0:T(8,128)(2,1)}), bf16[32,128,512]{2,1,0:T(8,128)(2,1)}, u32[]{:S(2)}, u32[]{:S(2)}) %all-to-all-start.1) | async-done | bytes 4194336 | tf_op jit(solution)/shard_map/all_to_all | solution.py:195
  128.3 8.7 %shard_map.136 = bf16[128,512]{1,0:T(8,128)(2,1)} custom-call(s32[1]{0:T(128)} %dynamic_slice.55.length_ref, bf16[128,512]{1,0:T(8,128)(2,1)} %copy.87.q_ref, bf16[128,512]{1,0:T(8,128)(2,1)} %copy.89.kn_ref, bf16[128,512]{1,0:T(8,128)(2,1)} %copy.91.vn_ref, bf16[4096,512]{1,0:T(8,128)(2,1)} %bitcast.108, bf16[4096,512]{1,0:T(8,128)(2,1)} %bitcast.16.v_ref), custom_call_target="tpu_custom_call" | custom-call | tf_op jit(solution)/shard_map/pallas_call | solution.py:99
  136.9 2.1 convolution_convert_fusion.1.x_ref
  139.1 16.4 %shard_map.137 = f32[128,2048]{1,0:T(8,128)} custom-call(bf16[128,2048]{1,0:T(8,128)(2,1)} %convolution_convert_fusion.1.x_ref, f32[128,2048]{1,0:T(8,128)} %convert_bitcast_fusion.base_ref), custom_call_target="tpu_custom_call" | custom-call | tf_op jit(solution)/shard_map/pallas_call | solution.py:142
  160.7 54.4 %all_to_all.21 = bf16[32,2,24,1024]{3,2,1,0:T(8,128)(2,1)} all-to-all(bf16[32,2,24,1024]{3,2,1,0:T(8,128)(2,1)S(1)} %bitcast.113), channel_id=1, replica_groups=mesh['grp'=32,'head'=4] {'grp'}, dimensions={0} | all-to-all | bytes 6291456 | tf_op jit(solution)/shard_map/all_to_all | solution.py:245
  216.3 1.8 fusion.26
  219.2 2.2 fusion.24
  223.7 2.2 fusion.23
  232.0 1.7 collective-permute-done.2
  234.3 2.0 pad_maximum_fusion
  236.3 5.9 %all-to-all-start.3 = ((bf16[32,2,24,1024]{3,2,1,0:T(8,128)(2,1)}), bf16[32,2,24,1024]{3,2,1,0:T(8,128)(2,1)}, u32[]{:S(2)}, u32[]{:S(2)}) async-start(bf16[32,2,24,1024]{3,2,1,0:T(8,128)(2,1)} %pad_maximum_fusion), calls=%async_computation.3 | async-start | bytes 6291456 | tf_op jit(solution)/shard_map/all_to_all | solution.py:266
  242.4 43.2 %all-to-all-done.3 = bf16[32,2,24,1024]{3,2,1,0:T(8,128)(2,1)} async-done(((bf16[32,2,24,1024]{3,2,1,0:T(8,128)(2,1)}), bf16[32,2,24,1024]{3,2,1,0:T(8,128)(2,1)}, u32[]{:S(2)}, u32[]{:S(2)}) %all-to-all-start.3) | async-done | bytes 3145760 | tf_op jit(solution)/shard_map/all_to_all | solution.py:266
  285.6 4.3 %convolution_reduce_fusion = f32[128,1024]{1,0:T(8,128)} fusion(bf16[3,128,1536]{2,1,0:T(8,128)(2,1)S(1)} %bitcast.143, bf16[1536,1024,1]{1,0,2:T(8,128)(2,1)} %bitcast.49), kind=kOutput, calls=%fused_computation.16 | convolution fusion | flops 1208221696 | bytes 4849664 | tf_op jit(solution)/shard_map/dot_general | solution.py:274
  292.0 7.7 %shard_map.138 = f32[128,512]{1,0:T(8,128)} custom-call(f32[128,512]{1,0:T(8,128)} %bitcast.144), custom_call_target="tpu_custom_call" | custom-call | tf_op jit(solution)/shard_map/pallas_call | solution.py:47
  299.8 1.7 fusion.16
  (82 shorter events, 25.8 us)
Async XLA Ops:
  0.0 136.9 %copy-start = (bf16[512,2048]{1,0:T(8,128)(2,1)S(1)}, bf16[512,2048]{1,0:T(8,128)(2,1)}, u32[]{:S(2)}) copy-start(bf16[512,2048]{1,0:T(8,128)(2,1)} %param.19) | copy-start | bytes 6291460
  66.8 61.4 %all-to-all-start.1 = ((bf16[32,128,512]{2,1,0:T(8,128)(2,1)}), bf16[32,128,512]{2,1,0:T(8,128)(2,1)}, u32[]{:S(2)}, u32[]{:S(2)}) async-start(bf16[32,128,512]{2,1,0:T(8,128)(2,1)} %get-tuple-element.7), calls=%async_computation.1 | async-start | bytes 8388608 | tf_op jit(solution)/shard_map/all_to_all | solution.py:195
  76.4 4.0 %copy-start.11 = (s32[32]{0:T(128)S(1)}, s32[32]{0:T(128)}, u32[]{:S(2)}) copy-start(s32[32]{0:T(128)} %param.21) | copy-start | bytes 388
  76.4 5.3 %copy-start.2 = (bf16[1,128,2048]{2,1,0:T(8,128)(2,1)S(1)}, bf16[1,128,2048]{2,1,0:T(8,128)(2,1)}, u32[]{:S(2)}) copy-start(bf16[1,128,2048]{2,1,0:T(8,128)(2,1)} %param.14) | copy-start | bytes 1572868
  76.4 5.7 %copy-start.7 = (f32[2048]{0:T(1024)S(1)}, f32[2048]{0:T(1024)}, u32[]{:S(2)}) copy-start(f32[2048]{0:T(1024)} %param.15) | copy-start | bytes 24580
  80.4 4.1 %copy-start.3 = (bf16[512,2048]{1,0:T(8,128)(2,1)S(1)}, bf16[512,2048]{1,0:T(8,128)(2,1)}, u32[]{:S(2)}) copy-start(bf16[512,2048]{1,0:T(8,128)(2,1)} %copy.86) | copy-start | bytes 6291460
  90.9 3.2 %copy-start.9 = (s32[1,128,8]{1,2,0:T(8,128)S(1)}, s32[1,128,8]{1,2,0:T(8,128)}, u32[]{:S(2)}) copy-start(s32[1,128,8]{1,2,0:T(8,128)} %param.23) | copy-start | bytes 12292
  90.9 4.1 %copy-start.10 = (f32[1,128,8]{1,2,0:T(8,128)S(1)}, f32[1,128,8]{1,2,0:T(8,128)}, u32[]{:S(2)}) copy-start(f32[1,128,8]{1,2,0:T(8,128)} %param.24) | copy-start | bytes 12292
  139.1 17.8 %copy-start.8 = (f32[2048]{0:T(1024)S(1)}, f32[2048]{0:T(1024)}, u32[]{:S(2)}) copy-start(f32[2048]{0:T(1024)} %param.22) | copy-start | bytes 24580
  160.7 54.4 %copy-start.5 = (bf16[2,256,2048]{2,1,0:T(8,128)(2,1)S(1)}, bf16[2,256,2048]{2,1,0:T(8,128)(2,1)}, u32[]{:S(2)}) copy-start(bf16[2,256,2048]{2,1,0:T(8,128)(2,1)} %param.27) | copy-start | bytes 6291460
  215.1 8.6 %collective-permute-start = (bf16[32,2,24,1024]{3,2,1,0:T(8,128)(2,1)}, bf16[32,2,24,1024]{3,2,1,0:T(8,128)(2,1)}, u32[]{:S(2)}, u32[]{:S(2)}) collective-permute-start(bf16[32,2,24,1024]{3,2,1,0:T(8,128)(2,1)} %all_to_all.21), channel_id=1, source_target_pairs={{0,1},{1,0},{2,3},{3,2},{4,5},{5,4},{6,7},{7,6},{8,9},{9,8},{10,11... | collective-permute-start | bytes 9437192 | tf_op jit(solution)/shard_map/ppermute | solution.py:247
  216.3 2.2 copy-start.6
  227.7 3.6 %collective-permute-start.1 = (bf16[768,1024]{1,0:T(8,128)(2,1)S(1)}, bf16[768,1024]{1,0:T(8,128)(2,1)S(1)}, u32[]{:S(2)}, u32[]{:S(2)}) collective-permute-start(bf16[768,1024]{1,0:T(8,128)(2,1)S(1)} %convolution_convert_fusion.4), channel_id=1, source_target_pairs={{0,1},{1,0},{2,3},{3,2},{4,5},{5,4},{6,7},{7,6},{8,9},{9,8},{10,11... | collective-permute-start | bytes 4718600 | tf_op jit(solution)/shard_map/ppermute | solution.py:259
  230.2 3.5 %collective-permute-start.2 = (bf16[768,1024]{1,0:T(8,128)(2,1)S(1)}, bf16[768,1024]{1,0:T(8,128)(2,1)S(1)}, u32[]{:S(2)}, u32[]{:S(2)}) collective-permute-start(bf16[768,1024]{1,0:T(8,128)(2,1)S(1)} %convolution_convert_fusion.2), channel_id=1, source_target_pairs={{0,1},{1,0},{2,3},{3,2},{4,5},{5,4},{6,7},{7,6},{8,9},{9,8},{10,11... | collective-permute-start | bytes 4718600 | tf_op jit(solution)/shard_map/ppermute | solution.py:259
  236.3 5.9 %copy-start.4 = (f32[128,1536]{1,0:T(8,128)S(1)}, f32[128,1536]{1,0:T(8,128)}, u32[]{:S(2)}) copy-start(f32[128,1536]{1,0:T(8,128)} %get-tuple-element.6) | copy-start | bytes 2359300
  236.3 49.3 %all-to-all-start.3 = ((bf16[32,2,24,1024]{3,2,1,0:T(8,128)(2,1)}), bf16[32,2,24,1024]{3,2,1,0:T(8,128)(2,1)}, u32[]{:S(2)}, u32[]{:S(2)}) async-start(bf16[32,2,24,1024]{3,2,1,0:T(8,128)(2,1)} %pad_maximum_fusion), calls=%async_computation.3 | async-start | bytes 6291456 | tf_op jit(solution)/shard_map/all_to_all | solution.py:266
  285.6 16.0 %copy-start.1 = (bf16[512,2048]{1,0:T(8,128)(2,1)S(1)}, bf16[512,2048]{1,0:T(8,128)(2,1)}, u32[]{:S(2)}) copy-start(bf16[512,2048]{1,0:T(8,128)(2,1)} %param.19) | copy-start | bytes 6291460

commit v9 on v8

--- a/solution.py
+++ b/solution.py
@@ -271,12 +271,17 @@
         piece = weighting.astype(jnp.bfloat16)
         weighting = weighting - piece.astype(jnp.float32)
         pieces.append(piece)
-    combined = jnp.dot(jnp.concatenate(pieces, axis=0), returned, preferred_element_type=jnp.float32)
-    combined = combined.reshape(3, tokens, half).sum(axis=0)
-    combined = combined.reshape(tokens, 2, share_width)
-    keep = lax.dynamic_index_in_dim(combined, chip, axis=1, keepdims=False)
-    give = lax.dynamic_index_in_dim(combined, 1 - chip, axis=1, keepdims=False)
-    moe_share = keep + peer_swap(give, True, 3)
+    stacked = jnp.concatenate(pieces, axis=0)
+    by_chip = returned.reshape(slots, 2, share_width)
+
+    def combine_block(which):
+        block = lax.dynamic_index_in_dim(by_chip, which, axis=1, keepdims=False)
+        products = jnp.dot(stacked, block, preferred_element_type=jnp.float32)
+        return products.reshape(3, tokens, share_width).sum(axis=0)
+
+    across_pairs = [(index, index ^ 2) for index in range(head_count)]
+    received = lax.ppermute(combine_block(1 - chip), "head", across_pairs)
+    moe_share = combine_block(chip) + received
     resid_share = lax.dynamic_slice_in_dim(resid, head_at * share_width, share_width, 1)
     return (resid_share + moe_share).astype(jnp.bfloat16)[None]
 

time: 302 us -> 312 us (1.033)
  local copies, waits for them, and re-layouts: 32.5 us -> 46.1 us
  Pallas kernels: 32.7 us -> 25 us
  waiting for transfers between devices: 71 us -> 76.4 us
    pallas_call x1 -> x0, Pallas kernels: 7.69 us -> none  [peer_swap(): pl.pallas_call(kernel, out_shape=jax.ShapeDtypeStruct(x.shape, x.dtype),...]
    ppermute x0 -> x1, waiting for transfers between devices: none -> 6.48 us  [on_device(): received = lax.ppermute(combine_block(1 - chip), 'head', across_pairs)]
    dynamic_slice x3 -> x1, local copies, waits for them, and re-layouts: 1.01 us -> 6.59 us  [combine_block(): block = lax.dynamic_index_in_dim(by_chip, which, axis=1, keepdims=False)]
    unnamed x28 -> x34, local copies, waits for them, and re-layouts: 2.03 us -> 6.91 us
    another operation x0 -> x1, local copies, waits for them, and re-layouts: none -> 4.77 us  [on_device(): by_chip = returned.reshape(slots, 2, share_width)]
  transfers between devices with their start and end apart: 5 -> 6, of which waited for: 4 -> 5; matrix products, arithmetic and copies ran while one was open for 14% -> 15% of each run, Pallas kernels for 0% -> 0%
where the time goes in v9:
time: 312 us; the launch traced here: 311 us
  blocking collectives  116 us (37%)
  waiting for transfers between devices  76.4 us (24%)
  local copies, waits for them, and re-layouts  46.1 us (15%)
  Pallas kernels  25 us (8%)
  matrix products  18.1 us (6%)
  other arithmetic  16.9 us (5%)
  starting transfers between devices  12.3 us (4%)
    all_to_all x1, blocking collectives, on_device(): lax.all_to_all(cache[part], 'grp', split_axis=0, concat_axis=0, tiled=True)  61.6 us
    all_to_all x1, blocking collectives, on_device(): lax.all_to_all(outgoing, 'grp', split_axis=0, concat_axis=0, tiled=True)  54.3 us
    all_to_all x1, waiting for transfers between devices, on_device(): lax.all_to_all(pair_sum, 'grp', split_axis=0, concat_axis=0, tiled=True)  42.2 us
    all_to_all x1, waiting for transfers between devices, on_device(): lax.all_to_all(cache[part], 'grp', split_axis=0, concat_axis=0, tiled=True)  24.9 us
    pallas_call x1, Pallas kernels, head_reduce(): pl.pallas_call(kernel, out_shape=jax.ShapeDtypeStruct(x.shape, jnp.float3...  16.4 us
    pallas_call x1, Pallas kernels, attend(): pl.pallas_call(kernel, grid_spec=grid_spec, out_shape=jax.ShapeDtypeStruc...  8.63 us
    reduce_sum x1, other arithmetic, on_device(): dispatch = jnp.sum(place.astype(jnp.float32), axis=1).astype(jnp.bfloat16)  6.97 us
    unnamed x34, local copies, waits for them, and re-layouts  6.91 us
  transfers between devices with their start and end apart: 6, of which 5 were waited for; matrix products, arithmetic and copies ran while one was open for 15% of the time, Pallas kernels for 0%

profile of v9, /device:TPU:10, one launch (start us, length us, event | category | flops | bytes accessed | tf_op | source)
XLA Modules:
  0.0 311.2 jit_solution(7094737158983505903)
XLA Ops:
  0.0 5.3 %slice_bitcast_fusion = (bf16[32,128,512]{2,1,0:T(8,128)(2,1)}, bf16[32,128,512]{2,1,0:T(8,128)(2,1)S(1)}) fusion(bf16[2,32,128,512]{3,2,1,0:T(8,128)(2,1)} %param.20), kind=kLoop, calls=%fused_computation.4 | loop fusion | bytes 16777216 | tf_op jit(solution)/shard_map/squeeze | solution.py:195
  5.3 61.6 %all_to_all.20 = bf16[32,128,512]{2,1,0:T(8,128)(2,1)} all-to-all(bf16[32,128,512]{2,1,0:T(8,128)(2,1)S(1)} %get-tuple-element.8), channel_id=1, replica_groups=mesh['grp'=32,'head'=4] {'grp'}, dimensions={0} | all-to-all | bytes 8388608 | tf_op jit(solution)/shard_map/all_to_all | solution.py:195
  66.9 5.6 %all-to-all-start.1 = ((bf16[32,128,512]{2,1,0:T(8,128)(2,1)}), bf16[32,128,512]{2,1,0:T(8,128)(2,1)}, u32[]{:S(2)}, u32[]{:S(2)}) async-start(bf16[32,128,512]{2,1,0:T(8,128)(2,1)} %get-tuple-element.7), calls=%async_computation.1 | async-start | bytes 8388608 | tf_op jit(solution)/shard_map/all_to_all | solution.py:195
  72.5 4.0 %copy.65 = bf16[512,2048]{1,0:T(8,128)(2,1)} copy(bf16[512,2048]{0,1:T(8,128)(2,1)} %bitcast.131) | data formatting | bytes 4194304 | tf_op jit(solution)/shard_map/dot_general | solution.py:185
  76.5 4.0 %copy.63 = bf16[512,2048]{1,0:T(8,128)(2,1)} copy(bf16[512,2048]{0,1:T(8,128)(2,1)} %bitcast.132) | data formatting | bytes 4194304 | tf_op jit(solution)/shard_map/dot_general | solution.py:182
  82.2 2.4 fusion.29
  87.1 4.0 %copy.67 = bf16[512,2048]{1,0:T(8,128)(2,1)} copy(bf16[512,2048]{0,1:T(8,128)(2,1)} %bitcast.133) | data formatting | bytes 4194304 | tf_op jit(solution)/shard_map/dot_general | solution.py:188
  91.0 2.4 convolution_convert_fusion.6
  95.2 7.0 %convert_reduce_fusion = (bf16[128,1536]{1,0:T(8,128)(2,1)S(1)}, f32[128,1536]{1,0:T(8,128)}) fusion(s32[128,8]{1,0:T(8,128)S(1)} %bitcast_add_fusion, f32[128,8]{1,0:T(8,128)S(1)} %copy.57), kind=kLoop, calls=%fused_computation | loop fusion | flops 7471104 | bytes 1187840 | tf_op jit(solution)/shard_map/reduce_sum | solution.py:224
  103.3 24.9 %all-to-all-done.1 = bf16[32,128,512]{2,1,0:T(8,128)(2,1)} async-done(((bf16[32,128,512]{2,1,0:T(8,128)(2,1)}), bf16[32,128,512]{2,1,0:T(8,128)(2,1)}, u32[]{:S(2)}, u32[]{:S(2)}) %all-to-all-start.1) | async-done | bytes 4194336 | tf_op jit(solution)/shard_map/all_to_all | solution.py:195
  128.3 8.6 %shard_map.136 = bf16[128,512]{1,0:T(8,128)(2,1)} custom-call(s32[1]{0:T(128)} %dynamic_slice.55.length_ref, bf16[128,512]{1,0:T(8,128)(2,1)} %copy.64.q_ref, bf16[128,512]{1,0:T(8,128)(2,1)} %copy.66.kn_ref, bf16[128,512]{1,0:T(8,128)(2,1)} %copy.68.vn_ref, bf16[4096,512]{1,0:T(8,128)(2,1)} %bitcast.107, bf16[4096,512]{1,0:T(8,128)(2,1)} %bitcast.16.v_ref), custom_call_target="tpu_custom_call" | custom-call | tf_op jit(solution)/shard_map/pallas_call | solution.py:99
  136.9 2.2 convolution_convert_fusion.1.x_ref
  139.1 16.4 %shard_map.137 = f32[128,2048]{1,0:T(8,128)} custom-call(bf16[128,2048]{1,0:T(8,128)(2,1)} %convolution_convert_fusion.1.x_ref, f32[128,2048]{1,0:T(8,128)} %convert_bitcast_fusion.base_ref), custom_call_target="tpu_custom_call" | custom-call | tf_op jit(solution)/shard_map/pallas_call | solution.py:142
  160.8 54.3 %all_to_all.21 = bf16[32,2,24,1024]{3,2,1,0:T(8,128)(2,1)S(1)} all-to-all(bf16[32,2,24,1024]{3,2,1,0:T(8,128)(2,1)S(1)} %bitcast.112), channel_id=1, replica_groups=mesh['grp'=32,'head'=4] {'grp'}, dimensions={0} | all-to-all | bytes 6291456 | tf_op jit(solution)/shard_map/all_to_all | solution.py:245
  216.6 2.3 copy.72
  218.9 2.3 copy.73
  221.1 1.8 fusion.36
  228.0 2.2 fusion.33
  238.6 2.0 pad_maximum_fusion
  240.6 5.9 %all-to-all-start.3 = ((bf16[32,2,24,1024]{3,2,1,0:T(8,128)(2,1)}), bf16[32,2,24,1024]{3,2,1,0:T(8,128)(2,1)}, u32[]{:S(2)}, u32[]{:S(2)}) async-start(bf16[32,2,24,1024]{3,2,1,0:T(8,128)(2,1)} %pad_maximum_fusion), calls=%async_computation.3 | async-start | bytes 6291456 | tf_op jit(solution)/shard_map/all_to_all | solution.py:266
  247.7 42.2 %all-to-all-done.3 = bf16[32,2,24,1024]{3,2,1,0:T(8,128)(2,1)} async-done(((bf16[32,2,24,1024]{3,2,1,0:T(8,128)(2,1)}), bf16[32,2,24,1024]{3,2,1,0:T(8,128)(2,1)}, u32[]{:S(2)}, u32[]{:S(2)}) %all-to-all-start.3) | async-done | bytes 3145760 | tf_op jit(solution)/shard_map/all_to_all | solution.py:266
  289.9 4.8 %reshape_reshape.3 = bf16[1536,2,512]{2,1,0:T(2,128)(2,1)S(1)} reshape(bf16[32,2,24,1024]{3,2,1,0:T(8,128)(2,1)} %all-to-all-done.3) | data formatting | bytes 6291456 | tf_op jit(solution)/shard_map/reshape;reshape | solution.py:275
  294.7 6.6 %constant_dynamic-slice_fusion = (bf16[1536,1,512]{2,1,0:T(2,128)(2,1)S(1)}, bf16[1536,1,512]{2,1,0:T(2,128)(2,1)S(1)}) fusion(bf16[1536,2,512]{2,1,0:T(2,128)(2,1)S(1)} %reshape_reshape.3, s32[]{:T(128)S(6)} %select_n.49, s32[]{:T(128)S(6)} %select_n.48), kind=kLoop, calls=%fused_computation.63 | loop fusion | bytes 6291464 | tf_op jit(solution)/shard_map/jit(dynamic_index_in_dim)/dynamic_slice | solution.py:278
  303.1 6.5 %collective-permute-done.3 = f32[128,512]{1,0:T(8,128)S(1)} collective-permute-done((f32[128,512]{1,0:T(8,128)S(1)}, f32[128,512]{1,0:T(8,128)S(1)}, u32[]{:S(2)}, u32[]{:S(2)}) %collective-permute-start.3) | collective-permute-done | bytes 262176 | tf_op jit(solution)/shard_map/ppermute | solution.py:283
  (88 shorter events, 31.6 us)
Async XLA Ops:
  0.0 136.9 %copy-start = (bf16[512,2048]{1,0:T(8,128)(2,1)S(1)}, bf16[512,2048]{1,0:T(8,128)(2,1)}, u32[]{:S(2)}) copy-start(bf16[512,2048]{1,0:T(8,128)(2,1)} %param.19) | copy-start | bytes 6291460
  66.9 61.4 %all-to-all-start.1 = ((bf16[32,128,512]{2,1,0:T(8,128)(2,1)}), bf16[32,128,512]{2,1,0:T(8,128)(2,1)}, u32[]{:S(2)}, u32[]{:S(2)}) async-start(bf16[32,128,512]{2,1,0:T(8,128)(2,1)} %get-tuple-element.7), calls=%async_computation.1 | async-start | bytes 8388608 | tf_op jit(solution)/shard_map/all_to_all | solution.py:195
  76.5 4.0 %copy-start.14 = (s32[32]{0:T(128)S(1)}, s32[32]{0:T(128)}, u32[]{:S(2)}) copy-start(s32[32]{0:T(128)} %param.21) | copy-start | bytes 388
  76.5 5.3 %copy-start.2 = (bf16[1,128,2048]{2,1,0:T(8,128)(2,1)S(1)}, bf16[1,128,2048]{2,1,0:T(8,128)(2,1)}, u32[]{:S(2)}) copy-start(bf16[1,128,2048]{2,1,0:T(8,128)(2,1)} %param.14) | copy-start | bytes 1572868
  76.5 5.7 %copy-start.10 = (f32[2048]{0:T(1024)S(1)}, f32[2048]{0:T(1024)}, u32[]{:S(2)}) copy-start(f32[2048]{0:T(1024)} %param.15) | copy-start | bytes 24580
  80.5 4.1 %copy-start.3 = (bf16[512,2048]{1,0:T(8,128)(2,1)S(1)}, bf16[512,2048]{1,0:T(8,128)(2,1)}, u32[]{:S(2)}) copy-start(bf16[512,2048]{1,0:T(8,128)(2,1)} %copy.63) | copy-start | bytes 6291460
  91.0 3.2 %copy-start.12 = (s32[1,128,8]{1,2,0:T(8,128)S(1)}, s32[1,128,8]{1,2,0:T(8,128)}, u32[]{:S(2)}) copy-start(s32[1,128,8]{1,2,0:T(8,128)} %param.23) | copy-start | bytes 12292
  91.0 4.1 %copy-start.13 = (f32[1,128,8]{1,2,0:T(8,128)S(1)}, f32[1,128,8]{1,2,0:T(8,128)}, u32[]{:S(2)}) copy-start(f32[1,128,8]{1,2,0:T(8,128)} %param.24) | copy-start | bytes 12292
  139.1 17.8 %copy-start.11 = (f32[2048]{0:T(1024)S(1)}, f32[2048]{0:T(1024)}, u32[]{:S(2)}) copy-start(f32[2048]{0:T(1024)} %param.22) | copy-start | bytes 24580
  160.8 54.3 %copy-start.7 = (bf16[2,256,2048]{2,1,0:T(8,128)(2,1)S(1)}, bf16[2,256,2048]{2,1,0:T(8,128)(2,1)}, u32[]{:S(2)}) copy-start(bf16[2,256,2048]{2,1,0:T(8,128)(2,1)} %param.27) | copy-start | bytes 6291460
  215.1 12.9 %collective-permute-start = (bf16[32,2,24,1024]{3,2,1,0:T(8,128)(2,1)S(1)}, bf16[32,2,24,1024]{3,2,1,0:T(8,128)(2,1)}, u32[]{:S(2)}, u32[]{:S(2)}) collective-permute-start(bf16[32,2,24,1024]{3,2,1,0:T(8,128)(2,1)S(1)} %all_to_all.21), channel_id=1, source_target_pairs={{0,1},{1,0},{2,3},{3,2},{4,5},{5,4},{6,7},{7,6},{8,9},{9,8},{10,11... | collective-permute-start | bytes 9437192 | tf_op jit(solution)/shard_map/ppermute | solution.py:247
  221.1 2.2 copy-start.8
  223.5 1.2 copy-start.4
  223.5 1.5 copy-start.5
  232.1 3.6 %collective-permute-start.1 = (bf16[768,1024]{1,0:T(8,128)(2,1)S(1)}, bf16[768,1024]{1,0:T(8,128)(2,1)S(1)}, u32[]{:S(2)}, u32[]{:S(2)}) collective-permute-start(bf16[768,1024]{1,0:T(8,128)(2,1)S(1)} %convolution_convert_fusion.4), channel_id=1, source_target_pairs={{0,1},{1,0},{2,3},{3,2},{4,5},{5,4},{6,7},{7,6},{8,9},{9,8},{10,11... | collective-permute-start | bytes 4718600 | tf_op jit(solution)/shard_map/ppermute | solution.py:259
  234.5 3.5 %collective-permute-start.2 = (bf16[768,1024]{1,0:T(8,128)(2,1)S(1)}, bf16[768,1024]{1,0:T(8,128)(2,1)S(1)}, u32[]{:S(2)}, u32[]{:S(2)}) collective-permute-start(bf16[768,1024]{1,0:T(8,128)(2,1)S(1)} %convolution_convert_fusion.2), channel_id=1, source_target_pairs={{0,1},{1,0},{2,3},{3,2},{4,5},{5,4},{6,7},{7,6},{8,9},{9,8},{10,11... | collective-permute-start | bytes 4718600 | tf_op jit(solution)/shard_map/ppermute | solution.py:259
  240.6 5.9 %copy-start.6 = (f32[128,1536]{1,0:T(8,128)S(1)}, f32[128,1536]{1,0:T(8,128)}, u32[]{:S(2)}) copy-start(f32[128,1536]{1,0:T(8,128)} %get-tuple-element.6) | copy-start | bytes 2359300
  240.6 49.3 %all-to-all-start.3 = ((bf16[32,2,24,1024]{3,2,1,0:T(8,128)(2,1)}), bf16[32,2,24,1024]{3,2,1,0:T(8,128)(2,1)}, u32[]{:S(2)}, u32[]{:S(2)}) async-start(bf16[32,2,24,1024]{3,2,1,0:T(8,128)(2,1)} %pad_maximum_fusion), calls=%async_computation.3 | async-start | bytes 6291456 | tf_op jit(solution)/shard_map/all_to_all | solution.py:266
  294.7 6.6 %copy-start.9 = (bf16[384,1536]{1,0:T(8,128)(2,1)S(1)}, bf16[384,1536]{1,0:T(8,128)(2,1)}, u32[]{:S(2)}) copy-start(bf16[384,1536]{1,0:T(8,128)(2,1)} %pad_maximum_fusion.1) | copy-start | bytes 3538948
  302.1 7.4 %collective-permute-start.3 = (f32[128,512]{1,0:T(8,128)S(1)}, f32[128,512]{1,0:T(8,128)S(1)}, u32[]{:S(2)}, u32[]{:S(2)}) collective-permute-start(f32[128,512]{1,0:T(8,128)S(1)} %fusion.14), channel_id=1, source_target_pairs={{0,2},{1,3},{2,0},{3,1},{4,6},{5,7},{6,4},{7,5},{8,10},{9,11},{10,... | collective-permute-start | bytes 786440 | tf_op jit(solution)/shard_map/ppermute | solution.py:283
  302.3 8.9 %copy-start.1 = (bf16[512,2048]{1,0:T(8,128)(2,1)S(1)}, bf16[512,2048]{1,0:T(8,128)(2,1)}, u32[]{:S(2)}) copy-start(bf16[512,2048]{1,0:T(8,128)(2,1)} %param.19) | copy-start | bytes 6291460

commit v10 on v8

--- a/solution.py
+++ b/solution.py
@@ -54,12 +54,15 @@
     )(x)
 
 
-def attend(length, query, key_new, value_new, keys, values):
+def attend(length, query, key_new, value_new, keys, values, w_out):
     tokens = query.shape[0]
     context = keys.shape[0]
     heads = query.shape[1] // HD
 
-    def kernel(length_ref, q_ref, kn_ref, vn_ref, k_ref, v_ref, o_ref):
+    width = w_out.shape[1]
+
+    def kernel(length_ref, q_ref, kn_ref, vn_ref, k_ref, v_ref, w_ref, o_ref, acc_ref):
+        head = pl.program_id(0)
         limit = length_ref[0]
         q = q_ref[...]
         contract = (((1,), (1,)), ((), ()))
@@ -81,7 +84,20 @@
         numer = numer + jnp.dot(
             prob_new.astype(jnp.bfloat16), vn_ref[...], preferred_element_type=jnp.float32
         )
-        o_ref[...] = (numer / total).astype(o_ref.dtype)
+        attended = (numer / total).astype(jnp.bfloat16)
+        term = jnp.dot(attended, w_ref[...], preferred_element_type=jnp.float32)
+
+        @pl.when(head == 0)
+        def _():
+            acc_ref[...] = term
+
+        @pl.when(head > 0)
+        def _():
+            acc_ref[...] += term
+
+        @pl.when(head == heads - 1)
+        def _():
+            o_ref[...] = acc_ref[...].astype(o_ref.dtype)
 
     per_head = pl.BlockSpec((tokens, HD), lambda h, n: (0, h))
     grid_spec = pltpu.PrefetchScalarGridSpec(
@@ -93,20 +109,22 @@
             per_head,
             pl.BlockSpec((context, HD), lambda h, n: (0, h)),
             pl.BlockSpec((context, HD), lambda h, n: (0, h)),
+            pl.BlockSpec((HD, width), lambda h, n: (h, 0)),
         ],
-        out_specs=per_head,
+        out_specs=pl.BlockSpec((tokens, width), lambda h, n: (0, 0)),
+        scratch_shapes=[pltpu.VMEM((tokens, width), jnp.float32)],
     )
     return pl.pallas_call(
         kernel,
         grid_spec=grid_spec,
-        out_shape=jax.ShapeDtypeStruct((tokens, heads * HD), jnp.bfloat16),
-    )(length.reshape(1), query, key_new, value_new, keys, values)
-
-
-def head_reduce(x, base, ident):
+        out_shape=jax.ShapeDtypeStruct((tokens, width), jnp.bfloat16),
+    )(length.reshape(1), query, key_new, value_new, keys, values, w_out)
+
+
+def head_reduce(x, base, gain, ident):
     mesh_kind = pl.DeviceIdType.MESH
 
-    def kernel(x_ref, base_ref, o_ref, slots, send_sem, recv_sem):
+    def kernel(x_ref, base_ref, gain_ref, o_ref, normed_ref, slots, send_sem, recv_sem):
         me = lax.axis_index("head")
         group = lax.axis_index("grp")
         partner = me + 1 - 2 * lax.rem(me, 2)
@@ -138,19 +156,25 @@
         for slot in range(3):
             total = total + slots[slot].astype(jnp.float32)
         o_ref[...] = total
-
+        scale = lax.rsqrt(jnp.mean(total * total, axis=-1, keepdims=True) + 1e-05)
+        normed_ref[...] = (total * scale * gain_ref[...]).astype(normed_ref.dtype)
+
+    vmem = pl.BlockSpec(memory_space=pltpu.VMEM)
     return pl.pallas_call(
         kernel,
-        out_shape=jax.ShapeDtypeStruct(x.shape, jnp.float32),
-        in_specs=[pl.BlockSpec(memory_space=pltpu.VMEM), pl.BlockSpec(memory_space=pltpu.VMEM)],
-        out_specs=pl.BlockSpec(memory_space=pltpu.VMEM),
+        out_shape=(
+            jax.ShapeDtypeStruct(x.shape, jnp.float32),
+            jax.ShapeDtypeStruct(x.shape, jnp.bfloat16),
+        ),
+        in_specs=[vmem, vmem, vmem],
+        out_specs=(vmem, vmem),
         scratch_shapes=[
             pltpu.VMEM((3,) + x.shape, x.dtype),
             pltpu.SemaphoreType.DMA((3,)),
             pltpu.SemaphoreType.DMA((3,)),
         ],
         compiler_params=pltpu.CompilerParams(collective_id=ident, has_side_effects=True),
-    )(x, base)
+    )(x, base, gain.reshape(1, -1))
 
 
 def on_device(
@@ -197,17 +221,16 @@
         )
         for part in range(2)
     ]
-    attended = attend(
+    projected = attend(
         length,
         query.reshape(tokens, heads_here * HD),
         key_new.reshape(tokens, heads_here * HD),
         value_new.reshape(tokens, heads_here * HD),
         keys,
         values,
-    )
-    projected = jnp.dot(attended, w_out, preferred_element_type=jnp.float32)
-    resid = head_reduce(projected.astype(jnp.bfloat16), rows, 0)
-    mixed_in = rms_norm(resid, mlp_gain).astype(jnp.bfloat16)
+        w_out,
+    )
+    resid, mixed_in = head_reduce(projected, rows, mlp_gain, 0)
     experts_here = w_gate.shape[0]
     expert_total = experts_here * group_count
     capacity = max(2, 3 * tokens * TOPK // (2 * expert_total))

time: 302 us -> 304 us (level)
    unnamed x28 -> x26, local copies, waits for them, and re-layouts: 2.03 us -> 6.87 us
    all_to_all x1, waiting for transfers between devices: 25 us -> 29 us  [on_device(): lax.all_to_all(cache[part], 'grp', split_axis=0, concat_axis=0, tiled=True)]
where the time goes in v10:
time: 304 us; the launch traced here: 303 us
  blocking collectives  116 us (38%)
  waiting for transfers between devices  72.5 us (24%)
  Pallas kernels  34.4 us (11%)
  local copies, waits for them, and re-layouts  33.7 us (11%)
  matrix products  17.8 us (6%)
  other arithmetic  15.6 us (5%)
  starting transfers between devices  12.1 us (4%)
    all_to_all x1, blocking collectives, on_device(): lax.all_to_all(cache[part], 'grp', split_axis=0, concat_axis=0, tiled=True)  61.6 us
    all_to_all x1, blocking collectives, on_device(): lax.all_to_all(outgoing, 'grp', split_axis=0, concat_axis=0, tiled=True)  54.5 us
    all_to_all x1, waiting for transfers between devices, on_device(): lax.all_to_all(pair_sum, 'grp', split_axis=0, concat_axis=0, tiled=True)  40.7 us
    all_to_all x1, waiting for transfers between devices, on_device(): lax.all_to_all(cache[part], 'grp', split_axis=0, concat_axis=0, tiled=True)  29 us
    pallas_call x1, Pallas kernels, head_reduce(): pl.pallas_call(kernel, out_shape=(jax.ShapeDtypeStruct(x.shape, jnp.float...  16.6 us
    pallas_call x1, Pallas kernels, attend(): pl.pallas_call(kernel, grid_spec=grid_spec, out_shape=jax.ShapeDtypeStruc...  10.1 us
    pallas_call x1, Pallas kernels, peer_swap(): pl.pallas_call(kernel, out_shape=jax.ShapeDtypeStruct(x.shape, x.dtype),...  7.7 us
    reduce_sum x1, other arithmetic, on_device(): dispatch = jnp.sum(place.astype(jnp.float32), axis=1).astype(jnp.bfloat16)  6.98 us
  transfers between devices with their start and end apart: 5, of which 4 were waited for; matrix products, arithmetic and copies ran while one was open for 14% of the time, Pallas kernels for 0%

profile of v10, /device:TPU:10, one launch (start us, length us, event | category | flops | bytes accessed | tf_op | source)
XLA Modules:
  0.0 302.7 jit_solution(16104044441108922196)
XLA Ops:
  0.0 5.1 %slice_bitcast_fusion = (bf16[32,128,512]{2,1,0:T(8,128)(2,1)}, bf16[32,128,512]{2,1,0:T(8,128)(2,1)S(1)}) fusion(bf16[2,32,128,512]{3,2,1,0:T(8,128)(2,1)} %param.20), kind=kLoop, calls=%fused_computation.4 | loop fusion | bytes 16777216 | tf_op jit(solution)/shard_map/squeeze | solution.py:219
  5.1 61.6 %all_to_all.20 = bf16[32,128,512]{2,1,0:T(8,128)(2,1)} all-to-all(bf16[32,128,512]{2,1,0:T(8,128)(2,1)S(1)} %get-tuple-element.12), channel_id=1, replica_groups=mesh['grp'=32,'head'=4] {'grp'}, dimensions={0} | all-to-all | bytes 8388608 | tf_op jit(solution)/shard_map/all_to_all | solution.py:219
  66.7 5.7 %all-to-all-start.1 = ((bf16[32,128,512]{2,1,0:T(8,128)(2,1)}), bf16[32,128,512]{2,1,0:T(8,128)(2,1)}, u32[]{:S(2)}, u32[]{:S(2)}) async-start(bf16[32,128,512]{2,1,0:T(8,128)(2,1)} %get-tuple-element.11), calls=%async_computation.1 | async-start | bytes 8388608 | tf_op jit(solution)/shard_map/all_to_all | solution.py:219
  72.5 2.5 copy.88
  74.9 3.0 copy.86
  79.6 2.4 fusion.19
  84.5 2.4 copy.90
  87.0 2.4 convolution_convert_fusion.5
  91.2 7.0 %convert_reduce_fusion = (bf16[128,1536]{1,0:T(8,128)(2,1)S(1)}, f32[128,1536]{1,0:T(8,128)}) fusion(s32[128,8]{1,0:T(8,128)S(1)} %bitcast_add_fusion.1, f32[128,8]{1,0:T(8,128)S(1)} %copy.77), kind=kLoop, calls=%fused_computation | loop fusion | flops 7471104 | bytes 1187840 | tf_op jit(solution)/shard_map/reduce_sum | solution.py:247
  99.3 29.0 %all-to-all-done.1 = bf16[32,128,512]{2,1,0:T(8,128)(2,1)} async-done(((bf16[32,128,512]{2,1,0:T(8,128)(2,1)}), bf16[32,128,512]{2,1,0:T(8,128)(2,1)}, u32[]{:S(2)}, u32[]{:S(2)}) %all-to-all-start.1) | async-done | bytes 4194336 | tf_op jit(solution)/shard_map/all_to_all | solution.py:219
  128.3 10.1 %shard_map.136.x_ref = bf16[128,2048]{1,0:T(8,128)(2,1)} custom-call(s32[1]{0:T(128)} %dynamic_slice.55.length_ref, bf16[128,512]{1,0:T(8,128)(2,1)} %copy.87.q_ref, bf16[128,512]{1,0:T(8,128)(2,1)} %copy.89.kn_ref, bf16[128,512]{1,0:T(8,128)(2,1)} %copy.91.vn_ref, bf16[4096,512]{1,0:T(8,128)(2,1)} %bitcast.107, bf16[4096,512]{1,0:T(8,128)(2,1)} %bitcast.16.v_ref, ...), custom_call_target="tpu_custom_call" | custom-call | tf_op jit(solution)/shard_map/pallas_call | solution.py:117
  138.4 16.6 %shard_map.137 = (f32[128,2048]{1,0:T(8,128)}, bf16[128,2048]{1,0:T(8,128)(2,1)}) custom-call(bf16[128,2048]{1,0:T(8,128)(2,1)} %shard_map.136.x_ref, f32[128,2048]{1,0:T(8,128)} %convert_bitcast_fusion.base_ref, f32[1,2048]{1,0:T(1,128)} %bitcast.151), custom_call_target="tpu_custom_call" | custom-call | tf_op jit(solution)/shard_map/pallas_call | solution.py:163
  158.4 54.5 %all_to_all.21 = bf16[32,2,24,1024]{3,2,1,0:T(8,128)(2,1)S(1)} all-to-all(bf16[32,2,24,1024]{3,2,1,0:T(8,128)(2,1)S(1)} %bitcast.112), channel_id=1, replica_groups=mesh['grp'=32,'head'=4] {'grp'}, dimensions={0} | all-to-all | bytes 6291456 | tf_op jit(solution)/shard_map/all_to_all | solution.py:268
  214.4 2.3 copy.93
  216.7 2.3 copy.94
  218.9 1.8 fusion.26
  225.9 2.2 fusion.23
  234.1 1.7 collective-permute-done.2
  236.4 1.9 pad_maximum_fusion
  238.4 5.7 %all-to-all-start.3 = ((bf16[32,2,24,1024]{3,2,1,0:T(8,128)(2,1)}), bf16[32,2,24,1024]{3,2,1,0:T(8,128)(2,1)S(1)}, u32[]{:S(2)}, u32[]{:S(2)}) async-start(bf16[32,2,24,1024]{3,2,1,0:T(8,128)(2,1)} %pad_maximum_fusion), calls=%async_computation.3 | async-start | bytes 6291456 | tf_op jit(solution)/shard_map/all_to_all | solution.py:289
  246.8 40.7 %all-to-all-done.3 = bf16[32,2,24,1024]{3,2,1,0:T(8,128)(2,1)S(1)} async-done(((bf16[32,2,24,1024]{3,2,1,0:T(8,128)(2,1)}), bf16[32,2,24,1024]{3,2,1,0:T(8,128)(2,1)S(1)}, u32[]{:S(2)}, u32[]{:S(2)}) %all-to-all-start.3) | async-done | bytes 3145760 | tf_op jit(solution)/shard_map/all_to_all | solution.py:289
  287.5 3.5 %convolution_reduce_fusion = f32[128,1024]{1,0:T(8,128)} fusion(bf16[3,128,1536]{2,1,0:T(8,128)(2,1)} %bitcast.143, bf16[1536,1024,1]{1,0,2:T(8,128)(2,1)S(1)} %bitcast.127), kind=kOutput, calls=%fused_computation.15 | convolution fusion | flops 1208221696 | bytes 4849664 | tf_op jit(solution)/shard_map/dot_general | solution.py:297
  293.1 7.7 %shard_map.138 = f32[128,512]{1,0:T(8,128)} custom-call(f32[128,512]{1,0:T(8,128)} %bitcast.144), custom_call_target="tpu_custom_call" | custom-call | tf_op jit(solution)/shard_map/pallas_call | solution.py:47
  301.0 1.7 fusion.16
  (76 shorter events, 28.5 us)
Async XLA Ops:
  66.7 5.8 %copy-start.3 = (bf16[2048,512]{1,0:T(8,128)(2,1)S(1)}, bf16[2048,512]{1,0:T(8,128)(2,1)}, u32[]{:S(2)}) copy-start(bf16[2048,512]{1,0:T(8,128)(2,1)} %param.17) | copy-start | bytes 6291460
  66.7 61.6 %all-to-all-start.1 = ((bf16[32,128,512]{2,1,0:T(8,128)(2,1)}), bf16[32,128,512]{2,1,0:T(8,128)(2,1)}, u32[]{:S(2)}, u32[]{:S(2)}) async-start(bf16[32,128,512]{2,1,0:T(8,128)(2,1)} %get-tuple-element.11), calls=%async_computation.1 | async-start | bytes 8388608 | tf_op jit(solution)/shard_map/all_to_all | solution.py:219
  74.9 3.0 copy-start.10
  74.9 4.3 %copy-start = (bf16[1,128,2048]{2,1,0:T(8,128)(2,1)S(1)}, bf16[1,128,2048]{2,1,0:T(8,128)(2,1)}, u32[]{:S(2)}) copy-start(bf16[1,128,2048]{2,1,0:T(8,128)(2,1)} %param.14) | copy-start | bytes 1572868
  74.9 4.7 %copy-start.7 = (f32[2048]{0:T(1024)S(1)}, f32[2048]{0:T(1024)}, u32[]{:S(2)}) copy-start(f32[2048]{0:T(1024)} %param.15) | copy-start | bytes 24580
  82.8 1.7 copy-start.4
  87.0 3.2 %copy-start.8 = (s32[1,128,8]{1,2,0:T(8,128)S(1)}, s32[1,128,8]{1,2,0:T(8,128)}, u32[]{:S(2)}) copy-start(s32[1,128,8]{1,2,0:T(8,128)} %param.23) | copy-start | bytes 12292
  87.0 4.1 %copy-start.9 = (f32[1,128,8]{1,2,0:T(8,128)S(1)}, f32[1,128,8]{1,2,0:T(8,128)}, u32[]{:S(2)}) copy-start(f32[1,128,8]{1,2,0:T(8,128)} %param.24) | copy-start | bytes 12292
  158.4 54.5 %copy-start.5 = (bf16[2,256,2048]{2,1,0:T(8,128)(2,1)S(1)}, bf16[2,256,2048]{2,1,0:T(8,128)(2,1)}, u32[]{:S(2)}) copy-start(bf16[2,256,2048]{2,1,0:T(8,128)(2,1)} %param.27) | copy-start | bytes 6291460
  212.9 12.9 %collective-permute-start = (bf16[32,2,24,1024]{3,2,1,0:T(8,128)(2,1)S(1)}, bf16[32,2,24,1024]{3,2,1,0:T(8,128)(2,1)}, u32[]{:S(2)}, u32[]{:S(2)}) collective-permute-start(bf16[32,2,24,1024]{3,2,1,0:T(8,128)(2,1)S(1)} %all_to_all.21), channel_id=1, source_target_pairs={{0,1},{1,0},{2,3},{3,2},{4,5},{5,4},{6,7},{7,6},{8,9},{9,8},{10,11... | collective-permute-start | bytes 9437192 | tf_op jit(solution)/shard_map/ppermute | solution.py:270
  218.9 2.2 copy-start.6
  221.3 1.2 copy-start.1
  221.3 1.5 copy-start.2
  229.9 3.6 %collective-permute-start.1 = (bf16[768,1024]{1,0:T(8,128)(2,1)S(1)}, bf16[768,1024]{1,0:T(8,128)(2,1)S(1)}, u32[]{:S(2)}, u32[]{:S(2)}) collective-permute-start(bf16[768,1024]{1,0:T(8,128)(2,1)S(1)} %convolution_convert_fusion.3), channel_id=1, source_target_pairs={{0,1},{1,0},{2,3},{3,2},{4,5},{5,4},{6,7},{7,6},{8,9},{9,8},{10,11... | collective-permute-start | bytes 4718600 | tf_op jit(solution)/shard_map/ppermute | solution.py:282
  232.3 3.5 %collective-permute-start.2 = (bf16[768,1024]{1,0:T(8,128)(2,1)S(1)}, bf16[768,1024]{1,0:T(8,128)(2,1)S(1)}, u32[]{:S(2)}, u32[]{:S(2)}) collective-permute-start(bf16[768,1024]{1,0:T(8,128)(2,1)S(1)} %convolution_convert_fusion.1), channel_id=1, source_target_pairs={{0,1},{1,0},{2,3},{3,2},{4,5},{5,4},{6,7},{7,6},{8,9},{9,8},{10,11... | collective-permute-start | bytes 4718600 | tf_op jit(solution)/shard_map/ppermute | solution.py:282
  238.4 49.1 %all-to-all-start.3 = ((bf16[32,2,24,1024]{3,2,1,0:T(8,128)(2,1)}), bf16[32,2,24,1024]{3,2,1,0:T(8,128)(2,1)S(1)}, u32[]{:S(2)}, u32[]{:S(2)}) async-start(bf16[32,2,24,1024]{3,2,1,0:T(8,128)(2,1)} %pad_maximum_fusion), calls=%async_computation.3 | async-start | bytes 6291456 | tf_op jit(solution)/shard_map/all_to_all | solution.py:289

commit v11 on v8

--- a/solution.py
+++ b/solution.py
@@ -59,28 +59,47 @@
     context = keys.shape[0]
     heads = query.shape[1] // HD
 
+    chunk = min(context, 256)
+    steps = context // chunk
+
     def kernel(length_ref, q_ref, kn_ref, vn_ref, k_ref, v_ref, o_ref):
         limit = length_ref[0]
         q = q_ref[...]
         contract = (((1,), (1,)), ((), ()))
-        score_old = lax.dot_general(q, k_ref[...], contract, preferred_element_type=jnp.float32)
         score_new = lax.dot_general(q, kn_ref[...], contract, preferred_element_type=jnp.float32)
-        allow_old = lax.broadcasted_iota(jnp.int32, score_old.shape, 1) < limit
         allow_new = lax.broadcasted_iota(jnp.int32, score_new.shape, 1) <= lax.broadcasted_iota(
             jnp.int32, score_new.shape, 0
         )
-        score_old = jnp.where(allow_old, score_old, -1e30)
         score_new = jnp.where(allow_new, score_new, -1e30)
-        top = jnp.maximum(
-            jnp.max(score_old, axis=1, keepdims=True), jnp.max(score_new, axis=1, keepdims=True)
-        )
-        prob_old = jnp.where(allow_old, jnp.exp(score_old - top), 0.0)
+
+        def scores(step):
+            start = pl.multiple_of(step * chunk, chunk)
+            score = lax.dot_general(
+                q, k_ref[pl.ds(start, chunk), :], contract, preferred_element_type=jnp.float32
+            )
+            allow = lax.broadcasted_iota(jnp.int32, score.shape, 1) + start < limit
+            return jnp.where(allow, score, -1e30), allow, start
+
+        def widest(step, top):
+            score, _, _ = scores(step)
+            return jnp.maximum(top, jnp.max(score, axis=1, keepdims=True))
+
+        top = lax.fori_loop(0, steps, widest, jnp.max(score_new, axis=1, keepdims=True))
         prob_new = jnp.where(allow_new, jnp.exp(score_new - top), 0.0)
-        total = jnp.sum(prob_old, axis=1, keepdims=True) + jnp.sum(prob_new, axis=1, keepdims=True)
-        numer = jnp.dot(prob_old.astype(jnp.bfloat16), v_ref[...], preferred_element_type=jnp.float32)
-        numer = numer + jnp.dot(
-            prob_new.astype(jnp.bfloat16), vn_ref[...], preferred_element_type=jnp.float32
-        )
+        total = jnp.sum(prob_new, axis=1, keepdims=True)
+        numer = jnp.dot(prob_new.astype(jnp.bfloat16), vn_ref[...], preferred_element_type=jnp.float32)
+
+        def accumulate(step, carry):
+            total, numer = carry
+            score, allow, start = scores(step)
+            prob = jnp.where(allow, jnp.exp(score - top), 0.0)
+            total = total + jnp.sum(prob, axis=1, keepdims=True)
+            numer = numer + jnp.dot(
+                prob.astype(jnp.bfloat16), v_ref[pl.ds(start, chunk), :], preferred_element_type=jnp.float32
+            )
+            return total, numer
+
+        total, numer = lax.fori_loop(0, steps, accumulate, (total, numer))
         o_ref[...] = (numer / total).astype(o_ref.dtype)
 
     per_head = pl.BlockSpec((tokens, HD), lambda h, n: (0, h))

time: 302 us -> 334 us (1.11)
  Pallas kernels: 32.7 us -> 64.8 us
    pallas_call x1, Pallas kernels: 8.67 us -> 40.8 us  [attend(): pl.pallas_call(kernel, grid_spec=grid_spec, out_shape=jax.ShapeDtypeStruc...]
  transfers between devices with their start and end apart: 5 -> 5, of which waited for: 4 -> 4; matrix products, arithmetic and copies ran while one was open for 14% -> 12% of each run, Pallas kernels for 0% -> 0%
where the time goes in v11:
time: 334 us
  blocking collectives  116 us (35%)
  waiting for transfers between devices  71 us (21%)
  Pallas kernels  64.8 us (19%)
  local copies, waits for them, and re-layouts  32.5 us (10%)
  matrix products  20.8 us (6%)
  other arithmetic  16 us (5%)
  starting transfers between devices  12.2 us (4%)
    all_to_all x1, blocking collectives, on_device(): lax.all_to_all(cache[part], 'grp', split_axis=0, concat_axis=0, tiled=True)  61.6 us
    all_to_all x1, blocking collectives, on_device(): lax.all_to_all(outgoing, 'grp', split_axis=0, concat_axis=0, tiled=True)  54.4 us
    all_to_all x1, waiting for transfers between devices, on_device(): lax.all_to_all(pair_sum, 'grp', split_axis=0, concat_axis=0, tiled=True)  43.2 us
    pallas_call x1, Pallas kernels, attend(): pl.pallas_call(kernel, grid_spec=grid_spec, out_shape=jax.ShapeDtypeStruc...  40.8 us
    all_to_all x1, waiting for transfers between devices, on_device(): lax.all_to_all(cache[part], 'grp', split_axis=0, concat_axis=0, tiled=True)  25 us
    pallas_call x1, Pallas kernels, head_reduce(): pl.pallas_call(kernel, out_shape=jax.ShapeDtypeStruct(x.shape, jnp.float3...  16.4 us
    pallas_call x1, Pallas kernels, peer_swap(): pl.pallas_call(kernel, out_shape=jax.ShapeDtypeStruct(x.shape, x.dtype),...  7.69 us
    reduce_sum x1, other arithmetic, on_device(): dispatch = jnp.sum(place.astype(jnp.float32), axis=1).astype(jnp.bfloat16)  6.97 us
  transfers between devices with their start and end apart: 5, of which 4 were waited for; matrix products, arithmetic and copies ran while one was open for 12% of the time, Pallas kernels for 0%

profile of v11, /device:TPU:10, one launch (start us, length us, event | category | flops | bytes accessed | tf_op | source)
XLA Modules:
  0.0 333.7 jit_solution(1657159337188111841)
XLA Ops:
  0.0 5.3 %slice_bitcast_fusion = (bf16[32,128,512]{2,1,0:T(8,128)(2,1)}, bf16[32,128,512]{2,1,0:T(8,128)(2,1)S(1)}) fusion(bf16[2,32,128,512]{3,2,1,0:T(8,128)(2,1)} %param.20), kind=kLoop, calls=%fused_computation.4 | loop fusion | bytes 16777216 | tf_op jit(solution)/shard_map/squeeze | solution.py:214
  5.3 61.6 %all_to_all.20 = bf16[32,128,512]{2,1,0:T(8,128)(2,1)} all-to-all(bf16[32,128,512]{2,1,0:T(8,128)(2,1)S(1)} %get-tuple-element.8), channel_id=1, replica_groups=mesh['grp'=32,'head'=4] {'grp'}, dimensions={0} | all-to-all | bytes 8388608 | tf_op jit(solution)/shard_map/all_to_all | solution.py:214
  66.8 5.6 %all-to-all-start.1 = ((bf16[32,128,512]{2,1,0:T(8,128)(2,1)}), bf16[32,128,512]{2,1,0:T(8,128)(2,1)}, u32[]{:S(2)}, u32[]{:S(2)}) async-start(bf16[32,128,512]{2,1,0:T(8,128)(2,1)} %get-tuple-element.7), calls=%async_computation.1 | async-start | bytes 8388608 | tf_op jit(solution)/shard_map/all_to_all | solution.py:214
  72.5 3.9 %copy.88 = bf16[512,2048]{1,0:T(8,128)(2,1)} copy(bf16[512,2048]{0,1:T(8,128)(2,1)} %bitcast.133) | data formatting | bytes 4194304 | tf_op jit(solution)/shard_map/dot_general | solution.py:204
  76.4 4.0 %copy.86 = bf16[512,2048]{1,0:T(8,128)(2,1)} copy(bf16[512,2048]{0,1:T(8,128)(2,1)} %bitcast.134) | data formatting | bytes 4194304 | tf_op jit(solution)/shard_map/dot_general | solution.py:201
  82.1 2.4 fusion.19
  87.0 3.9 %copy.90 = bf16[512,2048]{1,0:T(8,128)(2,1)} copy(bf16[512,2048]{0,1:T(8,128)(2,1)} %bitcast.135) | data formatting | bytes 4194304 | tf_op jit(solution)/shard_map/dot_general | solution.py:207
  90.9 2.4 convolution_convert_fusion.6
  95.1 7.0 %convert_reduce_fusion = (bf16[128,1536]{1,0:T(8,128)(2,1)S(1)}, f32[128,1536]{1,0:T(8,128)}) fusion(s32[128,8]{1,0:T(8,128)S(1)} %bitcast_add_fusion.1, f32[128,8]{1,0:T(8,128)S(1)} %copy.77), kind=kLoop, calls=%fused_computation | loop fusion | flops 7471104 | bytes 1187840 | tf_op jit(solution)/shard_map/reduce_sum | solution.py:243
  103.2 25.0 %all-to-all-done.1 = bf16[32,128,512]{2,1,0:T(8,128)(2,1)} async-done(((bf16[32,128,512]{2,1,0:T(8,128)(2,1)}), bf16[32,128,512]{2,1,0:T(8,128)(2,1)}, u32[]{:S(2)}, u32[]{:S(2)}) %all-to-all-start.1) | async-done | bytes 4194336 | tf_op jit(solution)/shard_map/all_to_all | solution.py:214
  128.3 40.8 %shard_map.136 = bf16[128,512]{1,0:T(8,128)(2,1)} custom-call(s32[1]{0:T(128)} %dynamic_slice.55.length_ref, bf16[128,512]{1,0:T(8,128)(2,1)} %copy.87.q_ref, bf16[128,512]{1,0:T(8,128)(2,1)} %copy.89.kn_ref, bf16[128,512]{1,0:T(8,128)(2,1)} %copy.91.vn_ref, bf16[4096,512]{1,0:T(8,128)(2,1)} %bitcast.108, bf16[4096,512]{1,0:T(8,128)(2,1)} %bitcast.16.v_ref), custom_call_target="tpu_custom_call" | custom-call | tf_op jit(solution)/shard_map/pallas_call | solution.py:118
  169.1 2.1 convolution_convert_fusion.1.x_ref
  171.2 16.4 %shard_map.137 = f32[128,2048]{1,0:T(8,128)} custom-call(bf16[128,2048]{1,0:T(8,128)(2,1)} %convolution_convert_fusion.1.x_ref, f32[128,2048]{1,0:T(8,128)} %convert_bitcast_fusion.base_ref), custom_call_target="tpu_custom_call" | custom-call | tf_op jit(solution)/shard_map/pallas_call | solution.py:161
  192.8 54.4 %all_to_all.21 = bf16[32,2,24,1024]{3,2,1,0:T(8,128)(2,1)} all-to-all(bf16[32,2,24,1024]{3,2,1,0:T(8,128)(2,1)S(1)} %bitcast.113), channel_id=1, replica_groups=mesh['grp'=32,'head'=4] {'grp'}, dimensions={0} | all-to-all | bytes 6291456 | tf_op jit(solution)/shard_map/all_to_all | solution.py:264
  248.4 1.8 fusion.26
  251.3 2.2 fusion.24
  255.8 2.2 fusion.23
  264.1 1.7 collective-permute-done.2
  266.4 2.0 pad_maximum_fusion
  268.4 5.9 %all-to-all-start.3 = ((bf16[32,2,24,1024]{3,2,1,0:T(8,128)(2,1)}), bf16[32,2,24,1024]{3,2,1,0:T(8,128)(2,1)}, u32[]{:S(2)}, u32[]{:S(2)}) async-start(bf16[32,2,24,1024]{3,2,1,0:T(8,128)(2,1)} %pad_maximum_fusion), calls=%async_computation.3 | async-start | bytes 6291456 | tf_op jit(solution)/shard_map/all_to_all | solution.py:285
  274.5 43.2 %all-to-all-done.3 = bf16[32,2,24,1024]{3,2,1,0:T(8,128)(2,1)} async-done(((bf16[32,2,24,1024]{3,2,1,0:T(8,128)(2,1)}), bf16[32,2,24,1024]{3,2,1,0:T(8,128)(2,1)}, u32[]{:S(2)}, u32[]{:S(2)}) %all-to-all-start.3) | async-done | bytes 3145760 | tf_op jit(solution)/shard_map/all_to_all | solution.py:285
  317.7 4.3 %convolution_reduce_fusion = f32[128,1024]{1,0:T(8,128)} fusion(bf16[3,128,1536]{2,1,0:T(8,128)(2,1)S(1)} %bitcast.143, bf16[1536,1024,1]{1,0,2:T(8,128)(2,1)} %bitcast.49), kind=kOutput, calls=%fused_computation.16 | convolution fusion | flops 1208221696 | bytes 4849664 | tf_op jit(solution)/shard_map/dot_general | solution.py:293
  324.1 7.7 %shard_map.138 = f32[128,512]{1,0:T(8,128)} custom-call(f32[128,512]{1,0:T(8,128)} %bitcast.144), custom_call_target="tpu_custom_call" | custom-call | tf_op jit(solution)/shard_map/pallas_call | solution.py:47
  331.9 1.7 fusion.16
  (82 shorter events, 25.8 us)
Async XLA Ops:
  0.0 169.1 %copy-start = (bf16[512,2048]{1,0:T(8,128)(2,1)S(1)}, bf16[512,2048]{1,0:T(8,128)(2,1)}, u32[]{:S(2)}) copy-start(bf16[512,2048]{1,0:T(8,128)(2,1)} %param.19) | copy-start | bytes 6291460
  66.8 61.4 %all-to-all-start.1 = ((bf16[32,128,512]{2,1,0:T(8,128)(2,1)}), bf16[32,128,512]{2,1,0:T(8,128)(2,1)}, u32[]{:S(2)}, u32[]{:S(2)}) async-start(bf16[32,128,512]{2,1,0:T(8,128)(2,1)} %get-tuple-element.7), calls=%async_computation.1 | async-start | bytes 8388608 | tf_op jit(solution)/shard_map/all_to_all | solution.py:214
  76.4 4.0 %copy-start.11 = (s32[32]{0:T(128)S(1)}, s32[32]{0:T(128)}, u32[]{:S(2)}) copy-start(s32[32]{0:T(128)} %param.21) | copy-start | bytes 388
  76.4 5.3 %copy-start.2 = (bf16[1,128,2048]{2,1,0:T(8,128)(2,1)S(1)}, bf16[1,128,2048]{2,1,0:T(8,128)(2,1)}, u32[]{:S(2)}) copy-start(bf16[1,128,2048]{2,1,0:T(8,128)(2,1)} %param.14) | copy-start | bytes 1572868
  76.4 5.7 %copy-start.7 = (f32[2048]{0:T(1024)S(1)}, f32[2048]{0:T(1024)}, u32[]{:S(2)}) copy-start(f32[2048]{0:T(1024)} %param.15) | copy-start | bytes 24580
  80.4 4.1 %copy-start.3 = (bf16[512,2048]{1,0:T(8,128)(2,1)S(1)}, bf16[512,2048]{1,0:T(8,128)(2,1)}, u32[]{:S(2)}) copy-start(bf16[512,2048]{1,0:T(8,128)(2,1)} %copy.86) | copy-start | bytes 6291460
  90.9 3.2 copy-start.9
  90.9 4.1 %copy-start.10 = (f32[1,128,8]{1,2,0:T(8,128)S(1)}, f32[1,128,8]{1,2,0:T(8,128)}, u32[]{:S(2)}) copy-start(f32[1,128,8]{1,2,0:T(8,128)} %param.24) | copy-start | bytes 12292
  171.2 17.8 %copy-start.8 = (f32[2048]{0:T(1024)S(1)}, f32[2048]{0:T(1024)}, u32[]{:S(2)}) copy-start(f32[2048]{0:T(1024)} %param.22) | copy-start | bytes 24580
  192.8 54.4 %copy-start.5 = (bf16[2,256,2048]{2,1,0:T(8,128)(2,1)S(1)}, bf16[2,256,2048]{2,1,0:T(8,128)(2,1)}, u32[]{:S(2)}) copy-start(bf16[2,256,2048]{2,1,0:T(8,128)(2,1)} %param.27) | copy-start | bytes 6291460
  247.2 8.6 %collective-permute-start = (bf16[32,2,24,1024]{3,2,1,0:T(8,128)(2,1)}, bf16[32,2,24,1024]{3,2,1,0:T(8,128)(2,1)}, u32[]{:S(2)}, u32[]{:S(2)}) collective-permute-start(bf16[32,2,24,1024]{3,2,1,0:T(8,128)(2,1)} %all_to_all.21), channel_id=1, source_target_pairs={{0,1},{1,0},{2,3},{3,2},{4,5},{5,4},{6,7},{7,6},{8,9},{9,8},{10,11... | collective-permute-start | bytes 9437192 | tf_op jit(solution)/shard_map/ppermute | solution.py:266
  248.4 2.2 copy-start.6
  259.9 3.6 %collective-permute-start.1 = (bf16[768,1024]{1,0:T(8,128)(2,1)S(1)}, bf16[768,1024]{1,0:T(8,128)(2,1)S(1)}, u32[]{:S(2)}, u32[]{:S(2)}) collective-permute-start(bf16[768,1024]{1,0:T(8,128)(2,1)S(1)} %convolution_convert_fusion.4), channel_id=1, source_target_pairs={{0,1},{1,0},{2,3},{3,2},{4,5},{5,4},{6,7},{7,6},{8,9},{9,8},{10,11... | collective-permute-start | bytes 4718600 | tf_op jit(solution)/shard_map/ppermute | solution.py:278
  262.3 3.5 %collective-permute-start.2 = (bf16[768,1024]{1,0:T(8,128)(2,1)S(1)}, bf16[768,1024]{1,0:T(8,128)(2,1)S(1)}, u32[]{:S(2)}, u32[]{:S(2)}) collective-permute-start(bf16[768,1024]{1,0:T(8,128)(2,1)S(1)} %convolution_convert_fusion.2), channel_id=1, source_target_pairs={{0,1},{1,0},{2,3},{3,2},{4,5},{5,4},{6,7},{7,6},{8,9},{9,8},{10,11... | collective-permute-start | bytes 4718600 | tf_op jit(solution)/shard_map/ppermute | solution.py:278
  268.4 5.9 %copy-start.4 = (f32[128,1536]{1,0:T(8,128)S(1)}, f32[128,1536]{1,0:T(8,128)}, u32[]{:S(2)}) copy-start(f32[128,1536]{1,0:T(8,128)} %get-tuple-element.6) | copy-start | bytes 2359300
  268.4 49.3 %all-to-all-start.3 = ((bf16[32,2,24,1024]{3,2,1,0:T(8,128)(2,1)}), bf16[32,2,24,1024]{3,2,1,0:T(8,128)(2,1)}, u32[]{:S(2)}, u32[]{:S(2)}) async-start(bf16[32,2,24,1024]{3,2,1,0:T(8,128)(2,1)} %pad_maximum_fusion), calls=%async_computation.3 | async-start | bytes 6291456 | tf_op jit(solution)/shard_map/all_to_all | solution.py:285
  317.7 16.0 %copy-start.1 = (bf16[512,2048]{1,0:T(8,128)(2,1)S(1)}, bf16[512,2048]{1,0:T(8,128)(2,1)}, u32[]{:S(2)}) copy-start(bf16[512,2048]{1,0:T(8,128)(2,1)} %param.19) | copy-start | bytes 6291460

commit v12 on v8

--- a/solution.py
+++ b/solution.py
@@ -103,54 +103,91 @@
     )(length.reshape(1), query, key_new, value_new, keys, values)
 
 
-def head_reduce(x, base, ident):
+def head_reduce(x, base, gain, ident):
+    rows, width = x.shape
+    share = width // 4
     mesh_kind = pl.DeviceIdType.MESH
 
-    def kernel(x_ref, base_ref, o_ref, slots, send_sem, recv_sem):
+    def kernel(x_ref, base_ref, gain_ref, resid_ref, normed_ref, part_in, send_buf, sum_in, sq_out, sq_in,
+               send_sem, recv_sem):
         me = lax.axis_index("head")
         group = lax.axis_index("grp")
-        partner = me + 1 - 2 * lax.rem(me, 2)
+        core = lax.rem(me, 2)
+        partner = me + 1 - 2 * core
         across = lax.rem(me + 2, 4)
         barrier = pltpu.get_barrier_semaphore()
         for peer in (partner, across):
             pl.semaphore_signal(barrier, inc=1, device_id=(group, peer), device_id_type=mesh_kind)
         pl.semaphore_wait(barrier, 2)
-        near = pltpu.make_async_remote_copy(
-            src_ref=x_ref, dst_ref=slots.at[0], send_sem=send_sem.at[0], recv_sem=recv_sem.at[0],
+
+        def columns(block):
+            return pl.ds(pl.multiple_of(block * share, share), share)
+
+        halves_out = []
+        for half in range(2):
+            copy = pltpu.make_async_remote_copy(
+                src_ref=x_ref.at[:, columns(2 * half + 1 - core)], dst_ref=part_in.at[half],
+                send_sem=send_sem.at[half], recv_sem=recv_sem.at[half],
+                device_id=(group, partner), device_id_type=mesh_kind,
+            )
+            copy.start()
+            halves_out.append(copy)
+        for half in range(2):
+            halves_out[half].wait_recv()
+            mine = x_ref[:, columns(2 * half + core)].astype(jnp.float32)
+            send_buf[half] = (mine + part_in[half].astype(jnp.float32)).astype(send_buf.dtype)
+        swap = pltpu.make_async_remote_copy(
+            src_ref=send_buf, dst_ref=sum_in, send_sem=send_sem.at[2], recv_sem=recv_sem.at[2],
+            device_id=(group, across), device_id_type=mesh_kind,
+        )
+        swap.start()
+        swap.wait_recv()
+        square = jnp.zeros((rows, 1), jnp.float32)
+        for half in range(2):
+            total = (
+                base_ref[:, columns(2 * half + core)]
+                + send_buf[half].astype(jnp.float32)
+                + sum_in[half].astype(jnp.float32)
+            )
+            resid_ref[half] = total
+            square = square + jnp.sum(total * total, axis=1, keepdims=True)
+        sq_out[...] = jnp.broadcast_to(square, sq_out.shape)
+        last = pltpu.make_async_remote_copy(
+            src_ref=sq_out, dst_ref=sq_in, send_sem=send_sem.at[3], recv_sem=recv_sem.at[3],
             device_id=(group, partner), device_id_type=mesh_kind,
         )
-        far = pltpu.make_async_remote_copy(
-            src_ref=x_ref, dst_ref=slots.at[1], send_sem=send_sem.at[1], recv_sem=recv_sem.at[1],
-            device_id=(group, across), device_id_type=mesh_kind,
-        )
-        near.start()
-        far.start()
-        far.wait_recv()
-        relay = pltpu.make_async_remote_copy(
-            src_ref=slots.at[1], dst_ref=slots.at[2], send_sem=send_sem.at[2],
-            recv_sem=recv_sem.at[2], device_id=(group, partner), device_id_type=mesh_kind,
-        )
-        relay.start()
-        near.wait()
-        far.wait_send()
-        relay.wait()
-        total = base_ref[...] + x_ref[...].astype(jnp.float32)
-        for slot in range(3):
-            total = total + slots[slot].astype(jnp.float32)
-        o_ref[...] = total
-
+        last.start()
+        last.wait_recv()
+        scale = lax.rsqrt((square + sq_in[:, 0:1]) / width + 1e-05)
+        for half in range(2):
+            normed_ref[:, half * share:(half + 1) * share] = (
+                resid_ref[half] * scale * gain_ref[:, columns(2 * half + core)]
+            ).astype(normed_ref.dtype)
+        for copy in halves_out:
+            copy.wait_send()
+        swap.wait_send()
+        last.wait_send()
+
+    vmem = pl.BlockSpec(memory_space=pltpu.VMEM)
     return pl.pallas_call(
         kernel,
-        out_shape=jax.ShapeDtypeStruct(x.shape, jnp.float32),
-        in_specs=[pl.BlockSpec(memory_space=pltpu.VMEM), pl.BlockSpec(memory_space=pltpu.VMEM)],
-        out_specs=pl.BlockSpec(memory_space=pltpu.VMEM),
+        out_shape=(
+            jax.ShapeDtypeStruct((2, rows, share), jnp.float32),
+            jax.ShapeDtypeStruct((rows, 2 * share), jnp.bfloat16),
+        ),
+        in_specs=[vmem, vmem, vmem],
+        out_specs=(vmem, vmem),
         scratch_shapes=[
-            pltpu.VMEM((3,) + x.shape, x.dtype),
-            pltpu.SemaphoreType.DMA((3,)),
-            pltpu.SemaphoreType.DMA((3,)),
+            pltpu.VMEM((2, rows, share), x.dtype),
+            pltpu.VMEM((2, rows, share), x.dtype),
+            pltpu.VMEM((2, rows, share), x.dtype),
+            pltpu.VMEM((rows, 128), jnp.float32),
+            pltpu.VMEM((rows, 128), jnp.float32),
+            pltpu.SemaphoreType.DMA((4,)),
+            pltpu.SemaphoreType.DMA((4,)),
         ],
         compiler_params=pltpu.CompilerParams(collective_id=ident, has_side_effects=True),
-    )(x, base)
+    )(x, base, gain.reshape(1, -1))
 
 
 def on_device(
@@ -206,8 +243,7 @@
         values,
     )
     projected = jnp.dot(attended, w_out, preferred_element_type=jnp.float32)
-    resid = head_reduce(projected.astype(jnp.bfloat16), rows, 0)
-    mixed_in = rms_norm(resid, mlp_gain).astype(jnp.bfloat16)
+    resid_blocks, mixed_half = head_reduce(projected.astype(jnp.bfloat16), rows, mlp_gain, 0)
     experts_here = w_gate.shape[0]
     expert_total = experts_here * group_count
     capacity = max(2, 3 * tokens * TOPK // (2 * expert_total))
@@ -239,7 +275,7 @@
 
     half = 2 * share_width
     outgoing = lax.dot_general(
-        dispatch, halves(mixed_in, core), (((0,), (0,)), ((), ())), preferred_element_type=jnp.float32
+        dispatch, mixed_half, (((0,), (0,)), ((), ())), preferred_element_type=jnp.float32
     ).astype(jnp.bfloat16)
     outgoing = outgoing.reshape(group_count, experts_here, capacity, half)
     arrived = lax.all_to_all(outgoing, "grp", split_axis=0, concat_axis=0, tiled=True)
@@ -277,7 +313,7 @@
     keep = lax.dynamic_index_in_dim(combined, chip, axis=1, keepdims=False)
     give = lax.dynamic_index_in_dim(combined, 1 - chip, axis=1, keepdims=False)
     moe_share = keep + peer_swap(give, True, 3)
-    resid_share = lax.dynamic_slice_in_dim(resid, head_at * share_width, share_width, 1)
+    resid_share = lax.dynamic_index_in_dim(resid_blocks, chip, axis=0, keepdims=False)
     return (resid_share + moe_share).astype(jnp.bfloat16)[None]
 
 

time: 302 us -> 294 us (0.974)
  Pallas kernels: 32.7 us -> 28.7 us
    pallas_call x1, Pallas kernels: 16.4 us -> 12.4 us  [head_reduce(): pl.pallas_call(kernel, out_shape=(jax.ShapeDtypeStruct((2, rows, share),...]
where the time goes in v12:
time: 294 us
  blocking collectives  115 us (39%)
  waiting for transfers between devices  71.1 us (24%)
  local copies, waits for them, and re-layouts  31.1 us (11%)
  Pallas kernels  28.7 us (10%)
  matrix products  21.7 us (7%)
  other arithmetic  13.2 us (4%)
  starting transfers between devices  12.3 us (4%)
    all_to_all x1, blocking collectives, on_device(): lax.all_to_all(cache[part], 'grp', split_axis=0, concat_axis=0, tiled=True)  61.6 us
    all_to_all x1, blocking collectives, on_device(): lax.all_to_all(outgoing, 'grp', split_axis=0, concat_axis=0, tiled=True)  53.6 us
    all_to_all x1, waiting for transfers between devices, on_device(): lax.all_to_all(pair_sum, 'grp', split_axis=0, concat_axis=0, tiled=True)  43.3 us
    all_to_all x1, waiting for transfers between devices, on_device(): lax.all_to_all(cache[part], 'grp', split_axis=0, concat_axis=0, tiled=True)  25.1 us
    pallas_call x1, Pallas kernels, head_reduce(): pl.pallas_call(kernel, out_shape=(jax.ShapeDtypeStruct((2, rows, share),...  12.4 us
    pallas_call x1, Pallas kernels, attend(): pl.pallas_call(kernel, grid_spec=grid_spec, out_shape=jax.ShapeDtypeStruc...  8.57 us
    pallas_call x1, Pallas kernels, peer_swap(): pl.pallas_call(kernel, out_shape=jax.ShapeDtypeStruct(x.shape, x.dtype),...  7.7 us
    reduce_sum x1, other arithmetic, on_device(): dispatch = jnp.sum(place.astype(jnp.float32), axis=1).astype(jnp.bfloat16)  6.98 us
  transfers between devices with their start and end apart: 5, of which 4 were waited for; matrix products, arithmetic and copies ran while one was open for 14% of the time, Pallas kernels for 0%

profile of v12, /device:TPU:10, one launch (start us, length us, event | category | flops | bytes accessed | tf_op | source)
XLA Modules:
  0.0 293.6 jit_solution(6694493607576438310)
XLA Ops:
  0.0 5.3 %slice_bitcast_fusion = (bf16[32,128,512]{2,1,0:T(8,128)(2,1)}, bf16[32,128,512]{2,1,0:T(8,128)(2,1)S(1)}) fusion(bf16[2,32,128,512]{3,2,1,0:T(8,128)(2,1)} %param.20), kind=kLoop, calls=%fused_computation.4 | loop fusion | bytes 16777216 | tf_op jit(solution)/shard_map/squeeze | solution.py:232
  5.3 61.6 %all_to_all.20 = bf16[32,128,512]{2,1,0:T(8,128)(2,1)} all-to-all(bf16[32,128,512]{2,1,0:T(8,128)(2,1)S(1)} %get-tuple-element.12), channel_id=1, replica_groups=mesh['grp'=32,'head'=4] {'grp'}, dimensions={0} | all-to-all | bytes 8388608 | tf_op jit(solution)/shard_map/all_to_all | solution.py:232
  66.8 5.7 %all-to-all-start.1 = ((bf16[32,128,512]{2,1,0:T(8,128)(2,1)}), bf16[32,128,512]{2,1,0:T(8,128)(2,1)}, u32[]{:S(2)}, u32[]{:S(2)}) async-start(bf16[32,128,512]{2,1,0:T(8,128)(2,1)} %get-tuple-element.11), calls=%async_computation.1 | async-start | bytes 8388608 | tf_op jit(solution)/shard_map/all_to_all | solution.py:232
  73.6 4.0 %copy.84 = bf16[512,2048]{1,0:T(8,128)(2,1)} copy(bf16[512,2048]{0,1:T(8,128)(2,1)} %bitcast.137) | data formatting | bytes 4194304 | tf_op jit(solution)/shard_map/dot_general | solution.py:222
  77.6 4.0 %copy.82 = bf16[512,2048]{1,0:T(8,128)(2,1)} copy(bf16[512,2048]{0,1:T(8,128)(2,1)} %bitcast.138) | data formatting | bytes 4194304 | tf_op jit(solution)/shard_map/dot_general | solution.py:219
  83.2 2.4 fusion.19
  88.1 4.0 %copy.86 = bf16[512,2048]{1,0:T(8,128)(2,1)} copy(bf16[512,2048]{0,1:T(8,128)(2,1)} %bitcast.139) | data formatting | bytes 4194304 | tf_op jit(solution)/shard_map/dot_general | solution.py:225
  92.1 2.4 convolution_convert_fusion.6
  95.2 7.0 %convert_reduce_fusion = (bf16[128,1536]{1,0:T(8,128)(2,1)S(1)}, f32[128,1536]{1,0:T(8,128)}) fusion(s32[128,8]{1,0:T(8,128)S(1)} %bitcast_add_fusion.1, f32[128,8]{1,0:T(8,128)S(1)} %copy.74), kind=kLoop, calls=%fused_computation | loop fusion | flops 7471104 | bytes 1187840 | tf_op jit(solution)/shard_map/reduce_sum | solution.py:260
  103.3 25.1 %all-to-all-done.1 = bf16[32,128,512]{2,1,0:T(8,128)(2,1)} async-done(((bf16[32,128,512]{2,1,0:T(8,128)(2,1)}), bf16[32,128,512]{2,1,0:T(8,128)(2,1)}, u32[]{:S(2)}, u32[]{:S(2)}) %all-to-all-start.1) | async-done | bytes 4194336 | tf_op jit(solution)/shard_map/all_to_all | solution.py:232
  128.4 8.6 %shard_map.136 = bf16[128,512]{1,0:T(8,128)(2,1)} custom-call(s32[1]{0:T(128)} %dynamic_slice.52.length_ref, bf16[128,512]{1,0:T(8,128)(2,1)} %copy.83.q_ref, bf16[128,512]{1,0:T(8,128)(2,1)} %copy.85.kn_ref, bf16[128,512]{1,0:T(8,128)(2,1)} %copy.87.vn_ref, bf16[4096,512]{1,0:T(8,128)(2,1)} %bitcast.112, bf16[4096,512]{1,0:T(8,128)(2,1)} %bitcast.16.v_ref), custom_call_target="tpu_custom_call" | custom-call | tf_op jit(solution)/shard_map/pallas_call | solution.py:99
  137.0 2.1 convolution_convert_fusion.1.x_ref
  139.1 12.4 %shard_map.137 = (f32[2,128,512]{2,1,0:T(8,128)}, bf16[128,1024]{1,0:T(8,128)(2,1)}) custom-call(bf16[128,2048]{1,0:T(8,128)(2,1)} %convolution_convert_fusion.1.x_ref, f32[128,2048]{1,0:T(8,128)} %convert_bitcast_fusion.base_ref, f32[1,2048]{1,0:T(1,128)} %bitcast.154), custom_call_target="tpu_custom_call" | custom-call | tf_op jit(solution)/shard_map/pallas_call | solution.py:172
  151.6 2.0 convolution_convert_fusion
  153.5 53.6 %all_to_all.21 = bf16[32,2,24,1024]{3,2,1,0:T(8,128)(2,1)} all-to-all(bf16[32,2,24,1024]{3,2,1,0:T(8,128)(2,1)S(1)} %bitcast.117), channel_id=1, replica_groups=mesh['grp'=32,'head'=4] {'grp'}, dimensions={0} | all-to-all | bytes 6291456 | tf_op jit(solution)/shard_map/all_to_all | solution.py:281
  208.3 1.8 fusion.27
  211.2 2.2 fusion.24
  215.7 2.2 fusion.23
  226.3 2.0 pad_maximum_fusion
  228.3 5.9 %all-to-all-start.3 = ((bf16[32,2,24,1024]{3,2,1,0:T(8,128)(2,1)}), bf16[32,2,24,1024]{3,2,1,0:T(8,128)(2,1)}, u32[]{:S(2)}, u32[]{:S(2)}) async-start(bf16[32,2,24,1024]{3,2,1,0:T(8,128)(2,1)} %pad_maximum_fusion), calls=%async_computation.3 | async-start | bytes 6291456 | tf_op jit(solution)/shard_map/all_to_all | solution.py:302
  234.4 43.3 %all-to-all-done.3 = bf16[32,2,24,1024]{3,2,1,0:T(8,128)(2,1)} async-done(((bf16[32,2,24,1024]{3,2,1,0:T(8,128)(2,1)}), bf16[32,2,24,1024]{3,2,1,0:T(8,128)(2,1)}, u32[]{:S(2)}, u32[]{:S(2)}) %all-to-all-start.3) | async-done | bytes 3145760 | tf_op jit(solution)/shard_map/all_to_all | solution.py:302
  277.7 4.2 %convolution_reduce_fusion = f32[128,1024]{1,0:T(8,128)} fusion(bf16[3,128,1536]{2,1,0:T(8,128)(2,1)S(1)} %bitcast.147, bf16[1536,1024,1]{1,0,2:T(8,128)(2,1)} %bitcast.50), kind=kOutput, calls=%fused_computation.16 | convolution fusion | flops 1208221696 | bytes 4849664 | tf_op jit(solution)/shard_map/dot_general | solution.py:310
  284.0 7.7 %shard_map.138 = f32[128,512]{1,0:T(8,128)} custom-call(f32[128,512]{1,0:T(8,128)} %bitcast.148), custom_call_target="tpu_custom_call" | custom-call | tf_op jit(solution)/shard_map/pallas_call | solution.py:47
  291.9 1.7 fusion.16
  (74 shorter events, 22.2 us)
Async XLA Ops:
  0.0 137.0 %copy-start = (bf16[512,2048]{1,0:T(8,128)(2,1)S(1)}, bf16[512,2048]{1,0:T(8,128)(2,1)}, u32[]{:S(2)}) copy-start(bf16[512,2048]{1,0:T(8,128)(2,1)} %param.19) | copy-start | bytes 6291460
  66.8 5.8 %copy-start.8 = (s32[1,128,8]{1,2,0:T(8,128)S(1)}, s32[1,128,8]{1,2,0:T(8,128)}, u32[]{:S(2)}) copy-start(s32[1,128,8]{1,2,0:T(8,128)} %param.23) | copy-start | bytes 12292
  66.8 6.7 %copy-start.9 = (f32[1,128,8]{1,2,0:T(8,128)S(1)}, f32[1,128,8]{1,2,0:T(8,128)}, u32[]{:S(2)}) copy-start(f32[1,128,8]{1,2,0:T(8,128)} %param.24) | copy-start | bytes 12292
  66.8 61.6 %all-to-all-start.1 = ((bf16[32,128,512]{2,1,0:T(8,128)(2,1)}), bf16[32,128,512]{2,1,0:T(8,128)(2,1)}, u32[]{:S(2)}, u32[]{:S(2)}) async-start(bf16[32,128,512]{2,1,0:T(8,128)(2,1)} %get-tuple-element.11), calls=%async_computation.1 | async-start | bytes 8388608 | tf_op jit(solution)/shard_map/all_to_all | solution.py:232
  77.6 4.0 %copy-start.10 = (s32[32]{0:T(128)S(1)}, s32[32]{0:T(128)}, u32[]{:S(2)}) copy-start(s32[32]{0:T(128)} %param.21) | copy-start | bytes 388
  77.6 5.2 %copy-start.2 = (bf16[1,128,2048]{2,1,0:T(8,128)(2,1)S(1)}, bf16[1,128,2048]{2,1,0:T(8,128)(2,1)}, u32[]{:S(2)}) copy-start(bf16[1,128,2048]{2,1,0:T(8,128)(2,1)} %param.14) | copy-start | bytes 1572868
  77.6 5.6 %copy-start.7 = (f32[2048]{0:T(1024)S(1)}, f32[2048]{0:T(1024)}, u32[]{:S(2)}) copy-start(f32[2048]{0:T(1024)} %param.15) | copy-start | bytes 24580
  81.6 4.0 %copy-start.3 = (bf16[512,2048]{1,0:T(8,128)(2,1)S(1)}, bf16[512,2048]{1,0:T(8,128)(2,1)}, u32[]{:S(2)}) copy-start(bf16[512,2048]{1,0:T(8,128)(2,1)} %copy.82) | copy-start | bytes 6291460
  153.5 53.6 %copy-start.5 = (bf16[2,256,2048]{2,1,0:T(8,128)(2,1)S(1)}, bf16[2,256,2048]{2,1,0:T(8,128)(2,1)}, u32[]{:S(2)}) copy-start(bf16[2,256,2048]{2,1,0:T(8,128)(2,1)} %param.27) | copy-start | bytes 6291460
  207.1 8.6 %collective-permute-start = (bf16[32,2,24,1024]{3,2,1,0:T(8,128)(2,1)}, bf16[32,2,24,1024]{3,2,1,0:T(8,128)(2,1)}, u32[]{:S(2)}, u32[]{:S(2)}) collective-permute-start(bf16[32,2,24,1024]{3,2,1,0:T(8,128)(2,1)} %all_to_all.21), channel_id=1, source_target_pairs={{0,1},{1,0},{2,3},{3,2},{4,5},{5,4},{6,7},{7,6},{8,9},{9,8},{10,11... | collective-permute-start | bytes 9437192 | tf_op jit(solution)/shard_map/ppermute | solution.py:283
  208.3 2.2 copy-start.6
  219.8 3.6 %collective-permute-start.2 = (bf16[768,1024]{1,0:T(8,128)(2,1)S(1)}, bf16[768,1024]{1,0:T(8,128)(2,1)S(1)}, u32[]{:S(2)}, u32[]{:S(2)}) collective-permute-start(bf16[768,1024]{1,0:T(8,128)(2,1)S(1)} %convolution_convert_fusion.2), channel_id=1, source_target_pairs={{0,1},{1,0},{2,3},{3,2},{4,5},{5,4},{6,7},{7,6},{8,9},{9,8},{10,11... | collective-permute-start | bytes 4718600 | tf_op jit(solution)/shard_map/ppermute | solution.py:295
  222.2 3.5 %collective-permute-start.1 = (bf16[768,1024]{1,0:T(8,128)(2,1)S(1)}, bf16[768,1024]{1,0:T(8,128)(2,1)S(1)}, u32[]{:S(2)}, u32[]{:S(2)}) collective-permute-start(bf16[768,1024]{1,0:T(8,128)(2,1)S(1)} %convolution_convert_fusion.4), channel_id=1, source_target_pairs={{0,1},{1,0},{2,3},{3,2},{4,5},{5,4},{6,7},{7,6},{8,9},{9,8},{10,11... | collective-permute-start | bytes 4718600 | tf_op jit(solution)/shard_map/ppermute | solution.py:295
  228.3 5.9 %copy-start.4 = (f32[128,1536]{1,0:T(8,128)S(1)}, f32[128,1536]{1,0:T(8,128)}, u32[]{:S(2)}) copy-start(f32[128,1536]{1,0:T(8,128)} %get-tuple-element.10) | copy-start | bytes 2359300
  228.3 49.4 %all-to-all-start.3 = ((bf16[32,2,24,1024]{3,2,1,0:T(8,128)(2,1)}), bf16[32,2,24,1024]{3,2,1,0:T(8,128)(2,1)}, u32[]{:S(2)}, u32[]{:S(2)}) async-start(bf16[32,2,24,1024]{3,2,1,0:T(8,128)(2,1)} %pad_maximum_fusion), calls=%async_computation.3 | async-start | bytes 6291456 | tf_op jit(solution)/shard_map/all_to_all | solution.py:302
  277.7 16.0 %copy-start.1 = (bf16[512,2048]{1,0:T(8,128)(2,1)S(1)}, bf16[512,2048]{1,0:T(8,128)(2,1)}, u32[]{:S(2)}) copy-start(bf16[512,2048]{1,0:T(8,128)(2,1)} %param.19) | copy-start | bytes 6291460

commit v13 on v12

--- a/solution.py
+++ b/solution.py
@@ -54,12 +54,15 @@
     )(x)
 
 
-def attend(length, query, key_new, value_new, keys, values):
+def attend(length, query, key_new, value_new, keys, values, w_out):
     tokens = query.shape[0]
     context = keys.shape[0]
     heads = query.shape[1] // HD
 
-    def kernel(length_ref, q_ref, kn_ref, vn_ref, k_ref, v_ref, o_ref):
+    width = w_out.shape[1]
+
+    def kernel(length_ref, q_ref, kn_ref, vn_ref, k_ref, v_ref, w_ref, o_ref, acc_ref):
+        head = pl.program_id(0)
         limit = length_ref[0]
         q = q_ref[...]
         contract = (((1,), (1,)), ((), ()))
@@ -81,7 +84,20 @@
         numer = numer + jnp.dot(
             prob_new.astype(jnp.bfloat16), vn_ref[...], preferred_element_type=jnp.float32
         )
-        o_ref[...] = (numer / total).astype(o_ref.dtype)
+        attended = (numer / total).astype(jnp.bfloat16)
+        term = jnp.dot(attended, w_ref[...], preferred_element_type=jnp.float32)
+
+        @pl.when(head == 0)
+        def _():
+            acc_ref[...] = term
+
+        @pl.when(head > 0)
+        def _():
+            acc_ref[...] += term
+
+        @pl.when(head == heads - 1)
+        def _():
+            o_ref[...] = acc_ref[...].astype(o_ref.dtype)
 
     per_head = pl.BlockSpec((tokens, HD), lambda h, n: (0, h))
     grid_spec = pltpu.PrefetchScalarGridSpec(
@@ -93,14 +109,16 @@
             per_head,
             pl.BlockSpec((context, HD), lambda h, n: (0, h)),
             pl.BlockSpec((context, HD), lambda h, n: (0, h)),
+            pl.BlockSpec((HD, width), lambda h, n: (h, 0)),
         ],
-        out_specs=per_head,
+        out_specs=pl.BlockSpec((tokens, width), lambda h, n: (0, 0)),
+        scratch_shapes=[pltpu.VMEM((tokens, width), jnp.float32)],
     )
     return pl.pallas_call(
         kernel,
         grid_spec=grid_spec,
-        out_shape=jax.ShapeDtypeStruct((tokens, heads * HD), jnp.bfloat16),
-    )(length.reshape(1), query, key_new, value_new, keys, values)
+        out_shape=jax.ShapeDtypeStruct((tokens, width), jnp.bfloat16),
+    )(length.reshape(1), query, key_new, value_new, keys, values, w_out)
 
 
 def head_reduce(x, base, gain, ident):
@@ -234,16 +252,16 @@
         )
         for part in range(2)
     ]
-    attended = attend(
+    projected = attend(
         length,
         query.reshape(tokens, heads_here * HD),
         key_new.reshape(tokens, heads_here * HD),
         value_new.reshape(tokens, heads_here * HD),
         keys,
         values,
-    )
-    projected = jnp.dot(attended, w_out, preferred_element_type=jnp.float32)
-    resid_blocks, mixed_half = head_reduce(projected.astype(jnp.bfloat16), rows, mlp_gain, 0)
+        w_out,
+    )
+    resid_blocks, mixed_half = head_reduce(projected, rows, mlp_gain, 0)
     experts_here = w_gate.shape[0]
     expert_total = experts_here * group_count
     capacity = max(2, 3 * tokens * TOPK // (2 * expert_total))

time: 294 us -> 297 us (1.010)
  matrix products: 21.7 us -> 18.7 us
    unnamed x25 -> x27, local copies, waits for them, and re-layouts: 1.58 us -> 6.44 us
    all_to_all x1, waiting for transfers between devices: 25.1 us -> 28.9 us  [on_device(): lax.all_to_all(cache[part], 'grp', split_axis=0, concat_axis=0, tiled=True)]
where the time goes in v13:
time: 297 us
  blocking collectives  115 us (39%)
  waiting for transfers between devices  72.4 us (24%)
  local copies, waits for them, and re-layouts  31.5 us (11%)
  Pallas kernels  30.3 us (10%)
  matrix products  18.7 us (6%)
  other arithmetic  15.6 us (5%)
  starting transfers between devices  12.3 us (4%)
    all_to_all x1, blocking collectives, on_device(): lax.all_to_all(cache[part], 'grp', split_axis=0, concat_axis=0, tiled=True)  61.6 us
    all_to_all x1, blocking collectives, on_device(): lax.all_to_all(outgoing, 'grp', split_axis=0, concat_axis=0, tiled=True)  53.8 us
    all_to_all x1, waiting for transfers between devices, on_device(): lax.all_to_all(pair_sum, 'grp', split_axis=0, concat_axis=0, tiled=True)  40.7 us
    all_to_all x1, waiting for transfers between devices, on_device(): lax.all_to_all(cache[part], 'grp', split_axis=0, concat_axis=0, tiled=True)  28.9 us
    pallas_call x1, Pallas kernels, head_reduce(): pl.pallas_call(kernel, out_shape=(jax.ShapeDtypeStruct((2, rows, share),...  12.5 us
    pallas_call x1, Pallas kernels, attend(): pl.pallas_call(kernel, grid_spec=grid_spec, out_shape=jax.ShapeDtypeStruc...  10.2 us
    pallas_call x1, Pallas kernels, peer_swap(): pl.pallas_call(kernel, out_shape=jax.ShapeDtypeStruct(x.shape, x.dtype),...  7.7 us
    reduce_sum x1, other arithmetic, on_device(): dispatch = jnp.sum(place.astype(jnp.float32), axis=1).astype(jnp.bfloat16)  6.98 us
  transfers between devices with their start and end apart: 5, of which 4 were waited for; matrix products, arithmetic and copies ran while one was open for 14% of the time, Pallas kernels for 0%

profile of v13, /device:TPU:10, one launch (start us, length us, event | category | flops | bytes accessed | tf_op | source)
XLA Modules:
  0.0 296.6 jit_solution(15966765560399082606)
XLA Ops:
  0.0 5.1 %slice_bitcast_fusion = (bf16[32,128,512]{2,1,0:T(8,128)(2,1)}, bf16[32,128,512]{2,1,0:T(8,128)(2,1)S(1)}) fusion(bf16[2,32,128,512]{3,2,1,0:T(8,128)(2,1)} %param.20), kind=kLoop, calls=%fused_computation.4 | loop fusion | bytes 16777216 | tf_op jit(solution)/shard_map/squeeze | solution.py:250
  5.1 61.6 %all_to_all.20 = bf16[32,128,512]{2,1,0:T(8,128)(2,1)} all-to-all(bf16[32,128,512]{2,1,0:T(8,128)(2,1)S(1)} %get-tuple-element.12), channel_id=1, replica_groups=mesh['grp'=32,'head'=4] {'grp'}, dimensions={0} | all-to-all | bytes 8388608 | tf_op jit(solution)/shard_map/all_to_all | solution.py:250
  66.7 5.7 %all-to-all-start.1 = ((bf16[32,128,512]{2,1,0:T(8,128)(2,1)}), bf16[32,128,512]{2,1,0:T(8,128)(2,1)}, u32[]{:S(2)}, u32[]{:S(2)}) async-start(bf16[32,128,512]{2,1,0:T(8,128)(2,1)} %get-tuple-element.11), calls=%async_computation.1 | async-start | bytes 8388608 | tf_op jit(solution)/shard_map/all_to_all | solution.py:250
  73.5 2.5 copy.84
  76.0 3.0 %copy.82 = bf16[512,2048]{1,0:T(8,128)(2,1)S(1)} copy(bf16[512,2048]{0,1:T(8,128)(2,1)} %bitcast.137) | data formatting | bytes 4194304 | tf_op jit(solution)/shard_map/dot_general | solution.py:237
  80.8 2.4 fusion.19
  85.6 2.4 copy.86
  88.1 2.4 convolution_convert_fusion.5
  91.3 7.0 %convert_reduce_fusion = (bf16[128,1536]{1,0:T(8,128)(2,1)S(1)}, f32[128,1536]{1,0:T(8,128)}) fusion(s32[128,8]{1,0:T(8,128)S(1)} %bitcast_add_fusion.1, f32[128,8]{1,0:T(8,128)S(1)} %copy.74), kind=kLoop, calls=%fused_computation | loop fusion | flops 7471104 | bytes 1187840 | tf_op jit(solution)/shard_map/reduce_sum | solution.py:278
  99.4 28.9 %all-to-all-done.1 = bf16[32,128,512]{2,1,0:T(8,128)(2,1)} async-done(((bf16[32,128,512]{2,1,0:T(8,128)(2,1)}), bf16[32,128,512]{2,1,0:T(8,128)(2,1)}, u32[]{:S(2)}, u32[]{:S(2)}) %all-to-all-start.1) | async-done | bytes 4194336 | tf_op jit(solution)/shard_map/all_to_all | solution.py:250
  128.3 10.2 %shard_map.136.x_ref = bf16[128,2048]{1,0:T(8,128)(2,1)} custom-call(s32[1]{0:T(128)} %dynamic_slice.52.length_ref, bf16[128,512]{1,0:T(8,128)(2,1)} %copy.83.q_ref, bf16[128,512]{1,0:T(8,128)(2,1)} %copy.85.kn_ref, bf16[128,512]{1,0:T(8,128)(2,1)} %copy.87.vn_ref, bf16[4096,512]{1,0:T(8,128)(2,1)} %bitcast.110, bf16[4096,512]{1,0:T(8,128)(2,1)} %bitcast.16.v_ref, ...), custom_call_target="tpu_custom_call" | custom-call | tf_op jit(solution)/shard_map/pallas_call | solution.py:117
  138.4 12.5 %shard_map.137 = (f32[2,128,512]{2,1,0:T(8,128)}, bf16[128,1024]{1,0:T(8,128)(2,1)}) custom-call(bf16[128,2048]{1,0:T(8,128)(2,1)} %shard_map.136.x_ref, f32[128,2048]{1,0:T(8,128)} %convert_bitcast_fusion.base_ref, f32[1,2048]{1,0:T(1,128)} %bitcast.153), custom_call_target="tpu_custom_call" | custom-call | tf_op jit(solution)/shard_map/pallas_call | solution.py:190
  150.9 1.9 convolution_convert_fusion
  152.9 53.8 %all_to_all.21 = bf16[32,2,24,1024]{3,2,1,0:T(8,128)(2,1)S(1)} all-to-all(bf16[32,2,24,1024]{3,2,1,0:T(8,128)(2,1)S(1)} %bitcast.115), channel_id=1, replica_groups=mesh['grp'=32,'head'=4] {'grp'}, dimensions={0} | all-to-all | bytes 6291456 | tf_op jit(solution)/shard_map/all_to_all | solution.py:299
  208.2 2.3 copy.89
  210.5 2.3 copy.88
  212.7 1.8 fusion.27
  219.6 2.2 fusion.23
  230.2 1.9 pad_maximum_fusion
  232.1 5.8 %all-to-all-start.3 = ((bf16[32,2,24,1024]{3,2,1,0:T(8,128)(2,1)}), bf16[32,2,24,1024]{3,2,1,0:T(8,128)(2,1)S(1)}, u32[]{:S(2)}, u32[]{:S(2)}) async-start(bf16[32,2,24,1024]{3,2,1,0:T(8,128)(2,1)} %pad_maximum_fusion), calls=%async_computation.3 | async-start | bytes 6291456 | tf_op jit(solution)/shard_map/all_to_all | solution.py:320
  240.7 40.7 %all-to-all-done.3 = bf16[32,2,24,1024]{3,2,1,0:T(8,128)(2,1)S(1)} async-done(((bf16[32,2,24,1024]{3,2,1,0:T(8,128)(2,1)}), bf16[32,2,24,1024]{3,2,1,0:T(8,128)(2,1)S(1)}, u32[]{:S(2)}, u32[]{:S(2)}) %all-to-all-start.3) | async-done | bytes 3145760 | tf_op jit(solution)/shard_map/all_to_all | solution.py:320
  281.4 3.5 %convolution_reduce_fusion = f32[128,1024]{1,0:T(8,128)} fusion(bf16[3,128,1536]{2,1,0:T(8,128)(2,1)} %bitcast.146, bf16[1536,1024,1]{1,0,2:T(8,128)(2,1)S(1)} %bitcast.130), kind=kOutput, calls=%fused_computation.15 | convolution fusion | flops 1208221696 | bytes 4849664 | tf_op jit(solution)/shard_map/dot_general | solution.py:328
  287.1 7.7 %shard_map.138 = f32[128,512]{1,0:T(8,128)} custom-call(f32[128,512]{1,0:T(8,128)} %bitcast.147), custom_call_target="tpu_custom_call" | custom-call | tf_op jit(solution)/shard_map/pallas_call | solution.py:47
  295.0 1.7 fusion.16
  (75 shorter events, 26.9 us)
Async XLA Ops:
  66.7 5.8 %copy-start.9 = (s32[1,128,8]{1,2,0:T(8,128)S(1)}, s32[1,128,8]{1,2,0:T(8,128)}, u32[]{:S(2)}) copy-start(s32[1,128,8]{1,2,0:T(8,128)} %param.23) | copy-start | bytes 12292
  66.7 6.7 %copy-start.10 = (f32[1,128,8]{1,2,0:T(8,128)S(1)}, f32[1,128,8]{1,2,0:T(8,128)}, u32[]{:S(2)}) copy-start(f32[1,128,8]{1,2,0:T(8,128)} %param.24) | copy-start | bytes 12292
  66.7 6.8 %copy-start.3 = (bf16[2048,512]{1,0:T(8,128)(2,1)S(1)}, bf16[2048,512]{1,0:T(8,128)(2,1)}, u32[]{:S(2)}) copy-start(bf16[2048,512]{1,0:T(8,128)(2,1)} %param.17) | copy-start | bytes 6291460
  66.7 61.6 %all-to-all-start.1 = ((bf16[32,128,512]{2,1,0:T(8,128)(2,1)}), bf16[32,128,512]{2,1,0:T(8,128)(2,1)}, u32[]{:S(2)}, u32[]{:S(2)}) async-start(bf16[32,128,512]{2,1,0:T(8,128)(2,1)} %get-tuple-element.11), calls=%async_computation.1 | async-start | bytes 8388608 | tf_op jit(solution)/shard_map/all_to_all | solution.py:250
  76.0 3.0 %copy-start.11 = (s32[32]{0:T(128)S(1)}, s32[32]{0:T(128)}, u32[]{:S(2)}) copy-start(s32[32]{0:T(128)} %param.21) | copy-start | bytes 388
  76.0 4.4 %copy-start = (bf16[1,128,2048]{2,1,0:T(8,128)(2,1)S(1)}, bf16[1,128,2048]{2,1,0:T(8,128)(2,1)}, u32[]{:S(2)}) copy-start(bf16[1,128,2048]{2,1,0:T(8,128)(2,1)} %param.14) | copy-start | bytes 1572868
  76.0 4.8 %copy-start.8 = (f32[2048]{0:T(1024)S(1)}, f32[2048]{0:T(1024)}, u32[]{:S(2)}) copy-start(f32[2048]{0:T(1024)} %param.15) | copy-start | bytes 24580
  84.0 1.7 copy-start.4
  152.9 53.8 %copy-start.5 = (bf16[2,256,2048]{2,1,0:T(8,128)(2,1)S(1)}, bf16[2,256,2048]{2,1,0:T(8,128)(2,1)}, u32[]{:S(2)}) copy-start(bf16[2,256,2048]{2,1,0:T(8,128)(2,1)} %param.27) | copy-start | bytes 6291460
  206.7 12.9 %collective-permute-start = (bf16[32,2,24,1024]{3,2,1,0:T(8,128)(2,1)S(1)}, bf16[32,2,24,1024]{3,2,1,0:T(8,128)(2,1)}, u32[]{:S(2)}, u32[]{:S(2)}) collective-permute-start(bf16[32,2,24,1024]{3,2,1,0:T(8,128)(2,1)S(1)} %all_to_all.21), channel_id=1, source_target_pairs={{0,1},{1,0},{2,3},{3,2},{4,5},{5,4},{6,7},{7,6},{8,9},{9,8},{10,11... | collective-permute-start | bytes 9437192 | tf_op jit(solution)/shard_map/ppermute | solution.py:301
  212.7 2.2 copy-start.6
  215.1 1.2 copy-start.1
  215.1 1.5 copy-start.2
  223.7 3.6 %collective-permute-start.2 = (bf16[768,1024]{1,0:T(8,128)(2,1)S(1)}, bf16[768,1024]{1,0:T(8,128)(2,1)S(1)}, u32[]{:S(2)}, u32[]{:S(2)}) collective-permute-start(bf16[768,1024]{1,0:T(8,128)(2,1)S(1)} %convolution_convert_fusion.1), channel_id=1, source_target_pairs={{0,1},{1,0},{2,3},{3,2},{4,5},{5,4},{6,7},{7,6},{8,9},{9,8},{10,11... | collective-permute-start | bytes 4718600 | tf_op jit(solution)/shard_map/ppermute | solution.py:313
  226.1 3.5 %collective-permute-start.1 = (bf16[768,1024]{1,0:T(8,128)(2,1)S(1)}, bf16[768,1024]{1,0:T(8,128)(2,1)S(1)}, u32[]{:S(2)}, u32[]{:S(2)}) collective-permute-start(bf16[768,1024]{1,0:T(8,128)(2,1)S(1)} %convolution_convert_fusion.3), channel_id=1, source_target_pairs={{0,1},{1,0},{2,3},{3,2},{4,5},{5,4},{6,7},{7,6},{8,9},{9,8},{10,11... | collective-permute-start | bytes 4718600 | tf_op jit(solution)/shard_map/ppermute | solution.py:313
  232.1 49.3 %all-to-all-start.3 = ((bf16[32,2,24,1024]{3,2,1,0:T(8,128)(2,1)}), bf16[32,2,24,1024]{3,2,1,0:T(8,128)(2,1)S(1)}, u32[]{:S(2)}, u32[]{:S(2)}) async-start(bf16[32,2,24,1024]{3,2,1,0:T(8,128)(2,1)} %pad_maximum_fusion), calls=%async_computation.3 | async-start | bytes 6291456 | tf_op jit(solution)/shard_map/all_to_all | solution.py:320
  284.9 10.0 %copy-start.7 = (f32[2,128,512]{2,1,0:T(8,128)S(1)}, f32[2,128,512]{2,1,0:T(8,128)}, u32[]{:S(2)}) copy-start(f32[2,128,512]{2,1,0:T(8,128)} %get-tuple-element.7) | copy-start | bytes 1572868

commit v14 on v12

--- a/solution.py
+++ b/solution.py
@@ -312,7 +312,7 @@
     combined = combined.reshape(tokens, 2, share_width)
     keep = lax.dynamic_index_in_dim(combined, chip, axis=1, keepdims=False)
     give = lax.dynamic_index_in_dim(combined, 1 - chip, axis=1, keepdims=False)
-    moe_share = keep + peer_swap(give, True, 3)
+    moe_share = keep + peer_swap(give.astype(jnp.bfloat16), True, 3).astype(jnp.float32)
     resid_share = lax.dynamic_index_in_dim(resid_blocks, chip, axis=0, keepdims=False)
     return (resid_share + moe_share).astype(jnp.bfloat16)[None]
 

time: 294 us -> 293 us (level)
  no operation moved by 1% of the time
where the time goes in v14:
time: 293 us; the launch traced here: 291 us
  blocking collectives  115 us (39%)
  waiting for transfers between devices  71.1 us (24%)
  local copies, waits for them, and re-layouts  31.1 us (11%)
  Pallas kernels  26.3 us (9%)
  matrix products  21.7 us (7%)
  other arithmetic  13 us (4%)
  starting transfers between devices  12.3 us (4%)
    all_to_all x1, blocking collectives, on_device(): lax.all_to_all(cache[part], 'grp', split_axis=0, concat_axis=0, tiled=True)  61.6 us
    all_to_all x1, blocking collectives, on_device(): lax.all_to_all(outgoing, 'grp', split_axis=0, concat_axis=0, tiled=True)  53.6 us
    all_to_all x1, waiting for transfers between devices, on_device(): lax.all_to_all(pair_sum, 'grp', split_axis=0, concat_axis=0, tiled=True)  43.3 us
    all_to_all x1, waiting for transfers between devices, on_device(): lax.all_to_all(cache[part], 'grp', split_axis=0, concat_axis=0, tiled=True)  25.1 us
    pallas_call x1, Pallas kernels, head_reduce(): pl.pallas_call(kernel, out_shape=(jax.ShapeDtypeStruct((2, rows, share),...  12.4 us
    pallas_call x1, Pallas kernels, attend(): pl.pallas_call(kernel, grid_spec=grid_spec, out_shape=jax.ShapeDtypeStruc...  8.57 us
    reduce_sum x1, other arithmetic, on_device(): dispatch = jnp.sum(place.astype(jnp.float32), axis=1).astype(jnp.bfloat16)  6.98 us
    all_to_all x1, starting transfers between devices, on_device(): lax.all_to_all(pair_sum, 'grp', split_axis=0, concat_axis=0, tiled=True)  5.88 us
  transfers between devices with their start and end apart: 5, of which 4 were waited for; matrix products, arithmetic and copies ran while one was open for 14% of the time, Pallas kernels for 0%

profile of v14, /device:TPU:10, one launch (start us, length us, event | category | flops | bytes accessed | tf_op | source)
XLA Modules:
  0.0 291.1 jit_solution(682950607153448466)
XLA Ops:
  0.0 5.3 %slice_bitcast_fusion = (bf16[32,128,512]{2,1,0:T(8,128)(2,1)}, bf16[32,128,512]{2,1,0:T(8,128)(2,1)S(1)}) fusion(bf16[2,32,128,512]{3,2,1,0:T(8,128)(2,1)} %param.20), kind=kLoop, calls=%fused_computation.4 | loop fusion | bytes 16777216 | tf_op jit(solution)/shard_map/squeeze | solution.py:232
  5.3 61.6 %all_to_all.20 = bf16[32,128,512]{2,1,0:T(8,128)(2,1)} all-to-all(bf16[32,128,512]{2,1,0:T(8,128)(2,1)S(1)} %get-tuple-element.12), channel_id=1, replica_groups=mesh['grp'=32,'head'=4] {'grp'}, dimensions={0} | all-to-all | bytes 8388608 | tf_op jit(solution)/shard_map/all_to_all | solution.py:232
  66.8 5.7 %all-to-all-start.1 = ((bf16[32,128,512]{2,1,0:T(8,128)(2,1)}), bf16[32,128,512]{2,1,0:T(8,128)(2,1)}, u32[]{:S(2)}, u32[]{:S(2)}) async-start(bf16[32,128,512]{2,1,0:T(8,128)(2,1)} %get-tuple-element.11), calls=%async_computation.1 | async-start | bytes 8388608 | tf_op jit(solution)/shard_map/all_to_all | solution.py:232
  73.6 4.0 %copy.84 = bf16[512,2048]{1,0:T(8,128)(2,1)} copy(bf16[512,2048]{0,1:T(8,128)(2,1)} %bitcast.138) | data formatting | bytes 4194304 | tf_op jit(solution)/shard_map/dot_general | solution.py:222
  77.6 4.0 %copy.82 = bf16[512,2048]{1,0:T(8,128)(2,1)} copy(bf16[512,2048]{0,1:T(8,128)(2,1)} %bitcast.139) | data formatting | bytes 4194304 | tf_op jit(solution)/shard_map/dot_general | solution.py:219
  83.2 2.4 fusion.19
  88.1 4.0 %copy.86 = bf16[512,2048]{1,0:T(8,128)(2,1)} copy(bf16[512,2048]{0,1:T(8,128)(2,1)} %bitcast.140) | data formatting | bytes 4194304 | tf_op jit(solution)/shard_map/dot_general | solution.py:225
  92.1 2.4 convolution_convert_fusion.6
  95.2 7.0 %convert_reduce_fusion = (bf16[128,1536]{1,0:T(8,128)(2,1)S(1)}, f32[128,1536]{1,0:T(8,128)}) fusion(s32[128,8]{1,0:T(8,128)S(1)} %bitcast_add_fusion.1, f32[128,8]{1,0:T(8,128)S(1)} %copy.74), kind=kLoop, calls=%fused_computation | loop fusion | flops 7471104 | bytes 1187840 | tf_op jit(solution)/shard_map/reduce_sum | solution.py:260
  103.3 25.1 %all-to-all-done.1 = bf16[32,128,512]{2,1,0:T(8,128)(2,1)} async-done(((bf16[32,128,512]{2,1,0:T(8,128)(2,1)}), bf16[32,128,512]{2,1,0:T(8,128)(2,1)}, u32[]{:S(2)}, u32[]{:S(2)}) %all-to-all-start.1) | async-done | bytes 4194336 | tf_op jit(solution)/shard_map/all_to_all | solution.py:232
  128.4 8.6 %shard_map.136 = bf16[128,512]{1,0:T(8,128)(2,1)} custom-call(s32[1]{0:T(128)} %dynamic_slice.52.length_ref, bf16[128,512]{1,0:T(8,128)(2,1)} %copy.83.q_ref, bf16[128,512]{1,0:T(8,128)(2,1)} %copy.85.kn_ref, bf16[128,512]{1,0:T(8,128)(2,1)} %copy.87.vn_ref, bf16[4096,512]{1,0:T(8,128)(2,1)} %bitcast.114, bf16[4096,512]{1,0:T(8,128)(2,1)} %bitcast.16.v_ref), custom_call_target="tpu_custom_call" | custom-call | tf_op jit(solution)/shard_map/pallas_call | solution.py:99
  137.0 2.1 convolution_convert_fusion.1.x_ref
  139.1 12.4 %shard_map.137 = (f32[2,128,512]{2,1,0:T(8,128)}, bf16[128,1024]{1,0:T(8,128)(2,1)}) custom-call(bf16[128,2048]{1,0:T(8,128)(2,1)} %convolution_convert_fusion.1.x_ref, f32[128,2048]{1,0:T(8,128)} %convert_bitcast_fusion.base_ref, f32[1,2048]{1,0:T(1,128)} %bitcast.157), custom_call_target="tpu_custom_call" | custom-call | tf_op jit(solution)/shard_map/pallas_call | solution.py:172
  151.6 2.0 convolution_convert_fusion
  153.5 53.6 %all_to_all.21 = bf16[32,2,24,1024]{3,2,1,0:T(8,128)(2,1)} all-to-all(bf16[32,2,24,1024]{3,2,1,0:T(8,128)(2,1)S(1)} %bitcast.119), channel_id=1, replica_groups=mesh['grp'=32,'head'=4] {'grp'}, dimensions={0} | all-to-all | bytes 6291456 | tf_op jit(solution)/shard_map/all_to_all | solution.py:281
  208.3 1.8 fusion.27
  211.2 2.2 fusion.24
  215.7 2.2 fusion.23
  224.0 1.7 collective-permute-done.1
  226.3 2.0 pad_maximum_fusion
  228.3 5.9 %all-to-all-start.3 = ((bf16[32,2,24,1024]{3,2,1,0:T(8,128)(2,1)}), bf16[32,2,24,1024]{3,2,1,0:T(8,128)(2,1)}, u32[]{:S(2)}, u32[]{:S(2)}) async-start(bf16[32,2,24,1024]{3,2,1,0:T(8,128)(2,1)} %pad_maximum_fusion), calls=%async_computation.3 | async-start | bytes 6291456 | tf_op jit(solution)/shard_map/all_to_all | solution.py:302
  234.4 43.3 %all-to-all-done.3 = bf16[32,2,24,1024]{3,2,1,0:T(8,128)(2,1)} async-done(((bf16[32,2,24,1024]{3,2,1,0:T(8,128)(2,1)}), bf16[32,2,24,1024]{3,2,1,0:T(8,128)(2,1)}, u32[]{:S(2)}, u32[]{:S(2)}) %all-to-all-start.3) | async-done | bytes 3145760 | tf_op jit(solution)/shard_map/all_to_all | solution.py:302
  277.7 4.2 %convolution_reduce_fusion = f32[128,1024]{1,0:T(8,128)} fusion(bf16[3,128,1536]{2,1,0:T(8,128)(2,1)S(1)} %bitcast.150, bf16[1536,1024,1]{1,0,2:T(8,128)(2,1)} %bitcast.50), kind=kOutput, calls=%fused_computation.16 | convolution fusion | flops 1208221696 | bytes 4849664 | tf_op jit(solution)/shard_map/dot_general | solution.py:310
  284.0 5.3 %shard_map.138 = bf16[128,512]{1,0:T(8,128)(2,1)} custom-call(bf16[128,512]{1,0:T(8,128)(2,1)} %bitcast.155), custom_call_target="tpu_custom_call" | custom-call | tf_op jit(solution)/shard_map/pallas_call | solution.py:47
  (77 shorter events, 22.1 us)
Async XLA Ops:
  0.0 137.0 %copy-start = (bf16[512,2048]{1,0:T(8,128)(2,1)S(1)}, bf16[512,2048]{1,0:T(8,128)(2,1)}, u32[]{:S(2)}) copy-start(bf16[512,2048]{1,0:T(8,128)(2,1)} %param.19) | copy-start | bytes 6291460
  66.8 5.8 %copy-start.9 = (s32[1,128,8]{1,2,0:T(8,128)S(1)}, s32[1,128,8]{1,2,0:T(8,128)}, u32[]{:S(2)}) copy-start(s32[1,128,8]{1,2,0:T(8,128)} %param.23) | copy-start | bytes 12292
  66.8 6.7 %copy-start.10 = (f32[1,128,8]{1,2,0:T(8,128)S(1)}, f32[1,128,8]{1,2,0:T(8,128)}, u32[]{:S(2)}) copy-start(f32[1,128,8]{1,2,0:T(8,128)} %param.24) | copy-start | bytes 12292
  66.8 61.6 %all-to-all-start.1 = ((bf16[32,128,512]{2,1,0:T(8,128)(2,1)}), bf16[32,128,512]{2,1,0:T(8,128)(2,1)}, u32[]{:S(2)}, u32[]{:S(2)}) async-start(bf16[32,128,512]{2,1,0:T(8,128)(2,1)} %get-tuple-element.11), calls=%async_computation.1 | async-start | bytes 8388608 | tf_op jit(solution)/shard_map/all_to_all | solution.py:232
  77.6 4.0 %copy-start.11 = (s32[32]{0:T(128)S(1)}, s32[32]{0:T(128)}, u32[]{:S(2)}) copy-start(s32[32]{0:T(128)} %param.21) | copy-start | bytes 388
  77.6 5.2 %copy-start.2 = (bf16[1,128,2048]{2,1,0:T(8,128)(2,1)S(1)}, bf16[1,128,2048]{2,1,0:T(8,128)(2,1)}, u32[]{:S(2)}) copy-start(bf16[1,128,2048]{2,1,0:T(8,128)(2,1)} %param.14) | copy-start | bytes 1572868
  77.6 5.6 %copy-start.8 = (f32[2048]{0:T(1024)S(1)}, f32[2048]{0:T(1024)}, u32[]{:S(2)}) copy-start(f32[2048]{0:T(1024)} %param.15) | copy-start | bytes 24580
  81.6 4.0 %copy-start.3 = (bf16[512,2048]{1,0:T(8,128)(2,1)S(1)}, bf16[512,2048]{1,0:T(8,128)(2,1)}, u32[]{:S(2)}) copy-start(bf16[512,2048]{1,0:T(8,128)(2,1)} %copy.82) | copy-start | bytes 6291460
  153.5 53.6 %copy-start.5 = (bf16[2,256,2048]{2,1,0:T(8,128)(2,1)S(1)}, bf16[2,256,2048]{2,1,0:T(8,128)(2,1)}, u32[]{:S(2)}) copy-start(bf16[2,256,2048]{2,1,0:T(8,128)(2,1)} %param.27) | copy-start | bytes 6291460
  207.1 8.6 %collective-permute-start = (bf16[32,2,24,1024]{3,2,1,0:T(8,128)(2,1)}, bf16[32,2,24,1024]{3,2,1,0:T(8,128)(2,1)}, u32[]{:S(2)}, u32[]{:S(2)}) collective-permute-start(bf16[32,2,24,1024]{3,2,1,0:T(8,128)(2,1)} %all_to_all.21), channel_id=1, source_target_pairs={{0,1},{1,0},{2,3},{3,2},{4,5},{5,4},{6,7},{7,6},{8,9},{9,8},{10,11... | collective-permute-start | bytes 9437192 | tf_op jit(solution)/shard_map/ppermute | solution.py:283
  208.3 2.2 copy-start.6
  219.8 3.6 %collective-permute-start.2 = (bf16[768,1024]{1,0:T(8,128)(2,1)S(1)}, bf16[768,1024]{1,0:T(8,128)(2,1)S(1)}, u32[]{:S(2)}, u32[]{:S(2)}) collective-permute-start(bf16[768,1024]{1,0:T(8,128)(2,1)S(1)} %convolution_convert_fusion.2), channel_id=1, source_target_pairs={{0,1},{1,0},{2,3},{3,2},{4,5},{5,4},{6,7},{7,6},{8,9},{9,8},{10,11... | collective-permute-start | bytes 4718600 | tf_op jit(solution)/shard_map/ppermute | solution.py:295
  222.2 3.5 %collective-permute-start.1 = (bf16[768,1024]{1,0:T(8,128)(2,1)S(1)}, bf16[768,1024]{1,0:T(8,128)(2,1)S(1)}, u32[]{:S(2)}, u32[]{:S(2)}) collective-permute-start(bf16[768,1024]{1,0:T(8,128)(2,1)S(1)} %convolution_convert_fusion.4), channel_id=1, source_target_pairs={{0,1},{1,0},{2,3},{3,2},{4,5},{5,4},{6,7},{7,6},{8,9},{9,8},{10,11... | collective-permute-start | bytes 4718600 | tf_op jit(solution)/shard_map/ppermute | solution.py:295
  228.3 5.9 %copy-start.4 = (f32[128,1536]{1,0:T(8,128)S(1)}, f32[128,1536]{1,0:T(8,128)}, u32[]{:S(2)}) copy-start(f32[128,1536]{1,0:T(8,128)} %get-tuple-element.10) | copy-start | bytes 2359300
  228.3 49.4 %all-to-all-start.3 = ((bf16[32,2,24,1024]{3,2,1,0:T(8,128)(2,1)}), bf16[32,2,24,1024]{3,2,1,0:T(8,128)(2,1)}, u32[]{:S(2)}, u32[]{:S(2)}) async-start(bf16[32,2,24,1024]{3,2,1,0:T(8,128)(2,1)} %pad_maximum_fusion), calls=%async_computation.3 | async-start | bytes 6291456 | tf_op jit(solution)/shard_map/all_to_all | solution.py:302
  277.7 13.5 %copy-start.1 = (bf16[512,2048]{1,0:T(8,128)(2,1)S(1)}, bf16[512,2048]{1,0:T(8,128)(2,1)}, u32[]{:S(2)}) copy-start(bf16[512,2048]{1,0:T(8,128)(2,1)} %param.19) | copy-start | bytes 6291460
  281.9 7.6 %copy-start.7 = (f32[2,128,512]{2,1,0:T(8,128)S(1)}, f32[2,128,512]{2,1,0:T(8,128)}, u32[]{:S(2)}) copy-start(f32[2,128,512]{2,1,0:T(8,128)} %get-tuple-element.7) | copy-start | bytes 1572868

commit v15 on v14

--- a/solution.py
+++ b/solution.py
@@ -294,11 +294,14 @@
         other_part = jnp.dot(act, halves(w_down[expert], other_core), preferred_element_type=jnp.float32)
         partner_part = lax.ppermute(other_part.astype(jnp.bfloat16), "head", partners)
         pair_sums.append(
-            (mine_part.astype(jnp.bfloat16).astype(jnp.float32) + partner_part.astype(jnp.float32))
-            .astype(jnp.bfloat16)
-            .reshape(group_count, capacity, half)
-        )
-    pair_sum = jnp.stack(pair_sums, axis=1)
+            (
+                mine_part.astype(jnp.bfloat16).reshape(group_count, capacity, half),
+                partner_part.reshape(group_count, capacity, half),
+            )
+        )
+    mine_all = jnp.stack([mine for mine, _ in pair_sums], axis=1).astype(jnp.float32)
+    partner_all = jnp.stack([other for _, other in pair_sums], axis=1).astype(jnp.float32)
+    pair_sum = (mine_all + partner_all).astype(jnp.bfloat16)
     returned = lax.all_to_all(pair_sum, "grp", split_axis=0, concat_axis=0, tiled=True)
     returned = returned.reshape(slots, half)
     weighting = jnp.sum(jnp.where(place, weights[:, :, None], 0.0), axis=1)

time: 293 us -> 293 us (level)
  transfers between devices with their start and end apart: 5 -> 5, of which waited for: 4 -> 3; matrix products, arithmetic and copies ran while one was open for 14% -> 14% of each run, Pallas kernels for 0% -> 0%
where the time goes in v15:
time: 293 us; the launch traced here: 291 us
  blocking collectives  115 us (39%)
  waiting for transfers between devices  70.5 us (24%)
  local copies, waits for them, and re-layouts  31.1 us (11%)
  Pallas kernels  26.3 us (9%)
  matrix products  21.6 us (7%)
  other arithmetic  13.8 us (5%)
  starting transfers between devices  12.3 us (4%)
    all_to_all x1, blocking collectives, on_device(): lax.all_to_all(cache[part], 'grp', split_axis=0, concat_axis=0, tiled=True)  61.6 us
    all_to_all x1, blocking collectives, on_device(): lax.all_to_all(outgoing, 'grp', split_axis=0, concat_axis=0, tiled=True)  53.6 us
    all_to_all x1, waiting for transfers between devices, on_device(): lax.all_to_all(pair_sum, 'grp', split_axis=0, concat_axis=0, tiled=True)  43.3 us
    all_to_all x1, waiting for transfers between devices, on_device(): lax.all_to_all(cache[part], 'grp', split_axis=0, concat_axis=0, tiled=True)  25.1 us
    pallas_call x1, Pallas kernels, head_reduce(): pl.pallas_call(kernel, out_shape=(jax.ShapeDtypeStruct((2, rows, share),...  12.4 us
    pallas_call x1, Pallas kernels, attend(): pl.pallas_call(kernel, grid_spec=grid_spec, out_shape=jax.ShapeDtypeStruc...  8.57 us
    reduce_sum x1, other arithmetic, on_device(): dispatch = jnp.sum(place.astype(jnp.float32), axis=1).astype(jnp.bfloat16)  6.98 us
    all_to_all x1, starting transfers between devices, on_device(): lax.all_to_all(pair_sum, 'grp', split_axis=0, concat_axis=0, tiled=True)  5.88 us
  transfers between devices with their start and end apart: 5, of which 3 were waited for; matrix products, arithmetic and copies ran while one was open for 14% of the time, Pallas kernels for 0%

profile of v15, /device:TPU:10, one launch (start us, length us, event | category | flops | bytes accessed | tf_op | source)
XLA Modules:
  0.0 291.3 jit_solution(14650101551178525976)
XLA Ops:
  0.0 5.3 %slice_bitcast_fusion = (bf16[32,128,512]{2,1,0:T(8,128)(2,1)}, bf16[32,128,512]{2,1,0:T(8,128)(2,1)S(1)}) fusion(bf16[2,32,128,512]{3,2,1,0:T(8,128)(2,1)} %param.20), kind=kLoop, calls=%fused_computation.5 | loop fusion | bytes 16777216 | tf_op jit(solution)/shard_map/squeeze | solution.py:232
  5.3 61.6 %all_to_all.20 = bf16[32,128,512]{2,1,0:T(8,128)(2,1)} all-to-all(bf16[32,128,512]{2,1,0:T(8,128)(2,1)S(1)} %get-tuple-element.12), channel_id=1, replica_groups=mesh['grp'=32,'head'=4] {'grp'}, dimensions={0} | all-to-all | bytes 8388608 | tf_op jit(solution)/shard_map/all_to_all | solution.py:232
  66.8 5.7 %all-to-all-start.1 = ((bf16[32,128,512]{2,1,0:T(8,128)(2,1)}), bf16[32,128,512]{2,1,0:T(8,128)(2,1)}, u32[]{:S(2)}, u32[]{:S(2)}) async-start(bf16[32,128,512]{2,1,0:T(8,128)(2,1)} %get-tuple-element.11), calls=%async_computation.1 | async-start | bytes 8388608 | tf_op jit(solution)/shard_map/all_to_all | solution.py:232
  73.6 4.0 %copy.88 = bf16[512,2048]{1,0:T(8,128)(2,1)} copy(bf16[512,2048]{0,1:T(8,128)(2,1)} %bitcast.146) | data formatting | bytes 4194304 | tf_op jit(solution)/shard_map/dot_general | solution.py:222
  77.6 4.0 %copy.86 = bf16[512,2048]{1,0:T(8,128)(2,1)} copy(bf16[512,2048]{0,1:T(8,128)(2,1)} %bitcast.147) | data formatting | bytes 4194304 | tf_op jit(solution)/shard_map/dot_general | solution.py:219
  83.2 2.4 fusion.19
  88.1 4.0 %copy.90 = bf16[512,2048]{1,0:T(8,128)(2,1)} copy(bf16[512,2048]{0,1:T(8,128)(2,1)} %bitcast.148) | data formatting | bytes 4194304 | tf_op jit(solution)/shard_map/dot_general | solution.py:225
  92.1 2.4 convolution_convert_fusion.6
  95.2 7.0 %convert_reduce_fusion = (bf16[128,1536]{1,0:T(8,128)(2,1)S(1)}, f32[128,1536]{1,0:T(8,128)}) fusion(s32[128,8]{1,0:T(8,128)S(1)} %bitcast_add_fusion.1, f32[128,8]{1,0:T(8,128)S(1)} %copy.76), kind=kLoop, calls=%fused_computation.1 | loop fusion | flops 7471104 | bytes 1187840 | tf_op jit(solution)/shard_map/reduce_sum | solution.py:260
  103.3 25.1 %all-to-all-done.1 = bf16[32,128,512]{2,1,0:T(8,128)(2,1)} async-done(((bf16[32,128,512]{2,1,0:T(8,128)(2,1)}), bf16[32,128,512]{2,1,0:T(8,128)(2,1)}, u32[]{:S(2)}, u32[]{:S(2)}) %all-to-all-start.1) | async-done | bytes 4194336 | tf_op jit(solution)/shard_map/all_to_all | solution.py:232
  128.4 8.6 %shard_map.136 = bf16[128,512]{1,0:T(8,128)(2,1)} custom-call(s32[1]{0:T(128)} %dynamic_slice.52.length_ref, bf16[128,512]{1,0:T(8,128)(2,1)} %copy.87.q_ref, bf16[128,512]{1,0:T(8,128)(2,1)} %copy.89.kn_ref, bf16[128,512]{1,0:T(8,128)(2,1)} %copy.91.vn_ref, bf16[4096,512]{1,0:T(8,128)(2,1)} %bitcast.120, bf16[4096,512]{1,0:T(8,128)(2,1)} %bitcast.16.v_ref), custom_call_target="tpu_custom_call" | custom-call | tf_op jit(solution)/shard_map/pallas_call | solution.py:99
  137.0 2.1 convolution_convert_fusion.1.x_ref
  139.1 12.4 %shard_map.137 = (f32[2,128,512]{2,1,0:T(8,128)}, bf16[128,1024]{1,0:T(8,128)(2,1)}) custom-call(bf16[128,2048]{1,0:T(8,128)(2,1)} %convolution_convert_fusion.1.x_ref, f32[128,2048]{1,0:T(8,128)} %convert_bitcast_fusion.base_ref, f32[1,2048]{1,0:T(1,128)} %bitcast.165), custom_call_target="tpu_custom_call" | custom-call | tf_op jit(solution)/shard_map/pallas_call | solution.py:172
  151.6 2.0 convolution_convert_fusion
  153.5 53.6 %all_to_all.21 = bf16[32,2,24,1024]{3,2,1,0:T(8,128)(2,1)} all-to-all(bf16[32,2,24,1024]{3,2,1,0:T(8,128)(2,1)S(1)} %bitcast.125), channel_id=1, replica_groups=mesh['grp'=32,'head'=4] {'grp'}, dimensions={0} | all-to-all | bytes 6291456 | tf_op jit(solution)/shard_map/all_to_all | solution.py:281
  208.3 1.8 fusion.27
  211.2 2.2 fusion.24
  215.7 2.2 fusion.23
  223.5 2.2 collective-permute-done.1
  225.7 2.8 add_convert_fusion
  228.5 5.9 %all-to-all-start.3 = ((bf16[32,2,24,1024]{3,2,1,0:T(8,128)(2,1)}), bf16[32,2,24,1024]{3,2,1,0:T(8,128)(2,1)}, u32[]{:S(2)}, u32[]{:S(2)}) async-start(bf16[32,2,24,1024]{3,2,1,0:T(8,128)(2,1)} %add_convert_fusion), calls=%async_computation.3 | async-start | bytes 6291456 | tf_op jit(solution)/shard_map/all_to_all | solution.py:305
  234.6 43.3 %all-to-all-done.3 = bf16[32,2,24,1024]{3,2,1,0:T(8,128)(2,1)} async-done(((bf16[32,2,24,1024]{3,2,1,0:T(8,128)(2,1)}), bf16[32,2,24,1024]{3,2,1,0:T(8,128)(2,1)}, u32[]{:S(2)}, u32[]{:S(2)}) %all-to-all-start.3) | async-done | bytes 3145760 | tf_op jit(solution)/shard_map/all_to_all | solution.py:305
  277.8 4.2 %convolution_reduce_fusion = f32[128,1024]{1,0:T(8,128)} fusion(bf16[3,128,1536]{2,1,0:T(8,128)(2,1)S(1)} %bitcast.158, bf16[1536,1024,1]{1,0,2:T(8,128)(2,1)} %bitcast.54), kind=kOutput, calls=%fused_computation.14 | convolution fusion | flops 1208221696 | bytes 4849664 | tf_op jit(solution)/shard_map/dot_general | solution.py:313
  284.2 5.3 %shard_map.138 = bf16[128,512]{1,0:T(8,128)(2,1)} custom-call(bf16[128,512]{1,0:T(8,128)(2,1)} %bitcast.163), custom_call_target="tpu_custom_call" | custom-call | tf_op jit(solution)/shard_map/pallas_call | solution.py:47
  (77 shorter events, 21.0 us)
Async XLA Ops:
  0.0 137.0 %copy-start = (bf16[512,2048]{1,0:T(8,128)(2,1)S(1)}, bf16[512,2048]{1,0:T(8,128)(2,1)}, u32[]{:S(2)}) copy-start(bf16[512,2048]{1,0:T(8,128)(2,1)} %param.19) | copy-start | bytes 6291460
  66.8 5.8 %copy-start.9 = (s32[1,128,8]{1,2,0:T(8,128)S(1)}, s32[1,128,8]{1,2,0:T(8,128)}, u32[]{:S(2)}) copy-start(s32[1,128,8]{1,2,0:T(8,128)} %param.23) | copy-start | bytes 12292
  66.8 6.7 %copy-start.10 = (f32[1,128,8]{1,2,0:T(8,128)S(1)}, f32[1,128,8]{1,2,0:T(8,128)}, u32[]{:S(2)}) copy-start(f32[1,128,8]{1,2,0:T(8,128)} %param.24) | copy-start | bytes 12292
  66.8 61.6 %all-to-all-start.1 = ((bf16[32,128,512]{2,1,0:T(8,128)(2,1)}), bf16[32,128,512]{2,1,0:T(8,128)(2,1)}, u32[]{:S(2)}, u32[]{:S(2)}) async-start(bf16[32,128,512]{2,1,0:T(8,128)(2,1)} %get-tuple-element.11), calls=%async_computation.1 | async-start | bytes 8388608 | tf_op jit(solution)/shard_map/all_to_all | solution.py:232
  77.6 4.0 %copy-start.11 = (s32[32]{0:T(128)S(1)}, s32[32]{0:T(128)}, u32[]{:S(2)}) copy-start(s32[32]{0:T(128)} %param.21) | copy-start | bytes 388
  77.6 5.2 %copy-start.2 = (bf16[1,128,2048]{2,1,0:T(8,128)(2,1)S(1)}, bf16[1,128,2048]{2,1,0:T(8,128)(2,1)}, u32[]{:S(2)}) copy-start(bf16[1,128,2048]{2,1,0:T(8,128)(2,1)} %param.14) | copy-start | bytes 1572868
  77.6 5.6 %copy-start.8 = (f32[2048]{0:T(1024)S(1)}, f32[2048]{0:T(1024)}, u32[]{:S(2)}) copy-start(f32[2048]{0:T(1024)} %param.15) | copy-start | bytes 24580
  81.6 4.0 %copy-start.3 = (bf16[512,2048]{1,0:T(8,128)(2,1)S(1)}, bf16[512,2048]{1,0:T(8,128)(2,1)}, u32[]{:S(2)}) copy-start(bf16[512,2048]{1,0:T(8,128)(2,1)} %copy.86) | copy-start | bytes 6291460
  153.5 53.6 %copy-start.5 = (bf16[2,256,2048]{2,1,0:T(8,128)(2,1)S(1)}, bf16[2,256,2048]{2,1,0:T(8,128)(2,1)}, u32[]{:S(2)}) copy-start(bf16[2,256,2048]{2,1,0:T(8,128)(2,1)} %param.27) | copy-start | bytes 6291460
  207.1 8.6 %collective-permute-start = (bf16[32,2,24,1024]{3,2,1,0:T(8,128)(2,1)}, bf16[32,2,24,1024]{3,2,1,0:T(8,128)(2,1)}, u32[]{:S(2)}, u32[]{:S(2)}) collective-permute-start(bf16[32,2,24,1024]{3,2,1,0:T(8,128)(2,1)} %all_to_all.21), channel_id=1, source_target_pairs={{0,1},{1,0},{2,3},{3,2},{4,5},{5,4},{6,7},{7,6},{8,9},{9,8},{10,11... | collective-permute-start | bytes 9437192 | tf_op jit(solution)/shard_map/ppermute | solution.py:283
  208.3 2.2 copy-start.6
  219.8 3.7 %collective-permute-start.2 = (bf16[768,1024]{1,0:T(8,128)(2,1)S(1)}, bf16[768,1024]{1,0:T(8,128)(2,1)S(1)}, u32[]{:S(2)}, u32[]{:S(2)}) collective-permute-start(bf16[768,1024]{1,0:T(8,128)(2,1)S(1)} %convolution_convert_fusion.2), channel_id=1, source_target_pairs={{0,1},{1,0},{2,3},{3,2},{4,5},{5,4},{6,7},{7,6},{8,9},{9,8},{10,11... | collective-permute-start | bytes 4718600 | tf_op jit(solution)/shard_map/ppermute | solution.py:295
  222.2 3.5 %collective-permute-start.1 = (bf16[768,1024]{1,0:T(8,128)(2,1)S(1)}, bf16[768,1024]{1,0:T(8,128)(2,1)S(1)}, u32[]{:S(2)}, u32[]{:S(2)}) collective-permute-start(bf16[768,1024]{1,0:T(8,128)(2,1)S(1)} %convolution_convert_fusion.3), channel_id=1, source_target_pairs={{0,1},{1,0},{2,3},{3,2},{4,5},{5,4},{6,7},{7,6},{8,9},{9,8},{10,11... | collective-permute-start | bytes 4718600 | tf_op jit(solution)/shard_map/ppermute | solution.py:295
  228.5 5.9 %copy-start.4 = (f32[128,1536]{1,0:T(8,128)S(1)}, f32[128,1536]{1,0:T(8,128)}, u32[]{:S(2)}) copy-start(f32[128,1536]{1,0:T(8,128)} %get-tuple-element.10) | copy-start | bytes 2359300
  228.5 49.4 %all-to-all-start.3 = ((bf16[32,2,24,1024]{3,2,1,0:T(8,128)(2,1)}), bf16[32,2,24,1024]{3,2,1,0:T(8,128)(2,1)}, u32[]{:S(2)}, u32[]{:S(2)}) async-start(bf16[32,2,24,1024]{3,2,1,0:T(8,128)(2,1)} %add_convert_fusion), calls=%async_computation.3 | async-start | bytes 6291456 | tf_op jit(solution)/shard_map/all_to_all | solution.py:305
  277.8 13.5 %copy-start.1 = (bf16[512,2048]{1,0:T(8,128)(2,1)S(1)}, bf16[512,2048]{1,0:T(8,128)(2,1)}, u32[]{:S(2)}) copy-start(bf16[512,2048]{1,0:T(8,128)(2,1)} %param.19) | copy-start | bytes 6291460
  282.1 7.6 %copy-start.7 = (f32[2,128,512]{2,1,0:T(8,128)S(1)}, f32[2,128,512]{2,1,0:T(8,128)}, u32[]{:S(2)}) copy-start(f32[2,128,512]{2,1,0:T(8,128)} %get-tuple-element.7) | copy-start | bytes 1572868

commit v16 on v14

--- a/solution.py
+++ b/solution.py
@@ -309,9 +309,10 @@
         pieces.append(piece)
     combined = jnp.dot(jnp.concatenate(pieces, axis=0), returned, preferred_element_type=jnp.float32)
     combined = combined.reshape(3, tokens, half).sum(axis=0)
-    combined = combined.reshape(tokens, 2, share_width)
-    keep = lax.dynamic_index_in_dim(combined, chip, axis=1, keepdims=False)
-    give = lax.dynamic_index_in_dim(combined, 1 - chip, axis=1, keepdims=False)
+    first_block = combined[:, :share_width]
+    second_block = combined[:, share_width:]
+    keep = jnp.where(chip == 0, first_block, second_block)
+    give = jnp.where(chip == 0, second_block, first_block)
     moe_share = keep + peer_swap(give.astype(jnp.bfloat16), True, 3).astype(jnp.float32)
     resid_share = lax.dynamic_index_in_dim(resid_blocks, chip, axis=0, keepdims=False)
     return (resid_share + moe_share).astype(jnp.bfloat16)[None]

time: 293 us -> 291 us (level)
  transfers between devices with their start and end apart: 5 -> 5, of which waited for: 4 -> 4; matrix products, arithmetic and copies ran while one was open for 14% -> 15% of each run, Pallas kernels for 0% -> 0%
where the time goes in v16:
time: 291 us; the launch traced here: 290 us
  blocking collectives  115 us (40%)
  waiting for transfers between devices  70.2 us (24%)
  local copies, waits for them, and re-layouts  28.9 us (10%)
  Pallas kernels  26.3 us (9%)
  matrix products  21.3 us (7%)
  other arithmetic  14.8 us (5%)
  starting transfers between devices  12.4 us (4%)
    all_to_all x1, blocking collectives, on_device(): lax.all_to_all(cache[part], 'grp', split_axis=0, concat_axis=0, tiled=True)  61.6 us
    all_to_all x1, blocking collectives, on_device(): lax.all_to_all(outgoing, 'grp', split_axis=0, concat_axis=0, tiled=True)  53.7 us
    all_to_all x1, waiting for transfers between devices, on_device(): lax.all_to_all(pair_sum, 'grp', split_axis=0, concat_axis=0, tiled=True)  42.3 us
    all_to_all x1, waiting for transfers between devices, on_device(): lax.all_to_all(cache[part], 'grp', split_axis=0, concat_axis=0, tiled=True)  25.1 us
    pallas_call x1, Pallas kernels, head_reduce(): pl.pallas_call(kernel, out_shape=(jax.ShapeDtypeStruct((2, rows, share),...  12.4 us
    pallas_call x1, Pallas kernels, attend(): pl.pallas_call(kernel, grid_spec=grid_spec, out_shape=jax.ShapeDtypeStruc...  8.57 us
    reduce_sum x1, other arithmetic, on_device(): dispatch = jnp.sum(place.astype(jnp.float32), axis=1).astype(jnp.bfloat16)  6.98 us
    all_to_all x1, starting transfers between devices, on_device(): lax.all_to_all(pair_sum, 'grp', split_axis=0, concat_axis=0, tiled=True)  6.01 us
  transfers between devices with their start and end apart: 5, of which 4 were waited for; matrix products, arithmetic and copies ran while one was open for 15% of the time, Pallas kernels for 0%

profile of v16, /device:TPU:10, one launch (start us, length us, event | category | flops | bytes accessed | tf_op | source)
XLA Modules:
  0.0 289.7 jit_solution(17240671927315531197)
XLA Ops:
  0.0 5.3 %slice_bitcast_fusion = (bf16[32,128,512]{2,1,0:T(8,128)(2,1)}, bf16[32,128,512]{2,1,0:T(8,128)(2,1)S(1)}) fusion(bf16[2,32,128,512]{3,2,1,0:T(8,128)(2,1)} %param.20), kind=kLoop, calls=%fused_computation.4 | loop fusion | bytes 16777216 | tf_op jit(solution)/shard_map/squeeze | solution.py:232
  5.3 61.6 %all_to_all.20 = bf16[32,128,512]{2,1,0:T(8,128)(2,1)} all-to-all(bf16[32,128,512]{2,1,0:T(8,128)(2,1)S(1)} %get-tuple-element.12), channel_id=1, replica_groups=mesh['grp'=32,'head'=4] {'grp'}, dimensions={0} | all-to-all | bytes 8388608 | tf_op jit(solution)/shard_map/all_to_all | solution.py:232
  66.8 5.7 %all-to-all-start.1 = ((bf16[32,128,512]{2,1,0:T(8,128)(2,1)}), bf16[32,128,512]{2,1,0:T(8,128)(2,1)}, u32[]{:S(2)}, u32[]{:S(2)}) async-start(bf16[32,128,512]{2,1,0:T(8,128)(2,1)} %get-tuple-element.11), calls=%async_computation.1 | async-start | bytes 8388608 | tf_op jit(solution)/shard_map/all_to_all | solution.py:232
  73.6 4.0 %copy.74 = bf16[512,2048]{1,0:T(8,128)(2,1)} copy(bf16[512,2048]{0,1:T(8,128)(2,1)} %bitcast.128) | data formatting | bytes 4194304 | tf_op jit(solution)/shard_map/dot_general | solution.py:222
  77.6 4.0 %copy.72 = bf16[512,2048]{1,0:T(8,128)(2,1)} copy(bf16[512,2048]{0,1:T(8,128)(2,1)} %bitcast.129) | data formatting | bytes 4194304 | tf_op jit(solution)/shard_map/dot_general | solution.py:219
  83.2 2.4 fusion.18
  88.1 4.0 %copy.76 = bf16[512,2048]{1,0:T(8,128)(2,1)} copy(bf16[512,2048]{0,1:T(8,128)(2,1)} %bitcast.130) | data formatting | bytes 4194304 | tf_op jit(solution)/shard_map/dot_general | solution.py:225
  92.1 2.4 convolution_convert_fusion.6
  95.2 7.0 %convert_reduce_fusion = (bf16[128,1536]{1,0:T(8,128)(2,1)S(1)}, f32[128,1536]{1,0:T(8,128)}) fusion(s32[128,8]{1,0:T(8,128)S(1)} %bitcast_add_fusion.1, f32[128,8]{1,0:T(8,128)S(1)} %copy.67), kind=kLoop, calls=%fused_computation | loop fusion | flops 7471104 | bytes 1187840 | tf_op jit(solution)/shard_map/reduce_sum | solution.py:260
  103.3 25.1 %all-to-all-done.1 = bf16[32,128,512]{2,1,0:T(8,128)(2,1)} async-done(((bf16[32,128,512]{2,1,0:T(8,128)(2,1)}), bf16[32,128,512]{2,1,0:T(8,128)(2,1)}, u32[]{:S(2)}, u32[]{:S(2)}) %all-to-all-start.1) | async-done | bytes 4194336 | tf_op jit(solution)/shard_map/all_to_all | solution.py:232
  128.4 8.6 %shard_map.136 = bf16[128,512]{1,0:T(8,128)(2,1)} custom-call(s32[1]{0:T(128)} %dynamic_slice.45.length_ref, bf16[128,512]{1,0:T(8,128)(2,1)} %copy.73.q_ref, bf16[128,512]{1,0:T(8,128)(2,1)} %copy.75.kn_ref, bf16[128,512]{1,0:T(8,128)(2,1)} %copy.77.vn_ref, bf16[4096,512]{1,0:T(8,128)(2,1)} %bitcast.104, bf16[4096,512]{1,0:T(8,128)(2,1)} %bitcast.16.v_ref), custom_call_target="tpu_custom_call" | custom-call | tf_op jit(solution)/shard_map/pallas_call | solution.py:99
  137.0 2.2 convolution_convert_fusion.1.x_ref
  139.2 12.4 %shard_map.137 = (f32[2,128,512]{2,1,0:T(8,128)}, bf16[128,1024]{1,0:T(8,128)(2,1)}) custom-call(bf16[128,2048]{1,0:T(8,128)(2,1)} %convolution_convert_fusion.1.x_ref, f32[128,2048]{1,0:T(8,128)} %convert_bitcast_fusion.base_ref, f32[1,2048]{1,0:T(1,128)} %bitcast.144), custom_call_target="tpu_custom_call" | custom-call | tf_op jit(solution)/shard_map/pallas_call | solution.py:172
  151.7 1.9 convolution_convert_fusion
  153.6 53.7 %all_to_all.21 = bf16[32,2,24,1024]{3,2,1,0:T(8,128)(2,1)} all-to-all(bf16[32,2,24,1024]{3,2,1,0:T(8,128)(2,1)S(1)} %bitcast.109), channel_id=1, replica_groups=mesh['grp'=32,'head'=4] {'grp'}, dimensions={0} | all-to-all | bytes 6291456 | tf_op jit(solution)/shard_map/all_to_all | solution.py:281
  208.6 1.8 fusion.26
  211.4 2.2 fusion.23
  216.0 2.2 fusion.22
  224.3 1.7 collective-permute-done.1
  226.6 2.0 pad_maximum_fusion
  228.6 6.0 %all-to-all-start.3 = ((bf16[32,2,24,1024]{3,2,1,0:T(8,128)(2,1)}), bf16[32,2,24,1024]{3,2,1,0:T(8,128)(2,1)}, u32[]{:S(2)}, u32[]{:S(2)}) async-start(bf16[32,2,24,1024]{3,2,1,0:T(8,128)(2,1)} %pad_maximum_fusion), calls=%async_computation.3 | async-start | bytes 6291456 | tf_op jit(solution)/shard_map/all_to_all | solution.py:302
  235.8 42.3 %all-to-all-done.3 = bf16[32,2,24,1024]{3,2,1,0:T(8,128)(2,1)} async-done(((bf16[32,2,24,1024]{3,2,1,0:T(8,128)(2,1)}), bf16[32,2,24,1024]{3,2,1,0:T(8,128)(2,1)}, u32[]{:S(2)}, u32[]{:S(2)}) %all-to-all-start.3) | async-done | bytes 3145760 | tf_op jit(solution)/shard_map/all_to_all | solution.py:302
  278.2 3.8 %convolution_reduce_fusion = f32[128,1024]{1,0:T(8,128)S(1)} fusion(bf16[3,128,1536]{2,1,0:T(8,128)(2,1)} %bitcast.138, bf16[1536,1024,1]{1,0,2:T(8,128)(2,1)} %bitcast.50), kind=kOutput, calls=%fused_computation.16 | convolution fusion | flops 1208221696 | bytes 4849664 | tf_op jit(solution)/shard_map/dot_general | solution.py:310
  282.7 5.3 %shard_map.138 = bf16[128,512]{1,0:T(8,128)(2,1)} custom-call(bf16[128,512]{1,0:T(8,128)(2,1)} %select_convert_fusion.x_ref), custom_call_target="tpu_custom_call" | custom-call | tf_op jit(solution)/shard_map/pallas_call | solution.py:47
  (73 shorter events, 21.6 us)
Async XLA Ops:
  0.0 137.0 %copy-start = (bf16[512,2048]{1,0:T(8,128)(2,1)S(1)}, bf16[512,2048]{1,0:T(8,128)(2,1)}, u32[]{:S(2)}) copy-start(bf16[512,2048]{1,0:T(8,128)(2,1)} %param.19) | copy-start | bytes 6291460
  66.8 5.8 %copy-start.9 = (s32[1,128,8]{1,2,0:T(8,128)S(1)}, s32[1,128,8]{1,2,0:T(8,128)}, u32[]{:S(2)}) copy-start(s32[1,128,8]{1,2,0:T(8,128)} %param.23) | copy-start | bytes 12292
  66.8 6.7 %copy-start.10 = (f32[1,128,8]{1,2,0:T(8,128)S(1)}, f32[1,128,8]{1,2,0:T(8,128)}, u32[]{:S(2)}) copy-start(f32[1,128,8]{1,2,0:T(8,128)} %param.24) | copy-start | bytes 12292
  66.8 61.6 %all-to-all-start.1 = ((bf16[32,128,512]{2,1,0:T(8,128)(2,1)}), bf16[32,128,512]{2,1,0:T(8,128)(2,1)}, u32[]{:S(2)}, u32[]{:S(2)}) async-start(bf16[32,128,512]{2,1,0:T(8,128)(2,1)} %get-tuple-element.11), calls=%async_computation.1 | async-start | bytes 8388608 | tf_op jit(solution)/shard_map/all_to_all | solution.py:232
  77.6 4.0 %copy-start.11 = (s32[32]{0:T(128)S(1)}, s32[32]{0:T(128)}, u32[]{:S(2)}) copy-start(s32[32]{0:T(128)} %param.21) | copy-start | bytes 388
  77.6 5.2 %copy-start.2 = (bf16[1,128,2048]{2,1,0:T(8,128)(2,1)S(1)}, bf16[1,128,2048]{2,1,0:T(8,128)(2,1)}, u32[]{:S(2)}) copy-start(bf16[1,128,2048]{2,1,0:T(8,128)(2,1)} %param.14) | copy-start | bytes 1572868
  77.6 5.6 %copy-start.8 = (f32[2048]{0:T(1024)S(1)}, f32[2048]{0:T(1024)}, u32[]{:S(2)}) copy-start(f32[2048]{0:T(1024)} %param.15) | copy-start | bytes 24580
  81.6 4.0 %copy-start.3 = (bf16[512,2048]{1,0:T(8,128)(2,1)S(1)}, bf16[512,2048]{1,0:T(8,128)(2,1)}, u32[]{:S(2)}) copy-start(bf16[512,2048]{1,0:T(8,128)(2,1)} %copy.72) | copy-start | bytes 6291460
  153.6 53.8 %copy-start.5 = (bf16[2,256,2048]{2,1,0:T(8,128)(2,1)S(1)}, bf16[2,256,2048]{2,1,0:T(8,128)(2,1)}, u32[]{:S(2)}) copy-start(bf16[2,256,2048]{2,1,0:T(8,128)(2,1)} %param.27) | copy-start | bytes 6291460
  207.4 8.6 %collective-permute-start = (bf16[32,2,24,1024]{3,2,1,0:T(8,128)(2,1)}, bf16[32,2,24,1024]{3,2,1,0:T(8,128)(2,1)}, u32[]{:S(2)}, u32[]{:S(2)}) collective-permute-start(bf16[32,2,24,1024]{3,2,1,0:T(8,128)(2,1)} %all_to_all.21), channel_id=1, source_target_pairs={{0,1},{1,0},{2,3},{3,2},{4,5},{5,4},{6,7},{7,6},{8,9},{9,8},{10,11... | collective-permute-start | bytes 9437192 | tf_op jit(solution)/shard_map/ppermute | solution.py:283
  208.6 2.2 copy-start.6
  220.1 3.6 %collective-permute-start.2 = (bf16[768,1024]{1,0:T(8,128)(2,1)S(1)}, bf16[768,1024]{1,0:T(8,128)(2,1)S(1)}, u32[]{:S(2)}, u32[]{:S(2)}) collective-permute-start(bf16[768,1024]{1,0:T(8,128)(2,1)S(1)} %convolution_convert_fusion.2), channel_id=1, source_target_pairs={{0,1},{1,0},{2,3},{3,2},{4,5},{5,4},{6,7},{7,6},{8,9},{9,8},{10,11... | collective-permute-start | bytes 4718600 | tf_op jit(solution)/shard_map/ppermute | solution.py:295
  222.5 3.5 %collective-permute-start.1 = (bf16[768,1024]{1,0:T(8,128)(2,1)S(1)}, bf16[768,1024]{1,0:T(8,128)(2,1)S(1)}, u32[]{:S(2)}, u32[]{:S(2)}) collective-permute-start(bf16[768,1024]{1,0:T(8,128)(2,1)S(1)} %convolution_convert_fusion.4), channel_id=1, source_target_pairs={{0,1},{1,0},{2,3},{3,2},{4,5},{5,4},{6,7},{7,6},{8,9},{9,8},{10,11... | collective-permute-start | bytes 4718600 | tf_op jit(solution)/shard_map/ppermute | solution.py:295
  228.6 6.0 %copy-start.4 = (f32[128,1536]{1,0:T(8,128)S(1)}, f32[128,1536]{1,0:T(8,128)}, u32[]{:S(2)}) copy-start(f32[128,1536]{1,0:T(8,128)} %get-tuple-element.10) | copy-start | bytes 2359300
  228.6 49.6 %all-to-all-start.3 = ((bf16[32,2,24,1024]{3,2,1,0:T(8,128)(2,1)}), bf16[32,2,24,1024]{3,2,1,0:T(8,128)(2,1)}, u32[]{:S(2)}, u32[]{:S(2)}) async-start(bf16[32,2,24,1024]{3,2,1,0:T(8,128)(2,1)} %pad_maximum_fusion), calls=%async_computation.3 | async-start | bytes 6291456 | tf_op jit(solution)/shard_map/all_to_all | solution.py:302
  278.2 9.8 %copy-start.7 = (f32[2,128,512]{2,1,0:T(8,128)S(1)}, f32[2,128,512]{2,1,0:T(8,128)}, u32[]{:S(2)}) copy-start(f32[2,128,512]{2,1,0:T(8,128)} %get-tuple-element.7) | copy-start | bytes 1572868
  278.2 11.5 %copy-start.1 = (bf16[512,2048]{1,0:T(8,128)(2,1)S(1)}, bf16[512,2048]{1,0:T(8,128)(2,1)}, u32[]{:S(2)}) copy-start(bf16[512,2048]{1,0:T(8,128)(2,1)} %param.19) | copy-start | bytes 6291460

commit v17 on v16

--- a/solution.py
+++ b/solution.py
@@ -265,12 +265,12 @@
     other_core = 1 - core
     def halves(array, which):
         split = array.reshape(array.shape[:-1] + (2, 2, share_width))
-        taken = lax.dynamic_index_in_dim(split, which, axis=split.ndim - 2, keepdims=False)
+        taken = jnp.where(which == 0, split[..., 0, :], split[..., 1, :])
         return taken.reshape(array.shape[:-1] + (2 * share_width,))
 
     def row_halves(array, which):
         split = array.reshape((2, 2, share_width) + array.shape[1:])
-        taken = lax.dynamic_index_in_dim(split, which, axis=1, keepdims=False)
+        taken = jnp.where(which == 0, split[:, 0], split[:, 1])
         return taken.reshape((2 * share_width,) + array.shape[1:])
 
     half = 2 * share_width

time: 291 us -> 300 us (1.031)
  blocking collectives: 115 us -> 61.6 us
  waiting for transfers between devices: 70.2 us -> 112 us
  starting transfers between devices: 12.4 us -> 26.9 us
  local copies, waits for them, and re-layouts: 28.9 us -> 32.8 us
    all_to_all x1 -> x0, blocking collectives: 53.7 us -> none  [on_device(): lax.all_to_all(outgoing, 'grp', split_axis=0, concat_axis=0, tiled=True)]
    all_to_all x0 -> x1, waiting for transfers between devices: none -> 42.5 us  [on_device(): lax.all_to_all(outgoing, 'grp', split_axis=0, concat_axis=0, tiled=True)]
    all_to_all x0 -> x1, starting transfers between devices: none -> 12.9 us  [on_device(): lax.all_to_all(outgoing, 'grp', split_axis=0, concat_axis=0, tiled=True)]
  transfers between devices with their start and end apart: 5 -> 6, of which waited for: 4 -> 5; matrix products, arithmetic and copies ran while one was open for 15% -> 16% of each run, Pallas kernels for 0% -> 0%
where the time goes in v17:
time: 300 us; the launch traced here: 299 us
  waiting for transfers between devices  112 us (37%)
  blocking collectives  61.6 us (21%)
  local copies, waits for them, and re-layouts  32.8 us (11%)
  starting transfers between devices  26.9 us (9%)
  Pallas kernels  26.5 us (9%)
  matrix products  23 us (8%)
  other arithmetic  15.3 us (5%)
    all_to_all x1, blocking collectives, on_device(): lax.all_to_all(cache[part], 'grp', split_axis=0, concat_axis=0, tiled=True)  61.6 us
    all_to_all x1, waiting for transfers between devices, on_device(): lax.all_to_all(outgoing, 'grp', split_axis=0, concat_axis=0, tiled=True)  42.5 us
    all_to_all x1, waiting for transfers between devices, on_device(): lax.all_to_all(pair_sum, 'grp', split_axis=0, concat_axis=0, tiled=True)  42.2 us
    all_to_all x1, waiting for transfers between devices, on_device(): lax.all_to_all(cache[part], 'grp', split_axis=0, concat_axis=0, tiled=True)  24.9 us
    all_to_all x1, starting transfers between devices, on_device(): lax.all_to_all(outgoing, 'grp', split_axis=0, concat_axis=0, tiled=True)  12.9 us
    pallas_call x1, Pallas kernels, head_reduce(): pl.pallas_call(kernel, out_shape=(jax.ShapeDtypeStruct((2, rows, share),...  12.4 us
    pallas_call x1, Pallas kernels, attend(): pl.pallas_call(kernel, grid_spec=grid_spec, out_shape=jax.ShapeDtypeStruc...  8.71 us
    all_to_all x1, starting transfers between devices, on_device(): lax.all_to_all(pair_sum, 'grp', split_axis=0, concat_axis=0, tiled=True)  7.76 us
  transfers between devices with their start and end apart: 6, of which 5 were waited for; matrix products, arithmetic and copies ran while one was open for 16% of the time, Pallas kernels for 0%

profile of v17, /device:TPU:10, one launch (start us, length us, event | category | flops | bytes accessed | tf_op | source)
XLA Modules:
  0.0 298.8 jit_solution(9385841570563389030)
XLA Ops:
  0.0 5.3 %slice_bitcast_fusion = (bf16[32,128,512]{2,1,0:T(8,128)(2,1)}, bf16[32,128,512]{2,1,0:T(8,128)(2,1)S(1)}) fusion(bf16[2,32,128,512]{3,2,1,0:T(8,128)(2,1)} %param.20), kind=kLoop, calls=%fused_computation.4 | loop fusion | bytes 16777216 | tf_op jit(solution)/shard_map/squeeze | solution.py:232
  5.3 61.6 %all_to_all.20 = bf16[32,128,512]{2,1,0:T(8,128)(2,1)} all-to-all(bf16[32,128,512]{2,1,0:T(8,128)(2,1)S(1)} %get-tuple-element.12), channel_id=1, replica_groups=mesh['grp'=32,'head'=4] {'grp'}, dimensions={0} | all-to-all | bytes 8388608 | tf_op jit(solution)/shard_map/all_to_all | solution.py:232
  66.9 5.6 %all-to-all-start.1 = ((bf16[32,128,512]{2,1,0:T(8,128)(2,1)}), bf16[32,128,512]{2,1,0:T(8,128)(2,1)}, u32[]{:S(2)}, u32[]{:S(2)}) async-start(bf16[32,128,512]{2,1,0:T(8,128)(2,1)} %get-tuple-element.11), calls=%async_computation.1 | async-start | bytes 8388608 | tf_op jit(solution)/shard_map/all_to_all | solution.py:232
  72.5 4.0 %copy.74 = bf16[512,2048]{1,0:T(8,128)(2,1)} copy(bf16[512,2048]{0,1:T(8,128)(2,1)} %bitcast.128) | data formatting | bytes 4194304 | tf_op jit(solution)/shard_map/dot_general | solution.py:222
  76.5 4.0 %copy.72 = bf16[512,2048]{1,0:T(8,128)(2,1)} copy(bf16[512,2048]{0,1:T(8,128)(2,1)} %bitcast.129) | data formatting | bytes 4194304 | tf_op jit(solution)/shard_map/dot_general | solution.py:219
  82.3 2.4 fusion.18
  87.1 4.0 %copy.76 = bf16[512,2048]{1,0:T(8,128)(2,1)} copy(bf16[512,2048]{0,1:T(8,128)(2,1)} %bitcast.130) | data formatting | bytes 4194304 | tf_op jit(solution)/shard_map/dot_general | solution.py:225
  91.1 2.4 convolution_convert_fusion.6
  95.3 7.0 %convert_reduce_fusion = (bf16[128,1536]{1,0:T(8,128)(2,1)S(1)}, f32[128,1536]{1,0:T(8,128)}) fusion(s32[128,8]{1,0:T(8,128)S(1)} %bitcast_add_fusion.1, f32[128,8]{1,0:T(8,128)S(1)} %copy.67), kind=kLoop, calls=%fused_computation | loop fusion | flops 7471104 | bytes 1187840 | tf_op jit(solution)/shard_map/reduce_sum | solution.py:260
  103.4 24.9 %all-to-all-done.1 = bf16[32,128,512]{2,1,0:T(8,128)(2,1)} async-done(((bf16[32,128,512]{2,1,0:T(8,128)(2,1)}), bf16[32,128,512]{2,1,0:T(8,128)(2,1)}, u32[]{:S(2)}, u32[]{:S(2)}) %all-to-all-start.1) | async-done | bytes 4194336 | tf_op jit(solution)/shard_map/all_to_all | solution.py:232
  128.3 8.7 %shard_map.136 = bf16[128,512]{1,0:T(8,128)(2,1)} custom-call(s32[1]{0:T(128)} %dynamic_slice.7.length_ref, bf16[128,512]{1,0:T(8,128)(2,1)} %copy.73.q_ref, bf16[128,512]{1,0:T(8,128)(2,1)} %copy.75.kn_ref, bf16[128,512]{1,0:T(8,128)(2,1)} %copy.77.vn_ref, bf16[4096,512]{1,0:T(8,128)(2,1)} %bitcast.104, bf16[4096,512]{1,0:T(8,128)(2,1)} %bitcast.16.v_ref), custom_call_target="tpu_custom_call" | custom-call | tf_op jit(solution)/shard_map/pallas_call | solution.py:99
  137.0 2.2 convolution_convert_fusion.1.x_ref
  139.2 12.4 %shard_map.137 = (f32[2,128,512]{2,1,0:T(8,128)}, bf16[128,1024]{1,0:T(8,128)(2,1)}) custom-call(bf16[128,2048]{1,0:T(8,128)(2,1)} %convolution_convert_fusion.1.x_ref, f32[128,2048]{1,0:T(8,128)} %convert_bitcast_fusion.base_ref, f32[1,2048]{1,0:T(1,128)} %bitcast.144), custom_call_target="tpu_custom_call" | custom-call | tf_op jit(solution)/shard_map/pallas_call | solution.py:172
  151.6 3.6 %convolution_convert_fusion = bf16[1536,1024]{1,0:T(8,128)(2,1)} fusion(bf16[128,1024]{1,0:T(8,128)(2,1)} %get-tuple-element.8, bf16[128,1536]{1,0:T(8,128)(2,1)S(1)} %get-tuple-element.9), kind=kOutput, calls=%fused_computation.7 | convolution fusion | flops 404226048 | bytes 3801088 | tf_op jit(solution)/shard_map/dot_general | solution.py:277
  155.3 12.9 %all-to-all-start.2 = ((bf16[32,2,24,1024]{3,2,1,0:T(8,128)(2,1)}), bf16[32,2,24,1024]{3,2,1,0:T(8,128)(2,1)}, u32[]{:S(2)}, u32[]{:S(2)}) async-start(bf16[32,2,24,1024]{3,2,1,0:T(8,128)(2,1)} %bitcast.109), calls=%async_computation.2 | async-start | bytes 6291456 | tf_op jit(solution)/shard_map/all_to_all | solution.py:281
  169.3 42.5 %all-to-all-done.2 = bf16[32,2,24,1024]{3,2,1,0:T(8,128)(2,1)} async-done(((bf16[32,2,24,1024]{3,2,1,0:T(8,128)(2,1)}), bf16[32,2,24,1024]{3,2,1,0:T(8,128)(2,1)}, u32[]{:S(2)}, u32[]{:S(2)}) %all-to-all-start.2) | async-done | bytes 3145760 | tf_op jit(solution)/shard_map/all_to_all | solution.py:281
  211.8 2.8 fusion.24
  218.9 2.2 fusion.23
  223.5 2.2 fusion.22
  234.1 2.0 pad_maximum_fusion
  236.1 7.8 %all-to-all-start.3 = ((bf16[32,2,24,1024]{3,2,1,0:T(8,128)(2,1)}), bf16[32,2,24,1024]{3,2,1,0:T(8,128)(2,1)}, u32[]{:S(2)}, u32[]{:S(2)}) async-start(bf16[32,2,24,1024]{3,2,1,0:T(8,128)(2,1)} %pad_maximum_fusion), calls=%async_computation.3 | async-start | bytes 6291456 | tf_op jit(solution)/shard_map/all_to_all | solution.py:302
  245.1 42.2 %all-to-all-done.3 = bf16[32,2,24,1024]{3,2,1,0:T(8,128)(2,1)} async-done(((bf16[32,2,24,1024]{3,2,1,0:T(8,128)(2,1)}), bf16[32,2,24,1024]{3,2,1,0:T(8,128)(2,1)}, u32[]{:S(2)}, u32[]{:S(2)}) %all-to-all-start.3) | async-done | bytes 3145760 | tf_op jit(solution)/shard_map/all_to_all | solution.py:302
  287.3 3.8 %convolution_reduce_fusion = f32[128,1024]{1,0:T(8,128)S(1)} fusion(bf16[3,128,1536]{2,1,0:T(8,128)(2,1)} %bitcast.138, bf16[1536,1024,1]{1,0,2:T(8,128)(2,1)} %bitcast.50), kind=kOutput, calls=%fused_computation.16 | convolution fusion | flops 1208221696 | bytes 4849664 | tf_op jit(solution)/shard_map/dot_general | solution.py:310
  291.8 5.3 %shard_map.138 = bf16[128,512]{1,0:T(8,128)(2,1)} custom-call(bf16[128,512]{1,0:T(8,128)(2,1)} %select_convert_fusion.x_ref), custom_call_target="tpu_custom_call" | custom-call | tf_op jit(solution)/shard_map/pallas_call | solution.py:47
  (74 shorter events, 26.7 us)
Async XLA Ops:
  0.0 137.0 %copy-start = (bf16[512,2048]{1,0:T(8,128)(2,1)S(1)}, bf16[512,2048]{1,0:T(8,128)(2,1)}, u32[]{:S(2)}) copy-start(bf16[512,2048]{1,0:T(8,128)(2,1)} %param.19) | copy-start | bytes 6291460
  66.9 61.4 %all-to-all-start.1 = ((bf16[32,128,512]{2,1,0:T(8,128)(2,1)}), bf16[32,128,512]{2,1,0:T(8,128)(2,1)}, u32[]{:S(2)}, u32[]{:S(2)}) async-start(bf16[32,128,512]{2,1,0:T(8,128)(2,1)} %get-tuple-element.11), calls=%async_computation.1 | async-start | bytes 8388608 | tf_op jit(solution)/shard_map/all_to_all | solution.py:232
  76.5 4.0 %copy-start.11 = (s32[32]{0:T(128)S(1)}, s32[32]{0:T(128)}, u32[]{:S(2)}) copy-start(s32[32]{0:T(128)} %param.21) | copy-start | bytes 388
  76.5 5.4 %copy-start.2 = (bf16[1,128,2048]{2,1,0:T(8,128)(2,1)S(1)}, bf16[1,128,2048]{2,1,0:T(8,128)(2,1)}, u32[]{:S(2)}) copy-start(bf16[1,128,2048]{2,1,0:T(8,128)(2,1)} %param.14) | copy-start | bytes 1572868
  76.5 5.8 %copy-start.8 = (f32[2048]{0:T(1024)S(1)}, f32[2048]{0:T(1024)}, u32[]{:S(2)}) copy-start(f32[2048]{0:T(1024)} %param.15) | copy-start | bytes 24580
  80.5 4.2 %copy-start.3 = (bf16[512,2048]{1,0:T(8,128)(2,1)S(1)}, bf16[512,2048]{1,0:T(8,128)(2,1)}, u32[]{:S(2)}) copy-start(bf16[512,2048]{1,0:T(8,128)(2,1)} %copy.72) | copy-start | bytes 6291460
  91.1 3.2 %copy-start.9 = (s32[1,128,8]{1,2,0:T(8,128)S(1)}, s32[1,128,8]{1,2,0:T(8,128)}, u32[]{:S(2)}) copy-start(s32[1,128,8]{1,2,0:T(8,128)} %param.23) | copy-start | bytes 12292
  91.1 4.1 %copy-start.10 = (f32[1,128,8]{1,2,0:T(8,128)S(1)}, f32[1,128,8]{1,2,0:T(8,128)}, u32[]{:S(2)}) copy-start(f32[1,128,8]{1,2,0:T(8,128)} %param.24) | copy-start | bytes 12292
  155.3 12.9 %copy-start.6 = (bf16[2,2048,256]{2,1,0:T(8,128)(2,1)S(1)}, bf16[2,2048,256]{2,1,0:T(8,128)(2,1)}, u32[]{:S(2)}) copy-start(bf16[2,2048,256]{2,1,0:T(8,128)(2,1)} %param.25) | copy-start | bytes 6291460
  155.3 56.5 %all-to-all-start.2 = ((bf16[32,2,24,1024]{3,2,1,0:T(8,128)(2,1)}), bf16[32,2,24,1024]{3,2,1,0:T(8,128)(2,1)}, u32[]{:S(2)}, u32[]{:S(2)}) async-start(bf16[32,2,24,1024]{3,2,1,0:T(8,128)(2,1)} %bitcast.109), calls=%async_computation.2 | async-start | bytes 6291456 | tf_op jit(solution)/shard_map/all_to_all | solution.py:281
  211.8 11.7 %collective-permute-start = (bf16[32,2,24,1024]{3,2,1,0:T(8,128)(2,1)}, bf16[32,2,24,1024]{3,2,1,0:T(8,128)(2,1)}, u32[]{:S(2)}, u32[]{:S(2)}) collective-permute-start(bf16[32,2,24,1024]{3,2,1,0:T(8,128)(2,1)} %all-to-all-done.2), channel_id=1, source_target_pairs={{0,1},{1,0},{2,3},{3,2},{4,5},{5,4},{6,7},{7,6},{8,9},{9,8},{10,11... | collective-permute-start | bytes 9437192 | tf_op jit(solution)/shard_map/ppermute | solution.py:283
  216.6 1.9 copy-start.4
  227.5 3.6 %collective-permute-start.1 = (bf16[768,1024]{1,0:T(8,128)(2,1)S(1)}, bf16[768,1024]{1,0:T(8,128)(2,1)S(1)}, u32[]{:S(2)}, u32[]{:S(2)}) collective-permute-start(bf16[768,1024]{1,0:T(8,128)(2,1)S(1)} %convolution_convert_fusion.4), channel_id=1, source_target_pairs={{0,1},{1,0},{2,3},{3,2},{4,5},{5,4},{6,7},{7,6},{8,9},{9,8},{10,11... | collective-permute-start | bytes 4718600 | tf_op jit(solution)/shard_map/ppermute | solution.py:295
  230.0 3.5 %collective-permute-start.2 = (bf16[768,1024]{1,0:T(8,128)(2,1)S(1)}, bf16[768,1024]{1,0:T(8,128)(2,1)S(1)}, u32[]{:S(2)}, u32[]{:S(2)}) collective-permute-start(bf16[768,1024]{1,0:T(8,128)(2,1)S(1)} %convolution_convert_fusion.2), channel_id=1, source_target_pairs={{0,1},{1,0},{2,3},{3,2},{4,5},{5,4},{6,7},{7,6},{8,9},{9,8},{10,11... | collective-permute-start | bytes 4718600 | tf_op jit(solution)/shard_map/ppermute | solution.py:295
  236.1 7.8 %copy-start.5 = (f32[128,1536]{1,0:T(8,128)S(1)}, f32[128,1536]{1,0:T(8,128)}, u32[]{:S(2)}) copy-start(f32[128,1536]{1,0:T(8,128)} %get-tuple-element.10) | copy-start | bytes 2359300
  236.1 51.2 %all-to-all-start.3 = ((bf16[32,2,24,1024]{3,2,1,0:T(8,128)(2,1)}), bf16[32,2,24,1024]{3,2,1,0:T(8,128)(2,1)}, u32[]{:S(2)}, u32[]{:S(2)}) async-start(bf16[32,2,24,1024]{3,2,1,0:T(8,128)(2,1)} %pad_maximum_fusion), calls=%async_computation.3 | async-start | bytes 6291456 | tf_op jit(solution)/shard_map/all_to_all | solution.py:302
  287.3 9.8 %copy-start.7 = (f32[2,128,512]{2,1,0:T(8,128)S(1)}, f32[2,128,512]{2,1,0:T(8,128)}, u32[]{:S(2)}) copy-start(f32[2,128,512]{2,1,0:T(8,128)} %get-tuple-element.7) | copy-start | bytes 1572868
  287.3 11.5 %copy-start.1 = (bf16[512,2048]{1,0:T(8,128)(2,1)S(1)}, bf16[512,2048]{1,0:T(8,128)(2,1)}, u32[]{:S(2)}) copy-start(bf16[512,2048]{1,0:T(8,128)(2,1)} %param.19) | copy-start | bytes 6291460

commit v18 on v16

--- a/solution.py
+++ b/solution.py
@@ -132,16 +132,19 @@
             )
             copy.start()
             halves_out.append(copy)
+        swaps = []
         for half in range(2):
             halves_out[half].wait_recv()
             mine = x_ref[:, columns(2 * half + core)].astype(jnp.float32)
             send_buf[half] = (mine + part_in[half].astype(jnp.float32)).astype(send_buf.dtype)
-        swap = pltpu.make_async_remote_copy(
-            src_ref=send_buf, dst_ref=sum_in, send_sem=send_sem.at[2], recv_sem=recv_sem.at[2],
-            device_id=(group, across), device_id_type=mesh_kind,
-        )
-        swap.start()
-        swap.wait_recv()
+            swap = pltpu.make_async_remote_copy(
+                src_ref=send_buf.at[half], dst_ref=sum_in.at[half], send_sem=send_sem.at[2 + half],
+                recv_sem=recv_sem.at[2 + half], device_id=(group, across), device_id_type=mesh_kind,
+            )
+            swap.start()
+            swaps.append(swap)
+        for swap in swaps:
+            swap.wait_recv()
         square = jnp.zeros((rows, 1), jnp.float32)
         for half in range(2):
             total = (
@@ -153,7 +156,7 @@
             square = square + jnp.sum(total * total, axis=1, keepdims=True)
         sq_out[...] = jnp.broadcast_to(square, sq_out.shape)
         last = pltpu.make_async_remote_copy(
-            src_ref=sq_out, dst_ref=sq_in, send_sem=send_sem.at[3], recv_sem=recv_sem.at[3],
+            src_ref=sq_out, dst_ref=sq_in, send_sem=send_sem.at[4], recv_sem=recv_sem.at[4],
             device_id=(group, partner), device_id_type=mesh_kind,
         )
         last.start()
@@ -165,7 +168,8 @@
             ).astype(normed_ref.dtype)
         for copy in halves_out:
             copy.wait_send()
-        swap.wait_send()
+        for swap in swaps:
+            swap.wait_send()
         last.wait_send()
 
     vmem = pl.BlockSpec(memory_space=pltpu.VMEM)
@@ -183,8 +187,8 @@
             pltpu.VMEM((2, rows, share), x.dtype),
             pltpu.VMEM((rows, 128), jnp.float32),
             pltpu.VMEM((rows, 128), jnp.float32),
-            pltpu.SemaphoreType.DMA((4,)),
-            pltpu.SemaphoreType.DMA((4,)),
+            pltpu.SemaphoreType.DMA((5,)),
+            pltpu.SemaphoreType.DMA((5,)),
         ],
         compiler_params=pltpu.CompilerParams(collective_id=ident, has_side_effects=True),
     )(x, base, gain.reshape(1, -1))

time: 291 us -> 291 us (level)
  no operation moved by 1% of the time
where the time goes in v18:
time: 291 us; the launch traced here: 289 us
  blocking collectives  115 us (40%)
  waiting for transfers between devices  70.1 us (24%)
  local copies, waits for them, and re-layouts  28.9 us (10%)
  Pallas kernels  26.3 us (9%)
  matrix products  21.3 us (7%)
  other arithmetic  14.8 us (5%)
  starting transfers between devices  12.4 us (4%)
    all_to_all x1, blocking collectives, on_device(): lax.all_to_all(cache[part], 'grp', split_axis=0, concat_axis=0, tiled=True)  61.6 us
    all_to_all x1, blocking collectives, on_device(): lax.all_to_all(outgoing, 'grp', split_axis=0, concat_axis=0, tiled=True)  53.6 us
    all_to_all x1, waiting for transfers between devices, on_device(): lax.all_to_all(pair_sum, 'grp', split_axis=0, concat_axis=0, tiled=True)  42.2 us
    all_to_all x1, waiting for transfers between devices, on_device(): lax.all_to_all(cache[part], 'grp', split_axis=0, concat_axis=0, tiled=True)  25.1 us
    pallas_call x1, Pallas kernels, head_reduce(): pl.pallas_call(kernel, out_shape=(jax.ShapeDtypeStruct((2, rows, share),...  12.4 us
    pallas_call x1, Pallas kernels, attend(): pl.pallas_call(kernel, grid_spec=grid_spec, out_shape=jax.ShapeDtypeStruc...  8.57 us
    reduce_sum x1, other arithmetic, on_device(): dispatch = jnp.sum(place.astype(jnp.float32), axis=1).astype(jnp.bfloat16)  6.98 us
    all_to_all x1, starting transfers between devices, on_device(): lax.all_to_all(pair_sum, 'grp', split_axis=0, concat_axis=0, tiled=True)  6.02 us
  transfers between devices with their start and end apart: 5, of which 4 were waited for; matrix products, arithmetic and copies ran while one was open for 15% of the time, Pallas kernels for 0%

profile of v18, /device:TPU:10, one launch (start us, length us, event | category | flops | bytes accessed | tf_op | source)
XLA Modules:
  0.0 289.4 jit_solution(9259307577186312444)
XLA Ops:
  0.0 5.3 %slice_bitcast_fusion = (bf16[32,128,512]{2,1,0:T(8,128)(2,1)}, bf16[32,128,512]{2,1,0:T(8,128)(2,1)S(1)}) fusion(bf16[2,32,128,512]{3,2,1,0:T(8,128)(2,1)} %param.20), kind=kLoop, calls=%fused_computation.4 | loop fusion | bytes 16777216 | tf_op jit(solution)/shard_map/squeeze | solution.py:236
  5.3 61.6 %all_to_all.20 = bf16[32,128,512]{2,1,0:T(8,128)(2,1)} all-to-all(bf16[32,128,512]{2,1,0:T(8,128)(2,1)S(1)} %get-tuple-element.12), channel_id=1, replica_groups=mesh['grp'=32,'head'=4] {'grp'}, dimensions={0} | all-to-all | bytes 8388608 | tf_op jit(solution)/shard_map/all_to_all | solution.py:236
  66.8 5.7 %all-to-all-start.1 = ((bf16[32,128,512]{2,1,0:T(8,128)(2,1)}), bf16[32,128,512]{2,1,0:T(8,128)(2,1)}, u32[]{:S(2)}, u32[]{:S(2)}) async-start(bf16[32,128,512]{2,1,0:T(8,128)(2,1)} %get-tuple-element.11), calls=%async_computation.1 | async-start | bytes 8388608 | tf_op jit(solution)/shard_map/all_to_all | solution.py:236
  73.6 4.0 %copy.74 = bf16[512,2048]{1,0:T(8,128)(2,1)} copy(bf16[512,2048]{0,1:T(8,128)(2,1)} %bitcast.128) | data formatting | bytes 4194304 | tf_op jit(solution)/shard_map/dot_general | solution.py:226
  77.6 4.0 %copy.72 = bf16[512,2048]{1,0:T(8,128)(2,1)} copy(bf16[512,2048]{0,1:T(8,128)(2,1)} %bitcast.129) | data formatting | bytes 4194304 | tf_op jit(solution)/shard_map/dot_general | solution.py:223
  83.2 2.4 fusion.18
  88.1 4.0 %copy.76 = bf16[512,2048]{1,0:T(8,128)(2,1)} copy(bf16[512,2048]{0,1:T(8,128)(2,1)} %bitcast.130) | data formatting | bytes 4194304 | tf_op jit(solution)/shard_map/dot_general | solution.py:229
  92.1 2.4 convolution_convert_fusion.6
  95.2 7.0 %convert_reduce_fusion = (bf16[128,1536]{1,0:T(8,128)(2,1)S(1)}, f32[128,1536]{1,0:T(8,128)}) fusion(s32[128,8]{1,0:T(8,128)S(1)} %bitcast_add_fusion.1, f32[128,8]{1,0:T(8,128)S(1)} %copy.67), kind=kLoop, calls=%fused_computation | loop fusion | flops 7471104 | bytes 1187840 | tf_op jit(solution)/shard_map/reduce_sum | solution.py:264
  103.3 25.1 %all-to-all-done.1 = bf16[32,128,512]{2,1,0:T(8,128)(2,1)} async-done(((bf16[32,128,512]{2,1,0:T(8,128)(2,1)}), bf16[32,128,512]{2,1,0:T(8,128)(2,1)}, u32[]{:S(2)}, u32[]{:S(2)}) %all-to-all-start.1) | async-done | bytes 4194336 | tf_op jit(solution)/shard_map/all_to_all | solution.py:236
  128.4 8.6 %shard_map.136 = bf16[128,512]{1,0:T(8,128)(2,1)} custom-call(s32[1]{0:T(128)} %dynamic_slice.45.length_ref, bf16[128,512]{1,0:T(8,128)(2,1)} %copy.73.q_ref, bf16[128,512]{1,0:T(8,128)(2,1)} %copy.75.kn_ref, bf16[128,512]{1,0:T(8,128)(2,1)} %copy.77.vn_ref, bf16[4096,512]{1,0:T(8,128)(2,1)} %bitcast.104, bf16[4096,512]{1,0:T(8,128)(2,1)} %bitcast.16.v_ref), custom_call_target="tpu_custom_call" | custom-call | tf_op jit(solution)/shard_map/pallas_call | solution.py:99
  137.0 2.2 convolution_convert_fusion.1.x_ref
  139.2 12.4 %shard_map.137 = (f32[2,128,512]{2,1,0:T(8,128)}, bf16[128,1024]{1,0:T(8,128)(2,1)}) custom-call(bf16[128,2048]{1,0:T(8,128)(2,1)} %convolution_convert_fusion.1.x_ref, f32[128,2048]{1,0:T(8,128)} %convert_bitcast_fusion.base_ref, f32[1,2048]{1,0:T(1,128)} %bitcast.144), custom_call_target="tpu_custom_call" | custom-call | tf_op jit(solution)/shard_map/pallas_call | solution.py:176
  151.6 1.9 convolution_convert_fusion
  153.6 53.6 %all_to_all.21 = bf16[32,2,24,1024]{3,2,1,0:T(8,128)(2,1)} all-to-all(bf16[32,2,24,1024]{3,2,1,0:T(8,128)(2,1)S(1)} %bitcast.109), channel_id=1, replica_groups=mesh['grp'=32,'head'=4] {'grp'}, dimensions={0} | all-to-all | bytes 6291456 | tf_op jit(solution)/shard_map/all_to_all | solution.py:285
  208.4 1.8 fusion.26
  211.3 2.2 fusion.23
  215.9 2.2 fusion.22
  224.1 1.7 collective-permute-done.1
  226.4 2.0 pad_maximum_fusion
  228.4 6.0 %all-to-all-start.3 = ((bf16[32,2,24,1024]{3,2,1,0:T(8,128)(2,1)}), bf16[32,2,24,1024]{3,2,1,0:T(8,128)(2,1)}, u32[]{:S(2)}, u32[]{:S(2)}) async-start(bf16[32,2,24,1024]{3,2,1,0:T(8,128)(2,1)} %pad_maximum_fusion), calls=%async_computation.3 | async-start | bytes 6291456 | tf_op jit(solution)/shard_map/all_to_all | solution.py:306
  235.7 42.2 %all-to-all-done.3 = bf16[32,2,24,1024]{3,2,1,0:T(8,128)(2,1)} async-done(((bf16[32,2,24,1024]{3,2,1,0:T(8,128)(2,1)}), bf16[32,2,24,1024]{3,2,1,0:T(8,128)(2,1)}, u32[]{:S(2)}, u32[]{:S(2)}) %all-to-all-start.3) | async-done | bytes 3145760 | tf_op jit(solution)/shard_map/all_to_all | solution.py:306
  277.9 3.8 %convolution_reduce_fusion = f32[128,1024]{1,0:T(8,128)S(1)} fusion(bf16[3,128,1536]{2,1,0:T(8,128)(2,1)} %bitcast.138, bf16[1536,1024,1]{1,0,2:T(8,128)(2,1)} %bitcast.50), kind=kOutput, calls=%fused_computation.16 | convolution fusion | flops 1208221696 | bytes 4849664 | tf_op jit(solution)/shard_map/dot_general | solution.py:314
  282.4 5.3 %shard_map.138 = bf16[128,512]{1,0:T(8,128)(2,1)} custom-call(bf16[128,512]{1,0:T(8,128)(2,1)} %select_convert_fusion.x_ref), custom_call_target="tpu_custom_call" | custom-call | tf_op jit(solution)/shard_map/pallas_call | solution.py:47
  (73 shorter events, 21.6 us)
Async XLA Ops:
  0.0 137.0 %copy-start = (bf16[512,2048]{1,0:T(8,128)(2,1)S(1)}, bf16[512,2048]{1,0:T(8,128)(2,1)}, u32[]{:S(2)}) copy-start(bf16[512,2048]{1,0:T(8,128)(2,1)} %param.19) | copy-start | bytes 6291460
  66.8 5.8 %copy-start.9 = (s32[1,128,8]{1,2,0:T(8,128)S(1)}, s32[1,128,8]{1,2,0:T(8,128)}, u32[]{:S(2)}) copy-start(s32[1,128,8]{1,2,0:T(8,128)} %param.23) | copy-start | bytes 12292
  66.8 6.7 %copy-start.10 = (f32[1,128,8]{1,2,0:T(8,128)S(1)}, f32[1,128,8]{1,2,0:T(8,128)}, u32[]{:S(2)}) copy-start(f32[1,128,8]{1,2,0:T(8,128)} %param.24) | copy-start | bytes 12292
  66.8 61.6 %all-to-all-start.1 = ((bf16[32,128,512]{2,1,0:T(8,128)(2,1)}), bf16[32,128,512]{2,1,0:T(8,128)(2,1)}, u32[]{:S(2)}, u32[]{:S(2)}) async-start(bf16[32,128,512]{2,1,0:T(8,128)(2,1)} %get-tuple-element.11), calls=%async_computation.1 | async-start | bytes 8388608 | tf_op jit(solution)/shard_map/all_to_all | solution.py:236
  77.6 4.0 %copy-start.11 = (s32[32]{0:T(128)S(1)}, s32[32]{0:T(128)}, u32[]{:S(2)}) copy-start(s32[32]{0:T(128)} %param.21) | copy-start | bytes 388
  77.6 5.2 %copy-start.2 = (bf16[1,128,2048]{2,1,0:T(8,128)(2,1)S(1)}, bf16[1,128,2048]{2,1,0:T(8,128)(2,1)}, u32[]{:S(2)}) copy-start(bf16[1,128,2048]{2,1,0:T(8,128)(2,1)} %param.14) | copy-start | bytes 1572868
  77.6 5.6 %copy-start.8 = (f32[2048]{0:T(1024)S(1)}, f32[2048]{0:T(1024)}, u32[]{:S(2)}) copy-start(f32[2048]{0:T(1024)} %param.15) | copy-start | bytes 24580
  81.6 4.0 %copy-start.3 = (bf16[512,2048]{1,0:T(8,128)(2,1)S(1)}, bf16[512,2048]{1,0:T(8,128)(2,1)}, u32[]{:S(2)}) copy-start(bf16[512,2048]{1,0:T(8,128)(2,1)} %copy.72) | copy-start | bytes 6291460
  153.6 53.6 %copy-start.5 = (bf16[2,256,2048]{2,1,0:T(8,128)(2,1)S(1)}, bf16[2,256,2048]{2,1,0:T(8,128)(2,1)}, u32[]{:S(2)}) copy-start(bf16[2,256,2048]{2,1,0:T(8,128)(2,1)} %param.27) | copy-start | bytes 6291460
  207.2 8.6 %collective-permute-start = (bf16[32,2,24,1024]{3,2,1,0:T(8,128)(2,1)}, bf16[32,2,24,1024]{3,2,1,0:T(8,128)(2,1)}, u32[]{:S(2)}, u32[]{:S(2)}) collective-permute-start(bf16[32,2,24,1024]{3,2,1,0:T(8,128)(2,1)} %all_to_all.21), channel_id=1, source_target_pairs={{0,1},{1,0},{2,3},{3,2},{4,5},{5,4},{6,7},{7,6},{8,9},{9,8},{10,11... | collective-permute-start | bytes 9437192 | tf_op jit(solution)/shard_map/ppermute | solution.py:287
  208.4 2.2 copy-start.6
  219.9 3.6 %collective-permute-start.2 = (bf16[768,1024]{1,0:T(8,128)(2,1)S(1)}, bf16[768,1024]{1,0:T(8,128)(2,1)S(1)}, u32[]{:S(2)}, u32[]{:S(2)}) collective-permute-start(bf16[768,1024]{1,0:T(8,128)(2,1)S(1)} %convolution_convert_fusion.2), channel_id=1, source_target_pairs={{0,1},{1,0},{2,3},{3,2},{4,5},{5,4},{6,7},{7,6},{8,9},{9,8},{10,11... | collective-permute-start | bytes 4718600 | tf_op jit(solution)/shard_map/ppermute | solution.py:299
  222.3 3.5 %collective-permute-start.1 = (bf16[768,1024]{1,0:T(8,128)(2,1)S(1)}, bf16[768,1024]{1,0:T(8,128)(2,1)S(1)}, u32[]{:S(2)}, u32[]{:S(2)}) collective-permute-start(bf16[768,1024]{1,0:T(8,128)(2,1)S(1)} %convolution_convert_fusion.4), channel_id=1, source_target_pairs={{0,1},{1,0},{2,3},{3,2},{4,5},{5,4},{6,7},{7,6},{8,9},{9,8},{10,11... | collective-permute-start | bytes 4718600 | tf_op jit(solution)/shard_map/ppermute | solution.py:299
  228.4 6.1 %copy-start.4 = (f32[128,1536]{1,0:T(8,128)S(1)}, f32[128,1536]{1,0:T(8,128)}, u32[]{:S(2)}) copy-start(f32[128,1536]{1,0:T(8,128)} %get-tuple-element.10) | copy-start | bytes 2359300
  228.4 49.5 %all-to-all-start.3 = ((bf16[32,2,24,1024]{3,2,1,0:T(8,128)(2,1)}), bf16[32,2,24,1024]{3,2,1,0:T(8,128)(2,1)}, u32[]{:S(2)}, u32[]{:S(2)}) async-start(bf16[32,2,24,1024]{3,2,1,0:T(8,128)(2,1)} %pad_maximum_fusion), calls=%async_computation.3 | async-start | bytes 6291456 | tf_op jit(solution)/shard_map/all_to_all | solution.py:306
  277.9 9.8 %copy-start.7 = (f32[2,128,512]{2,1,0:T(8,128)S(1)}, f32[2,128,512]{2,1,0:T(8,128)}, u32[]{:S(2)}) copy-start(f32[2,128,512]{2,1,0:T(8,128)} %get-tuple-element.7) | copy-start | bytes 1572868
  277.9 11.5 %copy-start.1 = (bf16[512,2048]{1,0:T(8,128)(2,1)S(1)}, bf16[512,2048]{1,0:T(8,128)(2,1)}, u32[]{:S(2)}) copy-start(bf16[512,2048]{1,0:T(8,128)(2,1)} %param.19) | copy-start | bytes 6291460

commit v19 on v18

--- a/solution.py
+++ b/solution.py
@@ -47,8 +47,8 @@
     return pl.pallas_call(
         kernel,
         out_shape=jax.ShapeDtypeStruct(x.shape, x.dtype),
-        in_specs=[pl.BlockSpec(memory_space=pl.ANY)],
-        out_specs=pl.BlockSpec(memory_space=pl.ANY),
+        in_specs=[pl.BlockSpec(memory_space=pltpu.VMEM)],
+        out_specs=pl.BlockSpec(memory_space=pltpu.VMEM),
         scratch_shapes=[pltpu.SemaphoreType.DMA(()), pltpu.SemaphoreType.DMA(())],
         compiler_params=pltpu.CompilerParams(collective_id=ident, has_side_effects=True),
     )(x)

time: 291 us -> 292 us (level)
  no operation moved by 1% of the time
where the time goes in v19:
time: 292 us; the launch traced here: 291 us
  blocking collectives  115 us (39%)
  waiting for transfers between devices  70.1 us (24%)
  local copies, waits for them, and re-layouts  28.9 us (10%)
  Pallas kernels  27.6 us (9%)
  matrix products  21.3 us (7%)
  other arithmetic  14.8 us (5%)
  starting transfers between devices  12.4 us (4%)
    all_to_all x1, blocking collectives, on_device(): lax.all_to_all(cache[part], 'grp', split_axis=0, concat_axis=0, tiled=True)  61.6 us
    all_to_all x1, blocking collectives, on_device(): lax.all_to_all(outgoing, 'grp', split_axis=0, concat_axis=0, tiled=True)  53.6 us
    all_to_all x1, waiting for transfers between devices, on_device(): lax.all_to_all(pair_sum, 'grp', split_axis=0, concat_axis=0, tiled=True)  42.2 us
    all_to_all x1, waiting for transfers between devices, on_device(): lax.all_to_all(cache[part], 'grp', split_axis=0, concat_axis=0, tiled=True)  25.1 us
    pallas_call x1, Pallas kernels, head_reduce(): pl.pallas_call(kernel, out_shape=(jax.ShapeDtypeStruct((2, rows, share),...  12.4 us
    pallas_call x1, Pallas kernels, attend(): pl.pallas_call(kernel, grid_spec=grid_spec, out_shape=jax.ShapeDtypeStruc...  8.57 us
    reduce_sum x1, other arithmetic, on_device(): dispatch = jnp.sum(place.astype(jnp.float32), axis=1).astype(jnp.bfloat16)  6.98 us
    pallas_call x1, Pallas kernels, peer_swap(): pl.pallas_call(kernel, out_shape=jax.ShapeDtypeStruct(x.shape, x.dtype),...  6.56 us
  transfers between devices with their start and end apart: 5, of which 4 were waited for; matrix products, arithmetic and copies ran while one was open for 15% of the time, Pallas kernels for 0%

profile of v19, /device:TPU:10, one launch (start us, length us, event | category | flops | bytes accessed | tf_op | source)
XLA Modules:
  0.0 290.7 jit_solution(12036611417512760701)
XLA Ops:
  0.0 5.3 %slice_bitcast_fusion = (bf16[32,128,512]{2,1,0:T(8,128)(2,1)}, bf16[32,128,512]{2,1,0:T(8,128)(2,1)S(1)}) fusion(bf16[2,32,128,512]{3,2,1,0:T(8,128)(2,1)} %param.20), kind=kLoop, calls=%fused_computation.4 | loop fusion | bytes 16777216 | tf_op jit(solution)/shard_map/squeeze | solution.py:236
  5.3 61.6 %all_to_all.20 = bf16[32,128,512]{2,1,0:T(8,128)(2,1)} all-to-all(bf16[32,128,512]{2,1,0:T(8,128)(2,1)S(1)} %get-tuple-element.12), channel_id=1, replica_groups=mesh['grp'=32,'head'=4] {'grp'}, dimensions={0} | all-to-all | bytes 8388608 | tf_op jit(solution)/shard_map/all_to_all | solution.py:236
  66.8 5.7 %all-to-all-start.1 = ((bf16[32,128,512]{2,1,0:T(8,128)(2,1)}), bf16[32,128,512]{2,1,0:T(8,128)(2,1)}, u32[]{:S(2)}, u32[]{:S(2)}) async-start(bf16[32,128,512]{2,1,0:T(8,128)(2,1)} %get-tuple-element.11), calls=%async_computation.1 | async-start | bytes 8388608 | tf_op jit(solution)/shard_map/all_to_all | solution.py:236
  73.6 4.0 %copy.74 = bf16[512,2048]{1,0:T(8,128)(2,1)} copy(bf16[512,2048]{0,1:T(8,128)(2,1)} %bitcast.128) | data formatting | bytes 4194304 | tf_op jit(solution)/shard_map/dot_general | solution.py:226
  77.6 4.0 %copy.72 = bf16[512,2048]{1,0:T(8,128)(2,1)} copy(bf16[512,2048]{0,1:T(8,128)(2,1)} %bitcast.129) | data formatting | bytes 4194304 | tf_op jit(solution)/shard_map/dot_general | solution.py:223
  83.2 2.4 fusion.18
  88.1 4.0 %copy.76 = bf16[512,2048]{1,0:T(8,128)(2,1)} copy(bf16[512,2048]{0,1:T(8,128)(2,1)} %bitcast.130) | data formatting | bytes 4194304 | tf_op jit(solution)/shard_map/dot_general | solution.py:229
  92.1 2.4 convolution_convert_fusion.6
  95.2 7.0 %convert_reduce_fusion = (bf16[128,1536]{1,0:T(8,128)(2,1)S(1)}, f32[128,1536]{1,0:T(8,128)}) fusion(s32[128,8]{1,0:T(8,128)S(1)} %bitcast_add_fusion.1, f32[128,8]{1,0:T(8,128)S(1)} %copy.67), kind=kLoop, calls=%fused_computation | loop fusion | flops 7471104 | bytes 1187840 | tf_op jit(solution)/shard_map/reduce_sum | solution.py:264
  103.3 25.1 %all-to-all-done.1 = bf16[32,128,512]{2,1,0:T(8,128)(2,1)} async-done(((bf16[32,128,512]{2,1,0:T(8,128)(2,1)}), bf16[32,128,512]{2,1,0:T(8,128)(2,1)}, u32[]{:S(2)}, u32[]{:S(2)}) %all-to-all-start.1) | async-done | bytes 4194336 | tf_op jit(solution)/shard_map/all_to_all | solution.py:236
  128.4 8.6 %shard_map.136 = bf16[128,512]{1,0:T(8,128)(2,1)} custom-call(s32[1]{0:T(128)} %dynamic_slice.45.length_ref, bf16[128,512]{1,0:T(8,128)(2,1)} %copy.73.q_ref, bf16[128,512]{1,0:T(8,128)(2,1)} %copy.75.kn_ref, bf16[128,512]{1,0:T(8,128)(2,1)} %copy.77.vn_ref, bf16[4096,512]{1,0:T(8,128)(2,1)} %bitcast.104, bf16[4096,512]{1,0:T(8,128)(2,1)} %bitcast.16.v_ref), custom_call_target="tpu_custom_call" | custom-call | tf_op jit(solution)/shard_map/pallas_call | solution.py:99
  137.0 2.2 convolution_convert_fusion.1.x_ref
  139.2 12.4 %shard_map.137 = (f32[2,128,512]{2,1,0:T(8,128)}, bf16[128,1024]{1,0:T(8,128)(2,1)}) custom-call(bf16[128,2048]{1,0:T(8,128)(2,1)} %convolution_convert_fusion.1.x_ref, f32[128,2048]{1,0:T(8,128)} %convert_bitcast_fusion.base_ref, f32[1,2048]{1,0:T(1,128)} %bitcast.144), custom_call_target="tpu_custom_call" | custom-call | tf_op jit(solution)/shard_map/pallas_call | solution.py:176
  151.6 1.9 convolution_convert_fusion
  153.6 53.6 %all_to_all.21 = bf16[32,2,24,1024]{3,2,1,0:T(8,128)(2,1)} all-to-all(bf16[32,2,24,1024]{3,2,1,0:T(8,128)(2,1)S(1)} %bitcast.109), channel_id=1, replica_groups=mesh['grp'=32,'head'=4] {'grp'}, dimensions={0} | all-to-all | bytes 6291456 | tf_op jit(solution)/shard_map/all_to_all | solution.py:285
  208.4 1.8 fusion.26
  211.3 2.2 fusion.23
  215.9 2.2 fusion.22
  224.1 1.7 collective-permute-done.1
  226.4 2.0 pad_maximum_fusion
  228.4 6.0 %all-to-all-start.3 = ((bf16[32,2,24,1024]{3,2,1,0:T(8,128)(2,1)}), bf16[32,2,24,1024]{3,2,1,0:T(8,128)(2,1)}, u32[]{:S(2)}, u32[]{:S(2)}) async-start(bf16[32,2,24,1024]{3,2,1,0:T(8,128)(2,1)} %pad_maximum_fusion), calls=%async_computation.3 | async-start | bytes 6291456 | tf_op jit(solution)/shard_map/all_to_all | solution.py:306
  235.7 42.2 %all-to-all-done.3 = bf16[32,2,24,1024]{3,2,1,0:T(8,128)(2,1)} async-done(((bf16[32,2,24,1024]{3,2,1,0:T(8,128)(2,1)}), bf16[32,2,24,1024]{3,2,1,0:T(8,128)(2,1)}, u32[]{:S(2)}, u32[]{:S(2)}) %all-to-all-start.3) | async-done | bytes 3145760 | tf_op jit(solution)/shard_map/all_to_all | solution.py:306
  277.9 3.8 %convolution_reduce_fusion = f32[128,1024]{1,0:T(8,128)S(1)} fusion(bf16[3,128,1536]{2,1,0:T(8,128)(2,1)} %bitcast.138, bf16[1536,1024,1]{1,0,2:T(8,128)(2,1)} %bitcast.50), kind=kOutput, calls=%fused_computation.16 | convolution fusion | flops 1208221696 | bytes 4849664 | tf_op jit(solution)/shard_map/dot_general | solution.py:314
  282.4 6.6 %shard_map.138 = bf16[128,512]{1,0:T(8,128)(2,1)} custom-call(bf16[128,512]{1,0:T(8,128)(2,1)} %select_convert_fusion.x_ref), custom_call_target="tpu_custom_call" | custom-call | tf_op jit(solution)/shard_map/pallas_call | solution.py:47
  (73 shorter events, 21.6 us)
Async XLA Ops:
  0.0 137.0 %copy-start = (bf16[512,2048]{1,0:T(8,128)(2,1)S(1)}, bf16[512,2048]{1,0:T(8,128)(2,1)}, u32[]{:S(2)}) copy-start(bf16[512,2048]{1,0:T(8,128)(2,1)} %param.19) | copy-start | bytes 6291460
  66.8 5.8 %copy-start.9 = (s32[1,128,8]{1,2,0:T(8,128)S(1)}, s32[1,128,8]{1,2,0:T(8,128)}, u32[]{:S(2)}) copy-start(s32[1,128,8]{1,2,0:T(8,128)} %param.23) | copy-start | bytes 12292
  66.8 6.7 %copy-start.10 = (f32[1,128,8]{1,2,0:T(8,128)S(1)}, f32[1,128,8]{1,2,0:T(8,128)}, u32[]{:S(2)}) copy-start(f32[1,128,8]{1,2,0:T(8,128)} %param.24) | copy-start | bytes 12292
  66.8 61.6 %all-to-all-start.1 = ((bf16[32,128,512]{2,1,0:T(8,128)(2,1)}), bf16[32,128,512]{2,1,0:T(8,128)(2,1)}, u32[]{:S(2)}, u32[]{:S(2)}) async-start(bf16[32,128,512]{2,1,0:T(8,128)(2,1)} %get-tuple-element.11), calls=%async_computation.1 | async-start | bytes 8388608 | tf_op jit(solution)/shard_map/all_to_all | solution.py:236
  77.6 4.0 %copy-start.11 = (s32[32]{0:T(128)S(1)}, s32[32]{0:T(128)}, u32[]{:S(2)}) copy-start(s32[32]{0:T(128)} %param.21) | copy-start | bytes 388
  77.6 5.2 %copy-start.2 = (bf16[1,128,2048]{2,1,0:T(8,128)(2,1)S(1)}, bf16[1,128,2048]{2,1,0:T(8,128)(2,1)}, u32[]{:S(2)}) copy-start(bf16[1,128,2048]{2,1,0:T(8,128)(2,1)} %param.14) | copy-start | bytes 1572868
  77.6 5.6 %copy-start.8 = (f32[2048]{0:T(1024)S(1)}, f32[2048]{0:T(1024)}, u32[]{:S(2)}) copy-start(f32[2048]{0:T(1024)} %param.15) | copy-start | bytes 24580
  81.6 4.0 %copy-start.3 = (bf16[512,2048]{1,0:T(8,128)(2,1)S(1)}, bf16[512,2048]{1,0:T(8,128)(2,1)}, u32[]{:S(2)}) copy-start(bf16[512,2048]{1,0:T(8,128)(2,1)} %copy.72) | copy-start | bytes 6291460
  153.6 53.6 %copy-start.5 = (bf16[2,256,2048]{2,1,0:T(8,128)(2,1)S(1)}, bf16[2,256,2048]{2,1,0:T(8,128)(2,1)}, u32[]{:S(2)}) copy-start(bf16[2,256,2048]{2,1,0:T(8,128)(2,1)} %param.27) | copy-start | bytes 6291460
  207.2 8.6 %collective-permute-start = (bf16[32,2,24,1024]{3,2,1,0:T(8,128)(2,1)}, bf16[32,2,24,1024]{3,2,1,0:T(8,128)(2,1)}, u32[]{:S(2)}, u32[]{:S(2)}) collective-permute-start(bf16[32,2,24,1024]{3,2,1,0:T(8,128)(2,1)} %all_to_all.21), channel_id=1, source_target_pairs={{0,1},{1,0},{2,3},{3,2},{4,5},{5,4},{6,7},{7,6},{8,9},{9,8},{10,11... | collective-permute-start | bytes 9437192 | tf_op jit(solution)/shard_map/ppermute | solution.py:287
  208.4 2.2 copy-start.6
  219.9 3.6 %collective-permute-start.2 = (bf16[768,1024]{1,0:T(8,128)(2,1)S(1)}, bf16[768,1024]{1,0:T(8,128)(2,1)S(1)}, u32[]{:S(2)}, u32[]{:S(2)}) collective-permute-start(bf16[768,1024]{1,0:T(8,128)(2,1)S(1)} %convolution_convert_fusion.2), channel_id=1, source_target_pairs={{0,1},{1,0},{2,3},{3,2},{4,5},{5,4},{6,7},{7,6},{8,9},{9,8},{10,11... | collective-permute-start | bytes 4718600 | tf_op jit(solution)/shard_map/ppermute | solution.py:299
  222.3 3.5 %collective-permute-start.1 = (bf16[768,1024]{1,0:T(8,128)(2,1)S(1)}, bf16[768,1024]{1,0:T(8,128)(2,1)S(1)}, u32[]{:S(2)}, u32[]{:S(2)}) collective-permute-start(bf16[768,1024]{1,0:T(8,128)(2,1)S(1)} %convolution_convert_fusion.4), channel_id=1, source_target_pairs={{0,1},{1,0},{2,3},{3,2},{4,5},{5,4},{6,7},{7,6},{8,9},{9,8},{10,11... | collective-permute-start | bytes 4718600 | tf_op jit(solution)/shard_map/ppermute | solution.py:299
  228.4 6.1 %copy-start.4 = (f32[128,1536]{1,0:T(8,128)S(1)}, f32[128,1536]{1,0:T(8,128)}, u32[]{:S(2)}) copy-start(f32[128,1536]{1,0:T(8,128)} %get-tuple-element.10) | copy-start | bytes 2359300
  228.4 49.5 %all-to-all-start.3 = ((bf16[32,2,24,1024]{3,2,1,0:T(8,128)(2,1)}), bf16[32,2,24,1024]{3,2,1,0:T(8,128)(2,1)}, u32[]{:S(2)}, u32[]{:S(2)}) async-start(bf16[32,2,24,1024]{3,2,1,0:T(8,128)(2,1)} %pad_maximum_fusion), calls=%async_computation.3 | async-start | bytes 6291456 | tf_op jit(solution)/shard_map/all_to_all | solution.py:306
  277.9 11.1 %copy-start.7 = (f32[2,128,512]{2,1,0:T(8,128)S(1)}, f32[2,128,512]{2,1,0:T(8,128)}, u32[]{:S(2)}) copy-start(f32[2,128,512]{2,1,0:T(8,128)} %get-tuple-element.7) | copy-start | bytes 1572868
  277.9 12.7 %copy-start.1 = (bf16[512,2048]{1,0:T(8,128)(2,1)S(1)}, bf16[512,2048]{1,0:T(8,128)(2,1)}, u32[]{:S(2)}) copy-start(bf16[512,2048]{1,0:T(8,128)(2,1)} %param.19) | copy-start | bytes 6291460
